TPU v7x, 1024 devices: a whole 8x8x8 slice. The times are simulated.
1024 devices in a mesh: gx: 16 (over y, core), gy: 8 (over x), gz: 8 (over z).
Axes of the slice: x: 8, y: 8, z: 8, core: 2. Of those that a mesh axis runs over, the one named last changes fastest.
Arguments:
- source: float32 [128, 256, 1024], P('gx', 'gy', 'gz'), may hold values from -24 to 24
- conductivity: float32 [128, 256, 1024], P('gx', 'gy', 'gz'), may hold values from 0.2 to 5
Outputs:
- pressure: float32 [128, 256, 1024], P('gx', 'gy', 'gz')
All inputs are finite; a program needn't handle non-finite values.
Results may differ from a plain program's by a relative error of at most 0.00002.
Values sent between devices are 32-bit elements; how exact they have to be, the bound alone decides.
No kernel may reach another device: no remote copies, remote signals or barrier semaphores. Data moves between devices by JAX's collectives and lax.ppermute only.
A program may use at most 64 MiB of HBM per device.

v0:
```python
import math

import jax
import jax.numpy as jnp
from jax import lax
from jax.sharding import PartitionSpec as P

spectrum_top = 1.9
spectrum_low = 0.475
omega_first = 1.0 / (
    (spectrum_top + spectrum_low) / 2 + (spectrum_top - spectrum_low) / 2 * math.cos(math.pi / 4)
)
omega_second = 1.0 / (
    (spectrum_top + spectrum_low) / 2
    + (spectrum_top - spectrum_low) / 2 * math.cos(3 * math.pi / 4)
)
face_pairs = ((0, 1), (0, -1), (1, 1), (1, -1), (2, 1), (2, -1))


def padded_2(cells, sides, width):
    for axis, dim in sides:
        count = lax.axis_size(axis)
        ends = count - 1
        head = lax.slice_in_dim(cells, 0, width, axis=dim)
        tail = lax.slice_in_dim(cells, cells.shape[dim] - width, cells.shape[dim], axis=dim)
        cells = jnp.concatenate(
            [
                lax.ppermute(tail, axis, [(i, (i + 1) % count) for i in range(ends)]),
                cells,
                lax.ppermute(head, axis, [((i + 1) % count, i) for i in range(ends)]),
            ],
            axis=dim,
        )
    return cells


def from_partner(block, axis, stride):
    count = lax.axis_size(axis)
    route = []
    for low in range(count):
        high = low | 1 << stride
        if high != low and high < count:
            route += [(low, high), (high, low)]
    return lax.ppermute(block, axis, route)


def interior(padded):
    return padded[1:-1, 1:-1, 1:-1]


def neighbour(padded, dimension, offset):
    starts = [1, 1, 1]
    limits = [padded.shape[0] - 1, padded.shape[1] - 1, padded.shape[2] - 1]
    starts[dimension] = 1 + offset
    limits[dimension] = padded.shape[dimension] - 1 + offset
    return lax.slice(padded, tuple(starts), tuple(limits))


def diagonal_of(coeff_pad):
    centre = interior(coeff_pad)
    result = jnp.zeros_like(centre)
    for dimension, offset in face_pairs:
        result = result + 0.5 * (centre + neighbour(coeff_pad, dimension, offset))
    return result


def operate(field_pad, coeff_pad):
    centre = interior(coeff_pad)
    values = interior(field_pad)
    result = jnp.zeros_like(centre)
    for dimension, offset in face_pairs:
        weight = 0.5 * (centre + neighbour(coeff_pad, dimension, offset))
        result = result + weight * (values - neighbour(field_pad, dimension, offset))
    return result


def sweep(field, field_pad, coeff_pad, rhs_field, diagonal, omega_value):
    return field + omega_value * (rhs_field - operate(field_pad, coeff_pad)) / diagonal


def restrict_axis(values, dimension):
    cells = (values.shape[dimension] - 2) // 2
    pieces = [
        lax.slice_in_dim(values, start_cell, start_cell + 2 * cells - 1, stride=2, axis=dimension)
        for start_cell in range(4)
    ]
    return (pieces[0] + 3.0 * pieces[1] + 3.0 * pieces[2] + pieces[3]) * 0.125


def restrict(padded):
    return restrict_axis(restrict_axis(restrict_axis(padded, 0), 1), 2)


def interpolate_axis(values, dimension):
    cells = values.shape[dimension] - 2
    lower_side = lax.slice_in_dim(values, 0, cells, axis=dimension)
    centre = lax.slice_in_dim(values, 1, cells + 1, axis=dimension)
    upper_side = lax.slice_in_dim(values, 2, cells + 2, axis=dimension)
    even_cells = 0.75 * centre + 0.25 * lower_side
    odd_cells = 0.75 * centre + 0.25 * upper_side
    paired = jnp.stack([even_cells, odd_cells], axis=dimension + 1)
    new_shape = list(values.shape)
    new_shape[dimension] = 2 * cells
    return paired.reshape(tuple(new_shape))


def interpolate(padded):
    return interpolate_axis(interpolate_axis(interpolate_axis(padded, 0), 1), 2)


def coarsen(values):
    first, second, third = values.shape
    return values.reshape(first // 2, 2, second // 2, 2, third // 2, 2).mean(axis=(1, 3, 5))


def fine_halo(values):
    return padded_2(values, (("gx", 0), ("gy", 1), ("gz", 2)), 1)


def middle_halo(values):
    return padded_2(values, (("gx", 0), ("gy", 1), ("gz", 2)), 1)


def parities():
    return (lax.axis_index("gx") % 2, lax.axis_index("gy") % 2, lax.axis_index("gz") % 2)


def box_rim(values):
    parity_first, parity_second, parity_third = parities()
    third_bits = lax.axis_size("gz").bit_length() - 1
    second_bits = lax.axis_size("gy").bit_length() - 1
    result = values
    for dimension, bit_index, parity in (
        (2, 0, parity_third),
        (1, third_bits, parity_second),
        (0, third_bits + second_bits, parity_first),
    ):
        length = result.shape[dimension]
        first_layer = lax.slice_in_dim(result, 0, 1, axis=dimension)
        last_layer = lax.slice_in_dim(result, length - 1, length, axis=dimension)
        lower_half = parity == 0
        outgoing = jnp.where(lower_half, last_layer, first_layer)
        incoming = from_partner(outgoing, ("gx", "gy", "gz"), bit_index)
        blank = jnp.zeros_like(incoming)
        result = jnp.concatenate(
            [
                jnp.where(lower_half, blank, incoming),
                result,
                jnp.where(lower_half, incoming, blank),
            ],
            axis=dimension,
        )
    return result


def local(source, conductivity):
    coeff_pad = fine_halo(conductivity)
    fine_diag = diagonal_of(coeff_pad)
    pressure = omega_first * source / fine_diag
    pressure = sweep(pressure, fine_halo(pressure), coeff_pad, source, fine_diag, omega_second)
    leftover = source - operate(fine_halo(pressure), coeff_pad)
    middle_rhs = 4.0 * restrict(fine_halo(leftover))
    middle_coeff = coarsen(conductivity)
    middle_pad = middle_halo(middle_coeff)
    middle_diag = diagonal_of(middle_pad)
    middle = omega_first * middle_rhs / middle_diag
    middle = sweep(middle, middle_halo(middle), middle_pad, middle_rhs, middle_diag, omega_second)
    middle_left = middle_rhs - operate(middle_halo(middle), middle_pad)
    coarse_rhs = 4.0 * restrict(middle_halo(middle_left))
    coarse_coeff = coarsen(middle_coeff)
    coarse_pad = box_rim(coarse_coeff)
    coarse_diag = diagonal_of(coarse_pad)
    coarse = omega_first * coarse_rhs / coarse_diag
    coarse = sweep(coarse, box_rim(coarse), coarse_pad, coarse_rhs, coarse_diag, omega_second)
    correction = interpolate(box_rim(coarse))
    middle = middle + correction
    for omega_value in (omega_first, omega_second):
        middle = sweep(
            middle, middle_halo(middle), middle_pad, middle_rhs, middle_diag, omega_value
        )
    pressure = pressure + interpolate(middle_halo(middle))
    for omega_value in (omega_first, omega_second):
        pressure = sweep(pressure, fine_halo(pressure), coeff_pad, source, fine_diag, omega_value)
    return pressure


def solution(mesh):
    in_specs = (P("gx", "gy", "gz"), P("gx", "gy", "gz"))
    out_specs = P("gx", "gy", "gz")
    return jax.shard_map(local, mesh=mesh, in_specs=in_specs, out_specs=out_specs, check_vma=False)
```

profile of v0, /device:TPU:191, one launch (start us, length us, event | category | flops | bytes accessed | tf_op | source)
XLA Modules:
  0.0 404.7 jit_solution(11235734484244944734)
XLA Ops:
  0.7 5.1 %collective-permute-start.1 = (f32[1,32,128]{2,1,0:T(8,128)S(1)}, f32[1,32,128]{2,1,0:T(8,128)S(1)}, u32[]{:S(2)}, u32[]{:S(2)}) collective-permute-start(f32[1,32,128]{2,1,0:T(8,128)S(1)} %get-tuple-element.54), channel_id=1, source_target_pairs={{0,64},{64,128},{128,192},{192,256},{256,320},{320,384},{384,448},... | collective-permute-start | bytes 49160 | tf_op jit(solution)/shard_map/ppermute | solution.py:28
  8.7 3.4 collective-permute-done
  21.6 4.9 %collective-permute-start.5 = (f32[10,34,1]{2,1,0:T(8,128)S(1)}, f32[10,34,1]{2,1,0:T(8,128)S(1)}, u32[]{:S(2)}, u32[]{:S(2)}) collective-permute-start(f32[10,34,1]{2,1,0:T(8,128)S(1)} %get-tuple-element.28), channel_id=1, source_target_pairs={{0,1},{1,2},{2,3},{3,4},{4,5},{5,6},{6,7},{8,9},{9,10},{10,11},{11... | collective-permute-start | bytes 4088 | tf_op jit(solution)/shard_map/ppermute | solution.py:28
  33.4 4.9 %collective-permute-start.7 = (f32[1,32,128]{2,1,0:T(8,128)S(1)}, f32[1,32,128]{2,1,0:T(8,128)S(1)}, u32[]{:S(2)}, u32[]{:S(2)}) collective-permute-start(f32[1,32,128]{2,1,0:T(8,128)S(1)} %get-tuple-element.52), channel_id=1, source_target_pairs={{0,64},{64,128},{128,192},{192,256},{256,320},{320,384},{384,448},... | collective-permute-start | bytes 49160 | tf_op jit(solution)/shard_map/ppermute | solution.py:28
  39.1 3.1 collective-permute-start.8
  46.7 4.9 %collective-permute-start.11 = (f32[10,34,1]{2,1,0:T(8,128)S(1)}, f32[10,34,1]{2,1,0:T(8,128)S(1)}, u32[]{:S(2)}, u32[]{:S(2)}) collective-permute-start(f32[10,34,1]{2,1,0:T(8,128)S(1)} %get-tuple-element.27), channel_id=1, source_target_pairs={{0,1},{1,2},{2,3},{3,4},{4,5},{5,6},{6,7},{8,9},{9,10},{10,11},{11... | collective-permute-start | bytes 4088 | tf_op jit(solution)/shard_map/ppermute | solution.py:28
  53.7 10.5 %reshape.25 = f32[4,2,16,2,64,2]{5,4,3,2,1,0:T(8,128)} reshape(f32[8,32,128]{2,1,0:T(8,128)} %param.3) | data formatting | bytes 262144 | tf_op jit(solution)/shard_map/reshape | solution.py:113
  64.2 4.0 reduce_sum.18
  70.6 7.0 %collective-permute-start.13 = (f32[1,32,128]{2,1,0:T(8,128)S(1)}, f32[1,32,128]{2,1,0:T(8,128)S(1)}, u32[]{:S(2)}, u32[]{:S(2)}) collective-permute-start(f32[1,32,128]{2,1,0:T(8,128)S(1)} %get-tuple-element.50), channel_id=1, source_target_pairs={{0,64},{64,128},{128,192},{192,256},{256,320},{320,384},{384,448},... | collective-permute-start | bytes 49160 | tf_op jit(solution)/shard_map/ppermute | solution.py:28
  78.4 3.1 collective-permute-start.14
  84.7 5.7 %collective-permute-start.25 = (f32[1,16,64]{2,1,0:T(8,128)S(1)}, f32[1,16,64]{2,1,0:T(8,128)S(1)}, u32[]{:S(2)}, u32[]{:S(2)}) collective-permute-start(f32[1,16,64]{2,1,0:T(8,128)S(1)} %get-tuple-element.102), channel_id=1, source_target_pairs={{0,64},{64,128},{128,192},{192,256},{256,320},{320,384},{384,448},... | collective-permute-start | bytes 12296 | tf_op jit(solution)/shard_map/ppermute | solution.py:28
  91.8 6.1 %collective-permute-start.17 = (f32[10,34,1]{2,1,0:T(8,128)S(1)}, f32[10,34,1]{2,1,0:T(8,128)S(1)}, u32[]{:S(2)}, u32[]{:S(2)}) collective-permute-start(f32[10,34,1]{2,1,0:T(8,128)S(1)} %get-tuple-element.25), channel_id=1, source_target_pairs={{0,1},{1,2},{2,3},{3,4},{4,5},{5,6},{6,7},{8,9},{9,10},{10,11},{11... | collective-permute-start | bytes 4088 | tf_op jit(solution)/shard_map/ppermute | solution.py:28
  100.7 5.5 %collective-permute-done.16 = f32[10,34,1]{2,1,0:T(8,128)S(1)} collective-permute-done((f32[10,34,1]{2,1,0:T(8,128)S(1)}, f32[10,34,1]{2,1,0:T(8,128)S(1)}, u32[]{:S(2)}, u32[]{:S(2)}) %collective-permute-start.16) | collective-permute-done | bytes 1392 | tf_op jit(solution)/shard_map/ppermute | solution.py:30
  108.3 4.9 %collective-permute-start.18 = (f32[1,32,128]{2,1,0:T(8,128)S(1)}, f32[1,32,128]{2,1,0:T(8,128)S(1)}, u32[]{:S(2)}, u32[]{:S(2)}) collective-permute-start(f32[1,32,128]{2,1,0:T(8,128)S(1)} %get-tuple-element.48), channel_id=1, source_target_pairs={{0,64},{64,128},{128,192},{192,256},{256,320},{320,384},{384,448},... | collective-permute-start | bytes 49160 | tf_op jit(solution)/shard_map/ppermute | solution.py:28
  113.2 4.3 %collective-permute-start.26 = (f32[6,1,64]{2,1,0:T(1,128)S(1)}, f32[6,1,64]{2,1,0:T(1,128)S(1)}, u32[]{:S(2)}, u32[]{:S(2)}) collective-permute-start(f32[6,1,64]{2,1,0:T(1,128)S(1)} %get-tuple-element.87), channel_id=1, source_target_pairs={{8,0},{16,8},{24,16},{32,24},{40,32},{48,40},{56,48},{9,1},{17,9},... | collective-permute-start | bytes 4616 | tf_op jit(solution)/shard_map/ppermute | solution.py:30
  118.8 4.0 collective-permute-start.21
  129.3 4.9 %collective-permute-start.22 = (f32[10,34,1]{2,1,0:T(8,128)S(1)}, f32[10,34,1]{2,1,0:T(8,128)S(1)}, u32[]{:S(2)}, u32[]{:S(2)}) collective-permute-start(f32[10,34,1]{2,1,0:T(8,128)S(1)} %get-tuple-element.22), channel_id=1, source_target_pairs={{0,1},{1,2},{2,3},{3,4},{4,5},{5,6},{6,7},{8,9},{9,10},{10,11},{11... | collective-permute-start | bytes 4088 | tf_op jit(solution)/shard_map/ppermute | solution.py:28
  136.1 4.6 %collective-permute-start.29 = (f32[6,18,1]{2,1,0:T(8,128)S(1)}, f32[6,18,1]{2,1,0:T(8,128)S(1)}, u32[]{:S(2)}, u32[]{:S(2)}) collective-permute-start(f32[6,18,1]{2,1,0:T(8,128)S(1)} %get-tuple-element.72), channel_id=1, source_target_pairs={{0,1},{1,2},{2,3},{3,4},{4,5},{5,6},{6,7},{8,9},{9,10},{10,11},{11... | collective-permute-start | bytes 1304 | tf_op jit(solution)/shard_map/ppermute | solution.py:28
  145.9 4.8 %collective-permute-start.31 = (f32[1,16,64]{2,1,0:T(8,128)S(1)}, f32[1,16,64]{2,1,0:T(8,128)S(1)}, u32[]{:S(2)}, u32[]{:S(2)}) collective-permute-start(f32[1,16,64]{2,1,0:T(8,128)S(1)} %get-tuple-element.100), channel_id=1, source_target_pairs={{0,64},{64,128},{128,192},{192,256},{256,320},{320,384},{384,448},... | collective-permute-start | bytes 12296 | tf_op jit(solution)/shard_map/ppermute | solution.py:28
  152.7 3.4 collective-permute-start.32
  157.4 3.2 collective-permute-done.33
  160.7 7.6 %collective-permute-start.35 = (f32[6,18,1]{2,1,0:T(8,128)S(1)}, f32[6,18,1]{2,1,0:T(8,128)S(1)}, u32[]{:S(2)}, u32[]{:S(2)}) collective-permute-start(f32[6,18,1]{2,1,0:T(8,128)S(1)} %get-tuple-element.71), channel_id=1, source_target_pairs={{0,1},{1,2},{2,3},{3,4},{4,5},{5,6},{6,7},{8,9},{9,10},{10,11},{11... | collective-permute-start | bytes 1304 | tf_op jit(solution)/shard_map/ppermute | solution.py:28
  170.4 4.1 %collective-permute-done.34 = f32[6,18,1]{2,1,0:T(8,128)S(1)} collective-permute-done((f32[6,18,1]{2,1,0:T(8,128)S(1)}, f32[6,18,1]{2,1,0:T(8,128)S(1)}, u32[]{:S(2)}, u32[]{:S(2)}) %collective-permute-start.34) | collective-permute-done | bytes 464 | tf_op jit(solution)/shard_map/ppermute | solution.py:30
  177.0 4.4 %collective-permute-start.37 = (f32[1,16,64]{2,1,0:T(8,128)S(1)}, f32[1,16,64]{2,1,0:T(8,128)S(1)}, u32[]{:S(2)}, u32[]{:S(2)}) collective-permute-start(f32[1,16,64]{2,1,0:T(8,128)S(1)} %get-tuple-element.98), channel_id=1, source_target_pairs={{0,64},{64,128},{128,192},{192,256},{256,320},{320,384},{384,448},... | collective-permute-start | bytes 12296 | tf_op jit(solution)/shard_map/ppermute | solution.py:28
  181.4 4.4 %collective-permute-start.49 = (f32[2,1,34]{2,1,0:T(1,128)S(1)}, f32[2,1,34]{2,1,0:T(1,128)S(1)}, u32[]{:S(2)}, u32[]{:S(2)}) collective-permute-start(f32[2,1,34]{2,1,0:T(1,128)S(1)} %broadcast_select_fusion.23), channel_id=1, source_target_pairs={{0,8},{8,0},{1,9},{9,1},{2,10},{10,2},{3,11},{11,3},{4,12},{12,4},... | collective-permute-start | bytes 824 | tf_op jit(solution)/shard_map/ppermute | solution.py:44
  189.1 4.2 %collective-permute-done.39 = f32[6,1,64]{2,1,0:T(1,128)S(1)} collective-permute-done((f32[6,1,64]{2,1,0:T(1,128)S(1)}, f32[6,1,64]{2,1,0:T(1,128)S(1)}, u32[]{:S(2)}, u32[]{:S(2)}) %collective-permute-start.39) | collective-permute-done | bytes 1568 | tf_op jit(solution)/shard_map/ppermute | solution.py:28
  193.4 3.6 collective-permute-start.41
  199.3 4.4 %collective-permute-done.40 = f32[6,18,1]{2,1,0:T(8,128)S(1)} collective-permute-done((f32[6,18,1]{2,1,0:T(8,128)S(1)}, f32[6,18,1]{2,1,0:T(8,128)S(1)}, u32[]{:S(2)}, u32[]{:S(2)}) %collective-permute-start.40) | collective-permute-done | bytes 464 | tf_op jit(solution)/shard_map/ppermute | solution.py:30
  205.7 5.6 %collective-permute-start.42 = (f32[1,16,64]{2,1,0:T(8,128)S(1)}, f32[1,16,64]{2,1,0:T(8,128)S(1)}, u32[]{:S(2)}, u32[]{:S(2)}) collective-permute-start(f32[1,16,64]{2,1,0:T(8,128)S(1)} %get-tuple-element.96), channel_id=1, source_target_pairs={{0,64},{64,128},{128,192},{192,256},{256,320},{320,384},{384,448},... | collective-permute-start | bytes 12296 | tf_op jit(solution)/shard_map/ppermute | solution.py:28
  213.3 3.6 collective-permute-start.45
  223.3 3.6 collective-permute-start.46
  238.4 7.0 %collective-permute-start.53 = (f32[1,10,34]{2,0,1:T(1,128)S(1)}, f32[1,10,34]{2,0,1:T(1,128)S(1)}, u32[]{:S(2)}, u32[]{:S(2)}) collective-permute-start(f32[1,10,34]{2,0,1:T(1,128)S(1)} %broadcast_select_fusion.5), channel_id=1, source_target_pairs={{0,64},{64,0},{1,65},{65,1},{2,66},{66,2},{3,67},{67,3},{4,68},{68... | collective-permute-start | bytes 4088 | tf_op jit(solution)/shard_map/ppermute | solution.py:44
  255.4 4.6 %collective-permute-start.56 = (f32[1,10,34]{2,0,1:T(1,128)S(1)}, f32[1,10,34]{2,0,1:T(1,128)S(1)}, u32[]{:S(2)}, u32[]{:S(2)}) collective-permute-start(f32[1,10,34]{2,0,1:T(1,128)S(1)} %broadcast_select_fusion.2), channel_id=1, source_target_pairs={{0,64},{64,0},{1,65},{65,1},{2,66},{66,2},{3,67},{67,3},{4,68},{68... | collective-permute-start | bytes 4088 | tf_op jit(solution)/shard_map/ppermute | solution.py:44
  263.5 4.5 %collective-permute-start.58 = (f32[1,16,64]{2,1,0:T(8,128)S(1)}, f32[1,16,64]{2,1,0:T(8,128)S(1)}, u32[]{:S(2)}, u32[]{:S(2)}) collective-permute-start(f32[1,16,64]{2,1,0:T(8,128)S(1)} %get-tuple-element.92), channel_id=1, source_target_pairs={{0,64},{64,128},{128,192},{192,256},{256,320},{320,384},{384,448},... | collective-permute-start | bytes 12296 | tf_op jit(solution)/shard_map/ppermute | solution.py:28
  276.1 3.7 collective-permute-start.62
  281.8 3.4 collective-permute-done.61
  285.3 4.2 %collective-permute-start.63 = (f32[1,16,64]{2,1,0:T(8,128)S(1)}, f32[1,16,64]{2,1,0:T(8,128)S(1)}, u32[]{:S(2)}, u32[]{:S(2)}) collective-permute-start(f32[1,16,64]{2,1,0:T(8,128)S(1)} %get-tuple-element.91), channel_id=1, source_target_pairs={{64,0},{128,64},{192,128},{256,192},{320,256},{384,320},{448,384},... | collective-permute-start | bytes 12296 | tf_op jit(solution)/shard_map/ppermute | solution.py:30
  289.5 5.9 %collective-permute-start.64 = (f32[1,16,64]{2,1,0:T(8,128)S(1)}, f32[1,16,64]{2,1,0:T(8,128)S(1)}, u32[]{:S(2)}, u32[]{:S(2)}) collective-permute-start(f32[1,16,64]{2,1,0:T(8,128)S(1)} %get-tuple-element.90), channel_id=1, source_target_pairs={{0,64},{64,128},{128,192},{192,256},{256,320},{320,384},{384,448},... | collective-permute-start | bytes 12296 | tf_op jit(solution)/shard_map/ppermute | solution.py:28
  303.3 5.2 %collective-permute-start.68 = (f32[6,18,1]{2,1,0:T(8,128)S(1)}, f32[6,18,1]{2,1,0:T(8,128)S(1)}, u32[]{:S(2)}, u32[]{:S(2)}) collective-permute-start(f32[6,18,1]{2,1,0:T(8,128)S(1)} %get-tuple-element.63), channel_id=1, source_target_pairs={{0,1},{1,2},{2,3},{3,4},{4,5},{5,6},{6,7},{8,9},{9,10},{10,11},{11... | collective-permute-start | bytes 1304 | tf_op jit(solution)/shard_map/ppermute | solution.py:28
  310.5 5.4 %collective-permute-done.67 = f32[6,18,1]{2,1,0:T(8,128)S(1)} collective-permute-done((f32[6,18,1]{2,1,0:T(8,128)S(1)}, f32[6,18,1]{2,1,0:T(8,128)S(1)}, u32[]{:S(2)}, u32[]{:S(2)}) %collective-permute-start.67) | collective-permute-done | bytes 464 | tf_op jit(solution)/shard_map/ppermute | solution.py:30
  318.7 6.5 %collective-permute-start.69 = (f32[1,16,64]{2,1,0:T(8,128)S(1)}, f32[1,16,64]{2,1,0:T(8,128)S(1)}, u32[]{:S(2)}, u32[]{:S(2)}) collective-permute-start(f32[1,16,64]{2,1,0:T(8,128)S(1)} %get-tuple-element.88), channel_id=1, source_target_pairs={{0,64},{64,128},{128,192},{192,256},{256,320},{320,384},{384,448},... | collective-permute-start | bytes 12296 | tf_op jit(solution)/shard_map/ppermute | solution.py:28
  335.2 3.6 collective-permute-start.73
  343.9 7.4 %collective-permute-start.76 = (f32[1,32,128]{2,1,0:T(8,128)S(1)}, f32[1,32,128]{2,1,0:T(8,128)S(1)}, u32[]{:S(2)}, u32[]{:S(2)}) collective-permute-start(f32[1,32,128]{2,1,0:T(8,128)S(1)} %get-tuple-element.44), channel_id=1, source_target_pairs={{0,64},{64,128},{128,192},{192,256},{256,320},{320,384},{384,448},... | collective-permute-start | bytes 49160 | tf_op jit(solution)/shard_map/ppermute | solution.py:28
  359.5 3.6 collective-permute-start.80
  367.2 3.9 collective-permute-done.79
  373.2 6.9 %collective-permute-start.82 = (f32[1,32,128]{2,1,0:T(8,128)S(1)}, f32[1,32,128]{2,1,0:T(8,128)S(1)}, u32[]{:S(2)}, u32[]{:S(2)}) collective-permute-start(f32[1,32,128]{2,1,0:T(8,128)S(1)} %get-tuple-element.42), channel_id=1, source_target_pairs={{0,64},{64,128},{128,192},{192,256},{256,320},{320,384},{384,448},... | collective-permute-start | bytes 49160 | tf_op jit(solution)/shard_map/ppermute | solution.py:28
  388.4 5.2 %collective-permute-start.86 = (f32[10,34,1]{2,1,0:T(8,128)S(1)}, f32[10,34,1]{2,1,0:T(8,128)S(1)}, u32[]{:S(2)}, u32[]{:S(2)}) collective-permute-start(f32[10,34,1]{2,1,0:T(8,128)S(1)} %get-tuple-element.19), channel_id=1, source_target_pairs={{0,1},{1,2},{2,3},{3,4},{4,5},{5,6},{6,7},{8,9},{9,10},{10,11},{11... | collective-permute-start | bytes 4088 | tf_op jit(solution)/shard_map/ppermute | solution.py:28
  398.1 5.8 %collective-permute-done.85 = f32[10,34,1]{2,1,0:T(8,128)S(1)} collective-permute-done((f32[10,34,1]{2,1,0:T(8,128)S(1)}, f32[10,34,1]{2,1,0:T(8,128)S(1)}, u32[]{:S(2)}, u32[]{:S(2)}) %collective-permute-start.85) | collective-permute-done | bytes 1392 | tf_op jit(solution)/shard_map/ppermute | solution.py:30
  (277 shorter events, 168.6 us)
Async XLA Ops:
  0.7 7.0 %collective-permute-start.1 = (f32[1,32,128]{2,1,0:T(8,128)S(1)}, f32[1,32,128]{2,1,0:T(8,128)S(1)}, u32[]{:S(2)}, u32[]{:S(2)}) collective-permute-start(f32[1,32,128]{2,1,0:T(8,128)S(1)} %get-tuple-element.54), channel_id=1, source_target_pairs={{0,64},{64,128},{128,192},{192,256},{256,320},{320,384},{384,448},... | collective-permute-start | bytes 49160 | tf_op jit(solution)/shard_map/ppermute | solution.py:28
  19.7 8.7 %collective-permute-start.4 = (f32[10,34,1]{2,1,0:T(8,128)S(1)}, f32[10,34,1]{2,1,0:T(8,128)S(1)}, u32[]{:S(2)}, u32[]{:S(2)}) collective-permute-start(f32[10,34,1]{2,1,0:T(8,128)S(1)} %get-tuple-element.29), channel_id=1, source_target_pairs={{1,0},{2,1},{3,2},{4,3},{5,4},{6,5},{7,6},{9,8},{10,9},{11,10},{12... | collective-permute-start | bytes 4088 | tf_op jit(solution)/shard_map/ppermute | solution.py:30
  21.6 8.5 %collective-permute-start.5 = (f32[10,34,1]{2,1,0:T(8,128)S(1)}, f32[10,34,1]{2,1,0:T(8,128)S(1)}, u32[]{:S(2)}, u32[]{:S(2)}) collective-permute-start(f32[10,34,1]{2,1,0:T(8,128)S(1)} %get-tuple-element.28), channel_id=1, source_target_pairs={{0,1},{1,2},{2,3},{3,4},{4,5},{5,6},{6,7},{8,9},{9,10},{10,11},{11... | collective-permute-start | bytes 4088 | tf_op jit(solution)/shard_map/ppermute | solution.py:28
  31.4 6.8 %collective-permute-start.6 = (f32[1,32,128]{2,1,0:T(8,128)S(1)}, f32[1,32,128]{2,1,0:T(8,128)S(1)}, u32[]{:S(2)}, u32[]{:S(2)}) collective-permute-start(f32[1,32,128]{2,1,0:T(8,128)S(1)} %get-tuple-element.53), channel_id=1, source_target_pairs={{64,0},{128,64},{192,128},{256,192},{320,256},{384,320},{448,384},... | collective-permute-start | bytes 49160 | tf_op jit(solution)/shard_map/ppermute | solution.py:30
  46.7 21.5 %collective-permute-start.11 = (f32[10,34,1]{2,1,0:T(8,128)S(1)}, f32[10,34,1]{2,1,0:T(8,128)S(1)}, u32[]{:S(2)}, u32[]{:S(2)}) collective-permute-start(f32[10,34,1]{2,1,0:T(8,128)S(1)} %get-tuple-element.27), channel_id=1, source_target_pairs={{0,1},{1,2},{2,3},{3,4},{4,5},{5,6},{6,7},{8,9},{9,10},{10,11},{11... | collective-permute-start | bytes 4088 | tf_op jit(solution)/shard_map/ppermute | solution.py:28
  51.6 16.6 %collective-permute-start.10 = (f32[10,34,1]{2,1,0:T(8,128)S(1)}, f32[10,34,1]{2,1,0:T(8,128)S(1)}, u32[]{:S(2)}, u32[]{:S(2)}) collective-permute-start(f32[10,34,1]{2,1,0:T(8,128)S(1)} %get-tuple-element.26), channel_id=1, source_target_pairs={{1,0},{2,1},{3,2},{4,3},{5,4},{6,5},{7,6},{9,8},{10,9},{11,10},{12... | collective-permute-start | bytes 4088 | tf_op jit(solution)/shard_map/ppermute | solution.py:30
  68.5 9.1 %collective-permute-start.12 = (f32[1,32,128]{2,1,0:T(8,128)S(1)}, f32[1,32,128]{2,1,0:T(8,128)S(1)}, u32[]{:S(2)}, u32[]{:S(2)}) collective-permute-start(f32[1,32,128]{2,1,0:T(8,128)S(1)} %get-tuple-element.51), channel_id=1, source_target_pairs={{64,0},{128,64},{192,128},{256,192},{320,256},{384,320},{448,384},... | collective-permute-start | bytes 49160 | tf_op jit(solution)/shard_map/ppermute | solution.py:30
  70.6 7.8 %collective-permute-start.13 = (f32[1,32,128]{2,1,0:T(8,128)S(1)}, f32[1,32,128]{2,1,0:T(8,128)S(1)}, u32[]{:S(2)}, u32[]{:S(2)}) collective-permute-start(f32[1,32,128]{2,1,0:T(8,128)S(1)} %get-tuple-element.50), channel_id=1, source_target_pairs={{0,64},{64,128},{128,192},{192,256},{256,320},{320,384},{384,448},... | collective-permute-start | bytes 49160 | tf_op jit(solution)/shard_map/ppermute | solution.py:28
  78.4 13.3 %collective-permute-start.14 = (f32[10,1,128]{2,1,0:T(1,128)S(1)}, f32[10,1,128]{2,1,0:T(1,128)S(1)}, u32[]{:S(2)}, u32[]{:S(2)}) collective-permute-start(f32[10,1,128]{2,1,0:T(1,128)S(1)} %get-tuple-element.37), channel_id=1, source_target_pairs={{8,0},{16,8},{24,16},{32,24},{40,32},{48,40},{56,48},{9,1},{17,9},... | collective-permute-start | bytes 15368 | tf_op jit(solution)/shard_map/ppermute | solution.py:30
  81.5 10.2 %collective-permute-start.15 = (f32[10,1,128]{2,1,0:T(1,128)S(1)}, f32[10,1,128]{2,1,0:T(1,128)S(1)}, u32[]{:S(2)}, u32[]{:S(2)}) collective-permute-start(f32[10,1,128]{2,1,0:T(1,128)S(1)} %get-tuple-element.36), channel_id=1, source_target_pairs={{0,8},{8,16},{16,24},{24,32},{32,40},{40,48},{48,56},{1,9},{9,17},... | collective-permute-start | bytes 15368 | tf_op jit(solution)/shard_map/ppermute | solution.py:28
  82.8 30.4 %collective-permute-start.24 = (f32[1,16,64]{2,1,0:T(8,128)S(1)}, f32[1,16,64]{2,1,0:T(8,128)S(1)}, u32[]{:S(2)}, u32[]{:S(2)}) collective-permute-start(f32[1,16,64]{2,1,0:T(8,128)S(1)} %get-tuple-element.103), channel_id=1, source_target_pairs={{64,0},{128,64},{192,128},{256,192},{320,256},{384,320},{448,384},... | collective-permute-start | bytes 12296 | tf_op jit(solution)/shard_map/ppermute | solution.py:30
  84.7 28.4 %collective-permute-start.25 = (f32[1,16,64]{2,1,0:T(8,128)S(1)}, f32[1,16,64]{2,1,0:T(8,128)S(1)}, u32[]{:S(2)}, u32[]{:S(2)}) collective-permute-start(f32[1,16,64]{2,1,0:T(8,128)S(1)} %get-tuple-element.102), channel_id=1, source_target_pairs={{0,64},{64,128},{128,192},{192,256},{256,320},{320,384},{384,448},... | collective-permute-start | bytes 12296 | tf_op jit(solution)/shard_map/ppermute | solution.py:28
  91.8 8.8 %collective-permute-start.17 = (f32[10,34,1]{2,1,0:T(8,128)S(1)}, f32[10,34,1]{2,1,0:T(8,128)S(1)}, u32[]{:S(2)}, u32[]{:S(2)}) collective-permute-start(f32[10,34,1]{2,1,0:T(8,128)S(1)} %get-tuple-element.25), channel_id=1, source_target_pairs={{0,1},{1,2},{2,3},{3,4},{4,5},{5,6},{6,7},{8,9},{9,10},{10,11},{11... | collective-permute-start | bytes 4088 | tf_op jit(solution)/shard_map/ppermute | solution.py:28
  98.0 8.2 %collective-permute-start.16 = (f32[10,34,1]{2,1,0:T(8,128)S(1)}, f32[10,34,1]{2,1,0:T(8,128)S(1)}, u32[]{:S(2)}, u32[]{:S(2)}) collective-permute-start(f32[10,34,1]{2,1,0:T(8,128)S(1)} %get-tuple-element.24), channel_id=1, source_target_pairs={{1,0},{2,1},{3,2},{4,3},{5,4},{6,5},{7,6},{9,8},{10,9},{11,10},{12... | collective-permute-start | bytes 4088 | tf_op jit(solution)/shard_map/ppermute | solution.py:30
  106.4 12.4 %collective-permute-start.19 = (f32[1,32,128]{2,1,0:T(8,128)S(1)}, f32[1,32,128]{2,1,0:T(8,128)S(1)}, u32[]{:S(2)}, u32[]{:S(2)}) collective-permute-start(f32[1,32,128]{2,1,0:T(8,128)S(1)} %get-tuple-element.49), channel_id=1, source_target_pairs={{64,0},{128,64},{192,128},{256,192},{320,256},{384,320},{448,384},... | collective-permute-start | bytes 49160 | tf_op jit(solution)/shard_map/ppermute | solution.py:30
  108.3 10.5 %collective-permute-start.18 = (f32[1,32,128]{2,1,0:T(8,128)S(1)}, f32[1,32,128]{2,1,0:T(8,128)S(1)}, u32[]{:S(2)}, u32[]{:S(2)}) collective-permute-start(f32[1,32,128]{2,1,0:T(8,128)S(1)} %get-tuple-element.48), channel_id=1, source_target_pairs={{0,64},{64,128},{128,192},{192,256},{256,320},{320,384},{384,448},... | collective-permute-start | bytes 49160 | tf_op jit(solution)/shard_map/ppermute | solution.py:28
  113.2 10.9 %collective-permute-start.26 = (f32[6,1,64]{2,1,0:T(1,128)S(1)}, f32[6,1,64]{2,1,0:T(1,128)S(1)}, u32[]{:S(2)}, u32[]{:S(2)}) collective-permute-start(f32[6,1,64]{2,1,0:T(1,128)S(1)} %get-tuple-element.87), channel_id=1, source_target_pairs={{8,0},{16,8},{24,16},{32,24},{40,32},{48,40},{56,48},{9,1},{17,9},... | collective-permute-start | bytes 4616 | tf_op jit(solution)/shard_map/ppermute | solution.py:30
  117.5 6.7 %collective-permute-start.27 = (f32[6,1,64]{2,1,0:T(1,128)S(1)}, f32[6,1,64]{2,1,0:T(1,128)S(1)}, u32[]{:S(2)}, u32[]{:S(2)}) collective-permute-start(f32[6,1,64]{2,1,0:T(1,128)S(1)} %get-tuple-element.86), channel_id=1, source_target_pairs={{0,8},{8,16},{16,24},{24,32},{32,40},{40,48},{48,56},{1,9},{9,17},... | collective-permute-start | bytes 4616 | tf_op jit(solution)/shard_map/ppermute | solution.py:28
  127.3 13.4 %collective-permute-start.23 = (f32[10,34,1]{2,1,0:T(8,128)S(1)}, f32[10,34,1]{2,1,0:T(8,128)S(1)}, u32[]{:S(2)}, u32[]{:S(2)}) collective-permute-start(f32[10,34,1]{2,1,0:T(8,128)S(1)} %get-tuple-element.23), channel_id=1, source_target_pairs={{1,0},{2,1},{3,2},{4,3},{5,4},{6,5},{7,6},{9,8},{10,9},{11,10},{12... | collective-permute-start | bytes 4088 | tf_op jit(solution)/shard_map/ppermute | solution.py:30
  129.3 11.5 %collective-permute-start.22 = (f32[10,34,1]{2,1,0:T(8,128)S(1)}, f32[10,34,1]{2,1,0:T(8,128)S(1)}, u32[]{:S(2)}, u32[]{:S(2)}) collective-permute-start(f32[10,34,1]{2,1,0:T(8,128)S(1)} %get-tuple-element.22), channel_id=1, source_target_pairs={{0,1},{1,2},{2,3},{3,4},{4,5},{5,6},{6,7},{8,9},{9,10},{10,11},{11... | collective-permute-start | bytes 4088 | tf_op jit(solution)/shard_map/ppermute | solution.py:28
  134.2 9.5 %collective-permute-start.28 = (f32[6,18,1]{2,1,0:T(8,128)S(1)}, f32[6,18,1]{2,1,0:T(8,128)S(1)}, u32[]{:S(2)}, u32[]{:S(2)}) collective-permute-start(f32[6,18,1]{2,1,0:T(8,128)S(1)} %get-tuple-element.73), channel_id=1, source_target_pairs={{1,0},{2,1},{3,2},{4,3},{5,4},{6,5},{7,6},{9,8},{10,9},{11,10},{12... | collective-permute-start | bytes 1304 | tf_op jit(solution)/shard_map/ppermute | solution.py:30
  136.1 7.6 %collective-permute-start.29 = (f32[6,18,1]{2,1,0:T(8,128)S(1)}, f32[6,18,1]{2,1,0:T(8,128)S(1)}, u32[]{:S(2)}, u32[]{:S(2)}) collective-permute-start(f32[6,18,1]{2,1,0:T(8,128)S(1)} %get-tuple-element.72), channel_id=1, source_target_pairs={{0,1},{1,2},{2,3},{3,4},{4,5},{5,6},{6,7},{8,9},{9,10},{10,11},{11... | collective-permute-start | bytes 1304 | tf_op jit(solution)/shard_map/ppermute | solution.py:28
  143.9 8.8 %collective-permute-start.30 = (f32[1,16,64]{2,1,0:T(8,128)S(1)}, f32[1,16,64]{2,1,0:T(8,128)S(1)}, u32[]{:S(2)}, u32[]{:S(2)}) collective-permute-start(f32[1,16,64]{2,1,0:T(8,128)S(1)} %get-tuple-element.101), channel_id=1, source_target_pairs={{64,0},{128,64},{192,128},{256,192},{320,256},{384,320},{448,384},... | collective-permute-start | bytes 12296 | tf_op jit(solution)/shard_map/ppermute | solution.py:30
  145.9 6.8 %collective-permute-start.31 = (f32[1,16,64]{2,1,0:T(8,128)S(1)}, f32[1,16,64]{2,1,0:T(8,128)S(1)}, u32[]{:S(2)}, u32[]{:S(2)}) collective-permute-start(f32[1,16,64]{2,1,0:T(8,128)S(1)} %get-tuple-element.100), channel_id=1, source_target_pairs={{0,64},{64,128},{128,192},{192,256},{256,320},{320,384},{384,448},... | collective-permute-start | bytes 12296 | tf_op jit(solution)/shard_map/ppermute | solution.py:28
  150.7 6.7 %collective-permute-start.48 = (f32[2,8,1]{2,1,0:T(8,128)S(1)}, f32[2,8,1]{2,1,0:T(8,128)S(1)}, u32[]{:S(2)}, u32[]{:S(2)}) collective-permute-start(f32[2,8,1]{2,1,0:T(8,128)S(1)} %slice_select_fusion.2), channel_id=1, source_target_pairs={{0,1},{1,0},{2,3},{3,2},{4,5},{5,4},{6,7},{7,6},{8,9},{9,8},{10,11... | collective-permute-start | bytes 200 | tf_op jit(solution)/shard_map/ppermute | solution.py:44
  160.7 9.6 %collective-permute-start.35 = (f32[6,18,1]{2,1,0:T(8,128)S(1)}, f32[6,18,1]{2,1,0:T(8,128)S(1)}, u32[]{:S(2)}, u32[]{:S(2)}) collective-permute-start(f32[6,18,1]{2,1,0:T(8,128)S(1)} %get-tuple-element.71), channel_id=1, source_target_pairs={{0,1},{1,2},{2,3},{3,4},{4,5},{5,6},{6,7},{8,9},{9,10},{10,11},{11... | collective-permute-start | bytes 1304 | tf_op jit(solution)/shard_map/ppermute | solution.py:28
  174.6 11.3 %collective-permute-start.36 = (f32[1,16,64]{2,1,0:T(8,128)S(1)}, f32[1,16,64]{2,1,0:T(8,128)S(1)}, u32[]{:S(2)}, u32[]{:S(2)}) collective-permute-start(f32[1,16,64]{2,1,0:T(8,128)S(1)} %get-tuple-element.99), channel_id=1, source_target_pairs={{64,0},{128,64},{192,128},{256,192},{320,256},{384,320},{448,384},... | collective-permute-start | bytes 12296 | tf_op jit(solution)/shard_map/ppermute | solution.py:30
  177.0 8.9 %collective-permute-start.37 = (f32[1,16,64]{2,1,0:T(8,128)S(1)}, f32[1,16,64]{2,1,0:T(8,128)S(1)}, u32[]{:S(2)}, u32[]{:S(2)}) collective-permute-start(f32[1,16,64]{2,1,0:T(8,128)S(1)} %get-tuple-element.98), channel_id=1, source_target_pairs={{0,64},{64,128},{128,192},{192,256},{256,320},{320,384},{384,448},... | collective-permute-start | bytes 12296 | tf_op jit(solution)/shard_map/ppermute | solution.py:28
  181.4 7.7 %collective-permute-start.49 = (f32[2,1,34]{2,1,0:T(1,128)S(1)}, f32[2,1,34]{2,1,0:T(1,128)S(1)}, u32[]{:S(2)}, u32[]{:S(2)}) collective-permute-start(f32[2,1,34]{2,1,0:T(1,128)S(1)} %broadcast_select_fusion.23), channel_id=1, source_target_pairs={{0,8},{8,0},{1,9},{9,1},{2,10},{10,2},{3,11},{11,3},{4,12},{12,4},... | collective-permute-start | bytes 824 | tf_op jit(solution)/shard_map/ppermute | solution.py:44
  197.1 6.6 %collective-permute-start.40 = (f32[6,18,1]{2,1,0:T(8,128)S(1)}, f32[6,18,1]{2,1,0:T(8,128)S(1)}, u32[]{:S(2)}, u32[]{:S(2)}) collective-permute-start(f32[6,18,1]{2,1,0:T(8,128)S(1)} %get-tuple-element.68), channel_id=1, source_target_pairs={{1,0},{2,1},{3,2},{4,3},{5,4},{6,5},{7,6},{9,8},{10,9},{11,10},{12... | collective-permute-start | bytes 1304 | tf_op jit(solution)/shard_map/ppermute | solution.py:30
  203.8 9.4 %collective-permute-start.43 = (f32[1,16,64]{2,1,0:T(8,128)S(1)}, f32[1,16,64]{2,1,0:T(8,128)S(1)}, u32[]{:S(2)}, u32[]{:S(2)}) collective-permute-start(f32[1,16,64]{2,1,0:T(8,128)S(1)} %get-tuple-element.97), channel_id=1, source_target_pairs={{64,0},{128,64},{192,128},{256,192},{320,256},{384,320},{448,384},... | collective-permute-start | bytes 12296 | tf_op jit(solution)/shard_map/ppermute | solution.py:30
  205.7 7.5 %collective-permute-start.42 = (f32[1,16,64]{2,1,0:T(8,128)S(1)}, f32[1,16,64]{2,1,0:T(8,128)S(1)}, u32[]{:S(2)}, u32[]{:S(2)}) collective-permute-start(f32[1,16,64]{2,1,0:T(8,128)S(1)} %get-tuple-element.96), channel_id=1, source_target_pairs={{0,64},{64,128},{128,192},{192,256},{256,320},{320,384},{384,448},... | collective-permute-start | bytes 12296 | tf_op jit(solution)/shard_map/ppermute | solution.py:28
  211.3 6.9 %collective-permute-start.50 = (f32[1,10,34]{2,0,1:T(1,128)S(1)}, f32[1,10,34]{2,0,1:T(1,128)S(1)}, u32[]{:S(2)}, u32[]{:S(2)}) collective-permute-start(f32[1,10,34]{2,0,1:T(1,128)S(1)} %broadcast_select_fusion.8), channel_id=1, source_target_pairs={{0,64},{64,0},{1,65},{65,1},{2,66},{66,2},{3,67},{67,3},{4,68},{68... | collective-permute-start | bytes 4088 | tf_op jit(solution)/shard_map/ppermute | solution.py:44
  238.4 7.8 %collective-permute-start.53 = (f32[1,10,34]{2,0,1:T(1,128)S(1)}, f32[1,10,34]{2,0,1:T(1,128)S(1)}, u32[]{:S(2)}, u32[]{:S(2)}) collective-permute-start(f32[1,10,34]{2,0,1:T(1,128)S(1)} %broadcast_select_fusion.5), channel_id=1, source_target_pairs={{0,64},{64,0},{1,65},{65,1},{2,66},{66,2},{3,67},{67,3},{4,68},{68... | collective-permute-start | bytes 4088 | tf_op jit(solution)/shard_map/ppermute | solution.py:44
  261.2 6.8 %collective-permute-start.57 = (f32[1,16,64]{2,1,0:T(8,128)S(1)}, f32[1,16,64]{2,1,0:T(8,128)S(1)}, u32[]{:S(2)}, u32[]{:S(2)}) collective-permute-start(f32[1,16,64]{2,1,0:T(8,128)S(1)} %get-tuple-element.93), channel_id=1, source_target_pairs={{64,0},{128,64},{192,128},{256,192},{320,256},{384,320},{448,384},... | collective-permute-start | bytes 12296 | tf_op jit(solution)/shard_map/ppermute | solution.py:30
  285.3 10.1 %collective-permute-start.63 = (f32[1,16,64]{2,1,0:T(8,128)S(1)}, f32[1,16,64]{2,1,0:T(8,128)S(1)}, u32[]{:S(2)}, u32[]{:S(2)}) collective-permute-start(f32[1,16,64]{2,1,0:T(8,128)S(1)} %get-tuple-element.91), channel_id=1, source_target_pairs={{64,0},{128,64},{192,128},{256,192},{320,256},{384,320},{448,384},... | collective-permute-start | bytes 12296 | tf_op jit(solution)/shard_map/ppermute | solution.py:30
  303.3 7.1 %collective-permute-start.68 = (f32[6,18,1]{2,1,0:T(8,128)S(1)}, f32[6,18,1]{2,1,0:T(8,128)S(1)}, u32[]{:S(2)}, u32[]{:S(2)}) collective-permute-start(f32[6,18,1]{2,1,0:T(8,128)S(1)} %get-tuple-element.63), channel_id=1, source_target_pairs={{0,1},{1,2},{2,3},{3,4},{4,5},{5,6},{6,7},{8,9},{9,10},{10,11},{11... | collective-permute-start | bytes 1304 | tf_op jit(solution)/shard_map/ppermute | solution.py:28
  308.6 7.3 %collective-permute-start.67 = (f32[6,18,1]{2,1,0:T(8,128)S(1)}, f32[6,18,1]{2,1,0:T(8,128)S(1)}, u32[]{:S(2)}, u32[]{:S(2)}) collective-permute-start(f32[6,18,1]{2,1,0:T(8,128)S(1)} %get-tuple-element.62), channel_id=1, source_target_pairs={{1,0},{2,1},{3,2},{4,3},{5,4},{6,5},{7,6},{9,8},{10,9},{11,10},{12... | collective-permute-start | bytes 1304 | tf_op jit(solution)/shard_map/ppermute | solution.py:30
  316.0 9.2 %collective-permute-start.70 = (f32[1,16,64]{2,1,0:T(8,128)S(1)}, f32[1,16,64]{2,1,0:T(8,128)S(1)}, u32[]{:S(2)}, u32[]{:S(2)}) collective-permute-start(f32[1,16,64]{2,1,0:T(8,128)S(1)} %get-tuple-element.89), channel_id=1, source_target_pairs={{64,0},{128,64},{192,128},{256,192},{320,256},{384,320},{448,384},... | collective-permute-start | bytes 12296 | tf_op jit(solution)/shard_map/ppermute | solution.py:30
  318.7 7.3 %collective-permute-start.69 = (f32[1,16,64]{2,1,0:T(8,128)S(1)}, f32[1,16,64]{2,1,0:T(8,128)S(1)}, u32[]{:S(2)}, u32[]{:S(2)}) collective-permute-start(f32[1,16,64]{2,1,0:T(8,128)S(1)} %get-tuple-element.88), channel_id=1, source_target_pairs={{0,64},{64,128},{128,192},{192,256},{256,320},{320,384},{384,448},... | collective-permute-start | bytes 12296 | tf_op jit(solution)/shard_map/ppermute | solution.py:28
  341.7 9.6 %collective-permute-start.75 = (f32[1,32,128]{2,1,0:T(8,128)S(1)}, f32[1,32,128]{2,1,0:T(8,128)S(1)}, u32[]{:S(2)}, u32[]{:S(2)}) collective-permute-start(f32[1,32,128]{2,1,0:T(8,128)S(1)} %get-tuple-element.45), channel_id=1, source_target_pairs={{64,0},{128,64},{192,128},{256,192},{320,256},{384,320},{448,384},... | collective-permute-start | bytes 49160 | tf_op jit(solution)/shard_map/ppermute | solution.py:30
  343.9 8.2 %collective-permute-start.76 = (f32[1,32,128]{2,1,0:T(8,128)S(1)}, f32[1,32,128]{2,1,0:T(8,128)S(1)}, u32[]{:S(2)}, u32[]{:S(2)}) collective-permute-start(f32[1,32,128]{2,1,0:T(8,128)S(1)} %get-tuple-element.44), channel_id=1, source_target_pairs={{0,64},{64,128},{128,192},{192,256},{256,320},{320,384},{384,448},... | collective-permute-start | bytes 49160 | tf_op jit(solution)/shard_map/ppermute | solution.py:28
  359.5 7.7 %collective-permute-start.80 = (f32[10,34,1]{2,1,0:T(8,128)S(1)}, f32[10,34,1]{2,1,0:T(8,128)S(1)}, u32[]{:S(2)}, u32[]{:S(2)}) collective-permute-start(f32[10,34,1]{2,1,0:T(8,128)S(1)} %get-tuple-element.21), channel_id=1, source_target_pairs={{0,1},{1,2},{2,3},{3,4},{4,5},{5,6},{6,7},{8,9},{9,10},{10,11},{11... | collective-permute-start | bytes 4088 | tf_op jit(solution)/shard_map/ppermute | solution.py:28
  363.1 8.0 %collective-permute-start.79 = (f32[10,34,1]{2,1,0:T(8,128)S(1)}, f32[10,34,1]{2,1,0:T(8,128)S(1)}, u32[]{:S(2)}, u32[]{:S(2)}) collective-permute-start(f32[10,34,1]{2,1,0:T(8,128)S(1)} %get-tuple-element.20), channel_id=1, source_target_pairs={{1,0},{2,1},{3,2},{4,3},{5,4},{6,5},{7,6},{9,8},{10,9},{11,10},{12... | collective-permute-start | bytes 4088 | tf_op jit(solution)/shard_map/ppermute | solution.py:30
  371.3 8.8 %collective-permute-start.81 = (f32[1,32,128]{2,1,0:T(8,128)S(1)}, f32[1,32,128]{2,1,0:T(8,128)S(1)}, u32[]{:S(2)}, u32[]{:S(2)}) collective-permute-start(f32[1,32,128]{2,1,0:T(8,128)S(1)} %get-tuple-element.43), channel_id=1, source_target_pairs={{64,0},{128,64},{192,128},{256,192},{320,256},{384,320},{448,384},... | collective-permute-start | bytes 49160 | tf_op jit(solution)/shard_map/ppermute | solution.py:30
  373.2 7.7 %collective-permute-start.82 = (f32[1,32,128]{2,1,0:T(8,128)S(1)}, f32[1,32,128]{2,1,0:T(8,128)S(1)}, u32[]{:S(2)}, u32[]{:S(2)}) collective-permute-start(f32[1,32,128]{2,1,0:T(8,128)S(1)} %get-tuple-element.42), channel_id=1, source_target_pairs={{0,64},{64,128},{128,192},{192,256},{256,320},{320,384},{384,448},... | collective-permute-start | bytes 49160 | tf_op jit(solution)/shard_map/ppermute | solution.py:28
  388.4 9.7 %collective-permute-start.86 = (f32[10,34,1]{2,1,0:T(8,128)S(1)}, f32[10,34,1]{2,1,0:T(8,128)S(1)}, u32[]{:S(2)}, u32[]{:S(2)}) collective-permute-start(f32[10,34,1]{2,1,0:T(8,128)S(1)} %get-tuple-element.19), channel_id=1, source_target_pairs={{0,1},{1,2},{2,3},{3,4},{4,5},{5,6},{6,7},{8,9},{9,10},{10,11},{11... | collective-permute-start | bytes 4088 | tf_op jit(solution)/shard_map/ppermute | solution.py:28
  393.6 10.2 %collective-permute-start.85 = (f32[10,34,1]{2,1,0:T(8,128)S(1)}, f32[10,34,1]{2,1,0:T(8,128)S(1)}, u32[]{:S(2)}, u32[]{:S(2)}) collective-permute-start(f32[10,34,1]{2,1,0:T(8,128)S(1)} %get-tuple-element.18), channel_id=1, source_target_pairs={{1,0},{2,1},{3,2},{4,3},{5,4},{6,5},{7,6},{9,8},{10,9},{11,10},{12... | collective-permute-start | bytes 4088 | tf_op jit(solution)/shard_map/ppermute | solution.py:30
  (41 other events, 222.0 us)
where the time goes:
time: 408 us; the launch traced here: 405 us
  starting transfers between devices  276 us (68%)
  waiting for transfers between devices  98.2 us (24%)
  local copies, waits for them, and re-layouts  18.5 us (5%)
  other arithmetic  10 us (2%)
    ppermute x39, starting transfers between devices, padded_2(): lax.ppermute(tail, axis, [(i, (i + 1) % count) for i in range(ends)])  152 us
    ppermute x39, starting transfers between devices, padded_2(): lax.ppermute(head, axis, [((i + 1) % count, i) for i in range(ends)])  95 us
    ppermute x39, waiting for transfers between devices, padded_2(): lax.ppermute(tail, axis, [(i, (i + 1) % count) for i in range(ends)])  51.1 us
    ppermute x39, waiting for transfers between devices, padded_2(): lax.ppermute(head, axis, [((i + 1) % count, i) for i in range(ends)])  37.7 us
    ppermute x9, starting transfers between devices, from_partner(): return lax.ppermute(block, axis, route)  29.3 us
    reshape x1, local copies, waits for them, and re-layouts, coarsen(): values.reshape(first // 2, 2, second // 2, 2, third // 2, 2)  10.5 us
    ppermute x9, waiting for transfers between devices, from_partner(): return lax.ppermute(block, axis, route)  9.43 us
  transfers between devices with their start and end apart: 87, of which 40 were waited for; matrix products, arithmetic and copies ran while one was open for 5% of the time, Pallas kernels for 0%

commit v1 on v0

v1 whole, which is shorter than its diff:
```python
import math

import jax
import jax.numpy as jnp
from jax import lax
from jax.sharding import PartitionSpec as P

spectrum_top = 1.9
spectrum_low = 0.475
mean_value = (spectrum_top + spectrum_low) / 2
half_range = (spectrum_top - spectrum_low) / 2
omega_first = 1.0 / (mean_value + half_range * math.cos(math.pi / 4))
omega_second = 1.0 / (mean_value + half_range * math.cos(3 * math.pi / 4))
HIGHEST = lax.Precision.HIGHEST


def swap(block, axis, outer):
    count = lax.axis_size(axis)
    route = []
    for low in range(1 if outer else 0, count - 1, 2):
        route += [(low, low + 1), (low + 1, low)]
    return lax.ppermute(block, axis, route)


def cut(values, start, stop, dim):
    return lax.slice_in_dim(values, start, stop, axis=dim)


def join(pieces, dim):
    return jnp.concatenate(pieces, axis=dim)


def ahead(values, dim):
    return jnp.roll(values, -1, dim)


def behind(values, dim):
    return jnp.roll(values, 1, dim)


def weights(coeff):
    faces = [0.5 * (coeff + ahead(coeff, dim)) for dim in range(3)]
    diagonal = sum(faces[dim] + behind(faces[dim], dim) for dim in range(3))
    inside = coeff > 0
    inverse = jnp.where(inside, 1.0 / jnp.where(inside, diagonal, 1.0), 0.0)
    return faces, inverse


def operate(field, faces):
    result = 0.0
    for dim in range(3):
        flux = faces[dim] * (field - ahead(field, dim))
        result = result + flux - behind(flux, dim)
    return result


def sweep(field, faces, inverse, rhs, omega):
    return field + omega * (rhs - operate(field, faces)) * inverse


def pre_smooth(faces, inverse, rhs):
    return sweep(omega_first * rhs * inverse, faces, inverse, rhs, omega_second)


def lane_map(rows, columns, entries):
    row = lax.broadcasted_iota(jnp.int32, (rows, columns), 0)
    column = lax.broadcasted_iota(jnp.int32, (rows, columns), 1)
    return entries(row, column).astype(jnp.float32)


def signed(index, size, after):
    return jnp.where(index < after, index, index - size)


def gather_weights(fine, coarse):
    step = fine - 2 * coarse
    return jnp.where((step == 0) | (step == 1), 0.375, jnp.where((step == -1) | (step == 2), 0.125, 0.0))


def mean_weights(fine, coarse):
    step = fine - 2 * coarse
    return jnp.where((step == 0) | (step == 1), 0.5, 0.0)


def spread_weights(coarse, fine):
    step = fine - 2 * coarse
    return jnp.where((step == 0) | (step == 1), 0.75, jnp.where((step == -1) | (step == 2), 0.25, 0.0))


def lanes_dot(values, matrix):
    return lax.dot_general(values, matrix, (((2,), (0,)), ((), ())), precision=HIGHEST)


def halves(values, dim):
    size = values.shape[dim]
    even = lax.slice_in_dim(values, 0, size - 1, stride=2, axis=dim)
    odd = lax.slice_in_dim(values, 1, size, stride=2, axis=dim)
    return even, odd


def restrict_two(values):
    for dim in (0, 1):
        even, odd = halves(values, dim)
        values = 0.375 * (even + odd) + 0.125 * (behind(odd, dim) + ahead(even, dim))
    return values


def mean_two(values):
    for dim in (0, 1):
        even, odd = halves(values, dim)
        values = 0.5 * (even + odd)
    return values


def spread_axis(values, dim):
    even = 0.75 * values + 0.25 * behind(values, dim)
    odd = 0.75 * values + 0.25 * ahead(values, dim)
    paired = jnp.stack([even, odd], axis=dim + 1)
    shape = list(values.shape)
    shape[dim] *= 2
    return paired.reshape(tuple(shape))


def take_lanes(values, matrix):
    rows = values.reshape(-1, values.shape[-1])
    return lax.dot_general(matrix, rows, (((0,), (1,)), ((), ())), precision=HIGHEST)


def put_lanes(strip, matrix, shape):
    rows = lax.dot_general(strip, matrix, (((0,), (0,)), ((), ())), precision=HIGHEST)
    return rows.reshape(shape)


def local(source, conductivity):
    low_x = lax.axis_index("gx") % 2 == 0
    low_y = lax.axis_index("gy") % 2 == 0
    low_z = lax.axis_index("gz") % 2 == 0

    def side(low, when_low, when_high):
        return jnp.where(low, when_low, when_high)

    cells = jnp.stack([source, conductivity])
    near = swap(side(low_x, cells[:, 4:], cells[:, :4]), "gx", False)
    far = swap(side(low_x, join([cells, near[:, :2]], 1), join([near[:, 2:], cells], 1)), "gx", True)
    cells = join([cells, side(low_x, join([near, far], 1), join([far, near], 1))], 1)

    near = swap(side(low_y, cells[:, :, 28:], cells[:, :, :4]), "gy", False)
    far = swap(side(low_y, cells[:, :, :12], cells[:, :, 20:]), "gy", True)
    cells = join([cells, side(low_y, join([near, far], 2), join([far, near], 2))], 2)

    base_near = side(low_z, 124, 0)
    base_far = side(low_z, 0, 118)
    near = swap(take_lanes(cells, lane_map(128, 4, lambda z, k: z == k + base_near)), "gz", False)
    far = swap(take_lanes(cells, lane_map(128, 10, lambda z, k: z == k + base_far)), "gz", True)
    to_near = side(low_z, 0, 124)
    to_far = side(low_z, 118, 0)
    added = put_lanes(near, lane_map(4, 128, lambda k, z: z == k + to_near), (2, 22, 48, 128))
    added = added + put_lanes(far, lane_map(10, 128, lambda k, z: z == k + to_far), (2, 22, 48, 128))
    source_wide, coeff = join([cells, added], 3)

    faces, inverse = weights(coeff)
    pre_pressure = pre_smooth(faces, inverse, source_wide)
    leftover = jnp.where(coeff > 0, source_wide - operate(pre_pressure, faces), 0.0)
    to_middle = lane_map(256, 128, lambda f, c: gather_weights(signed(f, 256, 192), signed(c, 128, 96)))
    mean_middle = lane_map(256, 128, lambda f, c: mean_weights(signed(f, 256, 192), signed(c, 128, 96)))
    middle_rhs = 4.0 * lanes_dot(restrict_two(leftover), to_middle)
    middle_coeff = lanes_dot(mean_two(coeff), mean_middle)

    pair = jnp.stack([middle_rhs, middle_coeff])
    base_near = side(low_z, 52, 0)
    to_near = side(low_z, 64, 116)
    near = swap(take_lanes(pair, lane_map(128, 12, lambda z, k: z == k + base_near)), "gz", False)
    lane = lax.broadcasted_iota(jnp.int32, (1, 1, 1, 128), 3)
    kept = (lane < 64) | side(low_z, lane >= 124, lane < 68)
    pair = jnp.where(kept, pair, put_lanes(near, lane_map(12, 128, lambda k, z: z == k + to_near), pair.shape))

    near = swap(side(low_y, pair[:, :, 4:16], pair[:, :, :12]), "gy", False)
    pair = side(
        low_y,
        join([pair[:, :, :16], near, pair[:, :, 20:]], 2),
        join([pair[:, :, :20], near], 2),
    )
    near = swap(side(low_x, join([pair[:, 7:], pair[:, :4]], 1), pair[:, :8]), "gx", False)
    middle_rhs, middle_coeff = side(
        low_x, join([pair[:, :4], near, pair[:, 7:]], 1), join([pair[:, :8], near], 1)
    )

    faces_m, inverse_m = weights(middle_coeff)
    middle = pre_smooth(faces_m, inverse_m, middle_rhs)
    middle_left = jnp.where(middle_coeff > 0, middle_rhs - operate(middle, faces_m), 0.0)

    def coarse_lane(c):
        return signed(c, 128, 48)

    def middle_lane(m):
        return signed(m, 128, 96)

    to_coarse = lane_map(128, 128, lambda m, c: gather_weights(middle_lane(m), coarse_lane(c)))
    mean_coarse = lane_map(128, 128, lambda m, c: mean_weights(middle_lane(m), coarse_lane(c)))
    from_coarse = lane_map(128, 128, lambda c, m: spread_weights(coarse_lane(c), middle_lane(m)))
    place = [lax.broadcasted_iota(jnp.int32, (8, 16, 128), dim) for dim in range(3)]
    in_box = (
        side(low_x, place[0] < 4, (place[0] < 2) | (place[0] >= 6))
        & side(low_y, place[1] < 14, (place[1] < 8) | (place[1] >= 10))
        & side(low_z, place[2] < 64, (place[2] < 32) | (place[2] >= 64))
    )
    coarse_rhs = jnp.where(in_box, 4.0 * lanes_dot(restrict_two(middle_left), to_coarse), 0.0)
    coarse_coeff = jnp.where(in_box, lanes_dot(mean_two(middle_coeff), mean_coarse), 0.0)
    faces_c, inverse_c = weights(coarse_coeff)
    coarse = pre_smooth(faces_c, inverse_c, coarse_rhs)
    correction = spread_axis(spread_axis(lanes_dot(coarse, from_coarse), 0), 1)
    middle = middle + correction

    def trim(values):
        values = join([values[:8], values[12:]], 0)
        return join([values[:, :20], values[:, 28:]], 1)

    middle = trim(middle)
    base_far = side(low_z, 0, 60)
    to_far = side(low_z, 124, 64)
    far = swap(take_lanes(middle, lane_map(128, 4, lambda z, k: z == k + base_far)), "gz", True)
    lane = lane[0]
    taken = side(low_z, lane >= 124, (lane >= 64) & (lane < 68))
    middle = jnp.where(taken, put_lanes(far, lane_map(4, 128, lambda k, z: z == k + to_far), middle.shape), middle)
    far = swap(side(low_y, middle[:, :4], middle[:, 12:16]), "gy", True)
    middle = side(
        low_y, join([middle[:, :20], far], 1), join([middle[:, :16], far, middle[:, 20:]], 1)
    )
    far = swap(side(low_x, middle[:4], middle[:4]), "gx", True)
    middle = side(low_x, join([middle[:8], far], 0), join([middle[:4], far, middle[8:]], 0))

    middle_rhs = trim(middle_rhs)
    faces_m, inverse_m = weights(trim(middle_coeff))
    middle = sweep(middle, faces_m, inverse_m, middle_rhs, omega_first)
    middle = sweep(middle, faces_m, inverse_m, middle_rhs, omega_second)

    def narrow(values):
        values = join([values[:10], values[20:]], 0)
        return join([values[:, :36], values[:, 44:]], 1)

    middle = join([middle[:6], middle[10:]], 0)
    middle = join([middle[:, :18], middle[:, 22:]], 1)
    to_fine = lane_map(128, 256, lambda c, f: spread_weights(signed(c, 128, 96), signed(f, 256, 192)))
    risen = spread_axis(spread_axis(lanes_dot(middle, to_fine), 0), 1)
    risen = join([risen[:10], risen[14:]], 0)
    coeff = narrow(coeff)
    source_wide = narrow(source_wide)
    faces, inverse = weights(coeff)
    pressure = narrow(pre_pressure) + jnp.where(coeff > 0, risen, 0.0)
    pressure = sweep(pressure, faces, inverse, source_wide, omega_first)
    pressure = sweep(pressure, faces, inverse, source_wide, omega_second)
    return pressure[:8, :32, :128]


def solution(mesh):
    spec = P("gx", "gy", "gz")
    return jax.shard_map(local, mesh=mesh, in_specs=(spec, spec), out_specs=spec, check_vma=False)
```

time: 408 us -> 135 us (0.33)
  the two profiles are of different devices: /device:TPU:191 before, /device:TPU:183 now
where the time goes in v1:
time: 135 us; the launch traced here: 134 us
  starting transfers between devices  49.4 us (37%)
  local copies, waits for them, and re-layouts  28.2 us (21%)
  other arithmetic  25.5 us (19%)
  waiting for transfers between devices  20 us (15%)
  matrix products  8.44 us (6%)
  between operations  2.21 us (2%)
    ppermute x12, starting transfers between devices, swap(): return lax.ppermute(block, axis, route)  49.4 us
    ppermute x12, waiting for transfers between devices, swap(): return lax.ppermute(block, axis, route)  20 us
    slice x73, local copies, waits for them, and re-layouts, ahead(): return jnp.roll(values, -1, dim)  7.52 us
    slice x4, local copies, waits for them, and re-layouts, halves(): odd = lax.slice_in_dim(values, 1, size, stride=2, axis=dim)  5.57 us
    slice x6, local copies, waits for them, and re-layouts, halves(): even = lax.slice_in_dim(values, 0, size - 1, stride=2, axis=dim)  5.05 us
    unnamed x52, local copies, waits for them, and re-layouts  4.43 us
    select_n x15, other arithmetic, side(): return jnp.where(low, when_low, when_high)  4.21 us
    concatenate x23, other arithmetic, join(): return jnp.concatenate(pieces, axis=dim)  4.11 us
  transfers between devices with their start and end apart: 12, of which 11 were waited for; matrix products, arithmetic and copies ran while one was open for 6% of the time, Pallas kernels for 0%

profile of v1, /device:TPU:183, one launch (start us, length us, event | category | flops | bytes accessed | tf_op | source)
XLA Modules:
  0.0 133.8 jit_solution(17971360174312359942)
XLA Ops:
  0.0 1.0 fusion.159
  1.0 2.7 %collective-permute-start = (f32[2,4,32,128]{3,2,1,0:T(8,128)S(1)}, f32[2,4,32,128]{3,2,1,0:T(8,128)S(1)}, u32[]{:S(2)}, u32[]{:S(2)}) collective-permute-start(f32[2,4,32,128]{3,2,1,0:T(8,128)S(1)} %fusion.159), channel_id=1, source_target_pairs={{0,64},{64,0},{128,192},{192,128},{256,320},{320,256},{384,448},{4... | collective-permute-start | bytes 393224 | tf_op jit(solution)/shard_map/ppermute | solution.py:22
  5.6 1.1 maximum_select_fusion.5
  6.8 4.4 %collective-permute-start.1 = (f32[2,10,32,128]{3,2,1,0:T(8,128)S(1)}, f32[2,10,32,128]{3,2,1,0:T(8,128)S(1)}, u32[]{:S(2)}, u32[]{:S(2)}) collective-permute-start(f32[2,10,32,128]{3,2,1,0:T(8,128)S(1)} %maximum_select_fusion.5), channel_id=1, source_target_pairs={{64,128},{128,64},{192,256},{256,192},{320,384},{384,320},{448,512... | collective-permute-start | bytes 983048 | tf_op jit(solution)/shard_map/ppermute | solution.py:22
  12.2 4.1 %collective-permute-done.1 = f32[2,10,32,128]{3,2,1,0:T(8,128)S(1)} collective-permute-done((f32[2,10,32,128]{3,2,1,0:T(8,128)S(1)}, f32[2,10,32,128]{3,2,1,0:T(8,128)S(1)}, u32[]{:S(2)}, u32[]{:S(2)}) %collective-permute-start.1) | collective-permute-done | bytes 327712 | tf_op jit(solution)/shard_map/ppermute | solution.py:22
  16.6 4.3 %collective-permute-start.3 = (f32[2,22,12,128]{3,2,1,0:T(8,128)S(1)}, f32[2,22,12,128]{3,2,1,0:T(8,128)S(1)}, u32[]{:S(2)}, u32[]{:S(2)}) collective-permute-start(f32[2,22,12,128]{3,2,1,0:T(8,128)S(1)} %slice_select_fusion), channel_id=1, source_target_pairs={{8,16},{16,8},{24,32},{32,24},{40,48},{48,40},{9,17},{17,9},{25,33... | collective-permute-start | bytes 811016 | tf_op jit(solution)/shard_map/ppermute | solution.py:22
  21.0 1.9 %collective-permute-start.2 = (f32[2,22,4,128]{3,2,1,0:T(4,128)S(1)}, f32[2,22,4,128]{3,2,1,0:T(4,128)S(1)}, u32[]{:S(2)}, u32[]{:S(2)}) collective-permute-start(f32[2,22,4,128]{3,2,1,0:T(4,128)S(1)} %maximum_select_fusion.9), channel_id=1, source_target_pairs={{0,8},{8,0},{16,24},{24,16},{32,40},{40,32},{48,56},{56,48},{1,9},... | collective-permute-start | bytes 270344 | tf_op jit(solution)/shard_map/ppermute | solution.py:22
  22.9 4.1 %collective-permute-done.2 = f32[2,22,4,128]{3,2,1,0:T(4,128)S(1)} collective-permute-done((f32[2,22,4,128]{3,2,1,0:T(4,128)S(1)}, f32[2,22,4,128]{3,2,1,0:T(4,128)S(1)}, u32[]{:S(2)}, u32[]{:S(2)}) %collective-permute-start.2) | collective-permute-done | bytes 90144 | tf_op jit(solution)/shard_map/ppermute | solution.py:22
  27.1 2.0 %collective-permute-done.3 = f32[2,22,12,128]{3,2,1,0:T(8,128)S(1)} collective-permute-done((f32[2,22,12,128]{3,2,1,0:T(8,128)S(1)}, f32[2,22,12,128]{3,2,1,0:T(8,128)S(1)}, u32[]{:S(2)}, u32[]{:S(2)}) %collective-permute-start.3) | collective-permute-done | bytes 270368 | tf_op jit(solution)/shard_map/ppermute | solution.py:22
  29.9 4.9 %collective-permute-start.5 = (f32[10,2112]{1,0:T(8,128)S(1)}, f32[10,2112]{1,0:T(8,128)S(1)}, u32[]{:S(2)}, u32[]{:S(2)}) collective-permute-start(f32[10,2112]{1,0:T(8,128)S(1)} %fusion.294), channel_id=1, source_target_pairs={{1,2},{2,1},{3,4},{4,3},{5,6},{6,5},{9,10},{10,9},{11,12},{12,11},... | collective-permute-start | bytes 253448 | tf_op jit(solution)/shard_map/ppermute | solution.py:22
  35.4 2.1 %collective-permute-start.4 = (f32[4,2112]{1,0:T(4,128)S(1)}, f32[4,2112]{1,0:T(4,128)S(1)}, u32[]{:S(2)}, u32[]{:S(2)}) collective-permute-start(f32[4,2112]{1,0:T(4,128)S(1)} %fusion.296), channel_id=1, source_target_pairs={{0,1},{1,0},{2,3},{3,2},{4,5},{5,4},{6,7},{7,6},{8,9},{9,8},{10,11... | collective-permute-start | bytes 101384 | tf_op jit(solution)/shard_map/ppermute | solution.py:22
  37.6 1.4 %collective-permute-done.5 = f32[10,2112]{1,0:T(8,128)S(1)} collective-permute-done((f32[10,2112]{1,0:T(8,128)S(1)}, f32[10,2112]{1,0:T(8,128)S(1)}, u32[]{:S(2)}, u32[]{:S(2)}) %collective-permute-start.5) | collective-permute-done | bytes 84512 | tf_op jit(solution)/shard_map/ppermute | solution.py:22
  38.9 1.1 fusion.333
  40.1 1.0 convolution_add_fusion
  42.7 1.0 slice-done
  44.6 1.1 multiply_multiply_fusion
  46.3 0.9 fusion.10
  47.5 1.1 fusion.18
  49.2 0.9 fusion.21
  50.4 1.0 fusion.27
  51.6 1.0 fusion.31
  52.5 2.5 %slice.1022 = f32[11,24,256]{2,1,0:T(8,128)} slice(f32[11,48,256]{2,1,0:T(8,128)} %fusion.31), slice={[0:11:1], [0:47:2], [0:256:1]} | slice | bytes 540672 | tf_op jit(solution)/shard_map/slice | solution.py:96
  55.0 2.5 %slice.1023 = f32[11,24,256]{2,1,0:T(8,128)} slice(f32[11,48,256]{2,1,0:T(8,128)} %fusion.31), slice={[0:11:1], [1:48:2], [0:256:1]} | slice | bytes 540672 | tf_op jit(solution)/shard_map/slice | solution.py:97
  57.4 1.7 %slice.1301 = f32[11,23,256]{2,1,0:T(8,128)} slice(f32[11,24,256]{2,1,0:T(8,128)} %slice.1022), slice={[0:11], [1:24], [0:256]} | slice | bytes 518144 | tf_op jit(solution)/shard_map/jit(_roll_static)/slice | solution.py:34
  59.1 0.9 slice.1302
  60.0 2.1 %add_multiply_fusion = f32[11,48,256]{2,1,0:T(8,128)} fusion(f32[22,48,256]{2,1,0:T(8,128)} %copy-done.1), kind=kLoop, calls=%fused_computation.74 | loop fusion | flops 270336 | bytes 1622016 | tf_op jit(solution)/shard_map/mul | solution.py:111
  62.1 2.5 %slice.1030 = f32[11,24,256]{2,1,0:T(8,128)} slice(f32[11,48,256]{2,1,0:T(8,128)} %add_multiply_fusion), slice={[0:11:1], [0:47:2], [0:256:1]} | slice | bytes 540672 | tf_op jit(solution)/shard_map/slice | solution.py:96
  64.6 2.5 %slice.1031 = f32[11,24,256]{2,1,0:T(8,128)} slice(f32[11,48,256]{2,1,0:T(8,128)} %add_multiply_fusion), slice={[0:11:1], [1:48:2], [0:256:1]} | slice | bytes 540672 | tf_op jit(solution)/shard_map/slice | solution.py:97
  67.0 0.9 maximum_bitcast_fusion
  68.1 0.9 copy-done.21
  70.5 2.2 %collective-permute-start.6 = (f32[12,528]{1,0:T(8,128)S(1)}, f32[12,528]{1,0:T(8,128)S(1)}, u32[]{:S(2)}, u32[]{:S(2)}) collective-permute-start(f32[12,528]{1,0:T(8,128)S(1)} %fusion.290), channel_id=1, source_target_pairs={{0,1},{1,0},{2,3},{3,2},{4,5},{5,4},{6,7},{7,6},{8,9},{9,8},{10,11... | collective-permute-start | bytes 76040 | tf_op jit(solution)/shard_map/ppermute | solution.py:22
  72.7 0.9 fusion.32
  74.4 0.8 collective-permute-done.6
  75.7 1.9 %collective-permute-start.7 = (f32[2,11,12,128]{3,2,1,0:T(8,128)S(1)}, f32[2,11,12,128]{3,2,1,0:T(8,128)S(1)}, u32[]{:S(2)}, u32[]{:S(2)}) collective-permute-start(f32[2,11,12,128]{3,2,1,0:T(8,128)S(1)} %slice_select_fusion.1), channel_id=1, source_target_pairs={{0,8},{8,0},{16,24},{24,16},{32,40},{40,32},{48,56},{56,48},{1,9},... | collective-permute-start | bytes 405512 | tf_op jit(solution)/shard_map/ppermute | solution.py:22
  78.4 0.8 fusion.35
  79.3 2.7 %collective-permute-done.7 = f32[2,11,12,128]{3,2,1,0:T(8,128)S(1)} collective-permute-done((f32[2,11,12,128]{3,2,1,0:T(8,128)S(1)}, f32[2,11,12,128]{3,2,1,0:T(8,128)S(1)}, u32[]{:S(2)}, u32[]{:S(2)}) %collective-permute-start.7) | collective-permute-done | bytes 135200 | tf_op jit(solution)/shard_map/ppermute | solution.py:22
  82.1 5.6 %collective-permute-start.8 = (f32[2,8,32,128]{3,2,1,0:T(8,128)S(1)}, f32[2,8,32,128]{3,2,1,0:T(8,128)S(1)}, u32[]{:S(2)}, u32[]{:S(2)}) collective-permute-start(f32[2,8,32,128]{3,2,1,0:T(8,128)S(1)} %get-tuple-element.60), channel_id=1, source_target_pairs={{0,64},{64,0},{128,192},{192,128},{256,320},{320,256},{384,448},{4... | collective-permute-start | bytes 786440 | tf_op jit(solution)/shard_map/ppermute | solution.py:22
  93.1 1.0 fusion.331
  94.5 1.2 multiply_multiply_fusion.2
  97.3 7.4 %collective-permute-start.9 = (f32[4,288]{1,0:T(4,128)S(1)}, f32[4,288]{1,0:T(4,128)S(1)}, u32[]{:S(2)}, u32[]{:S(2)}) collective-permute-start(f32[4,288]{1,0:T(4,128)S(1)} %fusion.292), channel_id=1, source_target_pairs={{1,2},{2,1},{3,4},{4,3},{5,6},{6,5},{9,10},{10,9},{11,12},{12,11},... | collective-permute-start | bytes 13832 | tf_op jit(solution)/shard_map/ppermute | solution.py:22
  104.8 1.0 collective-permute-done.9
  106.1 4.3 %collective-permute-start.10 = (f32[12,4,128]{2,1,0:T(4,128)S(1)}, f32[12,4,128]{2,1,0:T(4,128)S(1)}, u32[]{:S(2)}, u32[]{:S(2)}) collective-permute-start(f32[12,4,128]{2,1,0:T(4,128)S(1)} %get-tuple-element.93), channel_id=1, source_target_pairs={{8,16},{16,8},{24,32},{32,24},{40,48},{48,40},{9,17},{17,9},{25,33... | collective-permute-start | bytes 73736 | tf_op jit(solution)/shard_map/ppermute | solution.py:22
  110.5 1.4 %collective-permute-done.10 = f32[12,4,128]{2,1,0:T(4,128)S(1)} collective-permute-done((f32[12,4,128]{2,1,0:T(4,128)S(1)}, f32[12,4,128]{2,1,0:T(4,128)S(1)}, u32[]{:S(2)}, u32[]{:S(2)}) %collective-permute-start.10) | collective-permute-done | bytes 24608 | tf_op jit(solution)/shard_map/ppermute | solution.py:22
  112.0 7.6 %collective-permute-start.11 = (f32[4,24,128]{2,1,0:T(8,128)S(1)}, f32[4,24,128]{2,1,0:T(8,128)S(1)}, u32[]{:S(2)}, u32[]{:S(2)}) collective-permute-start(f32[4,24,128]{2,1,0:T(8,128)S(1)} %get-tuple-element.91), channel_id=1, source_target_pairs={{64,128},{128,64},{192,256},{256,192},{320,384},{384,320},{448,512... | collective-permute-start | bytes 147464 | tf_op jit(solution)/shard_map/ppermute | solution.py:22
  119.6 1.5 %collective-permute-done.11 = f32[4,24,128]{2,1,0:T(8,128)S(1)} collective-permute-done((f32[4,24,128]{2,1,0:T(8,128)S(1)}, f32[4,24,128]{2,1,0:T(8,128)S(1)}, u32[]{:S(2)}, u32[]{:S(2)}) %collective-permute-start.11) | collective-permute-done | bytes 49184 | tf_op jit(solution)/shard_map/ppermute | solution.py:22
  123.8 0.9 slice_bitcast_fusion.6
  125.2 1.2 fusion.67
  128.9 0.9 copy-done.7
  (322 shorter events, 28.8 us)
Async XLA Ops:
  1.0 15.5 %copy-start.4 = (f32[8,32,128]{2,1,0:T(8,128)S(1)}, f32[8,32,128]{2,1,0:T(8,128)}, u32[]{:S(2)}) copy-start(f32[8,32,128]{2,1,0:T(8,128)} %param.2) | copy-start | bytes 393220
  1.0 15.5 %copy-start.5 = (f32[8,32,128]{2,1,0:T(8,128)S(1)}, f32[8,32,128]{2,1,0:T(8,128)}, u32[]{:S(2)}) copy-start(f32[8,32,128]{2,1,0:T(8,128)} %param.3) | copy-start | bytes 393220
  1.0 4.6 %collective-permute-start = (f32[2,4,32,128]{3,2,1,0:T(8,128)S(1)}, f32[2,4,32,128]{3,2,1,0:T(8,128)S(1)}, u32[]{:S(2)}, u32[]{:S(2)}) collective-permute-start(f32[2,4,32,128]{3,2,1,0:T(8,128)S(1)} %fusion.159), channel_id=1, source_target_pairs={{0,64},{64,0},{128,192},{192,128},{256,320},{320,256},{384,448},{4... | collective-permute-start | bytes 393224 | tf_op jit(solution)/shard_map/ppermute | solution.py:22
  6.8 9.6 %collective-permute-start.1 = (f32[2,10,32,128]{3,2,1,0:T(8,128)S(1)}, f32[2,10,32,128]{3,2,1,0:T(8,128)S(1)}, u32[]{:S(2)}, u32[]{:S(2)}) collective-permute-start(f32[2,10,32,128]{3,2,1,0:T(8,128)S(1)} %maximum_select_fusion.5), channel_id=1, source_target_pairs={{64,128},{128,64},{192,256},{256,192},{320,384},{384,320},{448,512... | collective-permute-start | bytes 983048 | tf_op jit(solution)/shard_map/ppermute | solution.py:22
  16.5 26.1 %copy-start = (f32[2,14,32,128]{3,2,1,0:T(8,128)}, f32[2,14,32,128]{3,2,1,0:T(8,128)S(1)}, u32[]{:S(2)}) copy-start(f32[2,14,32,128]{3,2,1,0:T(8,128)S(1)} %maximum_select_fusion.2) | copy-start | bytes 1376260
  16.6 12.5 %collective-permute-start.3 = (f32[2,22,12,128]{3,2,1,0:T(8,128)S(1)}, f32[2,22,12,128]{3,2,1,0:T(8,128)S(1)}, u32[]{:S(2)}, u32[]{:S(2)}) collective-permute-start(f32[2,22,12,128]{3,2,1,0:T(8,128)S(1)} %slice_select_fusion), channel_id=1, source_target_pairs={{8,16},{16,8},{24,32},{32,24},{40,48},{48,40},{9,17},{17,9},{25,33... | collective-permute-start | bytes 811016 | tf_op jit(solution)/shard_map/ppermute | solution.py:22
  21.0 6.1 %collective-permute-start.2 = (f32[2,22,4,128]{3,2,1,0:T(4,128)S(1)}, f32[2,22,4,128]{3,2,1,0:T(4,128)S(1)}, u32[]{:S(2)}, u32[]{:S(2)}) collective-permute-start(f32[2,22,4,128]{3,2,1,0:T(4,128)S(1)} %maximum_select_fusion.9), channel_id=1, source_target_pairs={{0,8},{8,0},{16,24},{24,16},{32,40},{40,32},{48,56},{56,48},{1,9},... | collective-permute-start | bytes 270344 | tf_op jit(solution)/shard_map/ppermute | solution.py:22
  29.2 13.4 %copy-start.3 = (f32[2,22,16,128]{3,2,1,0:T(8,128)}, f32[2,22,16,128]{3,2,1,0:T(8,128)S(1)}, u32[]{:S(2)}) copy-start(f32[2,22,16,128]{3,2,1,0:T(8,128)S(1)} %maximum_select_fusion.3) | copy-start | bytes 1081348
  29.9 9.0 %collective-permute-start.5 = (f32[10,2112]{1,0:T(8,128)S(1)}, f32[10,2112]{1,0:T(8,128)S(1)}, u32[]{:S(2)}, u32[]{:S(2)}) collective-permute-start(f32[10,2112]{1,0:T(8,128)S(1)} %fusion.294), channel_id=1, source_target_pairs={{1,2},{2,1},{3,4},{4,3},{5,6},{6,5},{9,10},{10,9},{11,12},{12,11},... | collective-permute-start | bytes 253448 | tf_op jit(solution)/shard_map/ppermute | solution.py:22
  35.4 4.7 %collective-permute-start.4 = (f32[4,2112]{1,0:T(4,128)S(1)}, f32[4,2112]{1,0:T(4,128)S(1)}, u32[]{:S(2)}, u32[]{:S(2)}) collective-permute-start(f32[4,2112]{1,0:T(4,128)S(1)} %fusion.296), channel_id=1, source_target_pairs={{0,1},{1,0},{2,3},{3,2},{4,5},{5,4},{6,7},{7,6},{8,9},{9,8},{10,11... | collective-permute-start | bytes 101384 | tf_op jit(solution)/shard_map/ppermute | solution.py:22
  41.2 1.4 %copy-start.2 = (f32[2112,128]{1,0:T(8,128)}, f32[2112,128]{1,0:T(8,128)S(1)}, u32[]{:S(2)}) copy-start(f32[2112,128]{1,0:T(8,128)S(1)} %convolution_add_fusion) | copy-start | bytes 3244036
  41.5 1.1 copy-start.1
  42.6 1.0 slice-start
  67.9 4.7 %copy-start.13 = (f32[2,48,256]{2,1,0:T(8,128)}, f32[2,48,256]{2,1,0:T(8,128)S(1)}, u32[]{:S(2)}) copy-start(f32[2,48,256]{2,1,0:T(8,128)S(1)} %get-tuple-element.35) | copy-start | bytes 294916
  67.9 4.7 %copy-start.19 = (f32[2,48,256]{2,1,0:T(8,128)}, f32[2,48,256]{2,1,0:T(8,128)S(1)}, u32[]{:S(2)}) copy-start(f32[2,48,256]{2,1,0:T(8,128)S(1)} %get-tuple-element.34) | copy-start | bytes 294916
  67.9 1.0 copy-start.21
  67.9 1.1 copy-start.16
  68.0 1.2 copy-start.17
  68.0 1.6 %copy-start.15 = (f32[11,24,256]{2,1,0:T(8,128)S(1)}, f32[11,24,256]{2,1,0:T(8,128)}, u32[]{:S(2)}) copy-start(f32[11,24,256]{2,1,0:T(8,128)} %slice.1022) | copy-start | bytes 811012
  68.0 1.6 %copy-start.22 = (f32[11,23,256]{2,1,0:T(8,128)S(1)}, f32[11,23,256]{2,1,0:T(8,128)}, u32[]{:S(2)}) copy-start(f32[11,23,256]{2,1,0:T(8,128)} %slice.1301) | copy-start | bytes 777220
  69.0 3.7 %copy-start.6 = (f32[10,48,256]{2,1,0:T(8,128)}, f32[10,48,256]{2,1,0:T(8,128)S(1)}, u32[]{:S(2)}) copy-start(f32[10,48,256]{2,1,0:T(8,128)S(1)} %get-tuple-element.33) | copy-start | bytes 1474564
  69.0 3.7 %copy-start.8 = (f32[10,48,256]{2,1,0:T(8,128)}, f32[10,48,256]{2,1,0:T(8,128)S(1)}, u32[]{:S(2)}) copy-start(f32[10,48,256]{2,1,0:T(8,128)S(1)} %get-tuple-element.32) | copy-start | bytes 1474564
  70.5 4.8 %collective-permute-start.6 = (f32[12,528]{1,0:T(8,128)S(1)}, f32[12,528]{1,0:T(8,128)S(1)}, u32[]{:S(2)}, u32[]{:S(2)}) collective-permute-start(f32[12,528]{1,0:T(8,128)S(1)} %fusion.290), channel_id=1, source_target_pairs={{0,1},{1,0},{2,3},{3,2},{4,5},{5,4},{6,7},{7,6},{8,9},{9,8},{10,11... | collective-permute-start | bytes 76040 | tf_op jit(solution)/shard_map/ppermute | solution.py:22
  73.6 2.1 %copy-start.25 = (pred[128]{0:T(512)(128)(4,1)S(1)}, pred[128]{0:T(512)(128)(4,1)}, u32[]{:S(2)}) copy-start(pred[128]{0:T(512)(128)(4,1)} %select_or_fusion) | copy-start | bytes 388
  75.7 6.2 %collective-permute-start.7 = (f32[2,11,12,128]{3,2,1,0:T(8,128)S(1)}, f32[2,11,12,128]{3,2,1,0:T(8,128)S(1)}, u32[]{:S(2)}, u32[]{:S(2)}) collective-permute-start(f32[2,11,12,128]{3,2,1,0:T(8,128)S(1)} %slice_select_fusion.1), channel_id=1, source_target_pairs={{0,8},{8,0},{16,24},{24,16},{32,40},{40,32},{48,56},{56,48},{1,9},... | collective-permute-start | bytes 405512 | tf_op jit(solution)/shard_map/ppermute | solution.py:22
  82.1 6.7 %collective-permute-start.8 = (f32[2,8,32,128]{3,2,1,0:T(8,128)S(1)}, f32[2,8,32,128]{3,2,1,0:T(8,128)S(1)}, u32[]{:S(2)}, u32[]{:S(2)}) collective-permute-start(f32[2,8,32,128]{3,2,1,0:T(8,128)S(1)} %get-tuple-element.60), channel_id=1, source_target_pairs={{0,64},{64,0},{128,192},{192,128},{256,320},{320,256},{384,448},{4... | collective-permute-start | bytes 786440 | tf_op jit(solution)/shard_map/ppermute | solution.py:22
  91.6 1.5 %copy-start.24 = (pred[128]{0:T(512)(128)(4,1)S(1)}, pred[128]{0:T(512)(128)(4,1)}, u32[]{:S(2)}) copy-start(pred[128]{0:T(512)(128)(4,1)} %get-tuple-element.120) | copy-start | bytes 388
  93.1 1.3 copy-start.23
  97.3 8.4 %collective-permute-start.9 = (f32[4,288]{1,0:T(4,128)S(1)}, f32[4,288]{1,0:T(4,128)S(1)}, u32[]{:S(2)}, u32[]{:S(2)}) collective-permute-start(f32[4,288]{1,0:T(4,128)S(1)} %fusion.292), channel_id=1, source_target_pairs={{1,2},{2,1},{3,4},{4,3},{5,6},{6,5},{9,10},{10,9},{11,12},{12,11},... | collective-permute-start | bytes 13832 | tf_op jit(solution)/shard_map/ppermute | solution.py:22
  106.1 5.8 %collective-permute-start.10 = (f32[12,4,128]{2,1,0:T(4,128)S(1)}, f32[12,4,128]{2,1,0:T(4,128)S(1)}, u32[]{:S(2)}, u32[]{:S(2)}) collective-permute-start(f32[12,4,128]{2,1,0:T(4,128)S(1)} %get-tuple-element.93), channel_id=1, source_target_pairs={{8,16},{16,8},{24,32},{32,24},{40,48},{48,40},{9,17},{17,9},{25,33... | collective-permute-start | bytes 73736 | tf_op jit(solution)/shard_map/ppermute | solution.py:22
  112.0 9.1 %collective-permute-start.11 = (f32[4,24,128]{2,1,0:T(8,128)S(1)}, f32[4,24,128]{2,1,0:T(8,128)S(1)}, u32[]{:S(2)}, u32[]{:S(2)}) collective-permute-start(f32[4,24,128]{2,1,0:T(8,128)S(1)} %get-tuple-element.91), channel_id=1, source_target_pairs={{64,128},{128,64},{192,256},{256,192},{320,384},{384,320},{448,512... | collective-permute-start | bytes 147464 | tf_op jit(solution)/shard_map/ppermute | solution.py:22
  127.4 1.0 copy-start.12
  127.4 1.1 copy-start.18
  128.8 1.0 copy-start.7
  128.8 1.2 copy-start.11
  128.8 1.2 copy-start.14
  130.0 0.9 copy-start.20
  130.2 1.0 copy-start.9
  130.2 1.2 copy-start.10

commit v2 on v1

v2 whole, which is shorter than its diff:
```python
import math

import jax
import jax.numpy as jnp
from jax import lax
from jax.experimental import pallas as pl
from jax.experimental.pallas import tpu as pltpu
from jax.sharding import PartitionSpec as P

spectrum_top = 1.9
spectrum_low = 0.475
mean_value = (spectrum_top + spectrum_low) / 2
half_range = (spectrum_top - spectrum_low) / 2
omega_first = 1.0 / (mean_value + half_range * math.cos(math.pi / 4))
omega_second = 1.0 / (mean_value + half_range * math.cos(3 * math.pi / 4))
HIGHEST = lax.Precision.HIGHEST


def swap(block, axis, outer):
    count = lax.axis_size(axis)
    route = []
    for low in range(1 if outer else 0, count - 1, 2):
        route += [(low, low + 1), (low + 1, low)]
    return lax.ppermute(block, axis, route)


def cut(values, start, stop, dim):
    return lax.slice_in_dim(values, start, stop, axis=dim)


def join(pieces, dim):
    return jnp.concatenate(pieces, axis=dim)


def turn(plane, dim, step):
    return pltpu.roll(plane, -step % plane.shape[dim], dim)


class Operator:
    def __init__(self, count, faces):
        self.count = count
        self.faces = faces

    def build(self, coeff, take):
        before = 0.5 * (coeff(self.count - 1) + coeff(0))
        for i in range(self.count):
            here = coeff(i)
            across = 0.5 * (here + coeff((i + 1) % self.count))
            rows = 0.5 * (here + turn(here, 0, 1))
            lanes = 0.5 * (here + turn(here, 1, 1))
            for place, face in enumerate((across, rows, lanes)):
                self.faces[place, i] = face
            diagonal = (across + before) + (rows + turn(rows, 0, -1)) + (lanes + turn(lanes, 1, -1))
            inside = here > 0
            take(i, jnp.where(inside, 1.0 / jnp.where(inside, diagonal, 1.0), 0.0))
            before = across

    def apply(self, field, take):
        last = self.count - 1
        before = self.faces[0, last] * (field[last] - field[0])
        for i in range(self.count):
            here = field[i]
            across = self.faces[0, i] * (here - field[(i + 1) % self.count])
            rows = self.faces[1, i] * (here - turn(here, 0, 1))
            lanes = self.faces[2, i] * (here - turn(here, 1, 1))
            take(i, (across - before) + (rows - turn(rows, 0, -1)) + (lanes - turn(lanes, 1, -1)))
            before = across


def sweep(operator, field, inverse, rhs, omega, store):
    def take(i, applied):
        store(i, field[i] + (omega * (rhs(i) - applied)) * inverse[i])

    operator.apply(field, take)


def halve_rows(piece, weights):
    count = piece.shape[0] // 2
    even = piece[pl.ds(0, count, 2), :]
    odd = piece[pl.ds(1, count, 2), :]
    if not weights:
        return even + odd
    return 0.375 * (even + odd) + 0.125 * (turn(odd, 0, -1) + turn(even, 0, 1))


def product(values, matrix):
    return jnp.dot(values, matrix, precision=HIGHEST, preferred_element_type=jnp.float32)


def lane_map(rows, columns, entries):
    row = lax.broadcasted_iota(jnp.int32, (rows, columns), 0)
    column = lax.broadcasted_iota(jnp.int32, (rows, columns), 1)
    return entries(row, column).astype(jnp.float32)


def signed(index, size, after):
    return jnp.where(index < after, index, index - size)


def gather_weights(fine, coarse):
    step = fine - 2 * coarse
    return jnp.where((step == 0) | (step == 1), 0.375, jnp.where((step == -1) | (step == 2), 0.125, 0.0))


def mean_weights(fine, coarse):
    step = fine - 2 * coarse
    return jnp.where((step == 0) | (step == 1), 0.5, 0.0)


def spread_weights(coarse, fine):
    step = fine - 2 * coarse
    return jnp.where((step == 0) | (step == 1), 0.75, jnp.where((step == -1) | (step == 2), 0.25, 0.0))


def fine_lane(f):
    return signed(f, 256, 192)


def middle_lane(m):
    return signed(m, 128, 96)


def coarse_lane(c):
    return signed(c, 128, 48)


def fine_plane(cells, added, kind, i):
    return jnp.concatenate([cells[kind, i], added[kind, i]], axis=1)


def restrict_planes(plane, j, count):
    return 0.375 * (plane[2 * j] + plane[2 * j + 1]) + 0.125 * (
        plane[(2 * j - 1) % count] + plane[(2 * j + 2) % count]
    )


def fine_kernel(cells, added, pair, pressure, faces, inverse, field, other, piece, packed):
    def coeff(i):
        return fine_plane(cells, added, 1, i)

    def rhs(i):
        return fine_plane(cells, added, 0, i)

    operator = Operator(22, faces)

    def begin(i, value):
        inverse[i] = value
        field[i] = omega_first * rhs(i) * value

    operator.build(coeff, begin)

    def store(i, value):
        other[i] = value
        if i < 10:
            pressure[i] = value
        elif i >= 20:
            pressure[i - 10] = value

    sweep(operator, field, inverse, rhs, omega_second, store)

    def leave(i, applied):
        field[i] = jnp.where(coeff(i) > 0, rhs(i) - applied, 0.0)

    operator.apply(other, leave)
    for j in range(11):
        planes = (restrict_planes(field, j, 22), coeff(2 * j) + coeff(2 * j + 1))
        for kind in range(2):
            for half in range(2):
                slot = piece.at[(2 * j + kind) * 2 + half]
                slot[...] = planes[kind][:, 128 * half : 128 * half + 128]
                packed[kind, pl.ds(24 * j, 24), pl.ds(128 * half, 128)] = halve_rows(slot, kind == 0)
    matrices = (
        lane_map(256, 128, lambda f, c: 4.0 * gather_weights(fine_lane(f), middle_lane(c))),
        lane_map(256, 128, lambda f, c: 0.25 * mean_weights(fine_lane(f), middle_lane(c))),
    )
    for kind in range(2):
        result = product(packed[kind], matrices[kind])
        for j in range(11):
            pair[kind, j] = result[24 * j : 24 * j + 24]


def box_kernel(pair, box, corrected, faces, inverse, field, other, piece, packed, low, low_faces, low_inverse, risen):
    def coeff(i):
        return pair[1, i]

    def rhs(i):
        return pair[0, i]

    operator = Operator(16, faces)

    def begin(i, value):
        inverse[i] = value
        field[i] = omega_first * rhs(i) * value

    operator.build(coeff, begin)

    def store(i, value):
        other[i] = value

    sweep(operator, field, inverse, rhs, omega_second, store)

    def leave(i, applied):
        field[i] = jnp.where(coeff(i) > 0, rhs(i) - applied, 0.0)

    operator.apply(other, leave)
    for j in range(8):
        planes = (restrict_planes(field, j, 16), coeff(2 * j) + coeff(2 * j + 1))
        for kind in range(2):
            slot = piece.at[2 * j + kind]
            slot[...] = planes[kind]
            packed[kind, pl.ds(16 * j, 16), :] = halve_rows(slot, kind == 0)
    matrices = (
        lane_map(128, 128, lambda m, c: 4.0 * gather_weights(middle_lane(m), coarse_lane(c))),
        lane_map(128, 128, lambda m, c: 0.25 * mean_weights(middle_lane(m), coarse_lane(c))),
    )
    for kind in range(2):
        result = product(packed[kind], matrices[kind])
        for j in range(8):
            low[kind, j] = result[16 * j : 16 * j + 16] * box[j]

    coarse = Operator(8, low_faces)

    def begin_low(i, value):
        low_inverse[i] = value
        low[2, i] = omega_first * low[0, i] * value

    coarse.build(lambda i: low[1, i], begin_low)

    def store_low(i, value):
        packed[0, pl.ds(16 * i, 16), :] = value

    sweep(coarse, low.at[2], low_inverse, lambda i: low[0, i], omega_second, store_low)
    result = product(
        packed[0], lane_map(128, 128, lambda c, m: spread_weights(coarse_lane(c), middle_lane(m)))
    )
    for j in range(8):
        spread_rows(result[16 * j : 16 * j + 16], risen.at[j])
    for place in range(12):
        i = place if place < 8 else place + 4
        near = (i // 2 + (1 if i % 2 else -1)) % 8
        corrected[place] = other[i] + (0.75 * risen[i // 2] + 0.25 * risen[near])


def spread_rows(values, target):
    count = values.shape[0]
    target[pl.ds(0, count, 2), :] = 0.75 * values + 0.25 * turn(values, 0, -1)
    target[pl.ds(1, count, 2), :] = 0.75 * values + 0.25 * turn(values, 0, 1)


def last_kernel(middle, pair, cells, added, pre, out, faces, inverse, field, faces_m, inverse_m, field_m, packed, risen):
    def coeff_m(i):
        return pair[1, i if i < 8 else i + 4]

    def rhs_m(i):
        return pair[0, i if i < 8 else i + 4]

    operator = Operator(12, faces_m)

    def keep_m(i, value):
        inverse_m[i] = value

    operator.build(coeff_m, keep_m)

    def store_m(i, value):
        field_m[i] = value

    sweep(operator, middle, inverse_m, rhs_m, omega_first, store_m)

    def store_packed(i, value):
        place = (i + 2) % 12
        if place < 8:
            packed[pl.ds(32 * place, 32), :] = value

    sweep(operator, field_m, inverse_m, rhs_m, omega_second, store_packed)

    def coeff(i):
        return fine_plane(cells, added, 1, i if i < 10 else i + 10)

    def rhs(i):
        return fine_plane(cells, added, 0, i if i < 10 else i + 10)

    fine = Operator(12, faces)

    def keep(i, value):
        inverse[i] = value

    fine.build(coeff, keep)
    result = product(
        packed[...], lane_map(128, 256, lambda c, f: spread_weights(middle_lane(c), fine_lane(f)))
    )
    for place in range(8):
        for half in range(2):
            spread_rows(
                result[32 * place : 32 * place + 32, 128 * half : 128 * half + 128],
                risen.at[2 * place + half],
            )

    def lifted(place):
        halves = [
            jnp.concatenate([risen[2 * place + half, 0:40], risen[2 * place + half, 56:64]], axis=0)
            for half in range(2)
        ]
        return jnp.concatenate(halves, axis=1)

    for i in range(12):
        fine_index = i if i < 10 else i - 12
        place = fine_index // 2 + 2
        near = place + (1 if fine_index % 2 else -1)
        value = 0.75 * lifted(place) + 0.25 * lifted(near)
        field[0, i] = pre[i] + jnp.where(coeff(i) > 0, value, 0.0)

    def store(i, value):
        field[1, i] = value

    sweep(fine, field.at[0], inverse, rhs, omega_first, store)

    def store_out(i, value):
        if i < 8:
            out[i] = value[:32, :128]

    sweep(fine, field.at[1], inverse, rhs, omega_second, store_out)


interpret = False
VMEM = pl.BlockSpec(memory_space=pltpu.VMEM)


def call(kernel, outs, scratch, *arguments):
    return pl.pallas_call(
        kernel,
        out_shape=[jax.ShapeDtypeStruct(shape, jnp.float32) for shape in outs],
        in_specs=[VMEM] * len(arguments),
        out_specs=[VMEM] * len(outs),
        scratch_shapes=[pltpu.VMEM(shape, jnp.float32) for shape in scratch],
        compiler_params=pltpu.CompilerParams(vmem_limit_bytes=24 * 1024 * 1024),
        interpret=interpret,
    )(*arguments)


def take_lanes(values, matrix):
    rows = values.reshape(-1, values.shape[-1])
    return lax.dot_general(matrix, rows, (((0,), (1,)), ((), ())), precision=HIGHEST)


def put_lanes(strip, matrix, shape):
    rows = lax.dot_general(strip, matrix, (((0,), (0,)), ((), ())), precision=HIGHEST)
    return rows.reshape(shape)


def local(source, conductivity):
    low_x = lax.axis_index("gx") % 2 == 0
    low_y = lax.axis_index("gy") % 2 == 0
    low_z = lax.axis_index("gz") % 2 == 0

    def side(low, when_low, when_high):
        return jnp.where(low, when_low, when_high)

    cells = jnp.stack([source, conductivity])
    near = swap(side(low_x, cells[:, 4:], cells[:, :4]), "gx", False)
    far = swap(side(low_x, join([cells, near[:, :2]], 1), join([near[:, 2:], cells], 1)), "gx", True)
    cells = join([cells, side(low_x, join([near, far], 1), join([far, near], 1))], 1)

    near = swap(side(low_y, cells[:, :, 28:], cells[:, :, :4]), "gy", False)
    far = swap(side(low_y, cells[:, :, :12], cells[:, :, 20:]), "gy", True)
    cells = join([cells, side(low_y, join([near, far], 2), join([far, near], 2))], 2)

    base_near = side(low_z, 124, 0)
    base_far = side(low_z, 0, 118)
    near = swap(take_lanes(cells, lane_map(128, 4, lambda z, k: z == k + base_near)), "gz", False)
    far = swap(take_lanes(cells, lane_map(128, 10, lambda z, k: z == k + base_far)), "gz", True)
    to_near = side(low_z, 0, 124)
    to_far = side(low_z, 118, 0)
    added = put_lanes(near, lane_map(4, 128, lambda k, z: z == k + to_near), (2, 22, 48, 128))
    added = added + put_lanes(far, lane_map(10, 128, lambda k, z: z == k + to_far), (2, 22, 48, 128))

    plane = (48, 256)
    pair, pre_pressure = call(
        fine_kernel,
        [(2, 11, 24, 128), (12, *plane)],
        [(3, 22, *plane), (22, *plane), (22, *plane), (22, *plane), (44, 48, 128), (2, 264, 256)],
        cells,
        added,
    )

    base_near = side(low_z, 52, 0)
    to_near = side(low_z, 64, 116)
    near = swap(take_lanes(pair, lane_map(128, 12, lambda z, k: z == k + base_near)), "gz", False)
    lane = lax.broadcasted_iota(jnp.int32, (1, 1, 1, 128), 3)
    kept = (lane < 64) | side(low_z, lane >= 124, lane < 68)
    pair = jnp.where(kept, pair, put_lanes(near, lane_map(12, 128, lambda k, z: z == k + to_near), pair.shape))

    near = swap(side(low_y, pair[:, :, 4:16], pair[:, :, :12]), "gy", False)
    pair = side(
        low_y,
        join([pair[:, :, :16], near, pair[:, :, 20:]], 2),
        join([pair[:, :, :20], near], 2),
    )
    near = swap(side(low_x, join([pair[:, 7:], pair[:, :4]], 1), pair[:, :8]), "gx", False)
    pair = side(low_x, join([pair[:, :4], near, pair[:, 7:]], 1), join([pair[:, :8], near], 1))

    place = [lax.broadcasted_iota(jnp.int32, (8, 16, 128), dim) for dim in range(3)]
    in_box = (
        side(low_x, place[0] < 4, (place[0] < 2) | (place[0] >= 6))
        & side(low_y, place[1] < 14, (place[1] < 8) | (place[1] >= 10))
        & side(low_z, place[2] < 64, (place[2] < 32) | (place[2] >= 64))
    )
    (middle,) = call(
        box_kernel,
        [(12, 32, 128)],
        [(3, 16, 32, 128), (16, 32, 128), (16, 32, 128), (16, 32, 128), (16, 32, 128), (2, 128, 128)]
        + [(3, 8, 16, 128), (3, 8, 16, 128), (8, 16, 128), (8, 32, 128)],
        pair,
        in_box.astype(jnp.float32),
    )

    base_far = side(low_z, 0, 60)
    to_far = side(low_z, 124, 64)
    far = swap(take_lanes(middle, lane_map(128, 4, lambda z, k: z == k + base_far)), "gz", True)
    lane = lane[0]
    taken = side(low_z, lane >= 124, (lane >= 64) & (lane < 68))
    middle = jnp.where(taken, put_lanes(far, lane_map(4, 128, lambda k, z: z == k + to_far), middle.shape), middle)
    far = swap(side(low_y, middle[:, :4], middle[:, 12:16]), "gy", True)
    middle = side(
        low_y, join([middle[:, :28], far], 1), join([middle[:, :16], far, middle[:, 20:]], 1)
    )
    far = swap(side(low_x, middle[:4], middle[:4]), "gx", True)
    middle = side(low_x, join([middle[:8], far], 0), join([middle[:4], far, middle[8:]], 0))

    (pressure,) = call(
        last_kernel,
        [(8, 32, 128)],
        [(3, 12, *plane), (12, *plane), (2, 12, *plane), (3, 12, 32, 128), (12, 32, 128), (12, 32, 128)]
        + [(256, 128), (16, 64, 128)],
        middle,
        pair,
        cells,
        added,
        pre_pressure,
    )
    return pressure


def solution(mesh):
    spec = P("gx", "gy", "gz")
    return jax.shard_map(local, mesh=mesh, in_specs=(spec, spec), out_specs=spec, check_vma=False)
```

time: 135 us -> 95 us (0.70)
  the two profiles are of different devices: /device:TPU:183 before, /device:TPU:185 now
where the time goes in v2:
time: 95 us; the launch traced here: 94.6 us
  starting transfers between devices  44.8 us (47%)
  waiting for transfers between devices  29.9 us (31%)
  Pallas kernels  10.5 us (11%)
  matrix products  4.6 us (5%)
  other arithmetic  4.15 us (4%)
    ppermute x12, starting transfers between devices, swap(): return lax.ppermute(block, axis, route)  44.8 us
    ppermute x12, waiting for transfers between devices, swap(): return lax.ppermute(block, axis, route)  29.9 us
    pallas_call x3, Pallas kernels, call(): pl.pallas_call(kernel, out_shape=[jax.ShapeDtypeStruct(shape, jnp.float32...  10.5 us
    select_n x16, other arithmetic, side(): return jnp.where(low, when_low, when_high)  3.06 us
    dot_general x4, matrix products, put_lanes(): lax.dot_general(strip, matrix, (((0,), (0,)), ((), ())), precision=HIGHEST)  2.87 us
  transfers between devices with their start and end apart: 12, of which 12 were waited for; matrix products, arithmetic and copies ran while one was open for 3% of the time, Pallas kernels for 0%

profile of v2, /device:TPU:185, one launch (start us, length us, event | category | flops | bytes accessed | tf_op | source)
XLA Modules:
  0.0 94.6 jit_solution(4652659026065257743)
XLA Ops:
  0.0 1.0 %fusion.1 = f32[2,4,32,128]{3,2,1,0:T(8,128)S(1)} fusion(f32[1,8,32,128]{3,2,1,0:T(8,128)} %bitcast.25, f32[1,8,32,128]{3,2,1,0:T(8,128)} %bitcast.30, pred[]{:T(512)S(6)} %eq.37), kind=kLoop, calls=%fused_computation.17 | loop fusion | flops 98304 | bytes 393217 | tf_op jit(solution)/shard_map/jit(_where)/select_n | solution.py:356
  1.0 0.0 copy-start
  1.0 0.0 copy-start.1
  1.0 2.7 %collective-permute-start = (f32[2,4,32,128]{3,2,1,0:T(8,128)S(1)}, f32[2,4,32,128]{3,2,1,0:T(8,128)S(1)}, u32[]{:S(2)}, u32[]{:S(2)}) collective-permute-start(f32[2,4,32,128]{3,2,1,0:T(8,128)S(1)} %fusion.1), channel_id=1, source_target_pairs={{0,64},{64,0},{128,192},{192,128},{256,320},{320,256},{384,448},{4... | collective-permute-start | bytes 393224 | tf_op jit(solution)/shard_map/ppermute | solution.py:24
  3.8 0.9 collective-permute-done
  4.7 1.1 %maximum_select_fusion.4 = f32[2,10,32,128]{3,2,1,0:T(8,128)S(1)} fusion(f32[2,2,32,128]{3,2,1,0:T(8,128)S(1)} %get-tuple-element.16, f32[1,8,32,128]{3,2,1,0:T(8,128)} %bitcast.31, f32[1,8,32,128]{3,2,1,0:T(8,128)} %bitcast.26, f32[2,2,32,128]{3,2,1,0:T(8,128)S(1)} %get-tuple-element.15, pred[]{:T(512)S(6)} %eq.37), kind=kLoop, calls=%fused_computation.8 | loop fusion | flops 409600 | bytes 720897 | tf_op jit(solution)/shard_map/jit(_where)/select_n | solution.py:356
  5.8 4.8 %collective-permute-start.1 = (f32[2,10,32,128]{3,2,1,0:T(8,128)S(1)}, f32[2,10,32,128]{3,2,1,0:T(8,128)S(1)}, u32[]{:S(2)}, u32[]{:S(2)}) collective-permute-start(f32[2,10,32,128]{3,2,1,0:T(8,128)S(1)} %maximum_select_fusion.4), channel_id=1, source_target_pairs={{64,128},{128,64},{192,256},{256,192},{320,384},{384,320},{448,512... | collective-permute-start | bytes 983048 | tf_op jit(solution)/shard_map/ppermute | solution.py:24
  10.7 4.8 %collective-permute-done.1 = f32[2,10,32,128]{3,2,1,0:T(8,128)S(1)} collective-permute-done((f32[2,10,32,128]{3,2,1,0:T(8,128)S(1)}, f32[2,10,32,128]{3,2,1,0:T(8,128)S(1)}, u32[]{:S(2)}, u32[]{:S(2)}) %collective-permute-start.1) | collective-permute-done | bytes 327712 | tf_op jit(solution)/shard_map/ppermute | solution.py:24
  15.5 0.0 copy-done
  15.5 0.0 copy-done.1
  15.6 2.2 %collective-permute-start.3 = (f32[2,22,12,128]{3,2,1,0:T(8,128)S(1)}, f32[2,22,12,128]{3,2,1,0:T(8,128)S(1)}, u32[]{:S(2)}, u32[]{:S(2)}) collective-permute-start(f32[2,22,12,128]{3,2,1,0:T(8,128)S(1)} %slice_select_fusion), channel_id=1, source_target_pairs={{8,16},{16,8},{24,32},{32,24},{40,48},{48,40},{9,17},{17,9},{25,33... | collective-permute-start | bytes 811016 | tf_op jit(solution)/shard_map/ppermute | solution.py:24
  17.9 2.3 %collective-permute-start.2 = (f32[2,22,4,128]{3,2,1,0:T(4,128)S(1)}, f32[2,22,4,128]{3,2,1,0:T(4,128)S(1)}, u32[]{:S(2)}, u32[]{:S(2)}) collective-permute-start(f32[2,22,4,128]{3,2,1,0:T(4,128)S(1)} %maximum_select_fusion.8), channel_id=1, source_target_pairs={{0,8},{8,0},{16,24},{24,16},{32,40},{40,32},{48,56},{56,48},{1,9},... | collective-permute-start | bytes 270344 | tf_op jit(solution)/shard_map/ppermute | solution.py:24
  20.2 4.1 %collective-permute-done.2 = f32[2,22,4,128]{3,2,1,0:T(4,128)S(1)} collective-permute-done((f32[2,22,4,128]{3,2,1,0:T(4,128)S(1)}, f32[2,22,4,128]{3,2,1,0:T(4,128)S(1)}, u32[]{:S(2)}, u32[]{:S(2)}) %collective-permute-start.2) | collective-permute-done | bytes 90144 | tf_op jit(solution)/shard_map/ppermute | solution.py:24
  24.3 4.2 %collective-permute-done.3 = f32[2,22,12,128]{3,2,1,0:T(8,128)S(1)} collective-permute-done((f32[2,22,12,128]{3,2,1,0:T(8,128)S(1)}, f32[2,22,12,128]{3,2,1,0:T(8,128)S(1)}, u32[]{:S(2)}, u32[]{:S(2)}) %collective-permute-start.3) | collective-permute-done | bytes 270368 | tf_op jit(solution)/shard_map/ppermute | solution.py:24
  28.5 0.1 maximum_select_fusion.2
  28.6 0.1 pad_maximum_fusion.cells
  28.7 0.6 fusion.8
  29.3 4.9 %collective-permute-start.5 = (f32[10,2112]{1,0:T(8,128)S(1)}, f32[10,2112]{1,0:T(8,128)S(1)}, u32[]{:S(2)}, u32[]{:S(2)}) collective-permute-start(f32[10,2112]{1,0:T(8,128)S(1)} %fusion.8), channel_id=1, source_target_pairs={{1,2},{2,1},{3,4},{4,3},{5,6},{6,5},{9,10},{10,9},{11,12},{12,11},... | collective-permute-start | bytes 253448 | tf_op jit(solution)/shard_map/ppermute | solution.py:24
  34.2 0.6 fusion.10
  34.8 1.9 %collective-permute-start.4 = (f32[4,2112]{1,0:T(4,128)S(1)}, f32[4,2112]{1,0:T(4,128)S(1)}, u32[]{:S(2)}, u32[]{:S(2)}) collective-permute-start(f32[4,2112]{1,0:T(4,128)S(1)} %fusion.10), channel_id=1, source_target_pairs={{0,1},{1,0},{2,3},{3,2},{4,5},{5,4},{6,7},{7,6},{8,9},{9,8},{10,11... | collective-permute-start | bytes 101384 | tf_op jit(solution)/shard_map/ppermute | solution.py:24
  36.8 1.2 %collective-permute-done.5 = f32[10,2112]{1,0:T(8,128)S(1)} collective-permute-done((f32[10,2112]{1,0:T(8,128)S(1)}, f32[10,2112]{1,0:T(8,128)S(1)}, u32[]{:S(2)}, u32[]{:S(2)}) %collective-permute-start.5) | collective-permute-done | bytes 84512 | tf_op jit(solution)/shard_map/ppermute | solution.py:24
  37.9 1.1 %fusion.18 = f32[2112,128]{1,0:T(8,128)S(1)} fusion(f32[10,2112]{1,0:T(8,128)S(1)} %collective-permute-done.5, s32[10]{0:T(128)S(1)} %iota_add_fusion.3), kind=kOutput, calls=%fused_computation.41 | convolution fusion | flops 32441600 | bytes 1165864 | tf_op jit(solution)/shard_map/dot_general | solution.py:346
  39.0 0.5 collective-permute-done.4
  39.5 1.0 %convolution_add_fusion = f32[2112,128]{1,0:T(8,128)S(1)} fusion(f32[2112,128]{1,0:T(8,128)S(1)} %fusion.18, f32[4,2112]{1,0:T(4,128)S(1)} %collective-permute-done.4, s32[4]{0:T(128)S(1)} %iota_add_fusion.5), kind=kOutput, calls=%fused_computation | convolution fusion | flops 13246976 | bytes 2196496 | tf_op jit(solution)/shard_map/dot_general | solution.py:346
  40.6 5.5 %shard_map.28 = (f32[2,11,24,128]{3,2,1,0:T(8,128)S(1)}, f32[12,48,256]{2,1,0:T(8,128)S(1)}) custom-call(f32[2,22,48,128]{3,2,1,0:T(8,128)S(1)} %pad_maximum_fusion.cells, f32[2,22,48,128]{3,2,1,0:T(8,128)S(1)} %bitcast.20), custom_call_target="tpu_custom_call" | custom-call | tf_op jit(solution)/shard_map/pallas_call | solution.py:329
  46.1 0.2 fusion.6
  46.3 1.9 %collective-permute-start.6 = (f32[12,528]{1,0:T(8,128)S(1)}, f32[12,528]{1,0:T(8,128)S(1)}, u32[]{:S(2)}, u32[]{:S(2)}) collective-permute-start(f32[12,528]{1,0:T(8,128)S(1)} %fusion.6), channel_id=1, source_target_pairs={{0,1},{1,0},{2,3},{3,2},{4,5},{5,4},{6,7},{7,6},{8,9},{9,8},{10,11... | collective-permute-start | bytes 76040 | tf_op jit(solution)/shard_map/ppermute | solution.py:24
  48.3 2.8 %collective-permute-done.6 = f32[12,528]{1,0:T(8,128)S(1)} collective-permute-done((f32[12,528]{1,0:T(8,128)S(1)}, f32[12,528]{1,0:T(8,128)S(1)}, u32[]{:S(2)}, u32[]{:S(2)}) %collective-permute-start.6) | collective-permute-done | bytes 25376 | tf_op jit(solution)/shard_map/ppermute | solution.py:24
  51.1 0.4 fusion.19
  51.6 1.9 %collective-permute-start.7 = (f32[2,11,12,128]{3,2,1,0:T(8,128)S(1)}, f32[2,11,12,128]{3,2,1,0:T(8,128)S(1)}, u32[]{:S(2)}, u32[]{:S(2)}) collective-permute-start(f32[2,11,12,128]{3,2,1,0:T(8,128)S(1)} %slice_select_fusion.1), channel_id=1, source_target_pairs={{0,8},{8,0},{16,24},{24,16},{32,40},{40,32},{48,56},{56,48},{1,9},... | collective-permute-start | bytes 405512 | tf_op jit(solution)/shard_map/ppermute | solution.py:24
  53.5 0.5 and_select_fusion
  54.1 3.7 %collective-permute-done.7 = f32[2,11,12,128]{3,2,1,0:T(8,128)S(1)} collective-permute-done((f32[2,11,12,128]{3,2,1,0:T(8,128)S(1)}, f32[2,11,12,128]{3,2,1,0:T(8,128)S(1)}, u32[]{:S(2)}, u32[]{:S(2)}) %collective-permute-start.7) | collective-permute-done | bytes 135200 | tf_op jit(solution)/shard_map/ppermute | solution.py:24
  57.8 0.1 maximum_select_fusion.3
  57.9 0.7 fusion.25
  58.6 5.9 %collective-permute-start.8 = (f32[2,8,32,128]{3,2,1,0:T(8,128)}, f32[2,8,32,128]{3,2,1,0:T(8,128)S(1)}, u32[]{:S(2)}, u32[]{:S(2)}) collective-permute-start(f32[2,8,32,128]{3,2,1,0:T(8,128)} %get-tuple-element.10), channel_id=1, source_target_pairs={{0,64},{64,0},{128,192},{192,128},{256,320},{320,256},{384,448},{4... | collective-permute-start | bytes 786440 | tf_op jit(solution)/shard_map/ppermute | solution.py:24
  64.6 0.1 and_convert_fusion.box
  64.7 1.2 %collective-permute-done.8 = f32[2,8,32,128]{3,2,1,0:T(8,128)S(1)} collective-permute-done((f32[2,8,32,128]{3,2,1,0:T(8,128)}, f32[2,8,32,128]{3,2,1,0:T(8,128)S(1)}, u32[]{:S(2)}, u32[]{:S(2)}) %collective-permute-start.8) | collective-permute-done | bytes 262176 | tf_op jit(solution)/shard_map/ppermute | solution.py:24
  65.9 0.1 maximum_select_fusion.pair
  66.0 1.6 %shard_map.29 = f32[12,32,128]{2,1,0:T(8,128)S(1)} custom-call(f32[2,16,32,128]{3,2,1,0:T(8,128)S(1)} %maximum_select_fusion.pair, f32[8,16,128]{2,1,0:T(8,128)S(1)} %and_convert_fusion.box), custom_call_target="tpu_custom_call" | custom-call | tf_op jit(solution)/shard_map/pallas_call | solution.py:329
  67.6 0.2 fusion.12
  67.8 7.4 %collective-permute-start.9 = (f32[4,384]{1,0:T(4,128)S(1)}, f32[4,384]{1,0:T(4,128)S(1)}, u32[]{:S(2)}, u32[]{:S(2)}) collective-permute-start(f32[4,384]{1,0:T(4,128)S(1)} %fusion.12), channel_id=1, source_target_pairs={{1,2},{2,1},{3,4},{4,3},{5,6},{6,5},{9,10},{10,9},{11,12},{12,11},... | collective-permute-start | bytes 18440 | tf_op jit(solution)/shard_map/ppermute | solution.py:24
  75.2 1.0 %collective-permute-done.9 = f32[4,384]{1,0:T(4,128)S(1)} collective-permute-done((f32[4,384]{1,0:T(4,128)S(1)}, f32[4,384]{1,0:T(4,128)S(1)}, u32[]{:S(2)}, u32[]{:S(2)}) %collective-permute-start.9) | collective-permute-done | bytes 6176 | tf_op jit(solution)/shard_map/ppermute | solution.py:24
  76.2 0.4 fusion.22
  76.6 2.2 %collective-permute-start.10 = (f32[12,4,128]{2,1,0:T(4,128)S(1)}, f32[12,4,128]{2,1,0:T(4,128)S(1)}, u32[]{:S(2)}, u32[]{:S(2)}) collective-permute-start(f32[12,4,128]{2,1,0:T(4,128)S(1)} %slice_select_fusion.2), channel_id=1, source_target_pairs={{8,16},{16,8},{24,32},{32,24},{40,48},{48,40},{9,17},{17,9},{25,33... | collective-permute-start | bytes 73736 | tf_op jit(solution)/shard_map/ppermute | solution.py:24
  78.8 3.6 %collective-permute-done.10 = f32[12,4,128]{2,1,0:T(4,128)S(1)} collective-permute-done((f32[12,4,128]{2,1,0:T(4,128)S(1)}, f32[12,4,128]{2,1,0:T(4,128)S(1)}, u32[]{:S(2)}, u32[]{:S(2)}) %collective-permute-start.10) | collective-permute-done | bytes 24608 | tf_op jit(solution)/shard_map/ppermute | solution.py:24
  82.5 6.7 %collective-permute-start.11 = (f32[4,32,128]{2,1,0:T(8,128)S(1)}, f32[4,32,128]{2,1,0:T(8,128)S(1)}, u32[]{:S(2)}, u32[]{:S(2)}) collective-permute-start(f32[4,32,128]{2,1,0:T(8,128)S(1)} %get-tuple-element.14), channel_id=1, source_target_pairs={{64,128},{128,64},{192,256},{256,192},{320,384},{384,320},{448,512... | collective-permute-start | bytes 196616 | tf_op jit(solution)/shard_map/ppermute | solution.py:24
  89.2 1.9 %collective-permute-done.11 = f32[4,32,128]{2,1,0:T(8,128)S(1)} collective-permute-done((f32[4,32,128]{2,1,0:T(8,128)S(1)}, f32[4,32,128]{2,1,0:T(8,128)S(1)}, u32[]{:S(2)}, u32[]{:S(2)}) %collective-permute-start.11) | collective-permute-done | bytes 65568 | tf_op jit(solution)/shard_map/ppermute | solution.py:24
  91.1 3.5 %shard_map.30 = f32[8,32,128]{2,1,0:T(8,128)} custom-call(f32[12,32,128]{2,1,0:T(8,128)S(1)} %maximum_select_fusion.7.middle, f32[2,16,32,128]{3,2,1,0:T(8,128)S(1)} %maximum_select_fusion.pair, f32[2,22,48,128]{3,2,1,0:T(8,128)S(1)} %pad_maximum_fusion.cells, f32[2,22,48,128]{3,2,1,0:T(8,128)S(1)} %bitcast.21, f32[12,48,256]{2,1,0:T(8,128)S(1)} %get-tuple-element.8.pre), custom_call_target="tpu_custom_call" | custom-call | tf_op jit(solution)/shard_map/pallas_call | solution.py:329
  (32 shorter events, 0.5 us)
Async XLA Ops:
  1.0 14.5 %copy-start = (f32[8,32,128]{2,1,0:T(8,128)S(1)}, f32[8,32,128]{2,1,0:T(8,128)}, u32[]{:S(2)}) copy-start(f32[8,32,128]{2,1,0:T(8,128)} %param.2) | copy-start | bytes 393220
  1.0 14.5 %copy-start.1 = (f32[8,32,128]{2,1,0:T(8,128)S(1)}, f32[8,32,128]{2,1,0:T(8,128)}, u32[]{:S(2)}) copy-start(f32[8,32,128]{2,1,0:T(8,128)} %param.3) | copy-start | bytes 393220
  1.0 3.7 %collective-permute-start = (f32[2,4,32,128]{3,2,1,0:T(8,128)S(1)}, f32[2,4,32,128]{3,2,1,0:T(8,128)S(1)}, u32[]{:S(2)}, u32[]{:S(2)}) collective-permute-start(f32[2,4,32,128]{3,2,1,0:T(8,128)S(1)} %fusion.1), channel_id=1, source_target_pairs={{0,64},{64,0},{128,192},{192,128},{256,320},{320,256},{384,448},{4... | collective-permute-start | bytes 393224 | tf_op jit(solution)/shard_map/ppermute | solution.py:24
  5.8 9.6 %collective-permute-start.1 = (f32[2,10,32,128]{3,2,1,0:T(8,128)S(1)}, f32[2,10,32,128]{3,2,1,0:T(8,128)S(1)}, u32[]{:S(2)}, u32[]{:S(2)}) collective-permute-start(f32[2,10,32,128]{3,2,1,0:T(8,128)S(1)} %maximum_select_fusion.4), channel_id=1, source_target_pairs={{64,128},{128,64},{192,256},{256,192},{320,384},{384,320},{448,512... | collective-permute-start | bytes 983048 | tf_op jit(solution)/shard_map/ppermute | solution.py:24
  15.6 12.9 %collective-permute-start.3 = (f32[2,22,12,128]{3,2,1,0:T(8,128)S(1)}, f32[2,22,12,128]{3,2,1,0:T(8,128)S(1)}, u32[]{:S(2)}, u32[]{:S(2)}) collective-permute-start(f32[2,22,12,128]{3,2,1,0:T(8,128)S(1)} %slice_select_fusion), channel_id=1, source_target_pairs={{8,16},{16,8},{24,32},{32,24},{40,48},{48,40},{9,17},{17,9},{25,33... | collective-permute-start | bytes 811016 | tf_op jit(solution)/shard_map/ppermute | solution.py:24
  17.9 6.4 %collective-permute-start.2 = (f32[2,22,4,128]{3,2,1,0:T(4,128)S(1)}, f32[2,22,4,128]{3,2,1,0:T(4,128)S(1)}, u32[]{:S(2)}, u32[]{:S(2)}) collective-permute-start(f32[2,22,4,128]{3,2,1,0:T(4,128)S(1)} %maximum_select_fusion.8), channel_id=1, source_target_pairs={{0,8},{8,0},{16,24},{24,16},{32,40},{40,32},{48,56},{56,48},{1,9},... | collective-permute-start | bytes 270344 | tf_op jit(solution)/shard_map/ppermute | solution.py:24
  29.3 8.7 %collective-permute-start.5 = (f32[10,2112]{1,0:T(8,128)S(1)}, f32[10,2112]{1,0:T(8,128)S(1)}, u32[]{:S(2)}, u32[]{:S(2)}) collective-permute-start(f32[10,2112]{1,0:T(8,128)S(1)} %fusion.8), channel_id=1, source_target_pairs={{1,2},{2,1},{3,4},{4,3},{5,6},{6,5},{9,10},{10,9},{11,12},{12,11},... | collective-permute-start | bytes 253448 | tf_op jit(solution)/shard_map/ppermute | solution.py:24
  34.8 4.7 %collective-permute-start.4 = (f32[4,2112]{1,0:T(4,128)S(1)}, f32[4,2112]{1,0:T(4,128)S(1)}, u32[]{:S(2)}, u32[]{:S(2)}) collective-permute-start(f32[4,2112]{1,0:T(4,128)S(1)} %fusion.10), channel_id=1, source_target_pairs={{0,1},{1,0},{2,3},{3,2},{4,5},{5,4},{6,7},{7,6},{8,9},{9,8},{10,11... | collective-permute-start | bytes 101384 | tf_op jit(solution)/shard_map/ppermute | solution.py:24
  46.3 4.8 %collective-permute-start.6 = (f32[12,528]{1,0:T(8,128)S(1)}, f32[12,528]{1,0:T(8,128)S(1)}, u32[]{:S(2)}, u32[]{:S(2)}) collective-permute-start(f32[12,528]{1,0:T(8,128)S(1)} %fusion.6), channel_id=1, source_target_pairs={{0,1},{1,0},{2,3},{3,2},{4,5},{5,4},{6,7},{7,6},{8,9},{9,8},{10,11... | collective-permute-start | bytes 76040 | tf_op jit(solution)/shard_map/ppermute | solution.py:24
  51.6 6.2 %collective-permute-start.7 = (f32[2,11,12,128]{3,2,1,0:T(8,128)S(1)}, f32[2,11,12,128]{3,2,1,0:T(8,128)S(1)}, u32[]{:S(2)}, u32[]{:S(2)}) collective-permute-start(f32[2,11,12,128]{3,2,1,0:T(8,128)S(1)} %slice_select_fusion.1), channel_id=1, source_target_pairs={{0,8},{8,0},{16,24},{24,16},{32,40},{40,32},{48,56},{56,48},{1,9},... | collective-permute-start | bytes 405512 | tf_op jit(solution)/shard_map/ppermute | solution.py:24
  58.6 7.3 %collective-permute-start.8 = (f32[2,8,32,128]{3,2,1,0:T(8,128)}, f32[2,8,32,128]{3,2,1,0:T(8,128)S(1)}, u32[]{:S(2)}, u32[]{:S(2)}) collective-permute-start(f32[2,8,32,128]{3,2,1,0:T(8,128)} %get-tuple-element.10), channel_id=1, source_target_pairs={{0,64},{64,0},{128,192},{192,128},{256,320},{320,256},{384,448},{4... | collective-permute-start | bytes 786440 | tf_op jit(solution)/shard_map/ppermute | solution.py:24
  65.9 10.6 %copy-start.2 = (pred[128]{0:T(512)(128)(4,1)S(1)}, pred[128]{0:T(512)(128)(4,1)}, u32[]{:S(2)}) copy-start(pred[128]{0:T(512)(128)(4,1)} %and_select_fusion) | copy-start | bytes 388
  67.8 8.4 %collective-permute-start.9 = (f32[4,384]{1,0:T(4,128)S(1)}, f32[4,384]{1,0:T(4,128)S(1)}, u32[]{:S(2)}, u32[]{:S(2)}) collective-permute-start(f32[4,384]{1,0:T(4,128)S(1)} %fusion.12), channel_id=1, source_target_pairs={{1,2},{2,1},{3,4},{4,3},{5,6},{6,5},{9,10},{10,9},{11,12},{12,11},... | collective-permute-start | bytes 18440 | tf_op jit(solution)/shard_map/ppermute | solution.py:24
  76.6 5.8 %collective-permute-start.10 = (f32[12,4,128]{2,1,0:T(4,128)S(1)}, f32[12,4,128]{2,1,0:T(4,128)S(1)}, u32[]{:S(2)}, u32[]{:S(2)}) collective-permute-start(f32[12,4,128]{2,1,0:T(4,128)S(1)} %slice_select_fusion.2), channel_id=1, source_target_pairs={{8,16},{16,8},{24,32},{32,24},{40,48},{48,40},{9,17},{17,9},{25,33... | collective-permute-start | bytes 73736 | tf_op jit(solution)/shard_map/ppermute | solution.py:24
  82.5 8.6 %collective-permute-start.11 = (f32[4,32,128]{2,1,0:T(8,128)S(1)}, f32[4,32,128]{2,1,0:T(8,128)S(1)}, u32[]{:S(2)}, u32[]{:S(2)}) collective-permute-start(f32[4,32,128]{2,1,0:T(8,128)S(1)} %get-tuple-element.14), channel_id=1, source_target_pairs={{64,128},{128,64},{192,256},{256,192},{320,384},{384,320},{448,512... | collective-permute-start | bytes 196616 | tf_op jit(solution)/shard_map/ppermute | solution.py:24

commit v3 on v2

--- a/solution.py
+++ b/solution.py
@@ -120,8 +120,15 @@
     return signed(m, 128, 96)
 
 
-def coarse_lane(c):
-    return signed(c, 128, 48)
+def coarse_lane(lane, odd):
+    after = jnp.where(lane < 32, lane, jnp.where((lane == 32) & (odd == 1), 4096, lane - odd))
+    before = jnp.where((lane == 127) & (odd == 0), 4096, lane - 127 - odd)
+    return jnp.where(lane < 64, after, before)
+
+
+def same_box(coarse, middle, odd):
+    edge = 32 * odd
+    return (coarse >= edge) == (middle >= 2 * edge)
 
 
 def fine_plane(cells, added, kind, i):
@@ -179,7 +186,7 @@
             pair[kind, j] = result[24 * j : 24 * j + 24]
 
 
-def box_kernel(pair, box, corrected, faces, inverse, field, other, piece, packed, low, low_faces, low_inverse, risen):
+def box_kernel(pair, box, parity, corrected, faces, inverse, field, other, piece, packed, low, low_faces, low_inverse, risen):
     def coeff(i):
         return pair[1, i]
 
@@ -209,9 +216,10 @@
             slot = piece.at[2 * j + kind]
             slot[...] = planes[kind]
             packed[kind, pl.ds(16 * j, 16), :] = halve_rows(slot, kind == 0)
+    odd = parity[0]
     matrices = (
-        lane_map(128, 128, lambda m, c: 4.0 * gather_weights(middle_lane(m), coarse_lane(c))),
-        lane_map(128, 128, lambda m, c: 0.25 * mean_weights(middle_lane(m), coarse_lane(c))),
+        lane_map(128, 128, lambda m, c: 4.0 * gather_weights(middle_lane(m), coarse_lane(c, odd))),
+        lane_map(128, 128, lambda m, c: 0.25 * mean_weights(middle_lane(m), coarse_lane(c, odd))),
     )
     for kind in range(2):
         result = product(packed[kind], matrices[kind])
@@ -230,9 +238,12 @@
         packed[0, pl.ds(16 * i, 16), :] = value
 
     sweep(coarse, low.at[2], low_inverse, lambda i: low[0, i], omega_second, store_low)
-    result = product(
-        packed[0], lane_map(128, 128, lambda c, m: spread_weights(coarse_lane(c), middle_lane(m)))
-    )
+
+    def spread_box(c, m):
+        coarse, fine = coarse_lane(c, odd), middle_lane(m)
+        return jnp.where(same_box(coarse, fine, odd), spread_weights(coarse, fine), 0.0)
+
+    result = product(packed[0], lane_map(128, 128, spread_box))
     for j in range(8):
         spread_rows(result[16 * j : 16 * j + 16], risen.at[j])
     for place in range(12):
@@ -323,13 +334,14 @@
 
 interpret = False
 VMEM = pl.BlockSpec(memory_space=pltpu.VMEM)
+SMEM = pl.BlockSpec(memory_space=pltpu.SMEM)
 
 
 def call(kernel, outs, scratch, *arguments):
     return pl.pallas_call(
         kernel,
         out_shape=[jax.ShapeDtypeStruct(shape, jnp.float32) for shape in outs],
-        in_specs=[VMEM] * len(arguments),
+        in_specs=[VMEM if value.ndim > 1 else SMEM for value in arguments],
         out_specs=[VMEM] * len(outs),
         scratch_shapes=[pltpu.VMEM(shape, jnp.float32) for shape in scratch],
         compiler_params=pltpu.CompilerParams(vmem_limit_bytes=24 * 1024 * 1024),
@@ -350,28 +362,29 @@
 def local(source, conductivity):
     low_x = lax.axis_index("gx") % 2 == 0
     low_y = lax.axis_index("gy") % 2 == 0
-    low_z = lax.axis_index("gz") % 2 == 0
+    odd_z = (lax.axis_index("gz") % 2).reshape(1)
 
     def side(low, when_low, when_high):
         return jnp.where(low, when_low, when_high)
 
     cells = jnp.stack([source, conductivity])
+    near = swap(side(low_y, cells[:, :, 28:], cells[:, :, :4]), "gy", False)
+    far = swap(side(low_y, cells[:, :, :12], cells[:, :, 20:]), "gy", True)
+    cells = join([cells, side(low_y, join([near, far], 2), join([far, near], 2))], 2)
+
     near = swap(side(low_x, cells[:, 4:], cells[:, :4]), "gx", False)
     far = swap(side(low_x, join([cells, near[:, :2]], 1), join([near[:, 2:], cells], 1)), "gx", True)
     cells = join([cells, side(low_x, join([near, far], 1), join([far, near], 1))], 1)
 
-    near = swap(side(low_y, cells[:, :, 28:], cells[:, :, :4]), "gy", False)
-    far = swap(side(low_y, cells[:, :, :12], cells[:, :, 20:]), "gy", True)
-    cells = join([cells, side(low_y, join([near, far], 2), join([far, near], 2))], 2)
-
-    base_near = side(low_z, 124, 0)
-    base_far = side(low_z, 0, 118)
-    near = swap(take_lanes(cells, lane_map(128, 4, lambda z, k: z == k + base_near)), "gz", False)
-    far = swap(take_lanes(cells, lane_map(128, 10, lambda z, k: z == k + base_far)), "gz", True)
-    to_near = side(low_z, 0, 124)
-    to_far = side(low_z, 118, 0)
-    added = put_lanes(near, lane_map(4, 128, lambda k, z: z == k + to_near), (2, 22, 48, 128))
-    added = added + put_lanes(far, lane_map(10, 128, lambda k, z: z == k + to_far), (2, 22, 48, 128))
+    strips = take_lanes(cells, lane_map(128, 64, lambda z, k: z == k + jnp.where(k < 32, 0, 64)))
+    count = lax.axis_size("gz")
+    after = lax.ppermute(strips[:32], "gz", [(i + 1, i) for i in range(count - 1)])
+    before = lax.ppermute(strips[32:], "gz", [(i, i + 1) for i in range(count - 1)])
+    added = put_lanes(
+        join([after, before], 0),
+        lane_map(64, 128, lambda k, z: z == k + jnp.where(k < 32, 0, 64)),
+        (2, 22, 48, 128),
+    )
 
     plane = (48, 256)
     pair, pre_pressure = call(
@@ -382,13 +395,6 @@
         added,
     )
 
-    base_near = side(low_z, 52, 0)
-    to_near = side(low_z, 64, 116)
-    near = swap(take_lanes(pair, lane_map(128, 12, lambda z, k: z == k + base_near)), "gz", False)
-    lane = lax.broadcasted_iota(jnp.int32, (1, 1, 1, 128), 3)
-    kept = (lane < 64) | side(low_z, lane >= 124, lane < 68)
-    pair = jnp.where(kept, pair, put_lanes(near, lane_map(12, 128, lambda k, z: z == k + to_near), pair.shape))
-
     near = swap(side(low_y, pair[:, :, 4:16], pair[:, :, :12]), "gy", False)
     pair = side(
         low_y,
@@ -402,7 +408,6 @@
     in_box = (
         side(low_x, place[0] < 4, (place[0] < 2) | (place[0] >= 6))
         & side(low_y, place[1] < 14, (place[1] < 8) | (place[1] >= 10))
-        & side(low_z, place[2] < 64, (place[2] < 32) | (place[2] >= 64))
     )
     (middle,) = call(
         box_kernel,
@@ -411,14 +416,9 @@
         + [(3, 8, 16, 128), (3, 8, 16, 128), (8, 16, 128), (8, 32, 128)],
         pair,
         in_box.astype(jnp.float32),
-    )
-
-    base_far = side(low_z, 0, 60)
-    to_far = side(low_z, 124, 64)
-    far = swap(take_lanes(middle, lane_map(128, 4, lambda z, k: z == k + base_far)), "gz", True)
-    lane = lane[0]
-    taken = side(low_z, lane >= 124, (lane >= 64) & (lane < 68))
-    middle = jnp.where(taken, put_lanes(far, lane_map(4, 128, lambda k, z: z == k + to_far), middle.shape), middle)
+        odd_z,
+    )
+
     far = swap(side(low_y, middle[:, :4], middle[:, 12:16]), "gy", True)
     middle = side(
         low_y, join([middle[:, :28], far], 1), join([middle[:, :16], far, middle[:, 20:]], 1)

time: 95 us -> 80.3 us (0.85)
  the two profiles are of different devices: /device:TPU:185 before, /device:TPU:439 now
where the time goes in v3:
time: 80.3 us; the launch traced here: 79.8 us
  starting transfers between devices  34.3 us (43%)
  waiting for transfers between devices  29.7 us (37%)
  Pallas kernels  10.5 us (13%)
  other arithmetic  3.13 us (4%)
  matrix products  1.77 us (2%)
    ppermute x8, starting transfers between devices, swap(): return lax.ppermute(block, axis, route)  26.2 us
    ppermute x8, waiting for transfers between devices, swap(): return lax.ppermute(block, axis, route)  23.6 us
    pallas_call x3, Pallas kernels, call(): pl.pallas_call(kernel, out_shape=[jax.ShapeDtypeStruct(shape, jnp.float32...  10.5 us
    ppermute x1, starting transfers between devices, local(): lax.ppermute(strips[32:], 'gz', [(i, i + 1) for i in range(count - 1)])  6.12 us
    ppermute x1, waiting for transfers between devices, local(): lax.ppermute(strips[:32], 'gz', [(i + 1, i) for i in range(count - 1)])  4.32 us
    select_n x14, other arithmetic, side(): return jnp.where(low, when_low, when_high)  2.2 us
    ppermute x1, starting transfers between devices, local(): lax.ppermute(strips[:32], 'gz', [(i + 1, i) for i in range(count - 1)])  1.92 us
    ppermute x1, waiting for transfers between devices, local(): lax.ppermute(strips[32:], 'gz', [(i, i + 1) for i in range(count - 1)])  1.76 us
  transfers between devices with their start and end apart: 10, of which 9 were waited for; matrix products, arithmetic and copies ran while one was open for 1% of the time, Pallas kernels for 0%

profile of v3, /device:TPU:439, one launch (start us, length us, event | category | flops | bytes accessed | tf_op | source)
XLA Modules:
  0.0 79.8 jit_solution(3337312866750572836)
XLA Ops:
  0.0 0.0 copy-start
  0.0 0.0 copy-start.1
  0.0 1.0 %fusion.5 = f32[2,8,12,128]{3,2,1,0:T(8,128)S(1)} fusion(f32[1,8,32,128]{3,2,1,0:T(8,128)} %bitcast.13, f32[1,8,32,128]{3,2,1,0:T(8,128)} %bitcast.18, pred[]{:T(512)S(6)} %eq.17), kind=kLoop, calls=%fused_computation.18 | loop fusion | flops 73728 | bytes 360449 | tf_op jit(solution)/shard_map/jit(_where)/select_n | solution.py:368
  1.0 4.3 %collective-permute-start.1 = (f32[2,8,12,128]{3,2,1,0:T(8,128)S(1)}, f32[2,8,12,128]{3,2,1,0:T(8,128)S(1)}, u32[]{:S(2)}, u32[]{:S(2)}) collective-permute-start(f32[2,8,12,128]{3,2,1,0:T(8,128)S(1)} %fusion.5), channel_id=1, source_target_pairs={{8,16},{16,8},{24,32},{32,24},{40,48},{48,40},{9,17},{17,9},{25,33... | collective-permute-start | bytes 294920 | tf_op jit(solution)/shard_map/ppermute | solution.py:24
  5.3 0.8 %maximum_select_fusion.8 = f32[2,8,4,128]{3,2,1,0:T(4,128)S(1)} fusion(f32[1,8,32,128]{3,2,1,0:T(8,128)} %bitcast.19, f32[1,8,32,128]{3,2,1,0:T(8,128)} %bitcast.14, pred[]{:T(512)S(6)} %eq.17), kind=kLoop, calls=%fused_computation.25 | loop fusion | flops 24576 | bytes 294913 | tf_op jit(solution)/shard_map/jit(_where)/select_n | solution.py:368
  6.2 1.9 %collective-permute-start = (f32[2,8,4,128]{3,2,1,0:T(4,128)S(1)}, f32[2,8,4,128]{3,2,1,0:T(4,128)S(1)}, u32[]{:S(2)}, u32[]{:S(2)}) collective-permute-start(f32[2,8,4,128]{3,2,1,0:T(4,128)S(1)} %maximum_select_fusion.8), channel_id=1, source_target_pairs={{0,8},{8,0},{16,24},{24,16},{32,40},{40,32},{48,56},{56,48},{1,9},... | collective-permute-start | bytes 98312 | tf_op jit(solution)/shard_map/ppermute | solution.py:24
  8.1 2.7 %collective-permute-done = f32[2,8,4,128]{3,2,1,0:T(4,128)S(1)} collective-permute-done((f32[2,8,4,128]{3,2,1,0:T(4,128)S(1)}, f32[2,8,4,128]{3,2,1,0:T(4,128)S(1)}, u32[]{:S(2)}, u32[]{:S(2)}) %collective-permute-start) | collective-permute-done | bytes 32800 | tf_op jit(solution)/shard_map/ppermute | solution.py:24
  10.8 0.0 collective-permute-done.1
  10.9 0.0 copy-done
  10.9 0.0 copy-done.1
  11.0 4.0 %collective-permute-start.2 = (f32[2,4,48,128]{3,2,1,0:T(8,128)S(1)}, f32[2,4,48,128]{3,2,1,0:T(8,128)S(1)}, u32[]{:S(2)}, u32[]{:S(2)}) collective-permute-start(f32[2,4,48,128]{3,2,1,0:T(8,128)S(1)} %slice_select_fusion), channel_id=1, source_target_pairs={{0,64},{64,0},{128,192},{192,128},{256,320},{320,256},{384,448},{4... | collective-permute-start | bytes 589832 | tf_op jit(solution)/shard_map/ppermute | solution.py:24
  15.0 1.0 %collective-permute-done.2 = f32[2,4,48,128]{3,2,1,0:T(8,128)S(1)} collective-permute-done((f32[2,4,48,128]{3,2,1,0:T(8,128)S(1)}, f32[2,4,48,128]{3,2,1,0:T(8,128)S(1)}, u32[]{:S(2)}, u32[]{:S(2)}) %collective-permute-start.2) | collective-permute-done | bytes 196640 | tf_op jit(solution)/shard_map/ppermute | solution.py:24
  16.1 4.8 %collective-permute-start.3 = (f32[2,10,48,128]{3,2,1,0:T(8,128)S(1)}, f32[2,10,48,128]{3,2,1,0:T(8,128)S(1)}, u32[]{:S(2)}, u32[]{:S(2)}) collective-permute-start(f32[2,10,48,128]{3,2,1,0:T(8,128)S(1)} %maximum_select_fusion.2), channel_id=1, source_target_pairs={{64,128},{128,64},{192,256},{256,192},{320,384},{384,320},{448,512... | collective-permute-start | bytes 1474568 | tf_op jit(solution)/shard_map/ppermute | solution.py:24
  20.9 6.6 %collective-permute-done.3 = f32[2,10,48,128]{3,2,1,0:T(8,128)S(1)} collective-permute-done((f32[2,10,48,128]{3,2,1,0:T(8,128)S(1)}, f32[2,10,48,128]{3,2,1,0:T(8,128)S(1)}, u32[]{:S(2)}, u32[]{:S(2)}) %collective-permute-start.3) | collective-permute-done | bytes 491552 | tf_op jit(solution)/shard_map/ppermute | solution.py:24
  27.5 0.1 pad_maximum_fusion.cells
  27.6 0.7 fusion.7
  28.3 1.9 %collective-permute-start.4 = (f32[32,2112]{1,0:T(8,128)S(1)}, f32[32,2112]{1,0:T(8,128)S(1)}, u32[]{:S(2)}, u32[]{:S(2)}) collective-permute-start(f32[32,2112]{1,0:T(8,128)S(1)} %get-tuple-element.9), channel_id=1, source_target_pairs={{1,0},{2,1},{3,2},{4,3},{5,4},{6,5},{7,6},{9,8},{10,9},{11,10},{12... | collective-permute-start | bytes 811016 | tf_op jit(solution)/shard_map/ppermute | solution.py:381
  30.3 6.1 %collective-permute-start.5 = (f32[32,2112]{1,0:T(8,128)S(1)}, f32[32,2112]{1,0:T(8,128)S(1)}, u32[]{:S(2)}, u32[]{:S(2)}) collective-permute-start(f32[32,2112]{1,0:T(8,128)S(1)} %get-tuple-element.10), channel_id=1, source_target_pairs={{0,1},{1,2},{2,3},{3,4},{4,5},{5,6},{6,7},{8,9},{9,10},{10,11},{11... | collective-permute-start | bytes 811016 | tf_op jit(solution)/shard_map/ppermute | solution.py:382
  36.4 4.3 %collective-permute-done.4 = f32[32,2112]{1,0:T(8,128)S(1)} collective-permute-done((f32[32,2112]{1,0:T(8,128)S(1)}, f32[32,2112]{1,0:T(8,128)S(1)}, u32[]{:S(2)}, u32[]{:S(2)}) %collective-permute-start.4) | collective-permute-done | bytes 270368 | tf_op jit(solution)/shard_map/ppermute | solution.py:381
  40.7 1.8 %collective-permute-done.5 = f32[32,2112]{1,0:T(8,128)S(1)} collective-permute-done((f32[32,2112]{1,0:T(8,128)S(1)}, f32[32,2112]{1,0:T(8,128)S(1)}, u32[]{:S(2)}, u32[]{:S(2)}) %collective-permute-start.5) | collective-permute-done | bytes 270368 | tf_op jit(solution)/shard_map/ppermute | solution.py:382
  42.5 1.1 %fusion = f32[2112,128]{1,0:T(8,128)S(1)} fusion(f32[32,2112]{1,0:T(8,128)S(1)} %collective-permute-done.5, f32[32,2112]{1,0:T(8,128)S(1)} %collective-permute-done.4, s32[64]{0:T(128)S(1)} %fusion.11), kind=kOutput, calls=%fused_computation.2 | convolution fusion | flops 207761408 | bytes 1622272 | tf_op jit(solution)/shard_map/dot_general | solution.py:358
  43.5 5.5 %shard_map.28 = (f32[2,11,24,128]{3,2,1,0:T(8,128)S(1)}, f32[12,48,256]{2,1,0:T(8,128)S(1)}) custom-call(f32[2,22,48,128]{3,2,1,0:T(8,128)S(1)} %pad_maximum_fusion.cells, f32[2,22,48,128]{3,2,1,0:T(8,128)S(1)} %bitcast.9), custom_call_target="tpu_custom_call" | custom-call | tf_op jit(solution)/shard_map/pallas_call | solution.py:341
  49.1 1.9 %collective-permute-start.6 = (f32[2,11,12,128]{3,2,1,0:T(8,128)S(1)}, f32[2,11,12,128]{3,2,1,0:T(8,128)S(1)}, u32[]{:S(2)}, u32[]{:S(2)}) collective-permute-start(f32[2,11,12,128]{3,2,1,0:T(8,128)S(1)} %slice_select_fusion.1), channel_id=1, source_target_pairs={{0,8},{8,0},{16,24},{24,16},{32,40},{40,32},{48,56},{56,48},{1,9},... | collective-permute-start | bytes 405512 | tf_op jit(solution)/shard_map/ppermute | solution.py:24
  51.1 6.0 %collective-permute-done.6 = f32[2,11,12,128]{3,2,1,0:T(8,128)S(1)} collective-permute-done((f32[2,11,12,128]{3,2,1,0:T(8,128)S(1)}, f32[2,11,12,128]{3,2,1,0:T(8,128)S(1)}, u32[]{:S(2)}, u32[]{:S(2)}) %collective-permute-start.6) | collective-permute-done | bytes 135200 | tf_op jit(solution)/shard_map/ppermute | solution.py:24
  57.1 0.1 maximum_select_fusion.3
  57.2 0.7 fusion.14
  57.9 2.8 %collective-permute-start.7 = (f32[2,8,32,128]{3,2,1,0:T(8,128)}, f32[2,8,32,128]{3,2,1,0:T(8,128)S(1)}, u32[]{:S(2)}, u32[]{:S(2)}) collective-permute-start(f32[2,8,32,128]{3,2,1,0:T(8,128)} %get-tuple-element.12), channel_id=1, source_target_pairs={{0,64},{64,0},{128,192},{192,128},{256,320},{320,256},{384,448},{4... | collective-permute-start | bytes 786440 | tf_op jit(solution)/shard_map/ppermute | solution.py:24
  60.7 0.1 and_convert_fusion.box
  60.8 1.2 %collective-permute-done.7 = f32[2,8,32,128]{3,2,1,0:T(8,128)S(1)} collective-permute-done((f32[2,8,32,128]{3,2,1,0:T(8,128)}, f32[2,8,32,128]{3,2,1,0:T(8,128)S(1)}, u32[]{:S(2)}, u32[]{:S(2)}) %collective-permute-start.7) | collective-permute-done | bytes 262176 | tf_op jit(solution)/shard_map/ppermute | solution.py:24
  62.0 0.1 maximum_select_fusion.1.pair
  62.1 1.6 %shard_map.29 = f32[12,32,128]{2,1,0:T(8,128)S(1)} custom-call(f32[2,16,32,128]{3,2,1,0:T(8,128)S(1)} %maximum_select_fusion.1.pair, f32[8,16,128]{2,1,0:T(8,128)S(1)} %and_convert_fusion.box, s32[1]{0:T(128)} %bitcast.4.parity), custom_call_target="tpu_custom_call" | custom-call | tf_op jit(solution)/shard_map/pallas_call | solution.py:341
  63.7 2.2 %collective-permute-start.8 = (f32[12,4,128]{2,1,0:T(4,128)S(1)}, f32[12,4,128]{2,1,0:T(4,128)S(1)}, u32[]{:S(2)}, u32[]{:S(2)}) collective-permute-start(f32[12,4,128]{2,1,0:T(4,128)S(1)} %slice_select_fusion.2), channel_id=1, source_target_pairs={{8,16},{16,8},{24,32},{32,24},{40,48},{48,40},{9,17},{17,9},{25,33... | collective-permute-start | bytes 73736 | tf_op jit(solution)/shard_map/ppermute | solution.py:24
  65.9 3.6 %collective-permute-done.8 = f32[12,4,128]{2,1,0:T(4,128)S(1)} collective-permute-done((f32[12,4,128]{2,1,0:T(4,128)S(1)}, f32[12,4,128]{2,1,0:T(4,128)S(1)}, u32[]{:S(2)}, u32[]{:S(2)}) %collective-permute-start.8) | collective-permute-done | bytes 24608 | tf_op jit(solution)/shard_map/ppermute | solution.py:24
  69.5 4.3 %collective-permute-start.9 = (f32[4,32,128]{2,1,0:T(8,128)S(1)}, f32[4,32,128]{2,1,0:T(8,128)S(1)}, u32[]{:S(2)}, u32[]{:S(2)}) collective-permute-start(f32[4,32,128]{2,1,0:T(8,128)S(1)} %get-tuple-element.16), channel_id=1, source_target_pairs={{64,128},{128,64},{192,256},{256,192},{320,384},{384,320},{448,512... | collective-permute-start | bytes 196616 | tf_op jit(solution)/shard_map/ppermute | solution.py:24
  73.9 2.4 %collective-permute-done.9 = f32[4,32,128]{2,1,0:T(8,128)S(1)} collective-permute-done((f32[4,32,128]{2,1,0:T(8,128)S(1)}, f32[4,32,128]{2,1,0:T(8,128)S(1)}, u32[]{:S(2)}, u32[]{:S(2)}) %collective-permute-start.9) | collective-permute-done | bytes 65568 | tf_op jit(solution)/shard_map/ppermute | solution.py:24
  76.4 3.5 %shard_map.30 = f32[8,32,128]{2,1,0:T(8,128)} custom-call(f32[12,32,128]{2,1,0:T(8,128)S(1)} %maximum_select_fusion.6.middle, f32[2,16,32,128]{3,2,1,0:T(8,128)S(1)} %maximum_select_fusion.1.pair, f32[2,22,48,128]{3,2,1,0:T(8,128)S(1)} %pad_maximum_fusion.cells, f32[2,22,48,128]{3,2,1,0:T(8,128)S(1)} %bitcast.10, f32[12,48,256]{2,1,0:T(8,128)S(1)} %get-tuple-element.8.pre), custom_call_target="tpu_custom_call" | custom-call | tf_op jit(solution)/shard_map/pallas_call | solution.py:341
  (21 shorter events, 0.4 us)
Async XLA Ops:
  0.0 10.9 %copy-start = (f32[8,32,128]{2,1,0:T(8,128)S(1)}, f32[8,32,128]{2,1,0:T(8,128)}, u32[]{:S(2)}) copy-start(f32[8,32,128]{2,1,0:T(8,128)} %param.2) | copy-start | bytes 393220
  0.0 10.9 %copy-start.1 = (f32[8,32,128]{2,1,0:T(8,128)S(1)}, f32[8,32,128]{2,1,0:T(8,128)}, u32[]{:S(2)}) copy-start(f32[8,32,128]{2,1,0:T(8,128)} %param.3) | copy-start | bytes 393220
  1.0 9.8 %collective-permute-start.1 = (f32[2,8,12,128]{3,2,1,0:T(8,128)S(1)}, f32[2,8,12,128]{3,2,1,0:T(8,128)S(1)}, u32[]{:S(2)}, u32[]{:S(2)}) collective-permute-start(f32[2,8,12,128]{3,2,1,0:T(8,128)S(1)} %fusion.5), channel_id=1, source_target_pairs={{8,16},{16,8},{24,32},{32,24},{40,48},{48,40},{9,17},{17,9},{25,33... | collective-permute-start | bytes 294920 | tf_op jit(solution)/shard_map/ppermute | solution.py:24
  6.2 4.7 %collective-permute-start = (f32[2,8,4,128]{3,2,1,0:T(4,128)S(1)}, f32[2,8,4,128]{3,2,1,0:T(4,128)S(1)}, u32[]{:S(2)}, u32[]{:S(2)}) collective-permute-start(f32[2,8,4,128]{3,2,1,0:T(4,128)S(1)} %maximum_select_fusion.8), channel_id=1, source_target_pairs={{0,8},{8,0},{16,24},{24,16},{32,40},{40,32},{48,56},{56,48},{1,9},... | collective-permute-start | bytes 98312 | tf_op jit(solution)/shard_map/ppermute | solution.py:24
  11.0 5.1 %collective-permute-start.2 = (f32[2,4,48,128]{3,2,1,0:T(8,128)S(1)}, f32[2,4,48,128]{3,2,1,0:T(8,128)S(1)}, u32[]{:S(2)}, u32[]{:S(2)}) collective-permute-start(f32[2,4,48,128]{3,2,1,0:T(8,128)S(1)} %slice_select_fusion), channel_id=1, source_target_pairs={{0,64},{64,0},{128,192},{192,128},{256,320},{320,256},{384,448},{4... | collective-permute-start | bytes 589832 | tf_op jit(solution)/shard_map/ppermute | solution.py:24
  16.1 11.4 %collective-permute-start.3 = (f32[2,10,48,128]{3,2,1,0:T(8,128)S(1)}, f32[2,10,48,128]{3,2,1,0:T(8,128)S(1)}, u32[]{:S(2)}, u32[]{:S(2)}) collective-permute-start(f32[2,10,48,128]{3,2,1,0:T(8,128)S(1)} %maximum_select_fusion.2), channel_id=1, source_target_pairs={{64,128},{128,64},{192,256},{256,192},{320,384},{384,320},{448,512... | collective-permute-start | bytes 1474568 | tf_op jit(solution)/shard_map/ppermute | solution.py:24
  28.3 12.4 %collective-permute-start.4 = (f32[32,2112]{1,0:T(8,128)S(1)}, f32[32,2112]{1,0:T(8,128)S(1)}, u32[]{:S(2)}, u32[]{:S(2)}) collective-permute-start(f32[32,2112]{1,0:T(8,128)S(1)} %get-tuple-element.9), channel_id=1, source_target_pairs={{1,0},{2,1},{3,2},{4,3},{5,4},{6,5},{7,6},{9,8},{10,9},{11,10},{12... | collective-permute-start | bytes 811016 | tf_op jit(solution)/shard_map/ppermute | solution.py:381
  30.3 12.2 %collective-permute-start.5 = (f32[32,2112]{1,0:T(8,128)S(1)}, f32[32,2112]{1,0:T(8,128)S(1)}, u32[]{:S(2)}, u32[]{:S(2)}) collective-permute-start(f32[32,2112]{1,0:T(8,128)S(1)} %get-tuple-element.10), channel_id=1, source_target_pairs={{0,1},{1,2},{2,3},{3,4},{4,5},{5,6},{6,7},{8,9},{9,10},{10,11},{11... | collective-permute-start | bytes 811016 | tf_op jit(solution)/shard_map/ppermute | solution.py:382
  49.1 8.0 %collective-permute-start.6 = (f32[2,11,12,128]{3,2,1,0:T(8,128)S(1)}, f32[2,11,12,128]{3,2,1,0:T(8,128)S(1)}, u32[]{:S(2)}, u32[]{:S(2)}) collective-permute-start(f32[2,11,12,128]{3,2,1,0:T(8,128)S(1)} %slice_select_fusion.1), channel_id=1, source_target_pairs={{0,8},{8,0},{16,24},{24,16},{32,40},{40,32},{48,56},{56,48},{1,9},... | collective-permute-start | bytes 405512 | tf_op jit(solution)/shard_map/ppermute | solution.py:24
  57.9 4.1 %collective-permute-start.7 = (f32[2,8,32,128]{3,2,1,0:T(8,128)}, f32[2,8,32,128]{3,2,1,0:T(8,128)S(1)}, u32[]{:S(2)}, u32[]{:S(2)}) collective-permute-start(f32[2,8,32,128]{3,2,1,0:T(8,128)} %get-tuple-element.12), channel_id=1, source_target_pairs={{0,64},{64,0},{128,192},{192,128},{256,320},{320,256},{384,448},{4... | collective-permute-start | bytes 786440 | tf_op jit(solution)/shard_map/ppermute | solution.py:24
  63.7 5.8 %collective-permute-start.8 = (f32[12,4,128]{2,1,0:T(4,128)S(1)}, f32[12,4,128]{2,1,0:T(4,128)S(1)}, u32[]{:S(2)}, u32[]{:S(2)}) collective-permute-start(f32[12,4,128]{2,1,0:T(4,128)S(1)} %slice_select_fusion.2), channel_id=1, source_target_pairs={{8,16},{16,8},{24,32},{32,24},{40,48},{48,40},{9,17},{17,9},{25,33... | collective-permute-start | bytes 73736 | tf_op jit(solution)/shard_map/ppermute | solution.py:24
  69.5 6.8 %collective-permute-start.9 = (f32[4,32,128]{2,1,0:T(8,128)S(1)}, f32[4,32,128]{2,1,0:T(8,128)S(1)}, u32[]{:S(2)}, u32[]{:S(2)}) collective-permute-start(f32[4,32,128]{2,1,0:T(8,128)S(1)} %get-tuple-element.16), channel_id=1, source_target_pairs={{64,128},{128,64},{192,256},{256,192},{320,384},{384,320},{448,512... | collective-permute-start | bytes 196616 | tf_op jit(solution)/shard_map/ppermute | solution.py:24

commit v4 on v3

v4 whole, which is shorter than its diff:
```python
import math

import jax
import jax.numpy as jnp
from jax import lax
from jax.experimental import pallas as pl
from jax.experimental.pallas import tpu as pltpu
from jax.sharding import PartitionSpec as P

spectrum_top = 1.9
spectrum_low = 0.475
mean_value = (spectrum_top + spectrum_low) / 2
half_range = (spectrum_top - spectrum_low) / 2
omega_first = 1.0 / (mean_value + half_range * math.cos(math.pi / 4))
omega_second = 1.0 / (mean_value + half_range * math.cos(3 * math.pi / 4))
HIGHEST = lax.Precision.HIGHEST


def swap(block, axis, outer):
    count = lax.axis_size(axis)
    route = []
    for low in range(1 if outer else 0, count - 1, 2):
        route += [(low, low + 1), (low + 1, low)]
    return lax.ppermute(block, axis, route)


def cut(values, start, stop, dim):
    return lax.slice_in_dim(values, start, stop, axis=dim)


def join(pieces, dim):
    return jnp.concatenate(pieces, axis=dim)


def turn(plane, dim, step):
    return pltpu.roll(plane, -step % plane.shape[dim], dim)


class Operator:
    def __init__(self, faces, planes):
        self.faces = faces
        self.planes = list(planes)

    def build(self, coeff, take):
        count = len(self.planes)
        before = coeff(count - 1) + coeff(0)
        for i in range(count):
            here = coeff(i)
            across = here + coeff((i + 1) % count)
            rows = here + turn(here, 0, 1)
            lanes = here + turn(here, 1, 1)
            for place, face in enumerate((across, rows, lanes)):
                self.faces[place, i] = face
            diagonal = (across + before) + (rows + turn(rows, 0, -1)) + (lanes + turn(lanes, 1, -1))
            take(i, jnp.where(here > 0, 1.0 / diagonal, 0.0))
            before = across

    def apply(self, field, take):
        count = len(self.planes)
        before = self.faces[0, self.planes[-1]] * (field(count - 1) - field(0))
        for i, place in enumerate(self.planes):
            here = field(i)
            across = self.faces[0, place] * (here - field((i + 1) % count))
            rows = self.faces[1, place] * (here - turn(here, 0, 1))
            lanes = self.faces[2, place] * (here - turn(here, 1, 1))
            take(i, (across - before) + (rows - turn(rows, 0, -1)) + (lanes - turn(lanes, 1, -1)))
            before = across


def sweep(operator, field, inverse, rhs, omega, store):
    def take(i, applied):
        store(i, field(i) + (omega * (rhs(i) - applied)) * inverse(i))

    operator.apply(field, take)


def plane_of(ref, *lead):
    return lambda i: ref[(*lead, i)]


def keep_in(ref, *lead):
    def store(i, value):
        ref[(*lead, i)] = value

    return store


def halve_rows(piece, weights):
    count = piece.shape[0] // 2
    even = piece[pl.ds(0, count, 2), :]
    odd = piece[pl.ds(1, count, 2), :]
    if not weights:
        return even + odd
    return 0.375 * (even + odd) + 0.125 * (turn(odd, 0, -1) + turn(even, 0, 1))


def product(values, matrix):
    return jnp.dot(values, matrix, precision=HIGHEST, preferred_element_type=jnp.float32)


def lane_map(rows, columns, entries):
    row = lax.broadcasted_iota(jnp.int32, (rows, columns), 0)
    column = lax.broadcasted_iota(jnp.int32, (rows, columns), 1)
    return entries(row, column).astype(jnp.float32)


def signed(index, size, after):
    return jnp.where(index < after, index, index - size)


def gather_weights(fine, coarse):
    step = fine - 2 * coarse
    return jnp.where((step == 0) | (step == 1), 0.375, jnp.where((step == -1) | (step == 2), 0.125, 0.0))


def mean_weights(fine, coarse):
    step = fine - 2 * coarse
    return jnp.where((step == 0) | (step == 1), 0.5, 0.0)


def spread_weights(coarse, fine):
    step = fine - 2 * coarse
    return jnp.where((step == 0) | (step == 1), 0.75, jnp.where((step == -1) | (step == 2), 0.25, 0.0))


def fine_lane(f):
    return signed(f, 256, 192)


def middle_lane(m):
    return signed(m, 128, 96)


def coarse_lane(lane, odd):
    after = jnp.where(lane < 32, lane, jnp.where((lane == 32) & (odd == 1), 4096, lane - odd))
    before = jnp.where((lane == 127) & (odd == 0), 4096, lane - 127 - odd)
    return jnp.where(lane < 64, after, before)


def same_box(coarse, middle, odd):
    edge = 32 * odd
    return (coarse >= edge) == (middle >= 2 * edge)


def restrict_planes(plane, j, count):
    return 0.375 * (plane(2 * j) + plane(2 * j + 1)) + 0.125 * (
        plane((2 * j - 1) % count) + plane((2 * j + 2) % count)
    )


def restrict_level(plane, coeff, count, piece, packed, matrices, store):
    rows, lanes = piece.shape[1:]
    halves = plane(0).shape[1] // lanes
    for j in range(count // 2):
        planes = (restrict_planes(plane, j, count), coeff(2 * j) + coeff(2 * j + 1))
        for kind in range(2):
            for half in range(halves):
                slot = piece.at[(2 * j + kind) * halves + half]
                slot[...] = planes[kind][:, lanes * half : lanes * half + lanes]
                packed[kind, pl.ds(rows // 2 * j, rows // 2), pl.ds(lanes * half, lanes)] = halve_rows(
                    slot, kind == 0
                )
    for kind in range(2):
        result = product(packed[kind], matrices[kind])
        for j in range(count // 2):
            store(kind, j, result[rows // 2 * j : rows // 2 * (j + 1)])


fine_places = [*range(10), 20, 21]
middle_places = [*range(8), *range(12, 16)]


def fine_kernel(wide, pair, kept, faces, inverse, rhs, pre, coeff, field, piece, packed):
    lane = lax.broadcasted_iota(jnp.int32, (48, 128), 1)
    edge = (lane < 32) | (lane >= 96)
    for i in range(22):
        halo = wide[2, i]
        rhs[i, :, 0:128] = 2.0 * wide[0, i]
        rhs[i, :, 128:256] = jnp.where(edge, 2.0 * halo, 0.0)
        coeff[i, :, 0:128] = wide[1, i]
        coeff[i, :, 128:256] = jnp.where(edge, pltpu.roll(halo, 64, 1), 0.0)
    operator = Operator(faces, range(22))

    def begin(i, value):
        inverse[i] = value
        field[i] = omega_first * rhs[i] * value

    operator.build(plane_of(coeff), begin)
    sweep(operator, plane_of(field), plane_of(inverse), plane_of(rhs), omega_second, keep_in(pre))

    def leave(i, applied):
        field[i] = jnp.where(coeff[i] > 0, rhs[i] - applied, 0.0)

    operator.apply(plane_of(pre), leave)
    matrices = (
        lane_map(256, 128, lambda f, c: 4.0 * gather_weights(fine_lane(f), middle_lane(c))),
        lane_map(256, 128, lambda f, c: 0.25 * mean_weights(fine_lane(f), middle_lane(c))),
    )

    def store(kind, j, value):
        pair[kind, j] = value

    restrict_level(plane_of(field), plane_of(coeff), 22, piece, packed, matrices, store)
    for i, place in enumerate(fine_places):
        for kind, values in enumerate((coeff, rhs, pre)):
            kept[kind, i] = values[place]


def box_kernel(pair, box, parity, corrected, kept, faces, inverse, field, other, piece, packed, low, low_faces, low_inverse, risen):
    rhs, coeff = plane_of(pair, 0), plane_of(pair, 1)
    operator = Operator(faces, range(16))

    def begin(i, value):
        inverse[i] = value
        field[i] = omega_first * rhs(i) * value

    operator.build(coeff, begin)
    sweep(operator, plane_of(field), plane_of(inverse), rhs, omega_second, keep_in(other))

    def leave(i, applied):
        field[i] = jnp.where(coeff(i) > 0, rhs(i) - applied, 0.0)

    operator.apply(plane_of(other), leave)
    odd = parity[0]
    matrices = (
        lane_map(128, 128, lambda m, c: 4.0 * gather_weights(middle_lane(m), coarse_lane(c, odd))),
        lane_map(128, 128, lambda m, c: 0.25 * mean_weights(middle_lane(m), coarse_lane(c, odd))),
    )

    def store(kind, j, value):
        low[kind, j] = value * box[j]

    restrict_level(plane_of(field), coeff, 16, piece, packed, matrices, store)
    coarse = Operator(low_faces, range(8))

    def begin_low(i, value):
        low_inverse[i] = value
        low[2, i] = omega_first * low[0, i] * value

    coarse.build(plane_of(low, 1), begin_low)

    def store_low(i, value):
        packed[0, pl.ds(16 * i, 16), :] = value

    sweep(coarse, plane_of(low, 2), plane_of(low_inverse), plane_of(low, 0), omega_second, store_low)

    def spread_box(c, m):
        coarse, fine = coarse_lane(c, odd), middle_lane(m)
        return jnp.where(same_box(coarse, fine, odd), spread_weights(coarse, fine), 0.0)

    result = product(packed[0], lane_map(128, 128, spread_box))
    for j in range(8):
        spread_rows(result[16 * j : 16 * j + 16], risen.at[j])
    for place, i in enumerate(middle_places):
        for kind, values in enumerate((faces.at[0], faces.at[1], faces.at[2], inverse, pair.at[0])):
            kept[kind, place] = values[i]
        near = (i // 2 + (1 if i % 2 else -1)) % 8
        corrected[place] = other[i] + (0.75 * risen[i // 2] + 0.25 * risen[near])


def spread_rows(values, target):
    count = values.shape[0]
    target[pl.ds(0, count, 2), :] = 0.75 * values + 0.25 * turn(values, 0, -1)
    target[pl.ds(1, count, 2), :] = 0.75 * values + 0.25 * turn(values, 0, 1)


def last_kernel(middle, kept_m, kept, out, faces, inverse, field, field_m, packed, risen):
    operator = Operator(kept_m, range(12))
    inverse_m, rhs_m = plane_of(kept_m, 3), plane_of(kept_m, 4)
    sweep(operator, plane_of(middle), inverse_m, rhs_m, omega_first, keep_in(field_m))

    def store_packed(i, value):
        place = (i + 2) % 12
        if place < 8:
            packed[pl.ds(32 * place, 32), :] = value

    sweep(operator, plane_of(field_m), inverse_m, rhs_m, omega_second, store_packed)
    result = product(
        packed[...], lane_map(128, 256, lambda c, f: spread_weights(middle_lane(c), fine_lane(f)))
    )
    for place in range(8):
        for half in range(2):
            spread_rows(
                result[32 * place : 32 * place + 32, 128 * half : 128 * half + 128],
                risen.at[2 * place + half],
            )

    def lifted(place):
        halves = [
            jnp.concatenate([risen[2 * place + half, 0:40], risen[2 * place + half, 56:64]], axis=0)
            for half in range(2)
        ]
        return jnp.concatenate(halves, axis=1)

    fine = Operator(faces, range(12))
    fine.build(plane_of(kept, 0), keep_in(inverse))
    for i in range(12):
        fine_index = i if i < 10 else i - 12
        place = fine_index // 2 + 2
        near = place + (1 if fine_index % 2 else -1)
        value = 0.75 * lifted(place) + 0.25 * lifted(near)
        field[0, i] = kept[2, i] + jnp.where(kept[0, i] > 0, value, 0.0)

    rhs_f, inverse_f = plane_of(kept, 1), plane_of(inverse)
    sweep(fine, plane_of(field, 0), inverse_f, rhs_f, omega_first, keep_in(field, 1))

    def store_out(i, value):
        if i < 8:
            out[i] = value[:32, :128]

    sweep(fine, plane_of(field, 1), inverse_f, rhs_f, omega_second, store_out)


interpret = False
VMEM = pl.BlockSpec(memory_space=pltpu.VMEM)
SMEM = pl.BlockSpec(memory_space=pltpu.SMEM)


def call(kernel, outs, scratch, *arguments):
    return pl.pallas_call(
        kernel,
        out_shape=[jax.ShapeDtypeStruct(shape, jnp.float32) for shape in outs],
        in_specs=[VMEM if value.ndim > 1 else SMEM for value in arguments],
        out_specs=[VMEM] * len(outs),
        scratch_shapes=[pltpu.VMEM(shape, jnp.float32) for shape in scratch],
        compiler_params=pltpu.CompilerParams(vmem_limit_bytes=24 * 1024 * 1024),
        interpret=interpret,
    )(*arguments)


def take_lanes(values, matrix):
    rows = values.reshape(-1, values.shape[-1])
    return lax.dot_general(matrix, rows, (((0,), (1,)), ((), ())), precision=HIGHEST)


def put_lanes(strip, matrix, shape):
    rows = lax.dot_general(strip, matrix, (((0,), (0,)), ((), ())), precision=HIGHEST)
    return rows.reshape(shape)


def local(source, conductivity):
    low_x = lax.axis_index("gx") % 2 == 0
    low_y = lax.axis_index("gy") % 2 == 0
    odd_z = (lax.axis_index("gz") % 2).reshape(1)

    def side(low, when_low, when_high):
        return jnp.where(low, when_low, when_high)

    cells = jnp.stack([source, conductivity])
    sent = lax.optimization_barrier(
        side(
            low_y,
            join([cells[:, :, :12], cells[:, :, 28:]], 2),
            join([cells[:, :, 20:], cells[:, :, :4]], 2),
        )
    )
    far = swap(sent[:, :, :12], "gy", True)
    near = swap(sent[:, :, 12:], "gy", False)
    cells = join([cells, side(low_y, join([near, far], 2), join([far, near], 2))], 2)

    strips = take_lanes(cells, lane_map(128, 64, lambda z, k: z == k + jnp.where(k < 32, 0, 64)))
    count = lax.axis_size("gz")
    after = lax.ppermute(strips[:32], "gz", [(i + 1, i) for i in range(count - 1)])
    before = lax.ppermute(strips[32:], "gz", [(i, i + 1) for i in range(count - 1)])
    rows = strips.shape[1] // 2
    halo = join([after[:, :rows], before[:, rows:], after[:, rows:], before[:, :rows]], 0)
    halo = put_lanes(halo, lane_map(128, 128, lambda k, z: k == z), (1, 8, 48, 128))
    cells = join([cells, halo], 0)

    far = swap(cells, "gx", True)
    near = swap(side(low_x, cells[:, 4:], cells[:, :4]), "gx", False)
    last = swap(side(low_x, near[:, :2], near[:, 2:]), "gx", True)
    wide = join([cells, side(low_x, join([near, last, far], 1), join([far, last, near], 1))], 1)

    plane = (48, 256)
    pair, kept = call(
        fine_kernel,
        [(2, 11, 24, 128), (3, 12, *plane)],
        [(3, 22, *plane)] + [(22, *plane)] * 5 + [(44, 48, 128), (2, 264, 256)],
        wide,
    )

    pair = side(low_x, join([pair[:, 7:], pair[:, :4]], 1), pair[:, :8])
    near = swap(side(low_y, pair[:, :, 4:16], pair[:, :, :12]), "gy", False)
    pair = side(
        low_y,
        join([pair[:, :, :16], near, pair[:, :, 20:]], 2),
        join([pair[:, :, :20], near], 2),
    )
    near = swap(pair, "gx", False)
    pair = side(low_x, join([pair[:, 4:], near, pair[:, :4]], 1), join([pair, near], 1))

    place = [lax.broadcasted_iota(jnp.int32, (8, 16, 128), dim) for dim in range(3)]
    in_box = (
        side(low_x, place[0] < 4, (place[0] < 2) | (place[0] >= 6))
        & side(low_y, place[1] < 14, (place[1] < 8) | (place[1] >= 10))
    )
    middle, kept_m = call(
        box_kernel,
        [(12, 32, 128), (5, 12, 32, 128)],
        [(3, 16, 32, 128), (16, 32, 128), (16, 32, 128), (16, 32, 128), (16, 32, 128), (2, 128, 128)]
        + [(3, 8, 16, 128), (3, 8, 16, 128), (8, 16, 128), (8, 32, 128)],
        pair,
        in_box.astype(jnp.float32),
        odd_z,
    )

    far = swap(side(low_y, middle[:, :4], middle[:, 12:16]), "gy", True)
    middle = side(
        low_y, join([middle[:, :28], far], 1), join([middle[:, :16], far, middle[:, 20:]], 1)
    )
    far = swap(side(low_x, middle[:4], middle[:4]), "gx", True)
    middle = side(low_x, join([middle[:8], far], 0), join([middle[:4], far, middle[8:]], 0))

    (pressure,) = call(
        last_kernel,
        [(8, 32, 128)],
        [(3, 12, *plane), (12, *plane), (2, 12, *plane), (12, 32, 128), (256, 128), (16, 64, 128)],
        middle,
        kept_m,
        kept,
    )
    return pressure


def solution(mesh):
    spec = P("gx", "gy", "gz")
    return jax.shard_map(local, mesh=mesh, in_specs=(spec, spec), out_specs=spec, check_vma=False)
```

time: 80.3 us -> 75.2 us (0.936)
  waiting for transfers between devices: 29.7 us -> 22.7 us
  starting transfers between devices: 34.3 us -> 38.1 us
  Pallas kernels: 10.5 us -> 9.34 us
  matrix products: 1.77 us -> 0.71 us
    ppermute x1, waiting for transfers between devices: 4.32 us -> 0.05 us  [local(): lax.ppermute(strips[:32], 'gz', [(i + 1, i) for i in range(count - 1)])]
    ppermute x8 -> x9, starting transfers between devices: 26.2 us -> 30 us  [swap(): return lax.ppermute(block, axis, route)]
    ppermute x8 -> x9, waiting for transfers between devices: 23.6 us -> 21.1 us  [swap(): return lax.ppermute(block, axis, route)]
    another operation x0 -> x2, other arithmetic: none -> 1.79 us  [local(): cells = jnp.stack([source, conductivity])]
    pallas_call x3, Pallas kernels: 10.5 us -> 9.34 us  [call(): pl.pallas_call(kernel, out_shape=[jax.ShapeDtypeStruct(shape, jnp.float32...]
    select_n x14, other arithmetic: 2.2 us -> 1.23 us  [side(): return jnp.where(low, when_low, when_high)]
  transfers between devices with their start and end apart: 10 -> 11, of which waited for: 9 -> 7; matrix products, arithmetic and copies ran while one was open for 1% -> 0% of each run, Pallas kernels for 0% -> 0%
where the time goes in v4:
time: 75.2 us; the launch traced here: 74.7 us
  starting transfers between devices  38.1 us (51%)
  waiting for transfers between devices  22.7 us (30%)
  Pallas kernels  9.34 us (12%)
  other arithmetic  3.32 us (4%)
    ppermute x9, starting transfers between devices, swap(): return lax.ppermute(block, axis, route)  30 us
    ppermute x9, waiting for transfers between devices, swap(): return lax.ppermute(block, axis, route)  21.1 us
    pallas_call x3, Pallas kernels, call(): pl.pallas_call(kernel, out_shape=[jax.ShapeDtypeStruct(shape, jnp.float32...  9.34 us
    ppermute x1, starting transfers between devices, local(): lax.ppermute(strips[32:], 'gz', [(i, i + 1) for i in range(count - 1)])  6.12 us
    ppermute x1, starting transfers between devices, local(): lax.ppermute(strips[:32], 'gz', [(i + 1, i) for i in range(count - 1)])  1.92 us
    another operation x2, other arithmetic, local(): cells = jnp.stack([source, conductivity])  1.79 us
    ppermute x1, waiting for transfers between devices, local(): lax.ppermute(strips[32:], 'gz', [(i, i + 1) for i in range(count - 1)])  1.56 us
  transfers between devices with their start and end apart: 11, of which 7 were waited for; matrix products, arithmetic and copies ran while one was open for 0% of the time, Pallas kernels for 0%

profile of v4, /device:TPU:439, one launch (start us, length us, event | category | flops | bytes accessed | tf_op | source)
XLA Modules:
  0.0 74.7 jit_solution(15456481887131936603)
XLA Ops:
  0.0 0.0 copy-start.1
  0.0 0.0 copy-start
  0.0 1.0 %fusion.8 = (f32[2,8,12,128]{3,2,1,0:T(8,128)S(1)}, f32[2,8,12,128]{3,2,1,0:T(8,128)S(1)}) fusion(f32[1,8,32,128]{3,2,1,0:T(8,128)} %bitcast.16, f32[1,8,32,128]{3,2,1,0:T(8,128)} %bitcast.10), kind=kLoop, calls=%fused_computation.25 | loop fusion | flops 49152 | bytes 458752 | tf_op jit(solution)/shard_map/stack | solution.py:349
  1.0 0.8 %fusion.15 = f32[2,8,4,128]{3,2,1,0:T(4,128)S(1)} fusion(f32[1,8,32,128]{3,2,1,0:T(8,128)} %bitcast.17, f32[1,8,32,128]{3,2,1,0:T(8,128)} %bitcast.11), kind=kLoop, calls=%fused_computation.37 | loop fusion | flops 8192 | bytes 294912 | tf_op jit(solution)/shard_map/stack | solution.py:349
  1.8 0.8 %fusion.11 = f32[2,8,16,128]{3,2,1,0:T(8,128)S(1)} fusion(f32[1,8,32,128]{3,2,1,0:T(8,128)} %bitcast.12, f32[1,8,32,128]{3,2,1,0:T(8,128)} %bitcast.18, f32[2,8,4,128]{3,2,1,0:T(4,128)S(1)} %fusion.15, f32[2,8,12,128]{3,2,1,0:T(8,128)S(1)} %get-tuple-element.18, f32[2,8,12,128]{3,2,1,0:T(8,128)S(1)} %get-tuple-element.17, pred[]{:T(512)S(6)} %eq.17), kind=kLoop, calls=%fused_computation.30 | loop fusion | flops 131072 | bytes 622593 | tf_op jit(solution)/shard_map/jit(_where)/select_n | solution.py:347
  2.6 4.3 %collective-permute-start.1 = (f32[2,8,12,128]{3,2,1,0:T(8,128)S(1)}, f32[2,8,12,128]{3,2,1,0:T(8,128)S(1)}, u32[]{:S(2)}, u32[]{:S(2)}) collective-permute-start(f32[2,8,12,128]{3,2,1,0:T(8,128)S(1)} %bitcast.26), channel_id=1, source_target_pairs={{8,16},{16,8},{24,32},{32,24},{40,48},{48,40},{9,17},{17,9},{25,33... | collective-permute-start | bytes 294920 | tf_op jit(solution)/shard_map/ppermute | solution.py:24
  7.0 1.9 %collective-permute-start = (f32[2,8,4,128]{3,2,1,0:T(4,128)S(1)}, f32[2,8,4,128]{3,2,1,0:T(4,128)S(1)}, u32[]{:S(2)}, u32[]{:S(2)}) collective-permute-start(f32[2,8,4,128]{3,2,1,0:T(4,128)S(1)} %slice.144), channel_id=1, source_target_pairs={{0,8},{8,0},{16,24},{24,16},{32,40},{40,32},{48,56},{56,48},{1,9},... | collective-permute-start | bytes 98312 | tf_op jit(solution)/shard_map/ppermute | solution.py:24
  8.9 2.7 %collective-permute-done = f32[2,8,4,128]{3,2,1,0:T(4,128)S(1)} collective-permute-done((f32[2,8,4,128]{3,2,1,0:T(4,128)S(1)}, f32[2,8,4,128]{3,2,1,0:T(4,128)S(1)}, u32[]{:S(2)}, u32[]{:S(2)}) %collective-permute-start) | collective-permute-done | bytes 32800 | tf_op jit(solution)/shard_map/ppermute | solution.py:24
  11.6 0.0 collective-permute-done.1
  11.7 0.0 copy-done.1
  11.7 0.0 copy-done
  11.7 0.4 fusion.13
  12.1 1.9 %collective-permute-start.2 = (f32[32,768]{1,0:T(8,128)S(1)}, f32[32,768]{1,0:T(8,128)S(1)}, u32[]{:S(2)}, u32[]{:S(2)}) collective-permute-start(f32[32,768]{1,0:T(8,128)S(1)} %get-tuple-element.21), channel_id=1, source_target_pairs={{1,0},{2,1},{3,2},{4,3},{5,4},{6,5},{7,6},{9,8},{10,9},{11,10},{12... | collective-permute-start | bytes 294920 | tf_op jit(solution)/shard_map/ppermute | solution.py:363
  14.1 6.1 %collective-permute-start.3 = (f32[32,768]{1,0:T(8,128)S(1)}, f32[32,768]{1,0:T(8,128)S(1)}, u32[]{:S(2)}, u32[]{:S(2)}) collective-permute-start(f32[32,768]{1,0:T(8,128)S(1)} %get-tuple-element.22), channel_id=1, source_target_pairs={{0,1},{1,2},{2,3},{3,4},{4,5},{5,6},{6,7},{8,9},{9,10},{10,11},{11... | collective-permute-start | bytes 294920 | tf_op jit(solution)/shard_map/ppermute | solution.py:364
  20.2 0.1 collective-permute-done.2
  20.3 1.6 %collective-permute-done.3 = f32[32,768]{1,0:T(8,128)S(1)} collective-permute-done((f32[32,768]{1,0:T(8,128)S(1)}, f32[32,768]{1,0:T(8,128)S(1)}, u32[]{:S(2)}, u32[]{:S(2)}) %collective-permute-start.3) | collective-permute-done | bytes 98336 | tf_op jit(solution)/shard_map/ppermute | solution.py:364
  21.8 0.3 fusion
  22.2 0.1 pad_maximum_fusion.1
  22.3 4.9 %collective-permute-start.4 = (f32[3,4,48,128]{3,2,1,0:T(8,128)S(1)}, f32[3,4,48,128]{3,2,1,0:T(8,128)S(1)}, u32[]{:S(2)}, u32[]{:S(2)}) collective-permute-start(f32[3,4,48,128]{3,2,1,0:T(8,128)S(1)} %slice_select_fusion), channel_id=1, source_target_pairs={{0,64},{64,0},{128,192},{192,128},{256,320},{320,256},{384,448},{4... | collective-permute-start | bytes 884744 | tf_op jit(solution)/shard_map/ppermute | solution.py:24
  27.1 4.4 %collective-permute-start.6 = (f32[3,8,48,128]{3,2,1,0:T(8,128)S(1)}, f32[3,8,48,128]{3,2,1,0:T(8,128)S(1)}, u32[]{:S(2)}, u32[]{:S(2)}) collective-permute-start(f32[3,8,48,128]{3,2,1,0:T(8,128)S(1)} %pad_maximum_fusion.1), channel_id=1, source_target_pairs={{64,128},{128,64},{192,256},{256,192},{320,384},{384,320},{448,512... | collective-permute-start | bytes 1769480 | tf_op jit(solution)/shard_map/ppermute | solution.py:24
  31.6 0.0 collective-permute-done.4
  31.6 2.3 %collective-permute-start.5 = (f32[3,2,48,128]{3,2,1,0:T(8,128)S(1)}, f32[3,2,48,128]{3,2,1,0:T(8,128)S(1)}, u32[]{:S(2)}, u32[]{:S(2)}) collective-permute-start(f32[3,2,48,128]{3,2,1,0:T(8,128)S(1)} %slice_select_fusion.1), channel_id=1, source_target_pairs={{64,128},{128,64},{192,256},{256,192},{320,384},{384,320},{448,512... | collective-permute-start | bytes 442376 | tf_op jit(solution)/shard_map/ppermute | solution.py:24
  34.0 7.2 %collective-permute-done.5 = f32[3,2,48,128]{3,2,1,0:T(8,128)S(1)} collective-permute-done((f32[3,2,48,128]{3,2,1,0:T(8,128)S(1)}, f32[3,2,48,128]{3,2,1,0:T(8,128)S(1)}, u32[]{:S(2)}, u32[]{:S(2)}) %collective-permute-start.5) | collective-permute-done | bytes 147488 | tf_op jit(solution)/shard_map/ppermute | solution.py:24
  41.1 0.0 collective-permute-done.6
  41.1 0.1 maximum_select_fusion
  41.2 0.1 pad_maximum_fusion.wide
  41.4 5.4 %shard_map.28 = (f32[2,11,24,128]{3,2,1,0:T(8,128)S(1)}, f32[3,12,48,256]{3,2,1,0:T(8,128)S(1)}) custom-call(f32[3,22,48,128]{3,2,1,0:T(8,128)S(1)} %pad_maximum_fusion.wide), custom_call_target="tpu_custom_call" | custom-call | tf_op jit(solution)/shard_map/pallas_call | solution.py:320
  46.9 1.9 %collective-permute-start.7 = (f32[2,8,12,128]{3,2,1,0:T(8,128)S(1)}, f32[2,8,12,128]{3,2,1,0:T(8,128)S(1)}, u32[]{:S(2)}, u32[]{:S(2)}) collective-permute-start(f32[2,8,12,128]{3,2,1,0:T(8,128)S(1)} %slice_select_fusion.2), channel_id=1, source_target_pairs={{0,8},{8,0},{16,24},{24,16},{32,40},{40,32},{48,56},{56,48},{1,9},... | collective-permute-start | bytes 294920 | tf_op jit(solution)/shard_map/ppermute | solution.py:24
  48.9 4.4 %collective-permute-done.7 = f32[2,8,12,128]{3,2,1,0:T(8,128)S(1)} collective-permute-done((f32[2,8,12,128]{3,2,1,0:T(8,128)S(1)}, f32[2,8,12,128]{3,2,1,0:T(8,128)S(1)}, u32[]{:S(2)}, u32[]{:S(2)}) %collective-permute-start.7) | collective-permute-done | bytes 98336 | tf_op jit(solution)/shard_map/ppermute | solution.py:24
  53.3 1.9 %collective-permute-start.8 = (f32[2,8,32,128]{3,2,1,0:T(8,128)S(1)}, f32[2,8,32,128]{3,2,1,0:T(8,128)S(1)}, u32[]{:S(2)}, u32[]{:S(2)}) collective-permute-start(f32[2,8,32,128]{3,2,1,0:T(8,128)S(1)} %maximum_select_fusion.2), channel_id=1, source_target_pairs={{0,64},{64,0},{128,192},{192,128},{256,320},{320,256},{384,448},{4... | collective-permute-start | bytes 786440 | tf_op jit(solution)/shard_map/ppermute | solution.py:24
  55.3 0.1 and_convert_fusion.box
  55.4 1.4 %collective-permute-done.8 = f32[2,8,32,128]{3,2,1,0:T(8,128)S(1)} collective-permute-done((f32[2,8,32,128]{3,2,1,0:T(8,128)S(1)}, f32[2,8,32,128]{3,2,1,0:T(8,128)S(1)}, u32[]{:S(2)}, u32[]{:S(2)}) %collective-permute-start.8) | collective-permute-done | bytes 262176 | tf_op jit(solution)/shard_map/ppermute | solution.py:24
  56.8 0.1 maximum_select_fusion.1.pair
  56.8 1.5 %shard_map.29 = (f32[12,32,128]{2,1,0:T(8,128)S(1)}, f32[5,12,32,128]{3,2,1,0:T(8,128)S(1)}) custom-call(f32[2,16,32,128]{3,2,1,0:T(8,128)S(1)} %maximum_select_fusion.1.pair, f32[8,16,128]{2,1,0:T(8,128)S(1)} %and_convert_fusion.box, s32[1]{0:T(128)} %bitcast.4.parity), custom_call_target="tpu_custom_call" | custom-call | tf_op jit(solution)/shard_map/pallas_call | solution.py:320
  58.4 2.2 %collective-permute-start.9 = (f32[12,4,128]{2,1,0:T(4,128)S(1)}, f32[12,4,128]{2,1,0:T(4,128)S(1)}, u32[]{:S(2)}, u32[]{:S(2)}) collective-permute-start(f32[12,4,128]{2,1,0:T(4,128)S(1)} %slice_select_fusion.3), channel_id=1, source_target_pairs={{8,16},{16,8},{24,32},{32,24},{40,48},{48,40},{9,17},{17,9},{25,33... | collective-permute-start | bytes 73736 | tf_op jit(solution)/shard_map/ppermute | solution.py:24
  60.6 3.5 %collective-permute-done.9 = f32[12,4,128]{2,1,0:T(4,128)S(1)} collective-permute-done((f32[12,4,128]{2,1,0:T(4,128)S(1)}, f32[12,4,128]{2,1,0:T(4,128)S(1)}, u32[]{:S(2)}, u32[]{:S(2)}) %collective-permute-start.9) | collective-permute-done | bytes 24608 | tf_op jit(solution)/shard_map/ppermute | solution.py:24
  64.2 6.1 %collective-permute-start.10 = (f32[4,32,128]{2,1,0:T(8,128)S(1)}, f32[4,32,128]{2,1,0:T(8,128)S(1)}, u32[]{:S(2)}, u32[]{:S(2)}) collective-permute-start(f32[4,32,128]{2,1,0:T(8,128)S(1)} %get-tuple-element.20), channel_id=1, source_target_pairs={{64,128},{128,64},{192,256},{256,192},{320,384},{384,320},{448,512... | collective-permute-start | bytes 196616 | tf_op jit(solution)/shard_map/ppermute | solution.py:24
  70.3 1.9 %collective-permute-done.10 = f32[4,32,128]{2,1,0:T(8,128)S(1)} collective-permute-done((f32[4,32,128]{2,1,0:T(8,128)S(1)}, f32[4,32,128]{2,1,0:T(8,128)S(1)}, u32[]{:S(2)}, u32[]{:S(2)}) %collective-permute-start.10) | collective-permute-done | bytes 65568 | tf_op jit(solution)/shard_map/ppermute | solution.py:24
  72.3 2.4 %shard_map.30 = f32[8,32,128]{2,1,0:T(8,128)} custom-call(f32[12,32,128]{2,1,0:T(8,128)S(1)} %maximum_select_fusion.5.middle, f32[5,12,32,128]{3,2,1,0:T(8,128)S(1)} %get-tuple-element.11.kept_m, f32[3,12,48,256]{3,2,1,0:T(8,128)S(1)} %get-tuple-element.12.kept), custom_call_target="tpu_custom_call" | custom-call | tf_op jit(solution)/shard_map/pallas_call | solution.py:320
  (25 shorter events, 0.4 us)
Async XLA Ops:
  0.0 11.7 %copy-start.1 = (f32[8,32,128]{2,1,0:T(8,128)S(1)}, f32[8,32,128]{2,1,0:T(8,128)}, u32[]{:S(2)}) copy-start(f32[8,32,128]{2,1,0:T(8,128)} %param.2) | copy-start | bytes 393220
  0.0 11.7 %copy-start = (f32[8,32,128]{2,1,0:T(8,128)S(1)}, f32[8,32,128]{2,1,0:T(8,128)}, u32[]{:S(2)}) copy-start(f32[8,32,128]{2,1,0:T(8,128)} %param.3) | copy-start | bytes 393220
  2.6 9.0 %collective-permute-start.1 = (f32[2,8,12,128]{3,2,1,0:T(8,128)S(1)}, f32[2,8,12,128]{3,2,1,0:T(8,128)S(1)}, u32[]{:S(2)}, u32[]{:S(2)}) collective-permute-start(f32[2,8,12,128]{3,2,1,0:T(8,128)S(1)} %bitcast.26), channel_id=1, source_target_pairs={{8,16},{16,8},{24,32},{32,24},{40,48},{48,40},{9,17},{17,9},{25,33... | collective-permute-start | bytes 294920 | tf_op jit(solution)/shard_map/ppermute | solution.py:24
  7.0 4.7 %collective-permute-start = (f32[2,8,4,128]{3,2,1,0:T(4,128)S(1)}, f32[2,8,4,128]{3,2,1,0:T(4,128)S(1)}, u32[]{:S(2)}, u32[]{:S(2)}) collective-permute-start(f32[2,8,4,128]{3,2,1,0:T(4,128)S(1)} %slice.144), channel_id=1, source_target_pairs={{0,8},{8,0},{16,24},{24,16},{32,40},{40,32},{48,56},{56,48},{1,9},... | collective-permute-start | bytes 98312 | tf_op jit(solution)/shard_map/ppermute | solution.py:24
  12.1 8.1 %collective-permute-start.2 = (f32[32,768]{1,0:T(8,128)S(1)}, f32[32,768]{1,0:T(8,128)S(1)}, u32[]{:S(2)}, u32[]{:S(2)}) collective-permute-start(f32[32,768]{1,0:T(8,128)S(1)} %get-tuple-element.21), channel_id=1, source_target_pairs={{1,0},{2,1},{3,2},{4,3},{5,4},{6,5},{7,6},{9,8},{10,9},{11,10},{12... | collective-permute-start | bytes 294920 | tf_op jit(solution)/shard_map/ppermute | solution.py:363
  14.1 7.7 %collective-permute-start.3 = (f32[32,768]{1,0:T(8,128)S(1)}, f32[32,768]{1,0:T(8,128)S(1)}, u32[]{:S(2)}, u32[]{:S(2)}) collective-permute-start(f32[32,768]{1,0:T(8,128)S(1)} %get-tuple-element.22), channel_id=1, source_target_pairs={{0,1},{1,2},{2,3},{3,4},{4,5},{5,6},{6,7},{8,9},{9,10},{10,11},{11... | collective-permute-start | bytes 294920 | tf_op jit(solution)/shard_map/ppermute | solution.py:364
  22.3 9.3 %collective-permute-start.4 = (f32[3,4,48,128]{3,2,1,0:T(8,128)S(1)}, f32[3,4,48,128]{3,2,1,0:T(8,128)S(1)}, u32[]{:S(2)}, u32[]{:S(2)}) collective-permute-start(f32[3,4,48,128]{3,2,1,0:T(8,128)S(1)} %slice_select_fusion), channel_id=1, source_target_pairs={{0,64},{64,0},{128,192},{192,128},{256,320},{320,256},{384,448},{4... | collective-permute-start | bytes 884744 | tf_op jit(solution)/shard_map/ppermute | solution.py:24
  27.1 14.0 %collective-permute-start.6 = (f32[3,8,48,128]{3,2,1,0:T(8,128)S(1)}, f32[3,8,48,128]{3,2,1,0:T(8,128)S(1)}, u32[]{:S(2)}, u32[]{:S(2)}) collective-permute-start(f32[3,8,48,128]{3,2,1,0:T(8,128)S(1)} %pad_maximum_fusion.1), channel_id=1, source_target_pairs={{64,128},{128,64},{192,256},{256,192},{320,384},{384,320},{448,512... | collective-permute-start | bytes 1769480 | tf_op jit(solution)/shard_map/ppermute | solution.py:24
  31.6 9.5 %collective-permute-start.5 = (f32[3,2,48,128]{3,2,1,0:T(8,128)S(1)}, f32[3,2,48,128]{3,2,1,0:T(8,128)S(1)}, u32[]{:S(2)}, u32[]{:S(2)}) collective-permute-start(f32[3,2,48,128]{3,2,1,0:T(8,128)S(1)} %slice_select_fusion.1), channel_id=1, source_target_pairs={{64,128},{128,64},{192,256},{256,192},{320,384},{384,320},{448,512... | collective-permute-start | bytes 442376 | tf_op jit(solution)/shard_map/ppermute | solution.py:24
  46.9 6.4 %collective-permute-start.7 = (f32[2,8,12,128]{3,2,1,0:T(8,128)S(1)}, f32[2,8,12,128]{3,2,1,0:T(8,128)S(1)}, u32[]{:S(2)}, u32[]{:S(2)}) collective-permute-start(f32[2,8,12,128]{3,2,1,0:T(8,128)S(1)} %slice_select_fusion.2), channel_id=1, source_target_pairs={{0,8},{8,0},{16,24},{24,16},{32,40},{40,32},{48,56},{56,48},{1,9},... | collective-permute-start | bytes 294920 | tf_op jit(solution)/shard_map/ppermute | solution.py:24
  53.3 3.4 %collective-permute-start.8 = (f32[2,8,32,128]{3,2,1,0:T(8,128)S(1)}, f32[2,8,32,128]{3,2,1,0:T(8,128)S(1)}, u32[]{:S(2)}, u32[]{:S(2)}) collective-permute-start(f32[2,8,32,128]{3,2,1,0:T(8,128)S(1)} %maximum_select_fusion.2), channel_id=1, source_target_pairs={{0,64},{64,0},{128,192},{192,128},{256,320},{320,256},{384,448},{4... | collective-permute-start | bytes 786440 | tf_op jit(solution)/shard_map/ppermute | solution.py:24
  58.4 5.8 %collective-permute-start.9 = (f32[12,4,128]{2,1,0:T(4,128)S(1)}, f32[12,4,128]{2,1,0:T(4,128)S(1)}, u32[]{:S(2)}, u32[]{:S(2)}) collective-permute-start(f32[12,4,128]{2,1,0:T(4,128)S(1)} %slice_select_fusion.3), channel_id=1, source_target_pairs={{8,16},{16,8},{24,32},{32,24},{40,48},{48,40},{9,17},{17,9},{25,33... | collective-permute-start | bytes 73736 | tf_op jit(solution)/shard_map/ppermute | solution.py:24
  64.2 8.0 %collective-permute-start.10 = (f32[4,32,128]{2,1,0:T(8,128)S(1)}, f32[4,32,128]{2,1,0:T(8,128)S(1)}, u32[]{:S(2)}, u32[]{:S(2)}) collective-permute-start(f32[4,32,128]{2,1,0:T(8,128)S(1)} %get-tuple-element.20), channel_id=1, source_target_pairs={{64,128},{128,64},{192,256},{256,192},{320,384},{384,320},{448,512... | collective-permute-start | bytes 196616 | tf_op jit(solution)/shard_map/ppermute | solution.py:24

commit v5 on v4

v5 whole, which is shorter than its diff:
```python
import math

import jax
import jax.numpy as jnp
from jax import lax
from jax.experimental import pallas as pl
from jax.experimental.pallas import tpu as pltpu
from jax.sharding import PartitionSpec as P

spectrum_top = 1.9
spectrum_low = 0.475
mean_value = (spectrum_top + spectrum_low) / 2
half_range = (spectrum_top - spectrum_low) / 2
omega_first = 1.0 / (mean_value + half_range * math.cos(math.pi / 4))
omega_second = 1.0 / (mean_value + half_range * math.cos(3 * math.pi / 4))
HIGHEST = lax.Precision.HIGHEST


def swap(block, axis, outer):
    count = lax.axis_size(axis)
    route = []
    for low in range(1 if outer else 0, count - 1, 2):
        route += [(low, low + 1), (low + 1, low)]
    return lax.ppermute(block, axis, route)


def cut(values, start, stop, dim):
    return lax.slice_in_dim(values, start, stop, axis=dim)


def join(pieces, dim):
    return jnp.concatenate(pieces, axis=dim)


def turn(plane, dim, step):
    return pltpu.roll(plane, -step % plane.shape[dim], dim)


class Operator:
    def __init__(self, faces):
        self.faces = faces

    def build(self, coeff, start, stop, take):
        before = coeff(start - 1) + coeff(start)
        self.faces[0, start - 1] = before
        for i in range(start, stop):
            here = coeff(i)
            across = here + coeff(i + 1)
            rows = here + turn(here, 0, 1)
            lanes = here + turn(here, 1, 1)
            for place, face in enumerate((across, rows, lanes)):
                self.faces[place, i] = face
            diagonal = (across + before) + (rows + turn(rows, 0, -1)) + (lanes + turn(lanes, 1, -1))
            take(i, jnp.where(here > 0, 1.0 / diagonal, 0.0))
            before = across

    def apply(self, field, start, stop, take):
        before = self.faces[0, start - 1] * (field(start - 1) - field(start))
        for i in range(start, stop):
            here = field(i)
            across = self.faces[0, i] * (here - field(i + 1))
            rows = self.faces[1, i] * (here - turn(here, 0, 1))
            lanes = self.faces[2, i] * (here - turn(here, 1, 1))
            take(i, (across - before) + (rows - turn(rows, 0, -1)) + (lanes - turn(lanes, 1, -1)))
            before = across


def sweep(operator, field, inverse, rhs, omega, start, stop, store):
    def take(i, applied):
        store(i, field(i) + (omega * (rhs(i) - applied)) * inverse(i))

    operator.apply(field, start, stop, take)


def plane_of(ref, *lead):
    return lambda i: ref[(*lead, i)]


def keep_in(ref, *lead):
    def store(i, value):
        ref[(*lead, i)] = value

    return store


def halve_rows(piece, weights):
    count = piece.shape[0] // 2
    even = piece[pl.ds(0, count, 2), :]
    odd = piece[pl.ds(1, count, 2), :]
    if not weights:
        return even + odd
    return 0.375 * (even + odd) + 0.125 * (turn(odd, 0, -1) + turn(even, 0, 1))


def product(values, matrix):
    return jnp.dot(values, matrix, precision=HIGHEST, preferred_element_type=jnp.float32)


def lane_map(rows, columns, entries):
    row = lax.broadcasted_iota(jnp.int32, (rows, columns), 0)
    column = lax.broadcasted_iota(jnp.int32, (rows, columns), 1)
    return entries(row, column).astype(jnp.float32)


def signed(index, size, after):
    return jnp.where(index < after, index, index - size)


def gather_weights(fine, coarse):
    step = fine - 2 * coarse
    return jnp.where((step == 0) | (step == 1), 0.375, jnp.where((step == -1) | (step == 2), 0.125, 0.0))


def mean_weights(fine, coarse):
    step = fine - 2 * coarse
    return jnp.where((step == 0) | (step == 1), 0.5, 0.0)


def spread_weights(coarse, fine):
    step = fine - 2 * coarse
    return jnp.where((step == 0) | (step == 1), 0.75, jnp.where((step == -1) | (step == 2), 0.25, 0.0))


def fine_lane(f):
    return signed(f, 256, 192)


def middle_lane(m):
    return signed(m, 128, 96)


def coarse_lane(lane, odd):
    after = jnp.where(lane < 32, lane, jnp.where((lane == 32) & (odd == 1), 4096, lane - odd))
    before = jnp.where((lane == 127) & (odd == 0), 4096, lane - 127 - odd)
    return jnp.where(lane < 64, after, before)


def same_box(coarse, middle, odd):
    edge = 32 * odd
    return (coarse >= edge) == (middle >= 2 * edge)


def restrict_level(plane, coeff, first, count, piece, packed, matrices, store):
    rows, lanes = piece.shape[1:]
    parts = packed.shape[2] // lanes
    for j in range(count):
        at = first + 2 * j
        planes = (
            0.375 * (plane(at) + plane(at + 1)) + 0.125 * (plane(at - 1) + plane(at + 2)),
            coeff(at) + coeff(at + 1),
        )
        for kind in range(2):
            for part in range(parts):
                slot = piece.at[(2 * j + kind) * parts + part]
                slot[...] = planes[kind][:, lanes * part : lanes * part + lanes]
                packed[kind, pl.ds(rows // 2 * j, rows // 2), pl.ds(lanes * part, lanes)] = halve_rows(
                    slot, kind == 0
                )
    for kind in range(2):
        result = product(packed[kind], matrices[kind])
        for j in range(count):
            store(kind, j, result[rows // 2 * j : rows // 2 * (j + 1)])


def first_kernel(source, conductivity, parity, far, near):
    for kind, values in enumerate((source, conductivity)):
        for odd in range(2):

            @pl.when(parity[0] == odd)
            def _(kind=kind, values=values, odd=odd):
                for i in range(8):
                    far[kind, i] = values[i, 20:32] if odd else values[i, 0:12]
                    near[kind, i] = values[i, 0:4] if odd else values[i, 28:32]


def fine_kernel(wide, pair, kept, faces, inverse, rhs, coeff, field, pre, piece, packed):
    lane = lax.broadcasted_iota(jnp.int32, (48, 128), 1)
    edge = (lane < 32) | (lane >= 96)
    for i in range(16):
        halo = wide[2, i]
        rhs[i, :, 0:128] = 2.0 * wide[0, i]
        rhs[i, :, 128:256] = jnp.where(edge, 2.0 * halo, 0.0)
        coeff[i, :, 0:128] = wide[1, i]
        coeff[i, :, 128:256] = jnp.where(edge, pltpu.roll(halo, 64, 1), 0.0)
    operator = Operator(faces)

    def begin(i, value):
        inverse[i] = value
        field[i] = omega_first * rhs[i] * value

    operator.build(plane_of(coeff), 1, 15, begin)

    def store_pre(i, value):
        pre[i] = value
        kept[0, i - 2] = coeff[i]
        kept[1, i - 2] = rhs[i]
        kept[2, i - 2] = value

    sweep(operator, plane_of(field), plane_of(inverse), plane_of(rhs), omega_second, 2, 14, store_pre)

    def leave(i, applied):
        field[i] = jnp.where(coeff[i] > 0, rhs[i] - applied, 0.0)

    operator.apply(plane_of(pre), 3, 13, leave)
    matrices = (
        lane_map(256, 128, lambda f, c: 4.0 * gather_weights(fine_lane(f), middle_lane(c))),
        lane_map(256, 128, lambda f, c: 0.25 * mean_weights(fine_lane(f), middle_lane(c))),
    )

    def store(kind, j, value):
        pair[kind, j] = value

    restrict_level(plane_of(field), plane_of(coeff), 4, 4, piece, packed, matrices, store)


def box_kernel(pair, box, parity, corrected, faces, inverse, field, other, piece, packed, low, low_faces, low_inverse, risen):
    rhs, coeff = plane_of(pair, 0), plane_of(pair, 1)
    operator = Operator(faces)

    def begin(i, value):
        inverse[i] = value
        field[i] = omega_first * rhs(i) * value

    operator.build(coeff, 1, 15, begin)
    sweep(operator, plane_of(field), plane_of(inverse), rhs, omega_second, 2, 14, keep_in(other))

    def leave(i, applied):
        field[i] = jnp.where(coeff(i) > 0, rhs(i) - applied, 0.0)

    operator.apply(plane_of(other), 3, 13, leave)
    odd = parity[0]
    matrices = (
        lane_map(128, 128, lambda m, c: 4.0 * gather_weights(middle_lane(m), coarse_lane(c, odd))),
        lane_map(128, 128, lambda m, c: 0.25 * mean_weights(middle_lane(m), coarse_lane(c, odd))),
    )
    in_box = box[...]

    def store(kind, j, value):
        low[kind, j + 1] = value * in_box

    restrict_level(plane_of(field), coeff, 4, 4, piece, packed, matrices, store)
    for place in (0, 5):
        for kind in range(3):
            low[kind, place] = jnp.zeros((16, 128), jnp.float32)
    coarse = Operator(low_faces)

    def begin_low(i, value):
        low_inverse[i] = value
        low[2, i] = omega_first * low[0, i] * value

    coarse.build(plane_of(low, 1), 1, 5, begin_low)

    def store_low(i, value):
        packed[0, pl.ds(16 * (i - 1), 16), :] = value

    sweep(coarse, plane_of(low, 2), plane_of(low_inverse), plane_of(low, 0), omega_second, 1, 5, store_low)

    def spread_box(c, m):
        coarse, fine = coarse_lane(c, odd), middle_lane(m)
        return jnp.where(same_box(coarse, fine, odd), spread_weights(coarse, fine), 0.0)

    result = product(packed[0], lane_map(128, 128, spread_box))
    for j in range(4):
        spread_rows(result[16 * j : 16 * j + 16], risen.at[j])
    for i in range(8):
        value = 0.75 * risen[i // 2]
        near = i // 2 + (1 if i % 2 else -1)
        if 0 <= near < 4:
            value = value + 0.25 * risen[near]
        corrected[i] = other[i + 4] + value


def spread_rows(values, target):
    count = values.shape[0]
    target[pl.ds(0, count, 2), :] = 0.75 * values + 0.25 * turn(values, 0, -1)
    target[pl.ds(1, count, 2), :] = 0.75 * values + 0.25 * turn(values, 0, 1)


def last_kernel(middle, pair, kept, out, faces, inverse, field, faces_m, inverse_m, field_m, packed, risen):
    operator = Operator(faces_m)
    rhs_m, at_m = plane_of(pair, 0), plane_of(inverse_m)
    operator.build(plane_of(pair, 1), 1, 11, keep_in(inverse_m))
    sweep(operator, plane_of(middle), at_m, rhs_m, omega_first, 1, 11, keep_in(field_m))

    def store_packed(i, value):
        packed[pl.ds(32 * (i - 2), 32), :] = value

    sweep(operator, plane_of(field_m), at_m, rhs_m, omega_second, 2, 10, store_packed)
    result = product(
        packed[...], lane_map(128, 256, lambda c, f: spread_weights(middle_lane(c), fine_lane(f)))
    )
    for place in range(8):
        for half in range(2):
            spread_rows(
                result[32 * place : 32 * place + 32, 128 * half : 128 * half + 128],
                risen.at[2 * place + half],
            )

    def lifted(place):
        halves = [
            jnp.concatenate([risen[2 * place + half, 0:40], risen[2 * place + half, 56:64]], axis=0)
            for half in range(2)
        ]
        return jnp.concatenate(halves, axis=1)

    fine = Operator(faces)
    coeff, rhs = plane_of(kept, 0), plane_of(kept, 1)
    fine.build(coeff, 1, 11, keep_in(inverse))
    for i in range(12):
        place = i // 2 + 1
        value = 0.75 * lifted(place) + 0.25 * lifted(place + (1 if i % 2 else -1))
        field[0, i] = kept[2, i] + jnp.where(coeff(i) > 0, value, 0.0)
    sweep(fine, plane_of(field, 0), plane_of(inverse), rhs, omega_first, 1, 11, keep_in(field, 1))

    def store_out(i, value):
        out[i - 2] = value[:32, :128]

    sweep(fine, plane_of(field, 1), plane_of(inverse), rhs, omega_second, 2, 10, store_out)


interpret = False
VMEM = pl.BlockSpec(memory_space=pltpu.VMEM)
SMEM = pl.BlockSpec(memory_space=pltpu.SMEM)


def call(kernel, outs, scratch, *arguments):
    return pl.pallas_call(
        kernel,
        out_shape=[jax.ShapeDtypeStruct(shape, jnp.float32) for shape in outs],
        in_specs=[VMEM if value.ndim > 1 else SMEM for value in arguments],
        out_specs=[VMEM] * len(outs),
        scratch_shapes=[pltpu.VMEM(shape, jnp.float32) for shape in scratch],
        compiler_params=pltpu.CompilerParams(vmem_limit_bytes=24 * 1024 * 1024),
        interpret=interpret,
    )(*arguments)


def take_lanes(values, matrix):
    rows = values.reshape(-1, values.shape[-1])
    return lax.dot_general(matrix, rows, (((0,), (1,)), ((), ())), precision=HIGHEST)


def put_lanes(strip, matrix, shape):
    rows = lax.dot_general(strip, matrix, (((0,), (0,)), ((), ())), precision=HIGHEST)
    return rows.reshape(shape)


def local(source, conductivity):
    low_x = lax.axis_index("gx") % 2 == 0
    low_y = lax.axis_index("gy") % 2 == 0
    odd_z = (lax.axis_index("gz") % 2).reshape(1)

    def side(low, when_low, when_high):
        return jnp.where(low, when_low, when_high)

    far, near = call(
        first_kernel,
        [(2, 8, 12, 128), (2, 8, 4, 128)],
        [],
        source,
        conductivity,
        (lax.axis_index("gy") % 2).reshape(1),
    )
    far = swap(far, "gy", True)
    near = swap(near, "gy", False)
    cells = jnp.stack([source, conductivity])
    cells = join([cells, side(low_y, join([near, far], 2), join([far, near], 2))], 2)

    strips = take_lanes(cells, lane_map(128, 64, lambda z, k: z == k + jnp.where(k < 32, 0, 64)))
    count = lax.axis_size("gz")
    after = lax.ppermute(strips[:32], "gz", [(i + 1, i) for i in range(count - 1)])
    before = lax.ppermute(strips[32:], "gz", [(i, i + 1) for i in range(count - 1)])
    rows = strips.shape[1] // 2
    halo = join([after[:, :rows], before[:, rows:], after[:, rows:], before[:, :rows]], 0)
    halo = put_lanes(halo, lane_map(128, 128, lambda k, z: k == z), (1, 8, 48, 128))
    cells = join([cells, halo], 0)

    far = swap(side(low_x, cells[:, :4], cells[:, 4:]), "gx", True)
    near = swap(side(low_x, cells[:, 4:], cells[:, :4]), "gx", False)
    wide = join([side(low_x, far, near), cells, side(low_x, near, far)], 1)

    plane = (48, 256)
    pair, kept = call(
        fine_kernel,
        [(2, 4, 24, 128), (3, 12, *plane)],
        [(3, 16, *plane)] + [(16, *plane)] * 5 + [(16, 48, 128), (2, 96, 256)],
        wide,
    )

    near = swap(side(low_y, pair[:, :, 4:16], pair[:, :, :12]), "gy", False)
    pair = side(
        low_y,
        join([pair[:, :, :16], near, pair[:, :, 20:]], 2),
        join([pair[:, :, :20], near], 2),
    )
    far = swap(pair, "gx", True)
    pair = side(low_x, join([far, pair], 1), join([pair, far], 1))
    near = swap(pair, "gx", False)
    pair = side(low_x, join([pair, near], 1), join([near, pair], 1))

    row = lax.broadcasted_iota(jnp.int32, (16, 128), 0)
    in_box = side(low_y, row < 14, (row < 8) | (row >= 10))
    (middle,) = call(
        box_kernel,
        [(8, 32, 128)],
        [(3, 16, 32, 128), (16, 32, 128), (16, 32, 128), (16, 32, 128), (8, 32, 128), (2, 64, 128)]
        + [(3, 6, 16, 128), (3, 6, 16, 128), (6, 16, 128), (4, 32, 128)],
        pair,
        in_box.astype(jnp.float32),
        odd_z,
    )

    far = swap(side(low_y, middle[:, :4], middle[:, 12:16]), "gy", True)
    middle = side(
        low_y, join([middle[:, :28], far], 1), join([middle[:, :16], far, middle[:, 20:]], 1)
    )
    far = swap(side(low_x, middle[:4], middle[4:]), "gx", True)
    middle = side(low_x, join([far, middle], 0), join([middle, far], 0))

    (pressure,) = call(
        last_kernel,
        [(8, 32, 128)],
        [(3, 12, *plane), (12, *plane), (2, 12, *plane), (3, 12, 32, 128), (12, 32, 128), (12, 32, 128)]
        + [(256, 128), (16, 64, 128)],
        middle,
        side(low_x, pair[:, :12], pair[:, 4:]),
        kept,
    )
    return pressure


def solution(mesh):
    spec = P("gx", "gy", "gz")
    return jax.shard_map(local, mesh=mesh, in_specs=(spec, spec), out_specs=spec, check_vma=False)
```

time: 75.2 us -> 73.5 us (0.977)
  starting transfers between devices: 38.1 us -> 41.3 us
  waiting for transfers between devices: 22.7 us -> 19.6 us
  local copies, waits for them, and re-layouts: 0.14 us -> 1.95 us
  other arithmetic: 3.32 us -> 1.53 us
  Pallas kernels: 9.34 us -> 7.65 us
    ppermute x9, starting transfers between devices: 30 us -> 33.2 us  [swap(): return lax.ppermute(block, axis, route)]
    ppermute x9, waiting for transfers between devices: 21.1 us -> 18 us  [swap(): return lax.ppermute(block, axis, route)]
    unnamed x4 -> x8, local copies, waits for them, and re-layouts: 0.01 us -> 1.82 us
    another operation x2 -> x0, other arithmetic: 1.79 us -> none  [local(): cells = jnp.stack([source, conductivity])]
    pallas_call x3 -> x4, Pallas kernels: 9.34 us -> 7.65 us  [call(): pl.pallas_call(kernel, out_shape=[jax.ShapeDtypeStruct(shape, jnp.float32...]
    concatenate x3, other arithmetic: 0.22 us -> 1.18 us  [join(): return jnp.concatenate(pieces, axis=dim)]
    select_n x14 -> x12, other arithmetic: 1.23 us -> 0.34 us  [side(): return jnp.where(low, when_low, when_high)]
  transfers between devices with their start and end apart: 11 -> 11, of which waited for: 7 -> 8; matrix products, arithmetic and copies ran while one was open for 0% -> 0% of each run, Pallas kernels for 0% -> 0%
where the time goes in v5:
time: 73.5 us; the launch traced here: 73.1 us
  starting transfers between devices  41.3 us (56%)
  waiting for transfers between devices  19.6 us (27%)
  Pallas kernels  7.65 us (10%)
  local copies, waits for them, and re-layouts  1.95 us (3%)
  other arithmetic  1.53 us (2%)
    ppermute x9, starting transfers between devices, swap(): return lax.ppermute(block, axis, route)  33.2 us
    ppermute x9, waiting for transfers between devices, swap(): return lax.ppermute(block, axis, route)  18 us
    pallas_call x4, Pallas kernels, call(): pl.pallas_call(kernel, out_shape=[jax.ShapeDtypeStruct(shape, jnp.float32...  7.65 us
    ppermute x1, starting transfers between devices, local(): lax.ppermute(strips[32:], 'gz', [(i, i + 1) for i in range(count - 1)])  6.13 us
    ppermute x1, starting transfers between devices, local(): lax.ppermute(strips[:32], 'gz', [(i + 1, i) for i in range(count - 1)])  1.92 us
    unnamed x8, local copies, waits for them, and re-layouts  1.82 us
    ppermute x1, waiting for transfers between devices, local(): lax.ppermute(strips[32:], 'gz', [(i, i + 1) for i in range(count - 1)])  1.56 us
  transfers between devices with their start and end apart: 11, of which 8 were waited for; matrix products, arithmetic and copies ran while one was open for 0% of the time, Pallas kernels for 0%

profile of v5, /device:TPU:439, one launch (start us, length us, event | category | flops | bytes accessed | tf_op | source)
XLA Modules:
  0.0 73.1 jit_solution(3186786569337822201)
XLA Ops:
  0.0 0.0 copy-start
  0.0 0.9 %copy-done = f32[8,32,128]{2,1,0:T(8,128)S(1)} copy-done((f32[8,32,128]{2,1,0:T(8,128)S(1)}, f32[8,32,128]{2,1,0:T(8,128)}, u32[]{:S(2)}) %copy-start) | copy-done | bytes 131096
  0.9 0.0 copy-start.2
  0.9 0.9 %copy-done.2 = f32[8,32,128]{2,1,0:T(8,128)S(1)} copy-done((f32[8,32,128]{2,1,0:T(8,128)S(1)}, f32[8,32,128]{2,1,0:T(8,128)}, u32[]{:S(2)}) %copy-start.2) | copy-done | bytes 131096
  1.8 4.3 %collective-permute-start.1 = (f32[2,8,12,128]{3,2,1,0:T(8,128)S(1)}, f32[2,8,12,128]{3,2,1,0:T(8,128)S(1)}, u32[]{:S(2)}, u32[]{:S(2)}) collective-permute-start(f32[2,8,12,128]{3,2,1,0:T(8,128)S(1)} %get-tuple-element.10), channel_id=1, source_target_pairs={{8,16},{16,8},{24,32},{32,24},{40,48},{48,40},{9,17},{17,9},{25,33... | collective-permute-start | bytes 294920 | tf_op jit(solution)/shard_map/ppermute | solution.py:24
  6.2 1.9 %collective-permute-start = (f32[2,8,4,128]{3,2,1,0:T(4,128)S(1)}, f32[2,8,4,128]{3,2,1,0:T(4,128)S(1)}, u32[]{:S(2)}, u32[]{:S(2)}) collective-permute-start(f32[2,8,4,128]{3,2,1,0:T(4,128)S(1)} %get-tuple-element.9), channel_id=1, source_target_pairs={{0,8},{8,0},{16,24},{24,16},{32,40},{40,32},{48,56},{56,48},{1,9},... | collective-permute-start | bytes 98312 | tf_op jit(solution)/shard_map/ppermute | solution.py:24
  8.1 2.7 %collective-permute-done = f32[2,8,4,128]{3,2,1,0:T(4,128)S(1)} collective-permute-done((f32[2,8,4,128]{3,2,1,0:T(4,128)S(1)}, f32[2,8,4,128]{3,2,1,0:T(4,128)S(1)}, u32[]{:S(2)}, u32[]{:S(2)}) %collective-permute-start) | collective-permute-done | bytes 32800 | tf_op jit(solution)/shard_map/ppermute | solution.py:24
  10.8 0.0 collective-permute-done.1
  10.9 0.0 copy-start.1
  10.9 0.0 copy-start.3
  10.9 1.0 %pad_maximum_fusion.2 = f32[2,8,48,128]{3,2,1,0:T(8,128)S(1)} fusion(f32[2,8,16,128]{3,2,1,0:T(8,128)S(1)} %maximum_select_fusion.3, f32[1,8,32,128]{3,2,1,0:T(8,128)} %bitcast.12, f32[1,8,32,128]{3,2,1,0:T(8,128)} %bitcast.9), kind=kLoop, calls=%fused_computation.4 | loop fusion | flops 196608 | bytes 786432 | tf_op jit(solution)/shard_map/concatenate | solution.py:32
  11.9 0.4 fusion.9
  12.3 1.9 %collective-permute-start.2 = (f32[32,768]{1,0:T(8,128)S(1)}, f32[32,768]{1,0:T(8,128)S(1)}, u32[]{:S(2)}, u32[]{:S(2)}) collective-permute-start(f32[32,768]{1,0:T(8,128)S(1)} %get-tuple-element.17), channel_id=1, source_target_pairs={{1,0},{2,1},{3,2},{4,3},{5,4},{6,5},{7,6},{9,8},{10,9},{11,10},{12... | collective-permute-start | bytes 294920 | tf_op jit(solution)/shard_map/ppermute | solution.py:371
  14.3 6.1 %collective-permute-start.3 = (f32[32,768]{1,0:T(8,128)S(1)}, f32[32,768]{1,0:T(8,128)S(1)}, u32[]{:S(2)}, u32[]{:S(2)}) collective-permute-start(f32[32,768]{1,0:T(8,128)S(1)} %get-tuple-element.18), channel_id=1, source_target_pairs={{0,1},{1,2},{2,3},{3,4},{4,5},{5,6},{6,7},{8,9},{9,10},{10,11},{11... | collective-permute-start | bytes 294920 | tf_op jit(solution)/shard_map/ppermute | solution.py:372
  20.4 0.1 collective-permute-done.2
  20.5 1.6 %collective-permute-done.3 = f32[32,768]{1,0:T(8,128)S(1)} collective-permute-done((f32[32,768]{1,0:T(8,128)S(1)}, f32[32,768]{1,0:T(8,128)S(1)}, u32[]{:S(2)}, u32[]{:S(2)}) %collective-permute-start.3) | collective-permute-done | bytes 98336 | tf_op jit(solution)/shard_map/ppermute | solution.py:372
  22.0 0.3 fusion
  22.4 0.0 copy-done.1
  22.4 0.0 copy-done.3
  22.5 7.4 %collective-permute-start.4 = (f32[3,4,48,128]{3,2,1,0:T(8,128)S(1)}, f32[3,4,48,128]{3,2,1,0:T(8,128)S(1)}, u32[]{:S(2)}, u32[]{:S(2)}) collective-permute-start(f32[3,4,48,128]{3,2,1,0:T(8,128)S(1)} %get-tuple-element.15), channel_id=1, source_target_pairs={{64,128},{128,64},{192,256},{256,192},{320,384},{384,320},{448,512... | collective-permute-start | bytes 884744 | tf_op jit(solution)/shard_map/ppermute | solution.py:24
  29.9 1.9 %collective-permute-start.5 = (f32[3,4,48,128]{3,2,1,0:T(8,128)S(1)}, f32[3,4,48,128]{3,2,1,0:T(8,128)S(1)}, u32[]{:S(2)}, u32[]{:S(2)}) collective-permute-start(f32[3,4,48,128]{3,2,1,0:T(8,128)S(1)} %get-tuple-element.16), channel_id=1, source_target_pairs={{0,64},{64,0},{128,192},{192,128},{256,320},{320,256},{384,448},{4... | collective-permute-start | bytes 884744 | tf_op jit(solution)/shard_map/ppermute | solution.py:24
  31.8 2.5 %collective-permute-done.4 = f32[3,4,48,128]{3,2,1,0:T(8,128)S(1)} collective-permute-done((f32[3,4,48,128]{3,2,1,0:T(8,128)S(1)}, f32[3,4,48,128]{3,2,1,0:T(8,128)S(1)}, u32[]{:S(2)}, u32[]{:S(2)}) %collective-permute-start.4) | collective-permute-done | bytes 294944 | tf_op jit(solution)/shard_map/ppermute | solution.py:24
  34.3 0.0 collective-permute-done.5
  34.3 0.1 pad_maximum_fusion.wide
  34.4 2.8 %shard_map.29 = (f32[2,4,24,128]{3,2,1,0:T(8,128)S(1)}, f32[3,12,48,256]{3,2,1,0:T(8,128)S(1)}) custom-call(f32[3,16,48,128]{3,2,1,0:T(8,128)S(1)} %pad_maximum_fusion.wide), custom_call_target="tpu_custom_call" | custom-call | tf_op jit(solution)/shard_map/pallas_call | solution.py:327
  37.2 1.9 %collective-permute-start.6 = (f32[2,4,12,128]{3,2,1,0:T(8,128)S(1)}, f32[2,4,12,128]{3,2,1,0:T(8,128)S(1)}, u32[]{:S(2)}, u32[]{:S(2)}) collective-permute-start(f32[2,4,12,128]{3,2,1,0:T(8,128)S(1)} %slice_select_fusion.4), channel_id=1, source_target_pairs={{0,8},{8,0},{16,24},{24,16},{32,40},{40,32},{48,56},{56,48},{1,9},... | collective-permute-start | bytes 147464 | tf_op jit(solution)/shard_map/ppermute | solution.py:24
  39.2 3.4 %collective-permute-done.6 = f32[2,4,12,128]{3,2,1,0:T(8,128)S(1)} collective-permute-done((f32[2,4,12,128]{3,2,1,0:T(8,128)S(1)}, f32[2,4,12,128]{3,2,1,0:T(8,128)S(1)}, u32[]{:S(2)}, u32[]{:S(2)}) %collective-permute-start.6) | collective-permute-done | bytes 49184 | tf_op jit(solution)/shard_map/ppermute | solution.py:24
  42.7 5.6 %collective-permute-start.7 = (f32[2,4,32,128]{3,2,1,0:T(8,128)S(1)}, f32[2,4,32,128]{3,2,1,0:T(8,128)S(1)}, u32[]{:S(2)}, u32[]{:S(2)}) collective-permute-start(f32[2,4,32,128]{3,2,1,0:T(8,128)S(1)} %maximum_select_fusion.4), channel_id=1, source_target_pairs={{64,128},{128,64},{192,256},{256,192},{320,384},{384,320},{448,512... | collective-permute-start | bytes 393224 | tf_op jit(solution)/shard_map/ppermute | solution.py:24
  48.3 2.6 %collective-permute-done.7 = f32[2,4,32,128]{3,2,1,0:T(8,128)S(1)} collective-permute-done((f32[2,4,32,128]{3,2,1,0:T(8,128)S(1)}, f32[2,4,32,128]{3,2,1,0:T(8,128)S(1)}, u32[]{:S(2)}, u32[]{:S(2)}) %collective-permute-start.7) | collective-permute-done | bytes 131104 | tf_op jit(solution)/shard_map/ppermute | solution.py:24
  50.9 1.9 %collective-permute-start.8 = (f32[2,8,32,128]{3,2,1,0:T(8,128)S(1)}, f32[2,8,32,128]{3,2,1,0:T(8,128)S(1)}, u32[]{:S(2)}, u32[]{:S(2)}) collective-permute-start(f32[2,8,32,128]{3,2,1,0:T(8,128)S(1)} %maximum_select_fusion.1), channel_id=1, source_target_pairs={{0,64},{64,0},{128,192},{192,128},{256,320},{320,256},{384,448},{4... | collective-permute-start | bytes 786440 | tf_op jit(solution)/shard_map/ppermute | solution.py:24
  52.9 1.5 %collective-permute-done.8 = f32[2,8,32,128]{3,2,1,0:T(8,128)S(1)} collective-permute-done((f32[2,8,32,128]{3,2,1,0:T(8,128)S(1)}, f32[2,8,32,128]{3,2,1,0:T(8,128)S(1)}, u32[]{:S(2)}, u32[]{:S(2)}) %collective-permute-start.8) | collective-permute-done | bytes 262176 | tf_op jit(solution)/shard_map/ppermute | solution.py:24
  54.4 0.1 iota.37.box
  54.5 1.4 %shard_map.30 = f32[8,32,128]{2,1,0:T(8,128)S(1)} custom-call(f32[2,16,32,128]{3,2,1,0:T(8,128)S(1)} %maximum_select_fusion.pair, f32[16,128]{1,0:T(8,128)S(1)} %iota.37.box, s32[1]{0:T(128)} %bitcast.5.parity), custom_call_target="tpu_custom_call" | custom-call | tf_op jit(solution)/shard_map/pallas_call | solution.py:327
  55.9 2.2 %collective-permute-start.9 = (f32[8,4,128]{2,1,0:T(4,128)S(1)}, f32[8,4,128]{2,1,0:T(4,128)S(1)}, u32[]{:S(2)}, u32[]{:S(2)}) collective-permute-start(f32[8,4,128]{2,1,0:T(4,128)S(1)} %slice_select_fusion.5), channel_id=1, source_target_pairs={{8,16},{16,8},{24,32},{32,24},{40,48},{48,40},{9,17},{17,9},{25,33... | collective-permute-start | bytes 49160 | tf_op jit(solution)/shard_map/ppermute | solution.py:24
  58.2 3.4 %collective-permute-done.9 = f32[8,4,128]{2,1,0:T(4,128)S(1)} collective-permute-done((f32[8,4,128]{2,1,0:T(4,128)S(1)}, f32[8,4,128]{2,1,0:T(4,128)S(1)}, u32[]{:S(2)}, u32[]{:S(2)}) %collective-permute-start.9) | collective-permute-done | bytes 16416 | tf_op jit(solution)/shard_map/ppermute | solution.py:24
  61.7 6.0 %collective-permute-start.10 = (f32[4,32,128]{2,1,0:T(8,128)S(1)}, f32[4,32,128]{2,1,0:T(8,128)S(1)}, u32[]{:S(2)}, u32[]{:S(2)}) collective-permute-start(f32[4,32,128]{2,1,0:T(8,128)S(1)} %slice_select_fusion.3), channel_id=1, source_target_pairs={{64,128},{128,64},{192,256},{256,192},{320,384},{384,320},{448,512... | collective-permute-start | bytes 196616 | tf_op jit(solution)/shard_map/ppermute | solution.py:24
  67.7 1.9 %collective-permute-done.10 = f32[4,32,128]{2,1,0:T(8,128)S(1)} collective-permute-done((f32[4,32,128]{2,1,0:T(8,128)S(1)}, f32[4,32,128]{2,1,0:T(8,128)S(1)}, u32[]{:S(2)}, u32[]{:S(2)}) %collective-permute-start.10) | collective-permute-done | bytes 65568 | tf_op jit(solution)/shard_map/ppermute | solution.py:24
  69.6 3.5 %shard_map.31 = f32[8,32,128]{2,1,0:T(8,128)} custom-call(f32[12,32,128]{2,1,0:T(8,128)S(1)} %maximum_select_fusion.2.middle, f32[2,12,32,128]{3,2,1,0:T(8,128)S(1)} %slice_select_fusion.pair, f32[3,12,48,256]{3,2,1,0:T(8,128)S(1)} %get-tuple-element.12.kept), custom_call_target="tpu_custom_call" | custom-call | tf_op jit(solution)/shard_map/pallas_call | solution.py:327
  (23 shorter events, 0.5 us)
Async XLA Ops:
  0.0 0.9 %copy-start = (f32[8,32,128]{2,1,0:T(8,128)S(1)}, f32[8,32,128]{2,1,0:T(8,128)}, u32[]{:S(2)}) copy-start(f32[8,32,128]{2,1,0:T(8,128)} %source.1) | copy-start | bytes 393220
  0.9 0.9 %copy-start.2 = (f32[8,32,128]{2,1,0:T(8,128)S(1)}, f32[8,32,128]{2,1,0:T(8,128)}, u32[]{:S(2)}) copy-start(f32[8,32,128]{2,1,0:T(8,128)} %conductivity.1) | copy-start | bytes 393220
  1.8 9.0 %collective-permute-start.1 = (f32[2,8,12,128]{3,2,1,0:T(8,128)S(1)}, f32[2,8,12,128]{3,2,1,0:T(8,128)S(1)}, u32[]{:S(2)}, u32[]{:S(2)}) collective-permute-start(f32[2,8,12,128]{3,2,1,0:T(8,128)S(1)} %get-tuple-element.10), channel_id=1, source_target_pairs={{8,16},{16,8},{24,32},{32,24},{40,48},{48,40},{9,17},{17,9},{25,33... | collective-permute-start | bytes 294920 | tf_op jit(solution)/shard_map/ppermute | solution.py:24
  6.2 4.7 %collective-permute-start = (f32[2,8,4,128]{3,2,1,0:T(4,128)S(1)}, f32[2,8,4,128]{3,2,1,0:T(4,128)S(1)}, u32[]{:S(2)}, u32[]{:S(2)}) collective-permute-start(f32[2,8,4,128]{3,2,1,0:T(4,128)S(1)} %get-tuple-element.9), channel_id=1, source_target_pairs={{0,8},{8,0},{16,24},{24,16},{32,40},{40,32},{48,56},{56,48},{1,9},... | collective-permute-start | bytes 98312 | tf_op jit(solution)/shard_map/ppermute | solution.py:24
  10.9 11.5 %copy-start.1 = (f32[8,32,128]{2,1,0:T(8,128)S(1)}, f32[8,32,128]{2,1,0:T(8,128)}, u32[]{:S(2)}) copy-start(f32[8,32,128]{2,1,0:T(8,128)} %source.1) | copy-start | bytes 393220
  10.9 11.5 %copy-start.3 = (f32[8,32,128]{2,1,0:T(8,128)S(1)}, f32[8,32,128]{2,1,0:T(8,128)}, u32[]{:S(2)}) copy-start(f32[8,32,128]{2,1,0:T(8,128)} %conductivity.1) | copy-start | bytes 393220
  12.3 8.1 %collective-permute-start.2 = (f32[32,768]{1,0:T(8,128)S(1)}, f32[32,768]{1,0:T(8,128)S(1)}, u32[]{:S(2)}, u32[]{:S(2)}) collective-permute-start(f32[32,768]{1,0:T(8,128)S(1)} %get-tuple-element.17), channel_id=1, source_target_pairs={{1,0},{2,1},{3,2},{4,3},{5,4},{6,5},{7,6},{9,8},{10,9},{11,10},{12... | collective-permute-start | bytes 294920 | tf_op jit(solution)/shard_map/ppermute | solution.py:371
  14.3 7.8 %collective-permute-start.3 = (f32[32,768]{1,0:T(8,128)S(1)}, f32[32,768]{1,0:T(8,128)S(1)}, u32[]{:S(2)}, u32[]{:S(2)}) collective-permute-start(f32[32,768]{1,0:T(8,128)S(1)} %get-tuple-element.18), channel_id=1, source_target_pairs={{0,1},{1,2},{2,3},{3,4},{4,5},{5,6},{6,7},{8,9},{9,10},{10,11},{11... | collective-permute-start | bytes 294920 | tf_op jit(solution)/shard_map/ppermute | solution.py:372
  22.5 11.8 %collective-permute-start.4 = (f32[3,4,48,128]{3,2,1,0:T(8,128)S(1)}, f32[3,4,48,128]{3,2,1,0:T(8,128)S(1)}, u32[]{:S(2)}, u32[]{:S(2)}) collective-permute-start(f32[3,4,48,128]{3,2,1,0:T(8,128)S(1)} %get-tuple-element.15), channel_id=1, source_target_pairs={{64,128},{128,64},{192,256},{256,192},{320,384},{384,320},{448,512... | collective-permute-start | bytes 884744 | tf_op jit(solution)/shard_map/ppermute | solution.py:24
  29.9 4.4 %collective-permute-start.5 = (f32[3,4,48,128]{3,2,1,0:T(8,128)S(1)}, f32[3,4,48,128]{3,2,1,0:T(8,128)S(1)}, u32[]{:S(2)}, u32[]{:S(2)}) collective-permute-start(f32[3,4,48,128]{3,2,1,0:T(8,128)S(1)} %get-tuple-element.16), channel_id=1, source_target_pairs={{0,64},{64,0},{128,192},{192,128},{256,320},{320,256},{384,448},{4... | collective-permute-start | bytes 884744 | tf_op jit(solution)/shard_map/ppermute | solution.py:24
  37.2 5.4 %collective-permute-start.6 = (f32[2,4,12,128]{3,2,1,0:T(8,128)S(1)}, f32[2,4,12,128]{3,2,1,0:T(8,128)S(1)}, u32[]{:S(2)}, u32[]{:S(2)}) collective-permute-start(f32[2,4,12,128]{3,2,1,0:T(8,128)S(1)} %slice_select_fusion.4), channel_id=1, source_target_pairs={{0,8},{8,0},{16,24},{24,16},{32,40},{40,32},{48,56},{56,48},{1,9},... | collective-permute-start | bytes 147464 | tf_op jit(solution)/shard_map/ppermute | solution.py:24
  42.7 8.3 %collective-permute-start.7 = (f32[2,4,32,128]{3,2,1,0:T(8,128)S(1)}, f32[2,4,32,128]{3,2,1,0:T(8,128)S(1)}, u32[]{:S(2)}, u32[]{:S(2)}) collective-permute-start(f32[2,4,32,128]{3,2,1,0:T(8,128)S(1)} %maximum_select_fusion.4), channel_id=1, source_target_pairs={{64,128},{128,64},{192,256},{256,192},{320,384},{384,320},{448,512... | collective-permute-start | bytes 393224 | tf_op jit(solution)/shard_map/ppermute | solution.py:24
  50.9 3.4 %collective-permute-start.8 = (f32[2,8,32,128]{3,2,1,0:T(8,128)S(1)}, f32[2,8,32,128]{3,2,1,0:T(8,128)S(1)}, u32[]{:S(2)}, u32[]{:S(2)}) collective-permute-start(f32[2,8,32,128]{3,2,1,0:T(8,128)S(1)} %maximum_select_fusion.1), channel_id=1, source_target_pairs={{0,64},{64,0},{128,192},{192,128},{256,320},{320,256},{384,448},{4... | collective-permute-start | bytes 786440 | tf_op jit(solution)/shard_map/ppermute | solution.py:24
  55.9 5.7 %collective-permute-start.9 = (f32[8,4,128]{2,1,0:T(4,128)S(1)}, f32[8,4,128]{2,1,0:T(4,128)S(1)}, u32[]{:S(2)}, u32[]{:S(2)}) collective-permute-start(f32[8,4,128]{2,1,0:T(4,128)S(1)} %slice_select_fusion.5), channel_id=1, source_target_pairs={{8,16},{16,8},{24,32},{32,24},{40,48},{48,40},{9,17},{17,9},{25,33... | collective-permute-start | bytes 49160 | tf_op jit(solution)/shard_map/ppermute | solution.py:24
  61.7 7.9 %collective-permute-start.10 = (f32[4,32,128]{2,1,0:T(8,128)S(1)}, f32[4,32,128]{2,1,0:T(8,128)S(1)}, u32[]{:S(2)}, u32[]{:S(2)}) collective-permute-start(f32[4,32,128]{2,1,0:T(8,128)S(1)} %slice_select_fusion.3), channel_id=1, source_target_pairs={{64,128},{128,64},{192,256},{256,192},{320,384},{384,320},{448,512... | collective-permute-start | bytes 196616 | tf_op jit(solution)/shard_map/ppermute | solution.py:24

commit v6 on v5

--- a/solution.py
+++ b/solution.py
@@ -22,6 +22,11 @@
     for low in range(1 if outer else 0, count - 1, 2):
         route += [(low, low + 1), (low + 1, low)]
     return lax.ppermute(block, axis, route)
+
+
+def shift(block, axis, step):
+    count = lax.axis_size(axis)
+    return lax.ppermute(block, axis, [(i, i + step) for i in range(count) if 0 <= i + step < count])
 
 
 def cut(values, start, stop, dim):
@@ -50,8 +55,9 @@
             lanes = here + turn(here, 1, 1)
             for place, face in enumerate((across, rows, lanes)):
                 self.faces[place, i] = face
-            diagonal = (across + before) + (rows + turn(rows, 0, -1)) + (lanes + turn(lanes, 1, -1))
-            take(i, jnp.where(here > 0, 1.0 / diagonal, 0.0))
+            if take is not None:
+                diagonal = (across + before) + (rows + turn(rows, 0, -1)) + (lanes + turn(lanes, 1, -1))
+                take(i, jnp.where(here > 0, 1.0 / diagonal, 0.0))
             before = across
 
     def apply(self, field, start, stop, take):
@@ -72,6 +78,39 @@
     operator.apply(field, start, stop, take)
 
 
+class BoxOperator:
+    def __init__(self, upper, lower, faces):
+        self.upper = upper
+        self.lower = lower
+        self.faces = faces
+
+    def build(self, coeff, start, stop, take):
+        before = coeff(start - 1) + coeff(start)
+        self.faces[0, start - 1] = before
+        for i in range(start, stop):
+            here = coeff(i)
+            across = here + coeff(i + 1)
+            rows = here + self.upper * turn(here, 0, 1)
+            back = here + self.lower * turn(here, 0, -1)
+            lanes = here + turn(here, 1, 1)
+            for place, face in enumerate((across, rows, lanes, back)):
+                self.faces[place, i] = face
+            diagonal = (across + before) + (rows + back) + (lanes + turn(lanes, 1, -1))
+            take(i, jnp.where(here > 0, 1.0 / diagonal, 0.0))
+            before = across
+
+    def apply(self, field, start, stop, take):
+        before = self.faces[0, start - 1] * (field(start - 1) - field(start))
+        for i in range(start, stop):
+            here = field(i)
+            across = self.faces[0, i] * (here - field(i + 1))
+            rows = self.faces[1, i] * (here - self.upper * turn(here, 0, 1))
+            back = self.faces[3, i] * (here - self.lower * turn(here, 0, -1))
+            lanes = self.faces[2, i] * (here - turn(here, 1, 1))
+            take(i, (across - before) + (rows + back) + (lanes - turn(lanes, 1, -1)))
+            before = across
+
+
 def plane_of(ref, *lead):
     return lambda i: ref[(*lead, i)]
 
@@ -83,13 +122,31 @@
     return store
 
 
-def halve_rows(piece, weights):
-    count = piece.shape[0] // 2
-    even = piece[pl.ds(0, count, 2), :]
-    odd = piece[pl.ds(1, count, 2), :]
+def halve_circular(plane, slot, weights):
+    count = plane.shape[0] // 2
+    slot[...] = plane
+    even = slot[pl.ds(0, count, 2), :]
+    odd = slot[pl.ds(1, count, 2), :]
     if not weights:
         return even + odd
     return 0.375 * (even + odd) + 0.125 * (turn(odd, 0, -1) + turn(even, 0, 1))
+
+
+def halve_own(plane, slot, weights):
+    slot[0:8] = plane[32:40]
+    slot[8:40] = plane[0:32]
+    slot[40:48] = plane[32:40]
+    even = slot[pl.ds(8, 16, 2), :]
+    odd = slot[pl.ds(9, 16, 2), :]
+    if not weights:
+        return even + odd
+    return 0.375 * (even + odd) + 0.125 * (slot[pl.ds(7, 16, 2), :] + slot[pl.ds(10, 16, 2), :])
+
+
+def near_rows(plane, own):
+    row = lax.broadcasted_iota(jnp.int32, (8, plane.shape[1]), 0)
+    edge = jnp.where(row < 4, plane[own : own + 8], plane[plane.shape[0] - 8 :])
+    return jnp.concatenate([plane[:own], edge], axis=0)
 
 
 def product(values, matrix):
@@ -140,8 +197,8 @@
     return (coarse >= edge) == (middle >= 2 * edge)
 
 
-def restrict_level(plane, coeff, first, count, piece, packed, matrices, store):
-    rows, lanes = piece.shape[1:]
+def restrict_level(plane, coeff, first, count, halve, rows, piece, packed, matrices, store):
+    lanes = piece.shape[2]
     parts = packed.shape[2] // lanes
     for j in range(count):
         at = first + 2 * j
@@ -152,29 +209,33 @@
         for kind in range(2):
             for part in range(parts):
                 slot = piece.at[(2 * j + kind) * parts + part]
-                slot[...] = planes[kind][:, lanes * part : lanes * part + lanes]
-                packed[kind, pl.ds(rows // 2 * j, rows // 2), pl.ds(lanes * part, lanes)] = halve_rows(
-                    slot, kind == 0
+                value = planes[kind][:, lanes * part : lanes * part + lanes]
+                packed[kind, pl.ds(rows * j, rows), pl.ds(lanes * part, lanes)] = halve(
+                    value, slot, kind == 0
                 )
     for kind in range(2):
         result = product(packed[kind], matrices[kind])
         for j in range(count):
-            store(kind, j, result[rows // 2 * j : rows // 2 * (j + 1)])
-
-
-def first_kernel(source, conductivity, parity, far, near):
-    for kind, values in enumerate((source, conductivity)):
-        for odd in range(2):
-
-            @pl.when(parity[0] == odd)
-            def _(kind=kind, values=values, odd=odd):
-                for i in range(8):
-                    far[kind, i] = values[i, 20:32] if odd else values[i, 0:12]
-                    near[kind, i] = values[i, 0:4] if odd else values[i, 28:32]
+            store(kind, j, result[rows * j : rows * j + rows])
+
+
+def first_kernel(source, conductivity, cells, low, high, done):
+    copies = [
+        pltpu.make_async_copy(values, cells.at[kind], done.at[kind])
+        for kind, values in enumerate((source, conductivity))
+    ]
+    for copy in copies:
+        copy.start()
+    for copy in copies:
+        copy.wait()
+    for kind in range(2):
+        for i in range(8):
+            low[kind, i] = cells[kind, i, 0:4]
+            high[kind, i] = cells[kind, i, 28:32]
 
 
 def fine_kernel(wide, pair, kept, faces, inverse, rhs, coeff, field, pre, piece, packed):
-    lane = lax.broadcasted_iota(jnp.int32, (48, 128), 1)
+    lane = lax.broadcasted_iota(jnp.int32, (40, 128), 1)
     edge = (lane < 32) | (lane >= 96)
     for i in range(16):
         halo = wide[2, i]
@@ -195,6 +256,7 @@
         kept[0, i - 2] = coeff[i]
         kept[1, i - 2] = rhs[i]
         kept[2, i - 2] = value
+        kept[3, i - 2] = inverse[i]
 
     sweep(operator, plane_of(field), plane_of(inverse), plane_of(rhs), omega_second, 2, 14, store_pre)
 
@@ -210,10 +272,10 @@
     def store(kind, j, value):
         pair[kind, j] = value
 
-    restrict_level(plane_of(field), plane_of(coeff), 4, 4, piece, packed, matrices, store)
-
-
-def box_kernel(pair, box, parity, corrected, faces, inverse, field, other, piece, packed, low, low_faces, low_inverse, risen):
+    restrict_level(plane_of(field), plane_of(coeff), 4, 4, halve_own, 16, piece, packed, matrices, store)
+
+
+def box_kernel(pair, box, parity, corrected, kept, faces, inverse, field, other, piece, packed, low, low_faces, low_inverse, risen):
     rhs, coeff = plane_of(pair, 0), plane_of(pair, 1)
     operator = Operator(faces)
 
@@ -233,16 +295,16 @@
         lane_map(128, 128, lambda m, c: 4.0 * gather_weights(middle_lane(m), coarse_lane(c, odd))),
         lane_map(128, 128, lambda m, c: 0.25 * mean_weights(middle_lane(m), coarse_lane(c, odd))),
     )
-    in_box = box[...]
 
     def store(kind, j, value):
-        low[kind, j + 1] = value * in_box
-
-    restrict_level(plane_of(field), coeff, 4, 4, piece, packed, matrices, store)
+        low[kind, j + 1] = value
+
+    restrict_level(plane_of(field), coeff, 4, 4, halve_circular, 24, piece, packed, matrices, store)
     for place in (0, 5):
         for kind in range(3):
-            low[kind, place] = jnp.zeros((16, 128), jnp.float32)
-    coarse = Operator(low_faces)
+            low[kind, place] = jnp.zeros((24, 128), jnp.float32)
+    upper, lower = box[0], box[1]
+    coarse = BoxOperator(upper, lower, low_faces)
 
     def begin_low(i, value):
         low_inverse[i] = value
@@ -251,7 +313,7 @@
     coarse.build(plane_of(low, 1), 1, 5, begin_low)
 
     def store_low(i, value):
-        packed[0, pl.ds(16 * (i - 1), 16), :] = value
+        packed[0, pl.ds(24 * (i - 1), 24), :] = value
 
     sweep(coarse, plane_of(low, 2), plane_of(low_inverse), plane_of(low, 0), omega_second, 1, 5, store_low)
 
@@ -261,29 +323,38 @@
 
     result = product(packed[0], lane_map(128, 128, spread_box))
     for j in range(4):
-        spread_rows(result[16 * j : 16 * j + 16], risen.at[j])
+        spread_rows(result[24 * j : 24 * j + 24], risen.at[j], upper, lower)
     for i in range(8):
         value = 0.75 * risen[i // 2]
         near = i // 2 + (1 if i % 2 else -1)
         if 0 <= near < 4:
             value = value + 0.25 * risen[near]
-        corrected[i] = other[i + 4] + value
-
-
-def spread_rows(values, target):
+        corrected[i] = near_rows(other[i + 4] + value, 16)
+    for kind in range(2):
+        for i in range(16):
+            kept[kind, i] = near_rows(pair[kind, i], 16)
+
+
+def spread_rows(values, target, upper=1.0, lower=1.0):
     count = values.shape[0]
-    target[pl.ds(0, count, 2), :] = 0.75 * values + 0.25 * turn(values, 0, -1)
-    target[pl.ds(1, count, 2), :] = 0.75 * values + 0.25 * turn(values, 0, 1)
-
-
-def last_kernel(middle, pair, kept, out, faces, inverse, field, faces_m, inverse_m, field_m, packed, risen):
-    operator = Operator(faces_m)
-    rhs_m, at_m = plane_of(pair, 0), plane_of(inverse_m)
-    operator.build(plane_of(pair, 1), 1, 11, keep_in(inverse_m))
+    target[pl.ds(0, count, 2), :] = 0.75 * values + 0.25 * (lower * turn(values, 0, -1))
+    target[pl.ds(1, count, 2), :] = 0.75 * values + 0.25 * (upper * turn(values, 0, 1))
+
+
+def face_kernel(pair, filled):
+    def take(i, value):
+        filled[3, i] = value
+
+    Operator(filled).build(plane_of(pair, 1), 1, 11, take)
+
+
+def last_kernel(middle, pair, filled, kept, out, faces, field, field_m, packed, risen):
+    operator = Operator(filled)
+    rhs_m, at_m = plane_of(pair, 0), plane_of(filled, 3)
     sweep(operator, plane_of(middle), at_m, rhs_m, omega_first, 1, 11, keep_in(field_m))
 
     def store_packed(i, value):
-        packed[pl.ds(32 * (i - 2), 32), :] = value
+        packed[pl.ds(24 * (i - 2), 24), :] = value
 
     sweep(operator, plane_of(field_m), at_m, rhs_m, omega_second, 2, 10, store_packed)
     result = product(
@@ -292,44 +363,47 @@
     for place in range(8):
         for half in range(2):
             spread_rows(
-                result[32 * place : 32 * place + 32, 128 * half : 128 * half + 128],
+                result[24 * place : 24 * place + 24, 128 * half : 128 * half + 128],
                 risen.at[2 * place + half],
             )
 
     def lifted(place):
         halves = [
-            jnp.concatenate([risen[2 * place + half, 0:40], risen[2 * place + half, 56:64]], axis=0)
-            for half in range(2)
+            near_rows(risen[2 * place + half], 32) for half in range(2)
         ]
         return jnp.concatenate(halves, axis=1)
 
     fine = Operator(faces)
     coeff, rhs = plane_of(kept, 0), plane_of(kept, 1)
-    fine.build(coeff, 1, 11, keep_in(inverse))
+    fine.build(coeff, 1, 11, None)
+    inverse = plane_of(kept, 3)
     for i in range(12):
         place = i // 2 + 1
         value = 0.75 * lifted(place) + 0.25 * lifted(place + (1 if i % 2 else -1))
         field[0, i] = kept[2, i] + jnp.where(coeff(i) > 0, value, 0.0)
-    sweep(fine, plane_of(field, 0), plane_of(inverse), rhs, omega_first, 1, 11, keep_in(field, 1))
+    sweep(fine, plane_of(field, 0), inverse, rhs, omega_first, 1, 11, keep_in(field, 1))
 
     def store_out(i, value):
         out[i - 2] = value[:32, :128]
 
-    sweep(fine, plane_of(field, 1), plane_of(inverse), rhs, omega_second, 2, 10, store_out)
+    sweep(fine, plane_of(field, 1), inverse, rhs, omega_second, 2, 10, store_out)
 
 
 interpret = False
 VMEM = pl.BlockSpec(memory_space=pltpu.VMEM)
 SMEM = pl.BlockSpec(memory_space=pltpu.SMEM)
-
-
-def call(kernel, outs, scratch, *arguments):
+ANY = pl.BlockSpec(memory_space=pl.ANY)
+
+
+def call(kernel, outs, scratch, *arguments, specs=None):
     return pl.pallas_call(
         kernel,
         out_shape=[jax.ShapeDtypeStruct(shape, jnp.float32) for shape in outs],
-        in_specs=[VMEM if value.ndim > 1 else SMEM for value in arguments],
+        in_specs=specs or [VMEM if value.ndim > 1 else SMEM for value in arguments],
         out_specs=[VMEM] * len(outs),
-        scratch_shapes=[pltpu.VMEM(shape, jnp.float32) for shape in scratch],
+        scratch_shapes=[
+            pltpu.VMEM(shape, jnp.float32) if isinstance(shape, tuple) else shape for shape in scratch
+        ],
         compiler_params=pltpu.CompilerParams(vmem_limit_bytes=24 * 1024 * 1024),
         interpret=interpret,
     )(*arguments)
@@ -353,77 +427,66 @@
     def side(low, when_low, when_high):
         return jnp.where(low, when_low, when_high)
 
-    far, near = call(
+    cells, low, high = call(
         first_kernel,
-        [(2, 8, 12, 128), (2, 8, 4, 128)],
-        [],
+        [(2, 8, 32, 128), (2, 8, 4, 128), (2, 8, 4, 128)],
+        [pltpu.SemaphoreType.DMA((2,))],
         source,
         conductivity,
-        (lax.axis_index("gy") % 2).reshape(1),
-    )
-    far = swap(far, "gy", True)
-    near = swap(near, "gy", False)
-    cells = jnp.stack([source, conductivity])
-    cells = join([cells, side(low_y, join([near, far], 2), join([far, near], 2))], 2)
+        specs=[ANY, ANY],
+    )
+    cells = join([cells, shift(low, "gy", -1), shift(high, "gy", 1)], 2)
 
     strips = take_lanes(cells, lane_map(128, 64, lambda z, k: z == k + jnp.where(k < 32, 0, 64)))
-    count = lax.axis_size("gz")
-    after = lax.ppermute(strips[:32], "gz", [(i + 1, i) for i in range(count - 1)])
-    before = lax.ppermute(strips[32:], "gz", [(i, i + 1) for i in range(count - 1)])
+    after = shift(strips[:32], "gz", -1)
+    before = shift(strips[32:], "gz", 1)
     rows = strips.shape[1] // 2
     halo = join([after[:, :rows], before[:, rows:], after[:, rows:], before[:, :rows]], 0)
-    halo = put_lanes(halo, lane_map(128, 128, lambda k, z: k == z), (1, 8, 48, 128))
+    halo = put_lanes(halo, lane_map(128, 128, lambda k, z: k == z), (1, 8, 40, 128))
     cells = join([cells, halo], 0)
 
     far = swap(side(low_x, cells[:, :4], cells[:, 4:]), "gx", True)
     near = swap(side(low_x, cells[:, 4:], cells[:, :4]), "gx", False)
     wide = join([side(low_x, far, near), cells, side(low_x, near, far)], 1)
 
-    plane = (48, 256)
+    plane = (40, 256)
     pair, kept = call(
         fine_kernel,
-        [(2, 4, 24, 128), (3, 12, *plane)],
-        [(3, 16, *plane)] + [(16, *plane)] * 5 + [(16, 48, 128), (2, 96, 256)],
+        [(2, 4, 16, 128), (4, 12, *plane)],
+        [(3, 16, *plane)] + [(16, *plane)] * 5 + [(16, 48, 128), (2, 64, 256)],
         wide,
     )
 
-    near = swap(side(low_y, pair[:, :, 4:16], pair[:, :, :12]), "gy", False)
-    pair = side(
-        low_y,
-        join([pair[:, :, :16], near, pair[:, :, 20:]], 2),
-        join([pair[:, :, :20], near], 2),
-    )
+    pair = join([pair, shift(pair, "gy", -1), shift(pair, "gy", 1)], 2)
     far = swap(pair, "gx", True)
     pair = side(low_x, join([far, pair], 1), join([pair, far], 1))
     near = swap(pair, "gx", False)
     pair = side(low_x, join([pair, near], 1), join([near, pair], 1))
 
-    row = lax.broadcasted_iota(jnp.int32, (16, 128), 0)
-    in_box = side(low_y, row < 14, (row < 8) | (row >= 10))
-    (middle,) = call(
+    row = lax.broadcasted_iota(jnp.int32, (24, 128), 0)
+    edges = side(low_y, row == 23, row == 7), side(low_y, row == 0, row == 8)
+    middle, pair = call(
         box_kernel,
-        [(8, 32, 128)],
-        [(3, 16, 32, 128), (16, 32, 128), (16, 32, 128), (16, 32, 128), (8, 32, 128), (2, 64, 128)]
-        + [(3, 6, 16, 128), (3, 6, 16, 128), (6, 16, 128), (4, 32, 128)],
+        [(8, 24, 128), (2, 16, 24, 128)],
+        [(3, 16, 48, 128), (16, 48, 128), (16, 48, 128), (16, 48, 128), (8, 48, 128), (2, 96, 128)]
+        + [(3, 6, 24, 128), (4, 6, 24, 128), (6, 24, 128), (4, 48, 128)],
         pair,
-        in_box.astype(jnp.float32),
+        jnp.stack([jnp.where(edge, 0.0, 1.0) for edge in edges]),
         odd_z,
     )
 
-    far = swap(side(low_y, middle[:, :4], middle[:, 12:16]), "gy", True)
-    middle = side(
-        low_y, join([middle[:, :28], far], 1), join([middle[:, :16], far, middle[:, 20:]], 1)
-    )
+    pair = side(low_x, pair[:, :12], pair[:, 4:])
+    (filled,) = call(face_kernel, [(4, 12, 24, 128)], [], pair)
     far = swap(side(low_x, middle[:4], middle[4:]), "gx", True)
     middle = side(low_x, join([far, middle], 0), join([middle, far], 0))
 
     (pressure,) = call(
         last_kernel,
         [(8, 32, 128)],
-        [(3, 12, *plane), (12, *plane), (2, 12, *plane), (3, 12, 32, 128), (12, 32, 128), (12, 32, 128)]
-        + [(256, 128), (16, 64, 128)],
+        [(3, 12, *plane), (2, 12, *plane), (12, 24, 128), (192, 128), (16, 48, 128)],
         middle,
-        side(low_x, pair[:, :12], pair[:, 4:]),
+        pair,
+        filled,
         kept,
     )
     return pressure

time: 73.5 us -> 66.2 us (0.901)
  the two profiles are of different devices: /device:TPU:439 before, /device:TPU:443 now
where the time goes in v6:
time: 66.2 us; the launch traced here: 65.8 us
  starting transfers between devices  40.4 us (61%)
  waiting for transfers between devices  15.8 us (24%)
  Pallas kernels  6.21 us (9%)
  local copies, waits for them, and re-layouts  2.13 us (3%)
  matrix products  0.69 us (1%)
    ppermute x5, starting transfers between devices, swap(): return lax.ppermute(block, axis, route)  21.8 us
    ppermute x6, starting transfers between devices, shift(): lax.ppermute(block, axis, [(i, i + step) for i in range(count) if 0 <= i...  18.6 us
    ppermute x5, waiting for transfers between devices, swap(): return lax.ppermute(block, axis, route)  8.33 us
    ppermute x6, waiting for transfers between devices, shift(): lax.ppermute(block, axis, [(i, i + step) for i in range(count) if 0 <= i...  7.43 us
    pallas_call x5, Pallas kernels, call(): pl.pallas_call(kernel, out_shape=[jax.ShapeDtypeStruct(shape, jnp.float32...  6.21 us
    unnamed x6, local copies, waits for them, and re-layouts  1.82 us
  transfers between devices with their start and end apart: 11, of which 8 were waited for; matrix products, arithmetic and copies ran while one was open for 0% of the time, Pallas kernels for 0%

profile of v6, /device:TPU:443, one launch (start us, length us, event | category | flops | bytes accessed | tf_op | source)
XLA Modules:
  0.0 65.8 jit_solution(13600122835361727832)
XLA Ops:
  0.0 0.0 copy-start
  0.0 0.9 %copy-done = f32[8,32,128]{2,1,0:T(8,128)S(1)} copy-done((f32[8,32,128]{2,1,0:T(8,128)S(1)}, f32[8,32,128]{2,1,0:T(8,128)}, u32[]{:S(2)}) %copy-start) | copy-done | bytes 131096
  0.9 0.0 copy-start.1
  0.9 0.9 %copy-done.1 = f32[8,32,128]{2,1,0:T(8,128)S(1)} copy-done((f32[8,32,128]{2,1,0:T(8,128)S(1)}, f32[8,32,128]{2,1,0:T(8,128)}, u32[]{:S(2)}) %copy-start.1) | copy-done | bytes 131096
  1.8 0.3 shard_map.28
  2.2 3.1 %collective-permute-start = (f32[2,8,4,128]{3,2,1,0:T(4,128)S(1)}, f32[2,8,4,128]{3,2,1,0:T(4,128)S(1)}, u32[]{:S(2)}, u32[]{:S(2)}) collective-permute-start(f32[2,8,4,128]{3,2,1,0:T(4,128)S(1)} %get-tuple-element.13), channel_id=1, source_target_pairs={{8,0},{16,8},{24,16},{32,24},{40,32},{48,40},{56,48},{9,1},{17,9},... | collective-permute-start | bytes 98312 | tf_op jit(solution)/shard_map/ppermute | solution.py:29
  5.2 2.2 %collective-permute-start.1 = (f32[2,8,4,128]{3,2,1,0:T(4,128)S(1)}, f32[2,8,4,128]{3,2,1,0:T(4,128)S(1)}, u32[]{:S(2)}, u32[]{:S(2)}) collective-permute-start(f32[2,8,4,128]{3,2,1,0:T(4,128)S(1)} %get-tuple-element.14), channel_id=1, source_target_pairs={{0,8},{8,16},{16,24},{24,32},{32,40},{40,48},{48,56},{1,9},{9,17},... | collective-permute-start | bytes 98312 | tf_op jit(solution)/shard_map/ppermute | solution.py:29
  7.5 0.0 collective-permute-done
  7.5 2.4 %collective-permute-done.1 = f32[2,8,4,128]{3,2,1,0:T(4,128)S(1)} collective-permute-done((f32[2,8,4,128]{3,2,1,0:T(4,128)S(1)}, f32[2,8,4,128]{3,2,1,0:T(4,128)S(1)}, u32[]{:S(2)}, u32[]{:S(2)}) %collective-permute-start.1) | collective-permute-done | bytes 32800 | tf_op jit(solution)/shard_map/ppermute | solution.py:29
  9.9 0.4 fusion.9
  10.3 1.9 %collective-permute-start.2 = (f32[32,640]{1,0:T(8,128)S(1)}, f32[32,640]{1,0:T(8,128)S(1)}, u32[]{:S(2)}, u32[]{:S(2)}) collective-permute-start(f32[32,640]{1,0:T(8,128)S(1)} %get-tuple-element.23), channel_id=1, source_target_pairs={{1,0},{2,1},{3,2},{4,3},{5,4},{6,5},{7,6},{9,8},{10,9},{11,10},{12... | collective-permute-start | bytes 245768 | tf_op jit(solution)/shard_map/ppermute | solution.py:29
  12.2 6.1 %collective-permute-start.3 = (f32[32,640]{1,0:T(8,128)S(1)}, f32[32,640]{1,0:T(8,128)S(1)}, u32[]{:S(2)}, u32[]{:S(2)}) collective-permute-start(f32[32,640]{1,0:T(8,128)S(1)} %get-tuple-element.24), channel_id=1, source_target_pairs={{0,1},{1,2},{2,3},{3,4},{4,5},{5,6},{6,7},{8,9},{9,10},{10,11},{11... | collective-permute-start | bytes 245768 | tf_op jit(solution)/shard_map/ppermute | solution.py:29
  18.4 0.0 collective-permute-done.2
  18.4 0.1 fusion.15
  18.5 1.4 %collective-permute-done.3 = f32[32,640]{1,0:T(8,128)S(1)} collective-permute-done((f32[32,640]{1,0:T(8,128)S(1)}, f32[32,640]{1,0:T(8,128)S(1)}, u32[]{:S(2)}, u32[]{:S(2)}) %collective-permute-start.3) | collective-permute-done | bytes 81952 | tf_op jit(solution)/shard_map/ppermute | solution.py:29
  19.8 0.1 fusion.16
  19.9 0.3 fusion
  20.3 7.4 %collective-permute-start.4 = (f32[3,4,40,128]{3,2,1,0:T(8,128)S(1)}, f32[3,4,40,128]{3,2,1,0:T(8,128)S(1)}, u32[]{:S(2)}, u32[]{:S(2)}) collective-permute-start(f32[3,4,40,128]{3,2,1,0:T(8,128)S(1)} %get-tuple-element.21), channel_id=1, source_target_pairs={{64,128},{128,64},{192,256},{256,192},{320,384},{384,320},{448,512... | collective-permute-start | bytes 737288 | tf_op jit(solution)/shard_map/ppermute | solution.py:24
  27.7 1.9 %collective-permute-start.5 = (f32[3,4,40,128]{3,2,1,0:T(8,128)S(1)}, f32[3,4,40,128]{3,2,1,0:T(8,128)S(1)}, u32[]{:S(2)}, u32[]{:S(2)}) collective-permute-start(f32[3,4,40,128]{3,2,1,0:T(8,128)S(1)} %get-tuple-element.22), channel_id=1, source_target_pairs={{0,64},{64,0},{128,192},{192,128},{256,320},{320,256},{384,448},{4... | collective-permute-start | bytes 737288 | tf_op jit(solution)/shard_map/ppermute | solution.py:24
  29.6 1.9 %collective-permute-done.4 = f32[3,4,40,128]{3,2,1,0:T(8,128)S(1)} collective-permute-done((f32[3,4,40,128]{3,2,1,0:T(8,128)S(1)}, f32[3,4,40,128]{3,2,1,0:T(8,128)S(1)}, u32[]{:S(2)}, u32[]{:S(2)}) %collective-permute-start.4) | collective-permute-done | bytes 245792 | tf_op jit(solution)/shard_map/ppermute | solution.py:24
  31.6 0.0 collective-permute-done.5
  31.6 0.1 pad_maximum_fusion.wide
  31.7 2.4 %shard_map.29 = (f32[2,4,16,128]{3,2,1,0:T(8,128)S(1)}, f32[4,12,40,256]{3,2,1,0:T(8,128)S(1)}) custom-call(f32[3,16,40,128]{3,2,1,0:T(8,128)S(1)} %pad_maximum_fusion.wide), custom_call_target="tpu_custom_call" | custom-call | tf_op jit(solution)/shard_map/pallas_call | solution.py:399
  34.1 3.4 %collective-permute-start.6 = (f32[2,4,16,128]{3,2,1,0:T(8,128)S(1)}, f32[2,4,16,128]{3,2,1,0:T(8,128)S(1)}, u32[]{:S(2)}, u32[]{:S(2)}) collective-permute-start(f32[2,4,16,128]{3,2,1,0:T(8,128)S(1)} %get-tuple-element.15), channel_id=1, source_target_pairs={{8,0},{16,8},{24,16},{32,24},{40,32},{48,40},{56,48},{9,1},{17,9},... | collective-permute-start | bytes 196616 | tf_op jit(solution)/shard_map/ppermute | solution.py:29
  37.5 1.9 %collective-permute-start.7 = (f32[2,4,16,128]{3,2,1,0:T(8,128)S(1)}, f32[2,4,16,128]{3,2,1,0:T(8,128)S(1)}, u32[]{:S(2)}, u32[]{:S(2)}) collective-permute-start(f32[2,4,16,128]{3,2,1,0:T(8,128)S(1)} %get-tuple-element.15), channel_id=1, source_target_pairs={{0,8},{8,16},{16,24},{24,32},{32,40},{40,48},{48,56},{1,9},{9,17},... | collective-permute-start | bytes 196616 | tf_op jit(solution)/shard_map/ppermute | solution.py:29
  39.4 0.5 collective-permute-done.6
  40.0 3.1 %collective-permute-done.7 = f32[2,4,16,128]{3,2,1,0:T(8,128)S(1)} collective-permute-done((f32[2,4,16,128]{3,2,1,0:T(8,128)S(1)}, f32[2,4,16,128]{3,2,1,0:T(8,128)S(1)}, u32[]{:S(2)}, u32[]{:S(2)}) %collective-permute-start.7) | collective-permute-done | bytes 65568 | tf_op jit(solution)/shard_map/ppermute | solution.py:29
  43.1 5.7 %collective-permute-start.8 = (f32[2,4,48,128]{3,2,1,0:T(8,128)S(1)}, f32[2,4,48,128]{3,2,1,0:T(8,128)S(1)}, u32[]{:S(2)}, u32[]{:S(2)}) collective-permute-start(f32[2,4,48,128]{3,2,1,0:T(8,128)S(1)} %constant_dynamic-update-slice_fusion), channel_id=1, source_target_pairs={{64,128},{128,64},{192,256},{256,192},{320,384},{384,320},{448,512... | collective-permute-start | bytes 589832 | tf_op jit(solution)/shard_map/ppermute | solution.py:24
  48.8 3.3 %collective-permute-done.8 = f32[2,4,48,128]{3,2,1,0:T(8,128)S(1)} collective-permute-done((f32[2,4,48,128]{3,2,1,0:T(8,128)S(1)}, f32[2,4,48,128]{3,2,1,0:T(8,128)S(1)}, u32[]{:S(2)}, u32[]{:S(2)}) %collective-permute-start.8) | collective-permute-done | bytes 196640 | tf_op jit(solution)/shard_map/ppermute | solution.py:24
  52.1 1.9 %collective-permute-start.9 = (f32[2,8,48,128]{3,2,1,0:T(8,128)S(1)}, f32[2,8,48,128]{3,2,1,0:T(8,128)S(1)}, u32[]{:S(2)}, u32[]{:S(2)}) collective-permute-start(f32[2,8,48,128]{3,2,1,0:T(8,128)S(1)} %maximum_select_fusion.1), channel_id=1, source_target_pairs={{0,64},{64,0},{128,192},{192,128},{256,320},{320,256},{384,448},{4... | collective-permute-start | bytes 1179656 | tf_op jit(solution)/shard_map/ppermute | solution.py:24
  54.1 0.1 iota.43
  54.2 0.1 iota.46
  54.2 1.5 %collective-permute-done.9 = f32[2,8,48,128]{3,2,1,0:T(8,128)S(1)} collective-permute-done((f32[2,8,48,128]{3,2,1,0:T(8,128)S(1)}, f32[2,8,48,128]{3,2,1,0:T(8,128)S(1)}, u32[]{:S(2)}, u32[]{:S(2)}) %collective-permute-start.9) | collective-permute-done | bytes 393248 | tf_op jit(solution)/shard_map/ppermute | solution.py:24
  55.8 0.1 maximum_select_fusion.pair
  55.8 1.5 %shard_map.30 = (f32[8,24,128]{2,1,0:T(8,128)S(1)}, f32[2,16,24,128]{3,2,1,0:T(8,128)S(1)}) custom-call(f32[2,16,48,128]{3,2,1,0:T(8,128)S(1)} %maximum_select_fusion.pair, f32[2,24,128]{2,1,0:T(8,128)S(1)} %pad_maximum_fusion.3.box, s32[1]{0:T(128)} %bitcast.2.parity), custom_call_target="tpu_custom_call" | custom-call | tf_op jit(solution)/shard_map/pallas_call | solution.py:399
  57.4 4.9 %collective-permute-start.10 = (f32[4,24,128]{2,1,0:T(8,128)S(1)}, f32[4,24,128]{2,1,0:T(8,128)S(1)}, u32[]{:S(2)}, u32[]{:S(2)}) collective-permute-start(f32[4,24,128]{2,1,0:T(8,128)S(1)} %slice_select_fusion.3), channel_id=1, source_target_pairs={{64,128},{128,64},{192,256},{256,192},{320,384},{384,320},{448,512... | collective-permute-start | bytes 147464 | tf_op jit(solution)/shard_map/ppermute | solution.py:24
  62.2 0.2 shard_map.31.filled
  62.4 1.5 %collective-permute-done.10 = f32[4,24,128]{2,1,0:T(8,128)S(1)} collective-permute-done((f32[4,24,128]{2,1,0:T(8,128)S(1)}, f32[4,24,128]{2,1,0:T(8,128)S(1)}, u32[]{:S(2)}, u32[]{:S(2)}) %collective-permute-start.10) | collective-permute-done | bytes 49184 | tf_op jit(solution)/shard_map/ppermute | solution.py:24
  64.0 1.8 %shard_map.32 = f32[8,32,128]{2,1,0:T(8,128)} custom-call(f32[12,24,128]{2,1,0:T(8,128)S(1)} %maximum_select_fusion.2.middle, f32[2,12,24,128]{3,2,1,0:T(8,128)S(1)} %slice_select_fusion.pair, f32[4,12,24,128]{3,2,1,0:T(8,128)S(1)} %shard_map.31.filled, f32[4,12,40,256]{3,2,1,0:T(8,128)S(1)} %get-tuple-element.18.kept), custom_call_target="tpu_custom_call" | custom-call | tf_op jit(solution)/shard_map/pallas_call | solution.py:399
  (15 shorter events, 0.3 us)
Async XLA Ops:
  0.0 0.9 %copy-start = (f32[8,32,128]{2,1,0:T(8,128)S(1)}, f32[8,32,128]{2,1,0:T(8,128)}, u32[]{:S(2)}) copy-start(f32[8,32,128]{2,1,0:T(8,128)} %source.1) | copy-start | bytes 393220
  0.9 0.9 %copy-start.1 = (f32[8,32,128]{2,1,0:T(8,128)S(1)}, f32[8,32,128]{2,1,0:T(8,128)}, u32[]{:S(2)}) copy-start(f32[8,32,128]{2,1,0:T(8,128)} %conductivity.1) | copy-start | bytes 393220
  2.2 5.3 %collective-permute-start = (f32[2,8,4,128]{3,2,1,0:T(4,128)S(1)}, f32[2,8,4,128]{3,2,1,0:T(4,128)S(1)}, u32[]{:S(2)}, u32[]{:S(2)}) collective-permute-start(f32[2,8,4,128]{3,2,1,0:T(4,128)S(1)} %get-tuple-element.13), channel_id=1, source_target_pairs={{8,0},{16,8},{24,16},{32,24},{40,32},{48,40},{56,48},{9,1},{17,9},... | collective-permute-start | bytes 98312 | tf_op jit(solution)/shard_map/ppermute | solution.py:29
  5.2 4.7 %collective-permute-start.1 = (f32[2,8,4,128]{3,2,1,0:T(4,128)S(1)}, f32[2,8,4,128]{3,2,1,0:T(4,128)S(1)}, u32[]{:S(2)}, u32[]{:S(2)}) collective-permute-start(f32[2,8,4,128]{3,2,1,0:T(4,128)S(1)} %get-tuple-element.14), channel_id=1, source_target_pairs={{0,8},{8,16},{16,24},{24,32},{32,40},{40,48},{48,56},{1,9},{9,17},... | collective-permute-start | bytes 98312 | tf_op jit(solution)/shard_map/ppermute | solution.py:29
  10.3 8.1 %collective-permute-start.2 = (f32[32,640]{1,0:T(8,128)S(1)}, f32[32,640]{1,0:T(8,128)S(1)}, u32[]{:S(2)}, u32[]{:S(2)}) collective-permute-start(f32[32,640]{1,0:T(8,128)S(1)} %get-tuple-element.23), channel_id=1, source_target_pairs={{1,0},{2,1},{3,2},{4,3},{5,4},{6,5},{7,6},{9,8},{10,9},{11,10},{12... | collective-permute-start | bytes 245768 | tf_op jit(solution)/shard_map/ppermute | solution.py:29
  12.2 7.6 %collective-permute-start.3 = (f32[32,640]{1,0:T(8,128)S(1)}, f32[32,640]{1,0:T(8,128)S(1)}, u32[]{:S(2)}, u32[]{:S(2)}) collective-permute-start(f32[32,640]{1,0:T(8,128)S(1)} %get-tuple-element.24), channel_id=1, source_target_pairs={{0,1},{1,2},{2,3},{3,4},{4,5},{5,6},{6,7},{8,9},{9,10},{10,11},{11... | collective-permute-start | bytes 245768 | tf_op jit(solution)/shard_map/ppermute | solution.py:29
  20.3 11.2 %collective-permute-start.4 = (f32[3,4,40,128]{3,2,1,0:T(8,128)S(1)}, f32[3,4,40,128]{3,2,1,0:T(8,128)S(1)}, u32[]{:S(2)}, u32[]{:S(2)}) collective-permute-start(f32[3,4,40,128]{3,2,1,0:T(8,128)S(1)} %get-tuple-element.21), channel_id=1, source_target_pairs={{64,128},{128,64},{192,256},{256,192},{320,384},{384,320},{448,512... | collective-permute-start | bytes 737288 | tf_op jit(solution)/shard_map/ppermute | solution.py:24
  27.7 3.9 %collective-permute-start.5 = (f32[3,4,40,128]{3,2,1,0:T(8,128)S(1)}, f32[3,4,40,128]{3,2,1,0:T(8,128)S(1)}, u32[]{:S(2)}, u32[]{:S(2)}) collective-permute-start(f32[3,4,40,128]{3,2,1,0:T(8,128)S(1)} %get-tuple-element.22), channel_id=1, source_target_pairs={{0,64},{64,0},{128,192},{192,128},{256,320},{320,256},{384,448},{4... | collective-permute-start | bytes 737288 | tf_op jit(solution)/shard_map/ppermute | solution.py:24
  34.1 5.9 %collective-permute-start.6 = (f32[2,4,16,128]{3,2,1,0:T(8,128)S(1)}, f32[2,4,16,128]{3,2,1,0:T(8,128)S(1)}, u32[]{:S(2)}, u32[]{:S(2)}) collective-permute-start(f32[2,4,16,128]{3,2,1,0:T(8,128)S(1)} %get-tuple-element.15), channel_id=1, source_target_pairs={{8,0},{16,8},{24,16},{32,24},{40,32},{48,40},{56,48},{9,1},{17,9},... | collective-permute-start | bytes 196616 | tf_op jit(solution)/shard_map/ppermute | solution.py:29
  37.5 5.6 %collective-permute-start.7 = (f32[2,4,16,128]{3,2,1,0:T(8,128)S(1)}, f32[2,4,16,128]{3,2,1,0:T(8,128)S(1)}, u32[]{:S(2)}, u32[]{:S(2)}) collective-permute-start(f32[2,4,16,128]{3,2,1,0:T(8,128)S(1)} %get-tuple-element.15), channel_id=1, source_target_pairs={{0,8},{8,16},{16,24},{24,32},{32,40},{40,48},{48,56},{1,9},{9,17},... | collective-permute-start | bytes 196616 | tf_op jit(solution)/shard_map/ppermute | solution.py:29
  43.1 9.0 %collective-permute-start.8 = (f32[2,4,48,128]{3,2,1,0:T(8,128)S(1)}, f32[2,4,48,128]{3,2,1,0:T(8,128)S(1)}, u32[]{:S(2)}, u32[]{:S(2)}) collective-permute-start(f32[2,4,48,128]{3,2,1,0:T(8,128)S(1)} %constant_dynamic-update-slice_fusion), channel_id=1, source_target_pairs={{64,128},{128,64},{192,256},{256,192},{320,384},{384,320},{448,512... | collective-permute-start | bytes 589832 | tf_op jit(solution)/shard_map/ppermute | solution.py:24
  52.1 3.6 %collective-permute-start.9 = (f32[2,8,48,128]{3,2,1,0:T(8,128)S(1)}, f32[2,8,48,128]{3,2,1,0:T(8,128)S(1)}, u32[]{:S(2)}, u32[]{:S(2)}) collective-permute-start(f32[2,8,48,128]{3,2,1,0:T(8,128)S(1)} %maximum_select_fusion.1), channel_id=1, source_target_pairs={{0,64},{64,0},{128,192},{192,128},{256,320},{320,256},{384,448},{4... | collective-permute-start | bytes 1179656 | tf_op jit(solution)/shard_map/ppermute | solution.py:24
  57.4 6.6 %collective-permute-start.10 = (f32[4,24,128]{2,1,0:T(8,128)S(1)}, f32[4,24,128]{2,1,0:T(8,128)S(1)}, u32[]{:S(2)}, u32[]{:S(2)}) collective-permute-start(f32[4,24,128]{2,1,0:T(8,128)S(1)} %slice_select_fusion.3), channel_id=1, source_target_pairs={{64,128},{128,64},{192,256},{256,192},{320,384},{384,320},{448,512... | collective-permute-start | bytes 147464 | tf_op jit(solution)/shard_map/ppermute | solution.py:24

commit v7 on v6

--- a/solution.py
+++ b/solution.py
@@ -219,46 +219,55 @@
             store(kind, j, result[rows * j : rows * j + rows])
 
 
-def first_kernel(source, conductivity, cells, low, high, done):
-    copies = [
-        pltpu.make_async_copy(values, cells.at[kind], done.at[kind])
-        for kind, values in enumerate((source, conductivity))
-    ]
-    for copy in copies:
-        copy.start()
-    for copy in copies:
-        copy.wait()
-    for kind in range(2):
-        for i in range(8):
-            low[kind, i] = cells[kind, i, 0:4]
-            high[kind, i] = cells[kind, i, 28:32]
-
-
-def fine_kernel(wide, pair, kept, faces, inverse, rhs, coeff, field, pre, piece, packed):
+class Joined:
+    def __init__(self, own, scratch):
+        self.own = own
+        self.scratch = scratch
+
+    def __getitem__(self, place):
+        lead, i = place[:-1], place[-1]
+        return self.own[(*lead, i - 4)] if 5 <= i <= 10 else self.scratch[place]
+
+    def __setitem__(self, place, value):
+        self.scratch[place] = value
+
+
+def halo_edge():
     lane = lax.broadcasted_iota(jnp.int32, (40, 128), 1)
-    edge = (lane < 32) | (lane >= 96)
+    return (lane < 32) | (lane >= 96)
+
+
+def stage_coeff(cells, coeff, i):
+    coeff[i, :, 0:128] = cells[1, i]
+    coeff[i, :, 128:256] = jnp.where(halo_edge(), pltpu.roll(cells[2, i], 64, 1), 0.0)
+
+
+def own_kernel(cells, faces, inverse, coeff):
+    for i in range(8):
+        stage_coeff(cells, coeff, i)
+    Operator(faces).build(plane_of(coeff), 1, 7, keep_in(inverse))
+
+
+def fine_kernel(wide, own_faces, own_inverse, pair, kept, faces, inverse, rhs, coeff, field, pre, piece, packed):
     for i in range(16):
-        halo = wide[2, i]
         rhs[i, :, 0:128] = 2.0 * wide[0, i]
-        rhs[i, :, 128:256] = jnp.where(edge, 2.0 * halo, 0.0)
-        coeff[i, :, 0:128] = wide[1, i]
-        coeff[i, :, 128:256] = jnp.where(edge, pltpu.roll(halo, 64, 1), 0.0)
-    operator = Operator(faces)
-
-    def begin(i, value):
-        inverse[i] = value
-        field[i] = omega_first * rhs[i] * value
-
-    operator.build(plane_of(coeff), 1, 15, begin)
+        rhs[i, :, 128:256] = jnp.where(halo_edge(), 2.0 * wide[2, i], 0.0)
+        stage_coeff(wide, coeff, i)
+    operator = Operator(Joined(own_faces, faces))
+    scratch, inverse = inverse, plane_of(Joined(own_inverse, inverse))
+    operator.build(plane_of(coeff), 1, 5, keep_in(scratch))
+    operator.build(plane_of(coeff), 11, 15, keep_in(scratch))
+    for i in range(1, 15):
+        field[i] = omega_first * rhs[i] * inverse(i)
 
     def store_pre(i, value):
         pre[i] = value
         kept[0, i - 2] = coeff[i]
         kept[1, i - 2] = rhs[i]
         kept[2, i - 2] = value
-        kept[3, i - 2] = inverse[i]
-
-    sweep(operator, plane_of(field), plane_of(inverse), plane_of(rhs), omega_second, 2, 14, store_pre)
+        kept[3, i - 2] = inverse(i)
+
+    sweep(operator, plane_of(field), inverse, plane_of(rhs), omega_second, 2, 14, store_pre)
 
     def leave(i, applied):
         field[i] = jnp.where(coeff[i] > 0, rhs[i] - applied, 0.0)
@@ -392,7 +401,7 @@
 interpret = False
 VMEM = pl.BlockSpec(memory_space=pltpu.VMEM)
 SMEM = pl.BlockSpec(memory_space=pltpu.SMEM)
-ANY = pl.BlockSpec(memory_space=pl.ANY)
+HBM = pl.BlockSpec(memory_space=pltpu.HBM)
 
 
 def call(kernel, outs, scratch, *arguments, specs=None):
@@ -427,14 +436,9 @@
     def side(low, when_low, when_high):
         return jnp.where(low, when_low, when_high)
 
-    cells, low, high = call(
-        first_kernel,
-        [(2, 8, 32, 128), (2, 8, 4, 128), (2, 8, 4, 128)],
-        [pltpu.SemaphoreType.DMA((2,))],
-        source,
-        conductivity,
-        specs=[ANY, ANY],
-    )
+    cells = jnp.stack([source, conductivity])
+    low, high = cells[:, :, :4], cells[:, :, 28:]
+    cells = lax.optimization_barrier(cells)
     cells = join([cells, shift(low, "gy", -1), shift(high, "gy", 1)], 2)
 
     strips = take_lanes(cells, lane_map(128, 64, lambda z, k: z == k + jnp.where(k < 32, 0, 64)))
@@ -445,6 +449,7 @@
     halo = put_lanes(halo, lane_map(128, 128, lambda k, z: k == z), (1, 8, 40, 128))
     cells = join([cells, halo], 0)
 
+    own = call(own_kernel, [(3, 8, 40, 256), (8, 40, 256)], [(8, 40, 256)], cells)
     far = swap(side(low_x, cells[:, :4], cells[:, 4:]), "gx", True)
     near = swap(side(low_x, cells[:, 4:], cells[:, :4]), "gx", False)
     wide = join([side(low_x, far, near), cells, side(low_x, near, far)], 1)
@@ -455,6 +460,7 @@
         [(2, 4, 16, 128), (4, 12, *plane)],
         [(3, 16, *plane)] + [(16, *plane)] * 5 + [(16, 48, 128), (2, 64, 256)],
         wide,
+        *own,
     )
 
     pair = join([pair, shift(pair, "gy", -1), shift(pair, "gy", 1)], 2)

time: 66.2 us -> 64.4 us (0.973)
  other arithmetic: 0.36 us -> 2.17 us
  local copies, waits for them, and re-layouts: 2.13 us -> 0.32 us
  waiting for transfers between devices: 15.8 us -> 14.5 us
    another operation x0 -> x2, other arithmetic: none -> 1.81 us  [local(): cells = jnp.stack([source, conductivity])]
    unnamed x6 -> x2, local copies, waits for them, and re-layouts: 1.82 us -> 0.01 us
    ppermute x6, waiting for transfers between devices: 7.43 us -> 6.44 us  [shift(): lax.ppermute(block, axis, [(i, i + step) for i in range(count) if 0 <= i...]
  transfers between devices with their start and end apart: 11 -> 11, of which waited for: 8 -> 8; matrix products, arithmetic and copies ran while one was open for 0% -> 2% of each run, Pallas kernels for 0% -> 1%
where the time goes in v7:
time: 64.4 us; the launch traced here: 64 us
  starting transfers between devices  40.4 us (63%)
  waiting for transfers between devices  14.5 us (23%)
  Pallas kernels  5.63 us (9%)
  other arithmetic  2.17 us (3%)
  matrix products  0.7 us (1%)
    ppermute x5, starting transfers between devices, swap(): return lax.ppermute(block, axis, route)  21.8 us
    ppermute x6, starting transfers between devices, shift(): lax.ppermute(block, axis, [(i, i + step) for i in range(count) if 0 <= i...  18.6 us
    ppermute x5, waiting for transfers between devices, swap(): return lax.ppermute(block, axis, route)  8.04 us
    ppermute x6, waiting for transfers between devices, shift(): lax.ppermute(block, axis, [(i, i + step) for i in range(count) if 0 <= i...  6.44 us
    pallas_call x5, Pallas kernels, call(): pl.pallas_call(kernel, out_shape=[jax.ShapeDtypeStruct(shape, jnp.float32...  5.63 us
    another operation x2, other arithmetic, local(): cells = jnp.stack([source, conductivity])  1.81 us
  transfers between devices with their start and end apart: 11, of which 8 were waited for; matrix products, arithmetic and copies ran while one was open for 2% of the time, Pallas kernels for 1%

profile of v7, /device:TPU:443, one launch (start us, length us, event | category | flops | bytes accessed | tf_op | source)
XLA Modules:
  0.0 64.0 jit_solution(10698553788341128407)
XLA Ops:
  0.0 0.8 %fusion.11 = (f32[2,8,4,128]{3,2,1,0:T(4,128)S(1)}, f32[2,8,4,128]{3,2,1,0:T(4,128)S(1)}) fusion(f32[1,8,32,128]{3,2,1,0:T(8,128)} %bitcast.9, f32[1,8,32,128]{3,2,1,0:T(8,128)} %bitcast.11), kind=kLoop, calls=%fused_computation.29 | loop fusion | flops 16384 | bytes 327680 | tf_op jit(solution)/shard_map/stack | solution.py:439
  0.8 3.1 %collective-permute-start = (f32[2,8,4,128]{3,2,1,0:T(4,128)S(1)}, f32[2,8,4,128]{3,2,1,0:T(4,128)S(1)}, u32[]{:S(2)}, u32[]{:S(2)}) collective-permute-start(f32[2,8,4,128]{3,2,1,0:T(4,128)S(1)} %get-tuple-element.21), channel_id=1, source_target_pairs={{8,0},{16,8},{24,16},{32,24},{40,32},{48,40},{56,48},{9,1},{17,9},... | collective-permute-start | bytes 98312 | tf_op jit(solution)/shard_map/ppermute | solution.py:29
  3.9 2.2 %collective-permute-start.1 = (f32[2,8,4,128]{3,2,1,0:T(4,128)S(1)}, f32[2,8,4,128]{3,2,1,0:T(4,128)S(1)}, u32[]{:S(2)}, u32[]{:S(2)}) collective-permute-start(f32[2,8,4,128]{3,2,1,0:T(4,128)S(1)} %get-tuple-element.22), channel_id=1, source_target_pairs={{0,8},{8,16},{16,24},{24,32},{32,40},{40,48},{48,56},{1,9},{9,17},... | collective-permute-start | bytes 98312 | tf_op jit(solution)/shard_map/ppermute | solution.py:29
  6.1 1.0 %pad_maximum_fusion.2 = f32[2,8,32,128]{3,2,1,0:T(8,128)S(1)} fusion(f32[1,8,32,128]{3,2,1,0:T(8,128)} %bitcast.12, f32[1,8,32,128]{3,2,1,0:T(8,128)} %bitcast.10), kind=kLoop, calls=%fused_computation.6 | loop fusion | flops 65536 | bytes 524288 | tf_op jit(solution)/shard_map/stack | solution.py:439
  7.1 0.0 collective-permute-done
  7.1 1.4 %collective-permute-done.1 = f32[2,8,4,128]{3,2,1,0:T(4,128)S(1)} collective-permute-done((f32[2,8,4,128]{3,2,1,0:T(4,128)S(1)}, f32[2,8,4,128]{3,2,1,0:T(4,128)S(1)}, u32[]{:S(2)}, u32[]{:S(2)}) %collective-permute-start.1) | collective-permute-done | bytes 32800 | tf_op jit(solution)/shard_map/ppermute | solution.py:29
  8.6 0.4 fusion.9
  9.0 1.9 %collective-permute-start.2 = (f32[32,640]{1,0:T(8,128)S(1)}, f32[32,640]{1,0:T(8,128)S(1)}, u32[]{:S(2)}, u32[]{:S(2)}) collective-permute-start(f32[32,640]{1,0:T(8,128)S(1)} %get-tuple-element.23), channel_id=1, source_target_pairs={{1,0},{2,1},{3,2},{4,3},{5,4},{6,5},{7,6},{9,8},{10,9},{11,10},{12... | collective-permute-start | bytes 245768 | tf_op jit(solution)/shard_map/ppermute | solution.py:29
  10.9 6.1 %collective-permute-start.3 = (f32[32,640]{1,0:T(8,128)S(1)}, f32[32,640]{1,0:T(8,128)S(1)}, u32[]{:S(2)}, u32[]{:S(2)}) collective-permute-start(f32[32,640]{1,0:T(8,128)S(1)} %get-tuple-element.24), channel_id=1, source_target_pairs={{0,1},{1,2},{2,3},{3,4},{4,5},{5,6},{6,7},{8,9},{9,10},{10,11},{11... | collective-permute-start | bytes 245768 | tf_op jit(solution)/shard_map/ppermute | solution.py:29
  17.0 0.0 collective-permute-done.2
  17.0 0.1 fusion.17
  17.1 1.4 %collective-permute-done.3 = f32[32,640]{1,0:T(8,128)S(1)} collective-permute-done((f32[32,640]{1,0:T(8,128)S(1)}, f32[32,640]{1,0:T(8,128)S(1)}, u32[]{:S(2)}, u32[]{:S(2)}) %collective-permute-start.3) | collective-permute-done | bytes 81952 | tf_op jit(solution)/shard_map/ppermute | solution.py:29
  18.5 0.1 fusion.18
  18.6 0.3 fusion
  19.0 7.4 %collective-permute-start.4 = (f32[3,4,40,128]{3,2,1,0:T(8,128)S(1)}, f32[3,4,40,128]{3,2,1,0:T(8,128)S(1)}, u32[]{:S(2)}, u32[]{:S(2)}) collective-permute-start(f32[3,4,40,128]{3,2,1,0:T(8,128)S(1)} %get-tuple-element.19), channel_id=1, source_target_pairs={{64,128},{128,64},{192,256},{256,192},{320,384},{384,320},{448,512... | collective-permute-start | bytes 737288 | tf_op jit(solution)/shard_map/ppermute | solution.py:24
  26.4 1.9 %collective-permute-start.5 = (f32[3,4,40,128]{3,2,1,0:T(8,128)S(1)}, f32[3,4,40,128]{3,2,1,0:T(8,128)S(1)}, u32[]{:S(2)}, u32[]{:S(2)}) collective-permute-start(f32[3,4,40,128]{3,2,1,0:T(8,128)S(1)} %get-tuple-element.20), channel_id=1, source_target_pairs={{0,64},{64,0},{128,192},{192,128},{256,320},{320,256},{384,448},{4... | collective-permute-start | bytes 737288 | tf_op jit(solution)/shard_map/ppermute | solution.py:24
  28.3 0.3 shard_map.28
  28.6 1.6 %collective-permute-done.4 = f32[3,4,40,128]{3,2,1,0:T(8,128)S(1)} collective-permute-done((f32[3,4,40,128]{3,2,1,0:T(8,128)S(1)}, f32[3,4,40,128]{3,2,1,0:T(8,128)S(1)}, u32[]{:S(2)}, u32[]{:S(2)}) %collective-permute-start.4) | collective-permute-done | bytes 245792 | tf_op jit(solution)/shard_map/ppermute | solution.py:24
  30.3 0.0 collective-permute-done.5
  30.3 0.1 pad_maximum_fusion.wide
  30.4 1.9 %shard_map.29 = (f32[2,4,16,128]{3,2,1,0:T(8,128)S(1)}, f32[4,12,40,256]{3,2,1,0:T(8,128)S(1)}) custom-call(f32[3,16,40,128]{3,2,1,0:T(8,128)S(1)} %pad_maximum_fusion.wide, f32[3,8,40,256]{3,2,1,0:T(8,128)S(1)} %get-tuple-element.11.own_faces, f32[8,40,256]{2,1,0:T(8,128)S(1)} %get-tuple-element.12.own_inverse), custom_call_target="tpu_custom_call" | custom-call | tf_op jit(solution)/shard_map/pallas_call | solution.py:408
  32.2 3.4 %collective-permute-start.6 = (f32[2,4,16,128]{3,2,1,0:T(8,128)S(1)}, f32[2,4,16,128]{3,2,1,0:T(8,128)S(1)}, u32[]{:S(2)}, u32[]{:S(2)}) collective-permute-start(f32[2,4,16,128]{3,2,1,0:T(8,128)S(1)} %get-tuple-element.13), channel_id=1, source_target_pairs={{8,0},{16,8},{24,16},{32,24},{40,32},{48,40},{56,48},{9,1},{17,9},... | collective-permute-start | bytes 196616 | tf_op jit(solution)/shard_map/ppermute | solution.py:29
  35.6 1.9 %collective-permute-start.7 = (f32[2,4,16,128]{3,2,1,0:T(8,128)S(1)}, f32[2,4,16,128]{3,2,1,0:T(8,128)S(1)}, u32[]{:S(2)}, u32[]{:S(2)}) collective-permute-start(f32[2,4,16,128]{3,2,1,0:T(8,128)S(1)} %get-tuple-element.13), channel_id=1, source_target_pairs={{0,8},{8,16},{16,24},{24,32},{32,40},{40,48},{48,56},{1,9},{9,17},... | collective-permute-start | bytes 196616 | tf_op jit(solution)/shard_map/ppermute | solution.py:29
  37.6 0.5 collective-permute-done.6
  38.1 3.1 %collective-permute-done.7 = f32[2,4,16,128]{3,2,1,0:T(8,128)S(1)} collective-permute-done((f32[2,4,16,128]{3,2,1,0:T(8,128)S(1)}, f32[2,4,16,128]{3,2,1,0:T(8,128)S(1)}, u32[]{:S(2)}, u32[]{:S(2)}) %collective-permute-start.7) | collective-permute-done | bytes 65568 | tf_op jit(solution)/shard_map/ppermute | solution.py:29
  41.2 5.7 %collective-permute-start.8 = (f32[2,4,48,128]{3,2,1,0:T(8,128)S(1)}, f32[2,4,48,128]{3,2,1,0:T(8,128)S(1)}, u32[]{:S(2)}, u32[]{:S(2)}) collective-permute-start(f32[2,4,48,128]{3,2,1,0:T(8,128)S(1)} %constant_dynamic-update-slice_fusion), channel_id=1, source_target_pairs={{64,128},{128,64},{192,256},{256,192},{320,384},{384,320},{448,512... | collective-permute-start | bytes 589832 | tf_op jit(solution)/shard_map/ppermute | solution.py:24
  46.9 3.3 %collective-permute-done.8 = f32[2,4,48,128]{3,2,1,0:T(8,128)S(1)} collective-permute-done((f32[2,4,48,128]{3,2,1,0:T(8,128)S(1)}, f32[2,4,48,128]{3,2,1,0:T(8,128)S(1)}, u32[]{:S(2)}, u32[]{:S(2)}) %collective-permute-start.8) | collective-permute-done | bytes 196640 | tf_op jit(solution)/shard_map/ppermute | solution.py:24
  50.3 1.9 %collective-permute-start.9 = (f32[2,8,48,128]{3,2,1,0:T(8,128)S(1)}, f32[2,8,48,128]{3,2,1,0:T(8,128)S(1)}, u32[]{:S(2)}, u32[]{:S(2)}) collective-permute-start(f32[2,8,48,128]{3,2,1,0:T(8,128)S(1)} %maximum_select_fusion.1), channel_id=1, source_target_pairs={{0,64},{64,0},{128,192},{192,128},{256,320},{320,256},{384,448},{4... | collective-permute-start | bytes 1179656 | tf_op jit(solution)/shard_map/ppermute | solution.py:24
  52.2 0.1 iota.43
  52.3 0.1 iota.46
  52.4 1.5 %collective-permute-done.9 = f32[2,8,48,128]{3,2,1,0:T(8,128)S(1)} collective-permute-done((f32[2,8,48,128]{3,2,1,0:T(8,128)S(1)}, f32[2,8,48,128]{3,2,1,0:T(8,128)S(1)}, u32[]{:S(2)}, u32[]{:S(2)}) %collective-permute-start.9) | collective-permute-done | bytes 393248 | tf_op jit(solution)/shard_map/ppermute | solution.py:24
  53.9 0.1 maximum_select_fusion.pair
  54.0 1.5 %shard_map.30 = (f32[8,24,128]{2,1,0:T(8,128)S(1)}, f32[2,16,24,128]{3,2,1,0:T(8,128)S(1)}) custom-call(f32[2,16,48,128]{3,2,1,0:T(8,128)S(1)} %maximum_select_fusion.pair, f32[2,24,128]{2,1,0:T(8,128)S(1)} %pad_maximum_fusion.4.box, s32[1]{0:T(128)} %bitcast.4.parity), custom_call_target="tpu_custom_call" | custom-call | tf_op jit(solution)/shard_map/pallas_call | solution.py:408
  55.5 4.9 %collective-permute-start.10 = (f32[4,24,128]{2,1,0:T(8,128)S(1)}, f32[4,24,128]{2,1,0:T(8,128)S(1)}, u32[]{:S(2)}, u32[]{:S(2)}) collective-permute-start(f32[4,24,128]{2,1,0:T(8,128)S(1)} %slice_select_fusion.3), channel_id=1, source_target_pairs={{64,128},{128,64},{192,256},{256,192},{320,384},{384,320},{448,512... | collective-permute-start | bytes 147464 | tf_op jit(solution)/shard_map/ppermute | solution.py:24
  60.4 0.2 shard_map.31.filled
  60.6 1.5 %collective-permute-done.10 = f32[4,24,128]{2,1,0:T(8,128)S(1)} collective-permute-done((f32[4,24,128]{2,1,0:T(8,128)S(1)}, f32[4,24,128]{2,1,0:T(8,128)S(1)}, u32[]{:S(2)}, u32[]{:S(2)}) %collective-permute-start.10) | collective-permute-done | bytes 49184 | tf_op jit(solution)/shard_map/ppermute | solution.py:24
  62.1 1.8 %shard_map.32 = f32[8,32,128]{2,1,0:T(8,128)} custom-call(f32[12,24,128]{2,1,0:T(8,128)S(1)} %maximum_select_fusion.2.middle, f32[2,12,24,128]{3,2,1,0:T(8,128)S(1)} %slice_select_fusion.pair, f32[4,12,24,128]{3,2,1,0:T(8,128)S(1)} %shard_map.31.filled, f32[4,12,40,256]{3,2,1,0:T(8,128)S(1)} %get-tuple-element.16.kept), custom_call_target="tpu_custom_call" | custom-call | tf_op jit(solution)/shard_map/pallas_call | solution.py:408
  (15 shorter events, 0.3 us)
Async XLA Ops:
  0.8 6.3 %collective-permute-start = (f32[2,8,4,128]{3,2,1,0:T(4,128)S(1)}, f32[2,8,4,128]{3,2,1,0:T(4,128)S(1)}, u32[]{:S(2)}, u32[]{:S(2)}) collective-permute-start(f32[2,8,4,128]{3,2,1,0:T(4,128)S(1)} %get-tuple-element.21), channel_id=1, source_target_pairs={{8,0},{16,8},{24,16},{32,24},{40,32},{48,40},{56,48},{9,1},{17,9},... | collective-permute-start | bytes 98312 | tf_op jit(solution)/shard_map/ppermute | solution.py:29
  3.9 4.7 %collective-permute-start.1 = (f32[2,8,4,128]{3,2,1,0:T(4,128)S(1)}, f32[2,8,4,128]{3,2,1,0:T(4,128)S(1)}, u32[]{:S(2)}, u32[]{:S(2)}) collective-permute-start(f32[2,8,4,128]{3,2,1,0:T(4,128)S(1)} %get-tuple-element.22), channel_id=1, source_target_pairs={{0,8},{8,16},{16,24},{24,32},{32,40},{40,48},{48,56},{1,9},{9,17},... | collective-permute-start | bytes 98312 | tf_op jit(solution)/shard_map/ppermute | solution.py:29
  9.0 8.1 %collective-permute-start.2 = (f32[32,640]{1,0:T(8,128)S(1)}, f32[32,640]{1,0:T(8,128)S(1)}, u32[]{:S(2)}, u32[]{:S(2)}) collective-permute-start(f32[32,640]{1,0:T(8,128)S(1)} %get-tuple-element.23), channel_id=1, source_target_pairs={{1,0},{2,1},{3,2},{4,3},{5,4},{6,5},{7,6},{9,8},{10,9},{11,10},{12... | collective-permute-start | bytes 245768 | tf_op jit(solution)/shard_map/ppermute | solution.py:29
  10.9 7.6 %collective-permute-start.3 = (f32[32,640]{1,0:T(8,128)S(1)}, f32[32,640]{1,0:T(8,128)S(1)}, u32[]{:S(2)}, u32[]{:S(2)}) collective-permute-start(f32[32,640]{1,0:T(8,128)S(1)} %get-tuple-element.24), channel_id=1, source_target_pairs={{0,1},{1,2},{2,3},{3,4},{4,5},{5,6},{6,7},{8,9},{9,10},{10,11},{11... | collective-permute-start | bytes 245768 | tf_op jit(solution)/shard_map/ppermute | solution.py:29
  19.0 11.2 %collective-permute-start.4 = (f32[3,4,40,128]{3,2,1,0:T(8,128)S(1)}, f32[3,4,40,128]{3,2,1,0:T(8,128)S(1)}, u32[]{:S(2)}, u32[]{:S(2)}) collective-permute-start(f32[3,4,40,128]{3,2,1,0:T(8,128)S(1)} %get-tuple-element.19), channel_id=1, source_target_pairs={{64,128},{128,64},{192,256},{256,192},{320,384},{384,320},{448,512... | collective-permute-start | bytes 737288 | tf_op jit(solution)/shard_map/ppermute | solution.py:24
  26.4 3.9 %collective-permute-start.5 = (f32[3,4,40,128]{3,2,1,0:T(8,128)S(1)}, f32[3,4,40,128]{3,2,1,0:T(8,128)S(1)}, u32[]{:S(2)}, u32[]{:S(2)}) collective-permute-start(f32[3,4,40,128]{3,2,1,0:T(8,128)S(1)} %get-tuple-element.20), channel_id=1, source_target_pairs={{0,64},{64,0},{128,192},{192,128},{256,320},{320,256},{384,448},{4... | collective-permute-start | bytes 737288 | tf_op jit(solution)/shard_map/ppermute | solution.py:24
  32.2 5.9 %collective-permute-start.6 = (f32[2,4,16,128]{3,2,1,0:T(8,128)S(1)}, f32[2,4,16,128]{3,2,1,0:T(8,128)S(1)}, u32[]{:S(2)}, u32[]{:S(2)}) collective-permute-start(f32[2,4,16,128]{3,2,1,0:T(8,128)S(1)} %get-tuple-element.13), channel_id=1, source_target_pairs={{8,0},{16,8},{24,16},{32,24},{40,32},{48,40},{56,48},{9,1},{17,9},... | collective-permute-start | bytes 196616 | tf_op jit(solution)/shard_map/ppermute | solution.py:29
  35.6 5.6 %collective-permute-start.7 = (f32[2,4,16,128]{3,2,1,0:T(8,128)S(1)}, f32[2,4,16,128]{3,2,1,0:T(8,128)S(1)}, u32[]{:S(2)}, u32[]{:S(2)}) collective-permute-start(f32[2,4,16,128]{3,2,1,0:T(8,128)S(1)} %get-tuple-element.13), channel_id=1, source_target_pairs={{0,8},{8,16},{16,24},{24,32},{32,40},{40,48},{48,56},{1,9},{9,17},... | collective-permute-start | bytes 196616 | tf_op jit(solution)/shard_map/ppermute | solution.py:29
  41.2 9.0 %collective-permute-start.8 = (f32[2,4,48,128]{3,2,1,0:T(8,128)S(1)}, f32[2,4,48,128]{3,2,1,0:T(8,128)S(1)}, u32[]{:S(2)}, u32[]{:S(2)}) collective-permute-start(f32[2,4,48,128]{3,2,1,0:T(8,128)S(1)} %constant_dynamic-update-slice_fusion), channel_id=1, source_target_pairs={{64,128},{128,64},{192,256},{256,192},{320,384},{384,320},{448,512... | collective-permute-start | bytes 589832 | tf_op jit(solution)/shard_map/ppermute | solution.py:24
  50.3 3.6 %collective-permute-start.9 = (f32[2,8,48,128]{3,2,1,0:T(8,128)S(1)}, f32[2,8,48,128]{3,2,1,0:T(8,128)S(1)}, u32[]{:S(2)}, u32[]{:S(2)}) collective-permute-start(f32[2,8,48,128]{3,2,1,0:T(8,128)S(1)} %maximum_select_fusion.1), channel_id=1, source_target_pairs={{0,64},{64,0},{128,192},{192,128},{256,320},{320,256},{384,448},{4... | collective-permute-start | bytes 1179656 | tf_op jit(solution)/shard_map/ppermute | solution.py:24
  55.5 6.6 %collective-permute-start.10 = (f32[4,24,128]{2,1,0:T(8,128)S(1)}, f32[4,24,128]{2,1,0:T(8,128)S(1)}, u32[]{:S(2)}, u32[]{:S(2)}) collective-permute-start(f32[4,24,128]{2,1,0:T(8,128)S(1)} %slice_select_fusion.3), channel_id=1, source_target_pairs={{64,128},{128,64},{192,256},{256,192},{320,384},{384,320},{448,512... | collective-permute-start | bytes 147464 | tf_op jit(solution)/shard_map/ppermute | solution.py:24

commit v8 on v7

--- a/solution.py
+++ b/solution.py
@@ -197,36 +197,38 @@
     return (coarse >= edge) == (middle >= 2 * edge)
 
 
-def restrict_level(plane, coeff, first, count, halve, rows, piece, packed, matrices, store):
+def between(plane, at):
+    return 0.375 * (plane(at) + plane(at + 1)) + 0.125 * (plane(at - 1) + plane(at + 2))
+
+
+def both(plane, at):
+    return plane(at) + plane(at + 1)
+
+
+def restrict_level(weights, plane, first, halve, rows, piece, packed, matrix, store):
     lanes = piece.shape[2]
-    parts = packed.shape[2] // lanes
-    for j in range(count):
-        at = first + 2 * j
-        planes = (
-            0.375 * (plane(at) + plane(at + 1)) + 0.125 * (plane(at - 1) + plane(at + 2)),
-            coeff(at) + coeff(at + 1),
-        )
-        for kind in range(2):
-            for part in range(parts):
-                slot = piece.at[(2 * j + kind) * parts + part]
-                value = planes[kind][:, lanes * part : lanes * part + lanes]
-                packed[kind, pl.ds(rows * j, rows), pl.ds(lanes * part, lanes)] = halve(
-                    value, slot, kind == 0
-                )
-    for kind in range(2):
-        result = product(packed[kind], matrices[kind])
-        for j in range(count):
-            store(kind, j, result[rows * j : rows * j + rows])
+    parts = packed.shape[1] // lanes
+    for j in range(4):
+        value = (between if weights else both)(plane, first + 2 * j)
+        for part in range(parts):
+            packed[pl.ds(rows * j, rows), pl.ds(lanes * part, lanes)] = halve(
+                value[:, lanes * part : lanes * part + lanes], piece.at[j * parts + part], weights
+            )
+    result = product(packed[...], matrix)
+    for j in range(4):
+        store(j, result[rows * j : rows * j + rows])
 
 
 class Joined:
-    def __init__(self, own, scratch):
+    def __init__(self, own, scratch, first, last, start):
         self.own = own
         self.scratch = scratch
+        self.planes = first, last, start
 
     def __getitem__(self, place):
+        first, last, start = self.planes
         lead, i = place[:-1], place[-1]
-        return self.own[(*lead, i - 4)] if 5 <= i <= 10 else self.scratch[place]
+        return self.own[(*lead, i - start)] if first <= i <= last else self.scratch[place]
 
     def __setitem__(self, place, value):
         self.scratch[place] = value
@@ -237,54 +239,81 @@
     return (lane < 32) | (lane >= 96)
 
 
-def stage_coeff(cells, coeff, i):
+def stage(cells, rhs, coeff, i):
+    edge = halo_edge()
+    rhs[i, :, 0:128] = 2.0 * cells[0, i]
+    rhs[i, :, 128:256] = jnp.where(edge, 2.0 * cells[2, i], 0.0)
     coeff[i, :, 0:128] = cells[1, i]
-    coeff[i, :, 128:256] = jnp.where(halo_edge(), pltpu.roll(cells[2, i], 64, 1), 0.0)
-
-
-def own_kernel(cells, faces, inverse, coeff):
+    coeff[i, :, 128:256] = jnp.where(edge, pltpu.roll(cells[2, i], 64, 1), 0.0)
+
+
+def own_kernel(cells, faces, inverse, pre, left, middle_coeff, rhs, coeff, field, piece, packed):
     for i in range(8):
-        stage_coeff(cells, coeff, i)
-    Operator(faces).build(plane_of(coeff), 1, 7, keep_in(inverse))
-
-
-def fine_kernel(wide, own_faces, own_inverse, pair, kept, faces, inverse, rhs, coeff, field, pre, piece, packed):
+        stage(cells, rhs, coeff, i)
+    operator = Operator(faces)
+
+    def begin(i, value):
+        inverse[i] = value
+        field[i] = omega_first * rhs[i] * value
+
+    operator.build(plane_of(coeff), 1, 7, begin)
+
+    def store_pre(i, value):
+        pre[i - 2] = value
+
+    sweep(operator, plane_of(field), plane_of(inverse), plane_of(rhs), omega_second, 2, 6, store_pre)
+
+    def leave(i, applied):
+        left[i - 3] = jnp.where(coeff[i] > 0, rhs[i] - applied, 0.0)
+
+    operator.apply(lambda i: pre[i - 2], 3, 5, leave)
+    matrix = lane_map(256, 128, lambda f, c: 0.25 * mean_weights(fine_lane(f), middle_lane(c)))
+    restrict_level(
+        False, plane_of(coeff), 0, halve_own, 16, piece, packed, matrix, keep_in(middle_coeff)
+    )
+
+
+def fine_kernel(
+    wide, own_faces, own_inverse, own_pre, own_left, own_coeff,
+    pair, kept, faces, inverse, rhs, coeff, field, pre, left, piece, packed,
+):
     for i in range(16):
-        rhs[i, :, 0:128] = 2.0 * wide[0, i]
-        rhs[i, :, 128:256] = jnp.where(halo_edge(), 2.0 * wide[2, i], 0.0)
-        stage_coeff(wide, coeff, i)
-    operator = Operator(Joined(own_faces, faces))
-    scratch, inverse = inverse, plane_of(Joined(own_inverse, inverse))
-    operator.build(plane_of(coeff), 1, 5, keep_in(scratch))
-    operator.build(plane_of(coeff), 11, 15, keep_in(scratch))
-    for i in range(1, 15):
-        field[i] = omega_first * rhs[i] * inverse(i)
-
-    def store_pre(i, value):
-        pre[i] = value
-        kept[0, i - 2] = coeff[i]
-        kept[1, i - 2] = rhs[i]
-        kept[2, i - 2] = value
-        kept[3, i - 2] = inverse(i)
-
-    sweep(operator, plane_of(field), inverse, plane_of(rhs), omega_second, 2, 14, store_pre)
+        stage(wide, rhs, coeff, i)
+    operator = Operator(Joined(own_faces, faces, 5, 10, 4))
+    for start in (1, 11):
+        operator.build(plane_of(coeff), start, start + 4, keep_in(inverse))
+    inverses = plane_of(Joined(own_inverse, inverse, 5, 10, 4))
+    smoothed = plane_of(Joined(own_pre, pre, 6, 9, 6))
+    leftover = plane_of(Joined(own_left, left, 7, 8, 7))
+    for i in (*range(1, 7), *range(9, 15)):
+        field[i] = omega_first * rhs[i] * inverses(i)
+    for start in (2, 10):
+        sweep(
+            operator, plane_of(field), inverses, plane_of(rhs), omega_second, start, start + 4, keep_in(pre)
+        )
+    for i in range(2, 14):
+        for kind, plane in enumerate((plane_of(coeff), plane_of(rhs), smoothed, inverses)):
+            kept[kind, i - 2] = plane(i)
 
     def leave(i, applied):
-        field[i] = jnp.where(coeff[i] > 0, rhs[i] - applied, 0.0)
-
-    operator.apply(plane_of(pre), 3, 13, leave)
-    matrices = (
-        lane_map(256, 128, lambda f, c: 4.0 * gather_weights(fine_lane(f), middle_lane(c))),
-        lane_map(256, 128, lambda f, c: 0.25 * mean_weights(fine_lane(f), middle_lane(c))),
-    )
-
-    def store(kind, j, value):
-        pair[kind, j] = value
-
-    restrict_level(plane_of(field), plane_of(coeff), 4, 4, halve_own, 16, piece, packed, matrices, store)
-
-
-def box_kernel(pair, box, parity, corrected, kept, faces, inverse, field, other, piece, packed, low, low_faces, low_inverse, risen):
+        left[i] = jnp.where(coeff[i] > 0, rhs[i] - applied, 0.0)
+
+    for start in (3, 9):
+        operator.apply(smoothed, start, start + 4, leave)
+    matrix = lane_map(256, 128, lambda f, c: 4.0 * gather_weights(fine_lane(f), middle_lane(c)))
+    restrict_level(True, leftover, 4, halve_own, 16, piece, packed, matrix, keep_in(pair, 0))
+    for j in range(4):
+        pair[1, j] = own_coeff[j]
+
+
+def box_kernel(narrow, box, parity, corrected, kept, pair, faces, inverse, field, other, piece, packed, low, low_faces, low_inverse, risen):
+    after = lax.broadcasted_iota(jnp.int32, (8, 128), 0) < 4
+    for kind in range(2):
+        for i in range(16):
+            pair[kind, i, 0:24] = narrow[kind, i, 0:24]
+            pair[kind, i, 24:32] = jnp.where(after, narrow[kind, i, 24:32], 0.0)
+            pair[kind, i, 32:40] = jnp.where(after, 0.0, narrow[kind, i, 24:32])
+            pair[kind, i, 40:48] = narrow[kind, i, 32:40]
     rhs, coeff = plane_of(pair, 0), plane_of(pair, 1)
     operator = Operator(faces)
 
@@ -300,15 +329,18 @@
 
     operator.apply(plane_of(other), 3, 13, leave)
     odd = parity[0]
-    matrices = (
-        lane_map(128, 128, lambda m, c: 4.0 * gather_weights(middle_lane(m), coarse_lane(c, odd))),
-        lane_map(128, 128, lambda m, c: 0.25 * mean_weights(middle_lane(m), coarse_lane(c, odd))),
-    )
-
-    def store(kind, j, value):
-        low[kind, j + 1] = value
-
-    restrict_level(plane_of(field), coeff, 4, 4, halve_circular, 24, piece, packed, matrices, store)
+    for kind, matrix in enumerate(
+        (
+            lane_map(128, 128, lambda m, c: 4.0 * gather_weights(middle_lane(m), coarse_lane(c, odd))),
+            lane_map(128, 128, lambda m, c: 0.25 * mean_weights(middle_lane(m), coarse_lane(c, odd))),
+        )
+    ):
+
+        def store(j, value, kind=kind):
+            low[kind, j + 1] = value
+
+        plane = coeff if kind else plane_of(field)
+        restrict_level(kind == 0, plane, 4, halve_circular, 24, piece.at[kind], packed.at[kind], matrix, store)
     for place in (0, 5):
         for kind in range(3):
             low[kind, place] = jnp.zeros((24, 128), jnp.float32)
@@ -449,21 +481,27 @@
     halo = put_lanes(halo, lane_map(128, 128, lambda k, z: k == z), (1, 8, 40, 128))
     cells = join([cells, halo], 0)
 
-    own = call(own_kernel, [(3, 8, 40, 256), (8, 40, 256)], [(8, 40, 256)], cells)
+    plane = (40, 256)
+    own = call(
+        own_kernel,
+        [(3, 8, *plane), (8, *plane), (4, *plane), (2, *plane), (4, 16, 128)],
+        [(8, *plane), (8, *plane), (8, *plane), (8, 48, 128), (64, 256)],
+        cells,
+    )
     far = swap(side(low_x, cells[:, :4], cells[:, 4:]), "gx", True)
     near = swap(side(low_x, cells[:, 4:], cells[:, :4]), "gx", False)
     wide = join([side(low_x, far, near), cells, side(low_x, near, far)], 1)
 
-    plane = (40, 256)
     pair, kept = call(
         fine_kernel,
         [(2, 4, 16, 128), (4, 12, *plane)],
-        [(3, 16, *plane)] + [(16, *plane)] * 5 + [(16, 48, 128), (2, 64, 256)],
+        [(3, 16, *plane)] + [(16, *plane)] * 6 + [(8, 48, 128), (64, 256)],
         wide,
         *own,
     )
 
-    pair = join([pair, shift(pair, "gy", -1), shift(pair, "gy", 1)], 2)
+    after, before = shift(pair, "gy", -1), shift(pair, "gy", 1)
+    pair = join([pair, after[:, :, :12], before[:, :, 4:]], 2)
     far = swap(pair, "gx", True)
     pair = side(low_x, join([far, pair], 1), join([pair, far], 1))
     near = swap(pair, "gx", False)
@@ -474,7 +512,9 @@
     middle, pair = call(
         box_kernel,
         [(8, 24, 128), (2, 16, 24, 128)],
-        [(3, 16, 48, 128), (16, 48, 128), (16, 48, 128), (16, 48, 128), (8, 48, 128), (2, 96, 128)]
+        [(2, 16, 48, 128), (3, 16, 48, 128)]
+        + [(16, 48, 128)] * 3
+        + [(2, 4, 48, 128), (2, 96, 128)]
         + [(3, 6, 24, 128), (4, 6, 24, 128), (6, 24, 128), (4, 48, 128)],
         pair,
         jnp.stack([jnp.where(edge, 0.0, 1.0) for edge in edges]),

time: 64.4 us -> 66.1 us (1.026)
  the two profiles are of different devices: /device:TPU:443 before, /device:TPU:439 now
where the time goes in v8:
time: 66.1 us; the launch traced here: 65.6 us
  starting transfers between devices  43.1 us (65%)
  waiting for transfers between devices  13.5 us (20%)
  Pallas kernels  5.59 us (8%)
  other arithmetic  2.17 us (3%)
  matrix products  0.7 us (1%)
    ppermute x6, starting transfers between devices, shift(): lax.ppermute(block, axis, [(i, i + step) for i in range(count) if 0 <= i...  21.6 us
    ppermute x5, starting transfers between devices, swap(): return lax.ppermute(block, axis, route)  21.5 us
    ppermute x5, waiting for transfers between devices, swap(): return lax.ppermute(block, axis, route)  7.24 us
    ppermute x6, waiting for transfers between devices, shift(): lax.ppermute(block, axis, [(i, i + step) for i in range(count) if 0 <= i...  6.23 us
    pallas_call x5, Pallas kernels, call(): pl.pallas_call(kernel, out_shape=[jax.ShapeDtypeStruct(shape, jnp.float32...  5.59 us
    another operation x2, other arithmetic, local(): cells = jnp.stack([source, conductivity])  1.81 us
  transfers between devices with their start and end apart: 11, of which 6 were waited for; matrix products, arithmetic and copies ran while one was open for 2% of the time, Pallas kernels for 1%

profile of v8, /device:TPU:439, one launch (start us, length us, event | category | flops | bytes accessed | tf_op | source)
XLA Modules:
  0.0 65.6 jit_solution(2278653277378837720)
XLA Ops:
  0.0 0.8 %fusion.11 = (f32[2,8,4,128]{3,2,1,0:T(4,128)S(1)}, f32[2,8,4,128]{3,2,1,0:T(4,128)S(1)}) fusion(f32[1,8,32,128]{3,2,1,0:T(8,128)} %bitcast.10, f32[1,8,32,128]{3,2,1,0:T(8,128)} %bitcast.12), kind=kLoop, calls=%fused_computation.30 | loop fusion | flops 16384 | bytes 327680 | tf_op jit(solution)/shard_map/stack | solution.py:471
  0.8 2.2 %collective-permute-start = (f32[2,8,4,128]{3,2,1,0:T(4,128)S(1)}, f32[2,8,4,128]{3,2,1,0:T(4,128)S(1)}, u32[]{:S(2)}, u32[]{:S(2)}) collective-permute-start(f32[2,8,4,128]{3,2,1,0:T(4,128)S(1)} %get-tuple-element.27), channel_id=1, source_target_pairs={{8,0},{16,8},{24,16},{32,24},{40,32},{48,40},{56,48},{9,1},{17,9},... | collective-permute-start | bytes 98312 | tf_op jit(solution)/shard_map/ppermute | solution.py:29
  3.0 4.3 %collective-permute-start.1 = (f32[2,8,4,128]{3,2,1,0:T(4,128)S(1)}, f32[2,8,4,128]{3,2,1,0:T(4,128)S(1)}, u32[]{:S(2)}, u32[]{:S(2)}) collective-permute-start(f32[2,8,4,128]{3,2,1,0:T(4,128)S(1)} %get-tuple-element.28), channel_id=1, source_target_pairs={{0,8},{8,16},{16,24},{24,32},{32,40},{40,48},{48,56},{1,9},{9,17},... | collective-permute-start | bytes 98312 | tf_op jit(solution)/shard_map/ppermute | solution.py:29
  7.3 1.0 %pad_maximum_fusion.2 = f32[2,8,32,128]{3,2,1,0:T(8,128)S(1)} fusion(f32[1,8,32,128]{3,2,1,0:T(8,128)} %bitcast.13, f32[1,8,32,128]{3,2,1,0:T(8,128)} %bitcast.11), kind=kLoop, calls=%fused_computation.5 | loop fusion | flops 65536 | bytes 524288 | tf_op jit(solution)/shard_map/stack | solution.py:471
  8.3 0.0 collective-permute-done
  8.3 0.0 collective-permute-done.1
  8.4 0.4 fusion.9
  8.8 1.9 %collective-permute-start.2 = (f32[32,640]{1,0:T(8,128)S(1)}, f32[32,640]{1,0:T(8,128)S(1)}, u32[]{:S(2)}, u32[]{:S(2)}) collective-permute-start(f32[32,640]{1,0:T(8,128)S(1)} %get-tuple-element.29), channel_id=1, source_target_pairs={{1,0},{2,1},{3,2},{4,3},{5,4},{6,5},{7,6},{9,8},{10,9},{11,10},{12... | collective-permute-start | bytes 245768 | tf_op jit(solution)/shard_map/ppermute | solution.py:29
  10.7 6.1 %collective-permute-start.3 = (f32[32,640]{1,0:T(8,128)S(1)}, f32[32,640]{1,0:T(8,128)S(1)}, u32[]{:S(2)}, u32[]{:S(2)}) collective-permute-start(f32[32,640]{1,0:T(8,128)S(1)} %get-tuple-element.30), channel_id=1, source_target_pairs={{0,1},{1,2},{2,3},{3,4},{4,5},{5,6},{6,7},{8,9},{9,10},{10,11},{11... | collective-permute-start | bytes 245768 | tf_op jit(solution)/shard_map/ppermute | solution.py:29
  16.8 0.0 collective-permute-done.2
  16.9 0.1 fusion.17
  16.9 1.4 %collective-permute-done.3 = f32[32,640]{1,0:T(8,128)S(1)} collective-permute-done((f32[32,640]{1,0:T(8,128)S(1)}, f32[32,640]{1,0:T(8,128)S(1)}, u32[]{:S(2)}, u32[]{:S(2)}) %collective-permute-start.3) | collective-permute-done | bytes 81952 | tf_op jit(solution)/shard_map/ppermute | solution.py:29
  18.3 0.1 fusion.18
  18.4 0.3 fusion
  18.8 7.1 %collective-permute-start.4 = (f32[3,4,40,128]{3,2,1,0:T(8,128)S(1)}, f32[3,4,40,128]{3,2,1,0:T(8,128)S(1)}, u32[]{:S(2)}, u32[]{:S(2)}) collective-permute-start(f32[3,4,40,128]{3,2,1,0:T(8,128)S(1)} %get-tuple-element.25), channel_id=1, source_target_pairs={{64,128},{128,64},{192,256},{256,192},{320,384},{384,320},{448,512... | collective-permute-start | bytes 737288 | tf_op jit(solution)/shard_map/ppermute | solution.py:24
  25.9 1.9 %collective-permute-start.5 = (f32[3,4,40,128]{3,2,1,0:T(8,128)S(1)}, f32[3,4,40,128]{3,2,1,0:T(8,128)S(1)}, u32[]{:S(2)}, u32[]{:S(2)}) collective-permute-start(f32[3,4,40,128]{3,2,1,0:T(8,128)S(1)} %get-tuple-element.26), channel_id=1, source_target_pairs={{0,64},{64,0},{128,192},{192,128},{256,320},{320,256},{384,448},{4... | collective-permute-start | bytes 737288 | tf_op jit(solution)/shard_map/ppermute | solution.py:24
  27.8 0.6 shard_map.28
  28.5 1.3 %collective-permute-done.4 = f32[3,4,40,128]{3,2,1,0:T(8,128)S(1)} collective-permute-done((f32[3,4,40,128]{3,2,1,0:T(8,128)S(1)}, f32[3,4,40,128]{3,2,1,0:T(8,128)S(1)}, u32[]{:S(2)}, u32[]{:S(2)}) %collective-permute-start.4) | collective-permute-done | bytes 245792 | tf_op jit(solution)/shard_map/ppermute | solution.py:24
  29.7 0.0 collective-permute-done.5
  29.8 0.1 pad_maximum_fusion.wide
  29.9 1.4 %shard_map.29 = (f32[2,4,16,128]{3,2,1,0:T(8,128)S(1)}, f32[4,12,40,256]{3,2,1,0:T(8,128)S(1)}) custom-call(f32[3,16,40,128]{3,2,1,0:T(8,128)S(1)} %pad_maximum_fusion.wide, f32[3,8,40,256]{3,2,1,0:T(8,128)S(1)} %get-tuple-element.14.own_faces, f32[8,40,256]{2,1,0:T(8,128)S(1)} %get-tuple-element.15.own_inverse, ...), custom_call_target="tpu_custom_call" | custom-call | tf_op jit(solution)/shard_map/pallas_call | solution.py:440
  31.3 5.2 %collective-permute-start.7 = (f32[2,4,16,128]{3,2,1,0:T(8,128)S(1)}, f32[2,4,16,128]{3,2,1,0:T(8,128)S(1)}, u32[]{:S(2)}, u32[]{:S(2)}) collective-permute-start(f32[2,4,16,128]{3,2,1,0:T(8,128)S(1)} %get-tuple-element.19), channel_id=1, source_target_pairs={{0,8},{8,16},{16,24},{24,32},{32,40},{40,48},{48,56},{1,9},{9,17},... | collective-permute-start | bytes 196616 | tf_op jit(solution)/shard_map/ppermute | solution.py:29
  36.5 1.9 %collective-permute-start.6 = (f32[2,4,16,128]{3,2,1,0:T(8,128)S(1)}, f32[2,4,16,128]{3,2,1,0:T(8,128)S(1)}, u32[]{:S(2)}, u32[]{:S(2)}) collective-permute-start(f32[2,4,16,128]{3,2,1,0:T(8,128)S(1)} %get-tuple-element.19), channel_id=1, source_target_pairs={{8,0},{16,8},{24,16},{32,24},{40,32},{48,40},{56,48},{9,1},{17,9},... | collective-permute-start | bytes 196616 | tf_op jit(solution)/shard_map/ppermute | solution.py:29
  38.4 0.0 collective-permute-done.7
  38.4 4.8 %collective-permute-done.6 = f32[2,4,16,128]{3,2,1,0:T(8,128)S(1)} collective-permute-done((f32[2,4,16,128]{3,2,1,0:T(8,128)S(1)}, f32[2,4,16,128]{3,2,1,0:T(8,128)S(1)}, u32[]{:S(2)}, u32[]{:S(2)}) %collective-permute-start.6) | collective-permute-done | bytes 65568 | tf_op jit(solution)/shard_map/ppermute | solution.py:29
  43.3 5.7 %collective-permute-start.8 = (f32[2,4,40,128]{3,2,1,0:T(8,128)S(1)}, f32[2,4,40,128]{3,2,1,0:T(8,128)S(1)}, u32[]{:S(2)}, u32[]{:S(2)}) collective-permute-start(f32[2,4,40,128]{3,2,1,0:T(8,128)S(1)} %pad_maximum_fusion.4), channel_id=1, source_target_pairs={{64,128},{128,64},{192,256},{256,192},{320,384},{384,320},{448,512... | collective-permute-start | bytes 491528 | tf_op jit(solution)/shard_map/ppermute | solution.py:24
  49.0 3.0 %collective-permute-done.8 = f32[2,4,40,128]{3,2,1,0:T(8,128)S(1)} collective-permute-done((f32[2,4,40,128]{3,2,1,0:T(8,128)S(1)}, f32[2,4,40,128]{3,2,1,0:T(8,128)S(1)}, u32[]{:S(2)}, u32[]{:S(2)}) %collective-permute-start.8) | collective-permute-done | bytes 163872 | tf_op jit(solution)/shard_map/ppermute | solution.py:24
  52.0 1.9 %collective-permute-start.9 = (f32[2,8,40,128]{3,2,1,0:T(8,128)S(1)}, f32[2,8,40,128]{3,2,1,0:T(8,128)S(1)}, u32[]{:S(2)}, u32[]{:S(2)}) collective-permute-start(f32[2,8,40,128]{3,2,1,0:T(8,128)S(1)} %maximum_select_fusion.1), channel_id=1, source_target_pairs={{0,64},{64,0},{128,192},{192,128},{256,320},{320,256},{384,448},{4... | collective-permute-start | bytes 983048 | tf_op jit(solution)/shard_map/ppermute | solution.py:24
  54.0 0.1 iota.43
  54.1 0.1 iota.46
  54.1 1.4 %collective-permute-done.9 = f32[2,8,40,128]{3,2,1,0:T(8,128)S(1)} collective-permute-done((f32[2,8,40,128]{3,2,1,0:T(8,128)S(1)}, f32[2,8,40,128]{3,2,1,0:T(8,128)S(1)}, u32[]{:S(2)}, u32[]{:S(2)}) %collective-permute-start.9) | collective-permute-done | bytes 327712 | tf_op jit(solution)/shard_map/ppermute | solution.py:24
  55.6 1.5 %shard_map.30 = (f32[8,24,128]{2,1,0:T(8,128)S(1)}, f32[2,16,24,128]{3,2,1,0:T(8,128)S(1)}) custom-call(f32[2,16,40,128]{3,2,1,0:T(8,128)S(1)} %maximum_select_fusion.narrow, f32[2,24,128]{2,1,0:T(8,128)S(1)} %pad_maximum_fusion.5.box, s32[1]{0:T(128)} %bitcast.4.parity), custom_call_target="tpu_custom_call" | custom-call | tf_op jit(solution)/shard_map/pallas_call | solution.py:440
  57.2 4.9 %collective-permute-start.10 = (f32[4,24,128]{2,1,0:T(8,128)S(1)}, f32[4,24,128]{2,1,0:T(8,128)S(1)}, u32[]{:S(2)}, u32[]{:S(2)}) collective-permute-start(f32[4,24,128]{2,1,0:T(8,128)S(1)} %slice_select_fusion.3), channel_id=1, source_target_pairs={{64,128},{128,64},{192,256},{256,192},{320,384},{384,320},{448,512... | collective-permute-start | bytes 147464 | tf_op jit(solution)/shard_map/ppermute | solution.py:24
  62.0 0.2 shard_map.31.filled
  62.2 1.5 %collective-permute-done.10 = f32[4,24,128]{2,1,0:T(8,128)S(1)} collective-permute-done((f32[4,24,128]{2,1,0:T(8,128)S(1)}, f32[4,24,128]{2,1,0:T(8,128)S(1)}, u32[]{:S(2)}, u32[]{:S(2)}) %collective-permute-start.10) | collective-permute-done | bytes 49184 | tf_op jit(solution)/shard_map/ppermute | solution.py:24
  63.8 1.8 %shard_map.32 = f32[8,32,128]{2,1,0:T(8,128)} custom-call(f32[12,24,128]{2,1,0:T(8,128)S(1)} %maximum_select_fusion.2.middle, f32[2,12,24,128]{3,2,1,0:T(8,128)S(1)} %slice_select_fusion.pair, f32[4,12,24,128]{3,2,1,0:T(8,128)S(1)} %shard_map.31.filled, f32[4,12,40,256]{3,2,1,0:T(8,128)S(1)} %get-tuple-element.22.kept), custom_call_target="tpu_custom_call" | custom-call | tf_op jit(solution)/shard_map/pallas_call | solution.py:440
  (15 shorter events, 0.3 us)
Async XLA Ops:
  0.8 7.5 %collective-permute-start = (f32[2,8,4,128]{3,2,1,0:T(4,128)S(1)}, f32[2,8,4,128]{3,2,1,0:T(4,128)S(1)}, u32[]{:S(2)}, u32[]{:S(2)}) collective-permute-start(f32[2,8,4,128]{3,2,1,0:T(4,128)S(1)} %get-tuple-element.27), channel_id=1, source_target_pairs={{8,0},{16,8},{24,16},{32,24},{40,32},{48,40},{56,48},{9,1},{17,9},... | collective-permute-start | bytes 98312 | tf_op jit(solution)/shard_map/ppermute | solution.py:29
  3.0 5.4 %collective-permute-start.1 = (f32[2,8,4,128]{3,2,1,0:T(4,128)S(1)}, f32[2,8,4,128]{3,2,1,0:T(4,128)S(1)}, u32[]{:S(2)}, u32[]{:S(2)}) collective-permute-start(f32[2,8,4,128]{3,2,1,0:T(4,128)S(1)} %get-tuple-element.28), channel_id=1, source_target_pairs={{0,8},{8,16},{16,24},{24,32},{32,40},{40,48},{48,56},{1,9},{9,17},... | collective-permute-start | bytes 98312 | tf_op jit(solution)/shard_map/ppermute | solution.py:29
  8.8 8.1 %collective-permute-start.2 = (f32[32,640]{1,0:T(8,128)S(1)}, f32[32,640]{1,0:T(8,128)S(1)}, u32[]{:S(2)}, u32[]{:S(2)}) collective-permute-start(f32[32,640]{1,0:T(8,128)S(1)} %get-tuple-element.29), channel_id=1, source_target_pairs={{1,0},{2,1},{3,2},{4,3},{5,4},{6,5},{7,6},{9,8},{10,9},{11,10},{12... | collective-permute-start | bytes 245768 | tf_op jit(solution)/shard_map/ppermute | solution.py:29
  10.7 7.6 %collective-permute-start.3 = (f32[32,640]{1,0:T(8,128)S(1)}, f32[32,640]{1,0:T(8,128)S(1)}, u32[]{:S(2)}, u32[]{:S(2)}) collective-permute-start(f32[32,640]{1,0:T(8,128)S(1)} %get-tuple-element.30), channel_id=1, source_target_pairs={{0,1},{1,2},{2,3},{3,4},{4,5},{5,6},{6,7},{8,9},{9,10},{10,11},{11... | collective-permute-start | bytes 245768 | tf_op jit(solution)/shard_map/ppermute | solution.py:29
  18.8 10.9 %collective-permute-start.4 = (f32[3,4,40,128]{3,2,1,0:T(8,128)S(1)}, f32[3,4,40,128]{3,2,1,0:T(8,128)S(1)}, u32[]{:S(2)}, u32[]{:S(2)}) collective-permute-start(f32[3,4,40,128]{3,2,1,0:T(8,128)S(1)} %get-tuple-element.25), channel_id=1, source_target_pairs={{64,128},{128,64},{192,256},{256,192},{320,384},{384,320},{448,512... | collective-permute-start | bytes 737288 | tf_op jit(solution)/shard_map/ppermute | solution.py:24
  25.9 3.9 %collective-permute-start.5 = (f32[3,4,40,128]{3,2,1,0:T(8,128)S(1)}, f32[3,4,40,128]{3,2,1,0:T(8,128)S(1)}, u32[]{:S(2)}, u32[]{:S(2)}) collective-permute-start(f32[3,4,40,128]{3,2,1,0:T(8,128)S(1)} %get-tuple-element.26), channel_id=1, source_target_pairs={{0,64},{64,0},{128,192},{192,128},{256,320},{320,256},{384,448},{4... | collective-permute-start | bytes 737288 | tf_op jit(solution)/shard_map/ppermute | solution.py:24
  31.3 7.1 %collective-permute-start.7 = (f32[2,4,16,128]{3,2,1,0:T(8,128)S(1)}, f32[2,4,16,128]{3,2,1,0:T(8,128)S(1)}, u32[]{:S(2)}, u32[]{:S(2)}) collective-permute-start(f32[2,4,16,128]{3,2,1,0:T(8,128)S(1)} %get-tuple-element.19), channel_id=1, source_target_pairs={{0,8},{8,16},{16,24},{24,32},{32,40},{40,48},{48,56},{1,9},{9,17},... | collective-permute-start | bytes 196616 | tf_op jit(solution)/shard_map/ppermute | solution.py:29
  36.5 6.8 %collective-permute-start.6 = (f32[2,4,16,128]{3,2,1,0:T(8,128)S(1)}, f32[2,4,16,128]{3,2,1,0:T(8,128)S(1)}, u32[]{:S(2)}, u32[]{:S(2)}) collective-permute-start(f32[2,4,16,128]{3,2,1,0:T(8,128)S(1)} %get-tuple-element.19), channel_id=1, source_target_pairs={{8,0},{16,8},{24,16},{32,24},{40,32},{48,40},{56,48},{9,1},{17,9},... | collective-permute-start | bytes 196616 | tf_op jit(solution)/shard_map/ppermute | solution.py:29
  43.3 8.7 %collective-permute-start.8 = (f32[2,4,40,128]{3,2,1,0:T(8,128)S(1)}, f32[2,4,40,128]{3,2,1,0:T(8,128)S(1)}, u32[]{:S(2)}, u32[]{:S(2)}) collective-permute-start(f32[2,4,40,128]{3,2,1,0:T(8,128)S(1)} %pad_maximum_fusion.4), channel_id=1, source_target_pairs={{64,128},{128,64},{192,256},{256,192},{320,384},{384,320},{448,512... | collective-permute-start | bytes 491528 | tf_op jit(solution)/shard_map/ppermute | solution.py:24
  52.0 3.5 %collective-permute-start.9 = (f32[2,8,40,128]{3,2,1,0:T(8,128)S(1)}, f32[2,8,40,128]{3,2,1,0:T(8,128)S(1)}, u32[]{:S(2)}, u32[]{:S(2)}) collective-permute-start(f32[2,8,40,128]{3,2,1,0:T(8,128)S(1)} %maximum_select_fusion.1), channel_id=1, source_target_pairs={{0,64},{64,0},{128,192},{192,128},{256,320},{320,256},{384,448},{4... | collective-permute-start | bytes 983048 | tf_op jit(solution)/shard_map/ppermute | solution.py:24
  57.2 6.6 %collective-permute-start.10 = (f32[4,24,128]{2,1,0:T(8,128)S(1)}, f32[4,24,128]{2,1,0:T(8,128)S(1)}, u32[]{:S(2)}, u32[]{:S(2)}) collective-permute-start(f32[4,24,128]{2,1,0:T(8,128)S(1)} %slice_select_fusion.3), channel_id=1, source_target_pairs={{64,128},{128,64},{192,256},{256,192},{320,384},{384,320},{448,512... | collective-permute-start | bytes 147464 | tf_op jit(solution)/shard_map/ppermute | solution.py:24

commit v9 on v8

--- a/solution.py
+++ b/solution.py
@@ -275,7 +275,7 @@
 
 def fine_kernel(
     wide, own_faces, own_inverse, own_pre, own_left, own_coeff,
-    pair, kept, faces, inverse, rhs, coeff, field, pre, left, piece, packed,
+    pair, low, high, kept, faces, inverse, rhs, coeff, field, pre, left, piece, packed,
 ):
     for i in range(16):
         stage(wide, rhs, coeff, i)
@@ -304,6 +304,10 @@
     restrict_level(True, leftover, 4, halve_own, 16, piece, packed, matrix, keep_in(pair, 0))
     for j in range(4):
         pair[1, j] = own_coeff[j]
+    for kind in range(2):
+        for j in range(4):
+            low[kind, j] = pair[kind, j, 0:12]
+            high[kind, j] = pair[kind, j, 4:16]
 
 
 def box_kernel(narrow, box, parity, corrected, kept, pair, faces, inverse, field, other, piece, packed, low, low_faces, low_inverse, risen):
@@ -492,16 +496,15 @@
     near = swap(side(low_x, cells[:, 4:], cells[:, :4]), "gx", False)
     wide = join([side(low_x, far, near), cells, side(low_x, near, far)], 1)
 
-    pair, kept = call(
+    pair, low, high, kept = call(
         fine_kernel,
-        [(2, 4, 16, 128), (4, 12, *plane)],
+        [(2, 4, 16, 128), (2, 4, 12, 128), (2, 4, 12, 128), (4, 12, *plane)],
         [(3, 16, *plane)] + [(16, *plane)] * 6 + [(8, 48, 128), (64, 256)],
         wide,
         *own,
     )
 
-    after, before = shift(pair, "gy", -1), shift(pair, "gy", 1)
-    pair = join([pair, after[:, :, :12], before[:, :, 4:]], 2)
+    pair = join([pair, shift(low, "gy", -1), shift(high, "gy", 1)], 2)
     far = swap(pair, "gx", True)
     pair = side(low_x, join([far, pair], 1), join([pair, far], 1))
     near = swap(pair, "gx", False)

time: 66.1 us -> 63.6 us (0.962)
  the two profiles are of different devices: /device:TPU:439 before, /device:TPU:443 now
where the time goes in v9:
time: 63.6 us; the launch traced here: 63.1 us
  starting transfers between devices  40.4 us (64%)
  waiting for transfers between devices  13.7 us (22%)
  Pallas kernels  5.6 us (9%)
  other arithmetic  2.17 us (3%)
  matrix products  0.7 us (1%)
    ppermute x5, starting transfers between devices, swap(): return lax.ppermute(block, axis, route)  21.8 us
    ppermute x6, starting transfers between devices, shift(): lax.ppermute(block, axis, [(i, i + step) for i in range(count) if 0 <= i...  18.6 us
    ppermute x5, waiting for transfers between devices, swap(): return lax.ppermute(block, axis, route)  7.24 us
    ppermute x6, waiting for transfers between devices, shift(): lax.ppermute(block, axis, [(i, i + step) for i in range(count) if 0 <= i...  6.46 us
    pallas_call x5, Pallas kernels, call(): pl.pallas_call(kernel, out_shape=[jax.ShapeDtypeStruct(shape, jnp.float32...  5.6 us
    another operation x2, other arithmetic, local(): cells = jnp.stack([source, conductivity])  1.81 us
  transfers between devices with their start and end apart: 11, of which 8 were waited for; matrix products, arithmetic and copies ran while one was open for 2% of the time, Pallas kernels for 1%

profile of v9, /device:TPU:443, one launch (start us, length us, event | category | flops | bytes accessed | tf_op | source)
XLA Modules:
  0.0 63.1 jit_solution(2496192760681681889)
XLA Ops:
  0.0 0.8 %fusion.11 = (f32[2,8,4,128]{3,2,1,0:T(4,128)S(1)}, f32[2,8,4,128]{3,2,1,0:T(4,128)S(1)}) fusion(f32[1,8,32,128]{3,2,1,0:T(8,128)} %bitcast.9, f32[1,8,32,128]{3,2,1,0:T(8,128)} %bitcast.11), kind=kLoop, calls=%fused_computation.30 | loop fusion | flops 16384 | bytes 327680 | tf_op jit(solution)/shard_map/stack | solution.py:475
  0.8 3.1 %collective-permute-start = (f32[2,8,4,128]{3,2,1,0:T(4,128)S(1)}, f32[2,8,4,128]{3,2,1,0:T(4,128)S(1)}, u32[]{:S(2)}, u32[]{:S(2)}) collective-permute-start(f32[2,8,4,128]{3,2,1,0:T(4,128)S(1)} %get-tuple-element.31), channel_id=1, source_target_pairs={{8,0},{16,8},{24,16},{32,24},{40,32},{48,40},{56,48},{9,1},{17,9},... | collective-permute-start | bytes 98312 | tf_op jit(solution)/shard_map/ppermute | solution.py:29
  3.9 2.2 %collective-permute-start.1 = (f32[2,8,4,128]{3,2,1,0:T(4,128)S(1)}, f32[2,8,4,128]{3,2,1,0:T(4,128)S(1)}, u32[]{:S(2)}, u32[]{:S(2)}) collective-permute-start(f32[2,8,4,128]{3,2,1,0:T(4,128)S(1)} %get-tuple-element.32), channel_id=1, source_target_pairs={{0,8},{8,16},{16,24},{24,32},{32,40},{40,48},{48,56},{1,9},{9,17},... | collective-permute-start | bytes 98312 | tf_op jit(solution)/shard_map/ppermute | solution.py:29
  6.1 1.0 %pad_maximum_fusion.2 = f32[2,8,32,128]{3,2,1,0:T(8,128)S(1)} fusion(f32[1,8,32,128]{3,2,1,0:T(8,128)} %bitcast.12, f32[1,8,32,128]{3,2,1,0:T(8,128)} %bitcast.10), kind=kLoop, calls=%fused_computation.5 | loop fusion | flops 65536 | bytes 524288 | tf_op jit(solution)/shard_map/stack | solution.py:475
  7.1 0.0 collective-permute-done
  7.1 1.4 %collective-permute-done.1 = f32[2,8,4,128]{3,2,1,0:T(4,128)S(1)} collective-permute-done((f32[2,8,4,128]{3,2,1,0:T(4,128)S(1)}, f32[2,8,4,128]{3,2,1,0:T(4,128)S(1)}, u32[]{:S(2)}, u32[]{:S(2)}) %collective-permute-start.1) | collective-permute-done | bytes 32800 | tf_op jit(solution)/shard_map/ppermute | solution.py:29
  8.6 0.4 fusion.9
  9.0 1.9 %collective-permute-start.2 = (f32[32,640]{1,0:T(8,128)S(1)}, f32[32,640]{1,0:T(8,128)S(1)}, u32[]{:S(2)}, u32[]{:S(2)}) collective-permute-start(f32[32,640]{1,0:T(8,128)S(1)} %get-tuple-element.33), channel_id=1, source_target_pairs={{1,0},{2,1},{3,2},{4,3},{5,4},{6,5},{7,6},{9,8},{10,9},{11,10},{12... | collective-permute-start | bytes 245768 | tf_op jit(solution)/shard_map/ppermute | solution.py:29
  10.9 6.1 %collective-permute-start.3 = (f32[32,640]{1,0:T(8,128)S(1)}, f32[32,640]{1,0:T(8,128)S(1)}, u32[]{:S(2)}, u32[]{:S(2)}) collective-permute-start(f32[32,640]{1,0:T(8,128)S(1)} %get-tuple-element.34), channel_id=1, source_target_pairs={{0,1},{1,2},{2,3},{3,4},{4,5},{5,6},{6,7},{8,9},{9,10},{10,11},{11... | collective-permute-start | bytes 245768 | tf_op jit(solution)/shard_map/ppermute | solution.py:29
  17.0 0.0 collective-permute-done.2
  17.0 0.1 fusion.17
  17.1 1.4 %collective-permute-done.3 = f32[32,640]{1,0:T(8,128)S(1)} collective-permute-done((f32[32,640]{1,0:T(8,128)S(1)}, f32[32,640]{1,0:T(8,128)S(1)}, u32[]{:S(2)}, u32[]{:S(2)}) %collective-permute-start.3) | collective-permute-done | bytes 81952 | tf_op jit(solution)/shard_map/ppermute | solution.py:29
  18.5 0.1 fusion.18
  18.6 0.3 fusion
  19.0 7.4 %collective-permute-start.4 = (f32[3,4,40,128]{3,2,1,0:T(8,128)S(1)}, f32[3,4,40,128]{3,2,1,0:T(8,128)S(1)}, u32[]{:S(2)}, u32[]{:S(2)}) collective-permute-start(f32[3,4,40,128]{3,2,1,0:T(8,128)S(1)} %get-tuple-element.29), channel_id=1, source_target_pairs={{64,128},{128,64},{192,256},{256,192},{320,384},{384,320},{448,512... | collective-permute-start | bytes 737288 | tf_op jit(solution)/shard_map/ppermute | solution.py:24
  26.4 1.9 %collective-permute-start.5 = (f32[3,4,40,128]{3,2,1,0:T(8,128)S(1)}, f32[3,4,40,128]{3,2,1,0:T(8,128)S(1)}, u32[]{:S(2)}, u32[]{:S(2)}) collective-permute-start(f32[3,4,40,128]{3,2,1,0:T(8,128)S(1)} %get-tuple-element.30), channel_id=1, source_target_pairs={{0,64},{64,0},{128,192},{192,128},{256,320},{320,256},{384,448},{4... | collective-permute-start | bytes 737288 | tf_op jit(solution)/shard_map/ppermute | solution.py:24
  28.3 0.6 %shard_map.28 = (f32[3,8,40,256]{3,2,1,0:T(8,128)S(1)}, f32[8,40,256]{2,1,0:T(8,128)S(1)}, f32[4,40,256]{2,1,0:T(8,128)S(1)}, f32[2,40,256]{2,1,0:T(8,128)S(1)}, f32[4,16,128]{2,1,0:T(8,128)S(1)}) custom-call(f32[3,8,40,128]{3,2,1,0:T(8,128)S(1)} %pad_maximum_fusion.1.cells), custom_call_target="tpu_custom_call" | custom-call | tf_op jit(solution)/shard_map/pallas_call | solution.py:444
  29.0 1.3 %collective-permute-done.4 = f32[3,4,40,128]{3,2,1,0:T(8,128)S(1)} collective-permute-done((f32[3,4,40,128]{3,2,1,0:T(8,128)S(1)}, f32[3,4,40,128]{3,2,1,0:T(8,128)S(1)}, u32[]{:S(2)}, u32[]{:S(2)}) %collective-permute-start.4) | collective-permute-done | bytes 245792 | tf_op jit(solution)/shard_map/ppermute | solution.py:24
  30.3 0.0 collective-permute-done.5
  30.3 0.1 pad_maximum_fusion.wide
  30.4 1.4 %shard_map.29 = (f32[2,4,16,128]{3,2,1,0:T(8,128)S(1)}, f32[2,4,12,128]{3,2,1,0:T(8,128)S(1)}, f32[2,4,12,128]{3,2,1,0:T(8,128)S(1)}, f32[4,12,40,256]{3,2,1,0:T(8,128)S(1)}) custom-call(f32[3,16,40,128]{3,2,1,0:T(8,128)S(1)} %pad_maximum_fusion.wide, f32[3,8,40,256]{3,2,1,0:T(8,128)S(1)} %get-tuple-element.16.own_faces, ...), custom_call_target="tpu_custom_call" | custom-call | tf_op jit(solution)/shard_map/pallas_call | solution.py:444
  31.8 3.4 %collective-permute-start.6 = (f32[2,4,12,128]{3,2,1,0:T(8,128)S(1)}, f32[2,4,12,128]{3,2,1,0:T(8,128)S(1)}, u32[]{:S(2)}, u32[]{:S(2)}) collective-permute-start(f32[2,4,12,128]{3,2,1,0:T(8,128)S(1)} %get-tuple-element.22), channel_id=1, source_target_pairs={{8,0},{16,8},{24,16},{32,24},{40,32},{48,40},{56,48},{9,1},{17,9},... | collective-permute-start | bytes 147464 | tf_op jit(solution)/shard_map/ppermute | solution.py:29
  35.2 1.9 %collective-permute-start.7 = (f32[2,4,12,128]{3,2,1,0:T(8,128)S(1)}, f32[2,4,12,128]{3,2,1,0:T(8,128)S(1)}, u32[]{:S(2)}, u32[]{:S(2)}) collective-permute-start(f32[2,4,12,128]{3,2,1,0:T(8,128)S(1)} %get-tuple-element.23), channel_id=1, source_target_pairs={{0,8},{8,16},{16,24},{24,32},{32,40},{40,48},{48,56},{1,9},{9,17},... | collective-permute-start | bytes 147464 | tf_op jit(solution)/shard_map/ppermute | solution.py:29
  37.1 0.6 collective-permute-done.6
  37.7 3.1 %collective-permute-done.7 = f32[2,4,12,128]{3,2,1,0:T(8,128)S(1)} collective-permute-done((f32[2,4,12,128]{3,2,1,0:T(8,128)S(1)}, f32[2,4,12,128]{3,2,1,0:T(8,128)S(1)}, u32[]{:S(2)}, u32[]{:S(2)}) %collective-permute-start.7) | collective-permute-done | bytes 49184 | tf_op jit(solution)/shard_map/ppermute | solution.py:29
  40.8 5.7 %collective-permute-start.8 = (f32[2,4,40,128]{3,2,1,0:T(8,128)S(1)}, f32[2,4,40,128]{3,2,1,0:T(8,128)S(1)}, u32[]{:S(2)}, u32[]{:S(2)}) collective-permute-start(f32[2,4,40,128]{3,2,1,0:T(8,128)S(1)} %pad_maximum_fusion.4), channel_id=1, source_target_pairs={{64,128},{128,64},{192,256},{256,192},{320,384},{384,320},{448,512... | collective-permute-start | bytes 491528 | tf_op jit(solution)/shard_map/ppermute | solution.py:24
  46.5 3.0 %collective-permute-done.8 = f32[2,4,40,128]{3,2,1,0:T(8,128)S(1)} collective-permute-done((f32[2,4,40,128]{3,2,1,0:T(8,128)S(1)}, f32[2,4,40,128]{3,2,1,0:T(8,128)S(1)}, u32[]{:S(2)}, u32[]{:S(2)}) %collective-permute-start.8) | collective-permute-done | bytes 163872 | tf_op jit(solution)/shard_map/ppermute | solution.py:24
  49.5 1.9 %collective-permute-start.9 = (f32[2,8,40,128]{3,2,1,0:T(8,128)S(1)}, f32[2,8,40,128]{3,2,1,0:T(8,128)S(1)}, u32[]{:S(2)}, u32[]{:S(2)}) collective-permute-start(f32[2,8,40,128]{3,2,1,0:T(8,128)S(1)} %maximum_select_fusion.1), channel_id=1, source_target_pairs={{0,64},{64,0},{128,192},{192,128},{256,320},{320,256},{384,448},{4... | collective-permute-start | bytes 983048 | tf_op jit(solution)/shard_map/ppermute | solution.py:24
  51.5 0.1 iota.43
  51.6 0.1 iota.46
  51.7 1.4 %collective-permute-done.9 = f32[2,8,40,128]{3,2,1,0:T(8,128)S(1)} collective-permute-done((f32[2,8,40,128]{3,2,1,0:T(8,128)S(1)}, f32[2,8,40,128]{3,2,1,0:T(8,128)S(1)}, u32[]{:S(2)}, u32[]{:S(2)}) %collective-permute-start.9) | collective-permute-done | bytes 327712 | tf_op jit(solution)/shard_map/ppermute | solution.py:24
  53.1 1.5 %shard_map.30 = (f32[8,24,128]{2,1,0:T(8,128)S(1)}, f32[2,16,24,128]{3,2,1,0:T(8,128)S(1)}) custom-call(f32[2,16,40,128]{3,2,1,0:T(8,128)S(1)} %maximum_select_fusion.narrow, f32[2,24,128]{2,1,0:T(8,128)S(1)} %pad_maximum_fusion.5.box, s32[1]{0:T(128)} %bitcast.4.parity), custom_call_target="tpu_custom_call" | custom-call | tf_op jit(solution)/shard_map/pallas_call | solution.py:444
  54.7 4.9 %collective-permute-start.10 = (f32[4,24,128]{2,1,0:T(8,128)S(1)}, f32[4,24,128]{2,1,0:T(8,128)S(1)}, u32[]{:S(2)}, u32[]{:S(2)}) collective-permute-start(f32[4,24,128]{2,1,0:T(8,128)S(1)} %slice_select_fusion.3), channel_id=1, source_target_pairs={{64,128},{128,64},{192,256},{256,192},{320,384},{384,320},{448,512... | collective-permute-start | bytes 147464 | tf_op jit(solution)/shard_map/ppermute | solution.py:24
  59.6 0.2 shard_map.31.filled
  59.7 1.5 %collective-permute-done.10 = f32[4,24,128]{2,1,0:T(8,128)S(1)} collective-permute-done((f32[4,24,128]{2,1,0:T(8,128)S(1)}, f32[4,24,128]{2,1,0:T(8,128)S(1)}, u32[]{:S(2)}, u32[]{:S(2)}) %collective-permute-start.10) | collective-permute-done | bytes 49184 | tf_op jit(solution)/shard_map/ppermute | solution.py:24
  61.3 1.8 %shard_map.32 = f32[8,32,128]{2,1,0:T(8,128)} custom-call(f32[12,24,128]{2,1,0:T(8,128)S(1)} %maximum_select_fusion.2.middle, f32[2,12,24,128]{3,2,1,0:T(8,128)S(1)} %slice_select_fusion.pair, f32[4,12,24,128]{3,2,1,0:T(8,128)S(1)} %shard_map.31.filled, f32[4,12,40,256]{3,2,1,0:T(8,128)S(1)} %get-tuple-element.26.kept), custom_call_target="tpu_custom_call" | custom-call | tf_op jit(solution)/shard_map/pallas_call | solution.py:444
  (14 shorter events, 0.3 us)
Async XLA Ops:
  0.8 6.3 %collective-permute-start = (f32[2,8,4,128]{3,2,1,0:T(4,128)S(1)}, f32[2,8,4,128]{3,2,1,0:T(4,128)S(1)}, u32[]{:S(2)}, u32[]{:S(2)}) collective-permute-start(f32[2,8,4,128]{3,2,1,0:T(4,128)S(1)} %get-tuple-element.31), channel_id=1, source_target_pairs={{8,0},{16,8},{24,16},{32,24},{40,32},{48,40},{56,48},{9,1},{17,9},... | collective-permute-start | bytes 98312 | tf_op jit(solution)/shard_map/ppermute | solution.py:29
  3.9 4.7 %collective-permute-start.1 = (f32[2,8,4,128]{3,2,1,0:T(4,128)S(1)}, f32[2,8,4,128]{3,2,1,0:T(4,128)S(1)}, u32[]{:S(2)}, u32[]{:S(2)}) collective-permute-start(f32[2,8,4,128]{3,2,1,0:T(4,128)S(1)} %get-tuple-element.32), channel_id=1, source_target_pairs={{0,8},{8,16},{16,24},{24,32},{32,40},{40,48},{48,56},{1,9},{9,17},... | collective-permute-start | bytes 98312 | tf_op jit(solution)/shard_map/ppermute | solution.py:29
  9.0 8.1 %collective-permute-start.2 = (f32[32,640]{1,0:T(8,128)S(1)}, f32[32,640]{1,0:T(8,128)S(1)}, u32[]{:S(2)}, u32[]{:S(2)}) collective-permute-start(f32[32,640]{1,0:T(8,128)S(1)} %get-tuple-element.33), channel_id=1, source_target_pairs={{1,0},{2,1},{3,2},{4,3},{5,4},{6,5},{7,6},{9,8},{10,9},{11,10},{12... | collective-permute-start | bytes 245768 | tf_op jit(solution)/shard_map/ppermute | solution.py:29
  10.9 7.6 %collective-permute-start.3 = (f32[32,640]{1,0:T(8,128)S(1)}, f32[32,640]{1,0:T(8,128)S(1)}, u32[]{:S(2)}, u32[]{:S(2)}) collective-permute-start(f32[32,640]{1,0:T(8,128)S(1)} %get-tuple-element.34), channel_id=1, source_target_pairs={{0,1},{1,2},{2,3},{3,4},{4,5},{5,6},{6,7},{8,9},{9,10},{10,11},{11... | collective-permute-start | bytes 245768 | tf_op jit(solution)/shard_map/ppermute | solution.py:29
  19.0 11.2 %collective-permute-start.4 = (f32[3,4,40,128]{3,2,1,0:T(8,128)S(1)}, f32[3,4,40,128]{3,2,1,0:T(8,128)S(1)}, u32[]{:S(2)}, u32[]{:S(2)}) collective-permute-start(f32[3,4,40,128]{3,2,1,0:T(8,128)S(1)} %get-tuple-element.29), channel_id=1, source_target_pairs={{64,128},{128,64},{192,256},{256,192},{320,384},{384,320},{448,512... | collective-permute-start | bytes 737288 | tf_op jit(solution)/shard_map/ppermute | solution.py:24
  26.4 3.9 %collective-permute-start.5 = (f32[3,4,40,128]{3,2,1,0:T(8,128)S(1)}, f32[3,4,40,128]{3,2,1,0:T(8,128)S(1)}, u32[]{:S(2)}, u32[]{:S(2)}) collective-permute-start(f32[3,4,40,128]{3,2,1,0:T(8,128)S(1)} %get-tuple-element.30), channel_id=1, source_target_pairs={{0,64},{64,0},{128,192},{192,128},{256,320},{320,256},{384,448},{4... | collective-permute-start | bytes 737288 | tf_op jit(solution)/shard_map/ppermute | solution.py:24
  31.8 5.9 %collective-permute-start.6 = (f32[2,4,12,128]{3,2,1,0:T(8,128)S(1)}, f32[2,4,12,128]{3,2,1,0:T(8,128)S(1)}, u32[]{:S(2)}, u32[]{:S(2)}) collective-permute-start(f32[2,4,12,128]{3,2,1,0:T(8,128)S(1)} %get-tuple-element.22), channel_id=1, source_target_pairs={{8,0},{16,8},{24,16},{32,24},{40,32},{48,40},{56,48},{9,1},{17,9},... | collective-permute-start | bytes 147464 | tf_op jit(solution)/shard_map/ppermute | solution.py:29
  35.2 5.6 %collective-permute-start.7 = (f32[2,4,12,128]{3,2,1,0:T(8,128)S(1)}, f32[2,4,12,128]{3,2,1,0:T(8,128)S(1)}, u32[]{:S(2)}, u32[]{:S(2)}) collective-permute-start(f32[2,4,12,128]{3,2,1,0:T(8,128)S(1)} %get-tuple-element.23), channel_id=1, source_target_pairs={{0,8},{8,16},{16,24},{24,32},{32,40},{40,48},{48,56},{1,9},{9,17},... | collective-permute-start | bytes 147464 | tf_op jit(solution)/shard_map/ppermute | solution.py:29
  40.8 8.7 %collective-permute-start.8 = (f32[2,4,40,128]{3,2,1,0:T(8,128)S(1)}, f32[2,4,40,128]{3,2,1,0:T(8,128)S(1)}, u32[]{:S(2)}, u32[]{:S(2)}) collective-permute-start(f32[2,4,40,128]{3,2,1,0:T(8,128)S(1)} %pad_maximum_fusion.4), channel_id=1, source_target_pairs={{64,128},{128,64},{192,256},{256,192},{320,384},{384,320},{448,512... | collective-permute-start | bytes 491528 | tf_op jit(solution)/shard_map/ppermute | solution.py:24
  49.5 3.5 %collective-permute-start.9 = (f32[2,8,40,128]{3,2,1,0:T(8,128)S(1)}, f32[2,8,40,128]{3,2,1,0:T(8,128)S(1)}, u32[]{:S(2)}, u32[]{:S(2)}) collective-permute-start(f32[2,8,40,128]{3,2,1,0:T(8,128)S(1)} %maximum_select_fusion.1), channel_id=1, source_target_pairs={{0,64},{64,0},{128,192},{192,128},{256,320},{320,256},{384,448},{4... | collective-permute-start | bytes 983048 | tf_op jit(solution)/shard_map/ppermute | solution.py:24
  54.7 6.6 %collective-permute-start.10 = (f32[4,24,128]{2,1,0:T(8,128)S(1)}, f32[4,24,128]{2,1,0:T(8,128)S(1)}, u32[]{:S(2)}, u32[]{:S(2)}) collective-permute-start(f32[4,24,128]{2,1,0:T(8,128)S(1)} %slice_select_fusion.3), channel_id=1, source_target_pairs={{64,128},{128,64},{192,256},{256,192},{320,384},{384,320},{448,512... | collective-permute-start | bytes 147464 | tf_op jit(solution)/shard_map/ppermute | solution.py:24

commit v10 on v9

--- a/solution.py
+++ b/solution.py
@@ -27,10 +27,6 @@
 def shift(block, axis, step):
     count = lax.axis_size(axis)
     return lax.ppermute(block, axis, [(i, i + step) for i in range(count) if 0 <= i + step < count])
-
-
-def cut(values, start, stop, dim):
-    return lax.slice_in_dim(values, start, stop, axis=dim)
 
 
 def join(pieces, dim):
@@ -464,7 +460,7 @@
     return rows.reshape(shape)
 
 
-def local(source, conductivity):
+def cycle(source, conductivity):
     low_x = lax.axis_index("gx") % 2 == 0
     low_y = lax.axis_index("gy") % 2 == 0
     odd_z = (lax.axis_index("gz") % 2).reshape(1)
@@ -543,4 +539,4 @@
 
 def solution(mesh):
     spec = P("gx", "gy", "gz")
-    return jax.shard_map(local, mesh=mesh, in_specs=(spec, spec), out_specs=spec, check_vma=False)
+    return jax.shard_map(cycle, mesh=mesh, in_specs=(spec, spec), out_specs=spec, check_vma=False)

time: 63.6 us -> 63.6 us (level)
  no operation moved by 1% of the time
where the time goes in v10:
time: 63.6 us; the launch traced here: 63.1 us
  starting transfers between devices  40.4 us (64%)
  waiting for transfers between devices  13.7 us (22%)
  Pallas kernels  5.6 us (9%)
  other arithmetic  2.17 us (3%)
  matrix products  0.7 us (1%)
    ppermute x5, starting transfers between devices, swap(): return lax.ppermute(block, axis, route)  21.8 us
    ppermute x6, starting transfers between devices, shift(): lax.ppermute(block, axis, [(i, i + step) for i in range(count) if 0 <= i...  18.6 us
    ppermute x5, waiting for transfers between devices, swap(): return lax.ppermute(block, axis, route)  7.24 us
    ppermute x6, waiting for transfers between devices, shift(): lax.ppermute(block, axis, [(i, i + step) for i in range(count) if 0 <= i...  6.46 us
    pallas_call x5, Pallas kernels, call(): pl.pallas_call(kernel, out_shape=[jax.ShapeDtypeStruct(shape, jnp.float32...  5.6 us
    another operation x2, other arithmetic, cycle(): cells = jnp.stack([source, conductivity])  1.81 us
  transfers between devices with their start and end apart: 11, of which 8 were waited for; matrix products, arithmetic and copies ran while one was open for 2% of the time, Pallas kernels for 1%

profile of v10, /device:TPU:443, one launch (start us, length us, event | category | flops | bytes accessed | tf_op | source)
XLA Modules:
  0.0 63.1 jit_solution(2496192760681681889)
XLA Ops:
  0.0 0.8 %fusion.11 = (f32[2,8,4,128]{3,2,1,0:T(4,128)S(1)}, f32[2,8,4,128]{3,2,1,0:T(4,128)S(1)}) fusion(f32[1,8,32,128]{3,2,1,0:T(8,128)} %bitcast.9, f32[1,8,32,128]{3,2,1,0:T(8,128)} %bitcast.11), kind=kLoop, calls=%fused_computation.30 | loop fusion | flops 16384 | bytes 327680 | tf_op jit(solution)/shard_map/stack | solution.py:471
  0.8 3.1 %collective-permute-start = (f32[2,8,4,128]{3,2,1,0:T(4,128)S(1)}, f32[2,8,4,128]{3,2,1,0:T(4,128)S(1)}, u32[]{:S(2)}, u32[]{:S(2)}) collective-permute-start(f32[2,8,4,128]{3,2,1,0:T(4,128)S(1)} %get-tuple-element.31), channel_id=1, source_target_pairs={{8,0},{16,8},{24,16},{32,24},{40,32},{48,40},{56,48},{9,1},{17,9},... | collective-permute-start | bytes 98312 | tf_op jit(solution)/shard_map/ppermute | solution.py:29
  3.9 2.2 %collective-permute-start.1 = (f32[2,8,4,128]{3,2,1,0:T(4,128)S(1)}, f32[2,8,4,128]{3,2,1,0:T(4,128)S(1)}, u32[]{:S(2)}, u32[]{:S(2)}) collective-permute-start(f32[2,8,4,128]{3,2,1,0:T(4,128)S(1)} %get-tuple-element.32), channel_id=1, source_target_pairs={{0,8},{8,16},{16,24},{24,32},{32,40},{40,48},{48,56},{1,9},{9,17},... | collective-permute-start | bytes 98312 | tf_op jit(solution)/shard_map/ppermute | solution.py:29
  6.1 1.0 %pad_maximum_fusion.2 = f32[2,8,32,128]{3,2,1,0:T(8,128)S(1)} fusion(f32[1,8,32,128]{3,2,1,0:T(8,128)} %bitcast.12, f32[1,8,32,128]{3,2,1,0:T(8,128)} %bitcast.10), kind=kLoop, calls=%fused_computation.5 | loop fusion | flops 65536 | bytes 524288 | tf_op jit(solution)/shard_map/stack | solution.py:471
  7.1 0.0 collective-permute-done
  7.1 1.4 %collective-permute-done.1 = f32[2,8,4,128]{3,2,1,0:T(4,128)S(1)} collective-permute-done((f32[2,8,4,128]{3,2,1,0:T(4,128)S(1)}, f32[2,8,4,128]{3,2,1,0:T(4,128)S(1)}, u32[]{:S(2)}, u32[]{:S(2)}) %collective-permute-start.1) | collective-permute-done | bytes 32800 | tf_op jit(solution)/shard_map/ppermute | solution.py:29
  8.6 0.4 fusion.9
  9.0 1.9 %collective-permute-start.2 = (f32[32,640]{1,0:T(8,128)S(1)}, f32[32,640]{1,0:T(8,128)S(1)}, u32[]{:S(2)}, u32[]{:S(2)}) collective-permute-start(f32[32,640]{1,0:T(8,128)S(1)} %get-tuple-element.33), channel_id=1, source_target_pairs={{1,0},{2,1},{3,2},{4,3},{5,4},{6,5},{7,6},{9,8},{10,9},{11,10},{12... | collective-permute-start | bytes 245768 | tf_op jit(solution)/shard_map/ppermute | solution.py:29
  10.9 6.1 %collective-permute-start.3 = (f32[32,640]{1,0:T(8,128)S(1)}, f32[32,640]{1,0:T(8,128)S(1)}, u32[]{:S(2)}, u32[]{:S(2)}) collective-permute-start(f32[32,640]{1,0:T(8,128)S(1)} %get-tuple-element.34), channel_id=1, source_target_pairs={{0,1},{1,2},{2,3},{3,4},{4,5},{5,6},{6,7},{8,9},{9,10},{10,11},{11... | collective-permute-start | bytes 245768 | tf_op jit(solution)/shard_map/ppermute | solution.py:29
  17.0 0.0 collective-permute-done.2
  17.0 0.1 fusion.17
  17.1 1.4 %collective-permute-done.3 = f32[32,640]{1,0:T(8,128)S(1)} collective-permute-done((f32[32,640]{1,0:T(8,128)S(1)}, f32[32,640]{1,0:T(8,128)S(1)}, u32[]{:S(2)}, u32[]{:S(2)}) %collective-permute-start.3) | collective-permute-done | bytes 81952 | tf_op jit(solution)/shard_map/ppermute | solution.py:29
  18.5 0.1 fusion.18
  18.6 0.3 fusion
  19.0 7.4 %collective-permute-start.4 = (f32[3,4,40,128]{3,2,1,0:T(8,128)S(1)}, f32[3,4,40,128]{3,2,1,0:T(8,128)S(1)}, u32[]{:S(2)}, u32[]{:S(2)}) collective-permute-start(f32[3,4,40,128]{3,2,1,0:T(8,128)S(1)} %get-tuple-element.29), channel_id=1, source_target_pairs={{64,128},{128,64},{192,256},{256,192},{320,384},{384,320},{448,512... | collective-permute-start | bytes 737288 | tf_op jit(solution)/shard_map/ppermute | solution.py:24
  26.4 1.9 %collective-permute-start.5 = (f32[3,4,40,128]{3,2,1,0:T(8,128)S(1)}, f32[3,4,40,128]{3,2,1,0:T(8,128)S(1)}, u32[]{:S(2)}, u32[]{:S(2)}) collective-permute-start(f32[3,4,40,128]{3,2,1,0:T(8,128)S(1)} %get-tuple-element.30), channel_id=1, source_target_pairs={{0,64},{64,0},{128,192},{192,128},{256,320},{320,256},{384,448},{4... | collective-permute-start | bytes 737288 | tf_op jit(solution)/shard_map/ppermute | solution.py:24
  28.3 0.6 %shard_map.28 = (f32[3,8,40,256]{3,2,1,0:T(8,128)S(1)}, f32[8,40,256]{2,1,0:T(8,128)S(1)}, f32[4,40,256]{2,1,0:T(8,128)S(1)}, f32[2,40,256]{2,1,0:T(8,128)S(1)}, f32[4,16,128]{2,1,0:T(8,128)S(1)}) custom-call(f32[3,8,40,128]{3,2,1,0:T(8,128)S(1)} %pad_maximum_fusion.1.cells), custom_call_target="tpu_custom_call" | custom-call | tf_op jit(solution)/shard_map/pallas_call | solution.py:440
  29.0 1.3 %collective-permute-done.4 = f32[3,4,40,128]{3,2,1,0:T(8,128)S(1)} collective-permute-done((f32[3,4,40,128]{3,2,1,0:T(8,128)S(1)}, f32[3,4,40,128]{3,2,1,0:T(8,128)S(1)}, u32[]{:S(2)}, u32[]{:S(2)}) %collective-permute-start.4) | collective-permute-done | bytes 245792 | tf_op jit(solution)/shard_map/ppermute | solution.py:24
  30.3 0.0 collective-permute-done.5
  30.3 0.1 pad_maximum_fusion.wide
  30.4 1.4 %shard_map.29 = (f32[2,4,16,128]{3,2,1,0:T(8,128)S(1)}, f32[2,4,12,128]{3,2,1,0:T(8,128)S(1)}, f32[2,4,12,128]{3,2,1,0:T(8,128)S(1)}, f32[4,12,40,256]{3,2,1,0:T(8,128)S(1)}) custom-call(f32[3,16,40,128]{3,2,1,0:T(8,128)S(1)} %pad_maximum_fusion.wide, f32[3,8,40,256]{3,2,1,0:T(8,128)S(1)} %get-tuple-element.16.own_faces, ...), custom_call_target="tpu_custom_call" | custom-call | tf_op jit(solution)/shard_map/pallas_call | solution.py:440
  31.8 3.4 %collective-permute-start.6 = (f32[2,4,12,128]{3,2,1,0:T(8,128)S(1)}, f32[2,4,12,128]{3,2,1,0:T(8,128)S(1)}, u32[]{:S(2)}, u32[]{:S(2)}) collective-permute-start(f32[2,4,12,128]{3,2,1,0:T(8,128)S(1)} %get-tuple-element.22), channel_id=1, source_target_pairs={{8,0},{16,8},{24,16},{32,24},{40,32},{48,40},{56,48},{9,1},{17,9},... | collective-permute-start | bytes 147464 | tf_op jit(solution)/shard_map/ppermute | solution.py:29
  35.2 1.9 %collective-permute-start.7 = (f32[2,4,12,128]{3,2,1,0:T(8,128)S(1)}, f32[2,4,12,128]{3,2,1,0:T(8,128)S(1)}, u32[]{:S(2)}, u32[]{:S(2)}) collective-permute-start(f32[2,4,12,128]{3,2,1,0:T(8,128)S(1)} %get-tuple-element.23), channel_id=1, source_target_pairs={{0,8},{8,16},{16,24},{24,32},{32,40},{40,48},{48,56},{1,9},{9,17},... | collective-permute-start | bytes 147464 | tf_op jit(solution)/shard_map/ppermute | solution.py:29
  37.1 0.6 collective-permute-done.6
  37.7 3.1 %collective-permute-done.7 = f32[2,4,12,128]{3,2,1,0:T(8,128)S(1)} collective-permute-done((f32[2,4,12,128]{3,2,1,0:T(8,128)S(1)}, f32[2,4,12,128]{3,2,1,0:T(8,128)S(1)}, u32[]{:S(2)}, u32[]{:S(2)}) %collective-permute-start.7) | collective-permute-done | bytes 49184 | tf_op jit(solution)/shard_map/ppermute | solution.py:29
  40.8 5.7 %collective-permute-start.8 = (f32[2,4,40,128]{3,2,1,0:T(8,128)S(1)}, f32[2,4,40,128]{3,2,1,0:T(8,128)S(1)}, u32[]{:S(2)}, u32[]{:S(2)}) collective-permute-start(f32[2,4,40,128]{3,2,1,0:T(8,128)S(1)} %pad_maximum_fusion.4), channel_id=1, source_target_pairs={{64,128},{128,64},{192,256},{256,192},{320,384},{384,320},{448,512... | collective-permute-start | bytes 491528 | tf_op jit(solution)/shard_map/ppermute | solution.py:24
  46.5 3.0 %collective-permute-done.8 = f32[2,4,40,128]{3,2,1,0:T(8,128)S(1)} collective-permute-done((f32[2,4,40,128]{3,2,1,0:T(8,128)S(1)}, f32[2,4,40,128]{3,2,1,0:T(8,128)S(1)}, u32[]{:S(2)}, u32[]{:S(2)}) %collective-permute-start.8) | collective-permute-done | bytes 163872 | tf_op jit(solution)/shard_map/ppermute | solution.py:24
  49.5 1.9 %collective-permute-start.9 = (f32[2,8,40,128]{3,2,1,0:T(8,128)S(1)}, f32[2,8,40,128]{3,2,1,0:T(8,128)S(1)}, u32[]{:S(2)}, u32[]{:S(2)}) collective-permute-start(f32[2,8,40,128]{3,2,1,0:T(8,128)S(1)} %maximum_select_fusion.1), channel_id=1, source_target_pairs={{0,64},{64,0},{128,192},{192,128},{256,320},{320,256},{384,448},{4... | collective-permute-start | bytes 983048 | tf_op jit(solution)/shard_map/ppermute | solution.py:24
  51.5 0.1 iota.43
  51.6 0.1 iota.46
  51.7 1.4 %collective-permute-done.9 = f32[2,8,40,128]{3,2,1,0:T(8,128)S(1)} collective-permute-done((f32[2,8,40,128]{3,2,1,0:T(8,128)S(1)}, f32[2,8,40,128]{3,2,1,0:T(8,128)S(1)}, u32[]{:S(2)}, u32[]{:S(2)}) %collective-permute-start.9) | collective-permute-done | bytes 327712 | tf_op jit(solution)/shard_map/ppermute | solution.py:24
  53.1 1.5 %shard_map.30 = (f32[8,24,128]{2,1,0:T(8,128)S(1)}, f32[2,16,24,128]{3,2,1,0:T(8,128)S(1)}) custom-call(f32[2,16,40,128]{3,2,1,0:T(8,128)S(1)} %maximum_select_fusion.narrow, f32[2,24,128]{2,1,0:T(8,128)S(1)} %pad_maximum_fusion.5.box, s32[1]{0:T(128)} %bitcast.4.parity), custom_call_target="tpu_custom_call" | custom-call | tf_op jit(solution)/shard_map/pallas_call | solution.py:440
  54.7 4.9 %collective-permute-start.10 = (f32[4,24,128]{2,1,0:T(8,128)S(1)}, f32[4,24,128]{2,1,0:T(8,128)S(1)}, u32[]{:S(2)}, u32[]{:S(2)}) collective-permute-start(f32[4,24,128]{2,1,0:T(8,128)S(1)} %slice_select_fusion.3), channel_id=1, source_target_pairs={{64,128},{128,64},{192,256},{256,192},{320,384},{384,320},{448,512... | collective-permute-start | bytes 147464 | tf_op jit(solution)/shard_map/ppermute | solution.py:24
  59.6 0.2 shard_map.31.filled
  59.7 1.5 %collective-permute-done.10 = f32[4,24,128]{2,1,0:T(8,128)S(1)} collective-permute-done((f32[4,24,128]{2,1,0:T(8,128)S(1)}, f32[4,24,128]{2,1,0:T(8,128)S(1)}, u32[]{:S(2)}, u32[]{:S(2)}) %collective-permute-start.10) | collective-permute-done | bytes 49184 | tf_op jit(solution)/shard_map/ppermute | solution.py:24
  61.3 1.8 %shard_map.32 = f32[8,32,128]{2,1,0:T(8,128)} custom-call(f32[12,24,128]{2,1,0:T(8,128)S(1)} %maximum_select_fusion.2.middle, f32[2,12,24,128]{3,2,1,0:T(8,128)S(1)} %slice_select_fusion.pair, f32[4,12,24,128]{3,2,1,0:T(8,128)S(1)} %shard_map.31.filled, f32[4,12,40,256]{3,2,1,0:T(8,128)S(1)} %get-tuple-element.26.kept), custom_call_target="tpu_custom_call" | custom-call | tf_op jit(solution)/shard_map/pallas_call | solution.py:440
  (14 shorter events, 0.3 us)
Async XLA Ops:
  0.8 6.3 %collective-permute-start = (f32[2,8,4,128]{3,2,1,0:T(4,128)S(1)}, f32[2,8,4,128]{3,2,1,0:T(4,128)S(1)}, u32[]{:S(2)}, u32[]{:S(2)}) collective-permute-start(f32[2,8,4,128]{3,2,1,0:T(4,128)S(1)} %get-tuple-element.31), channel_id=1, source_target_pairs={{8,0},{16,8},{24,16},{32,24},{40,32},{48,40},{56,48},{9,1},{17,9},... | collective-permute-start | bytes 98312 | tf_op jit(solution)/shard_map/ppermute | solution.py:29
  3.9 4.7 %collective-permute-start.1 = (f32[2,8,4,128]{3,2,1,0:T(4,128)S(1)}, f32[2,8,4,128]{3,2,1,0:T(4,128)S(1)}, u32[]{:S(2)}, u32[]{:S(2)}) collective-permute-start(f32[2,8,4,128]{3,2,1,0:T(4,128)S(1)} %get-tuple-element.32), channel_id=1, source_target_pairs={{0,8},{8,16},{16,24},{24,32},{32,40},{40,48},{48,56},{1,9},{9,17},... | collective-permute-start | bytes 98312 | tf_op jit(solution)/shard_map/ppermute | solution.py:29
  9.0 8.1 %collective-permute-start.2 = (f32[32,640]{1,0:T(8,128)S(1)}, f32[32,640]{1,0:T(8,128)S(1)}, u32[]{:S(2)}, u32[]{:S(2)}) collective-permute-start(f32[32,640]{1,0:T(8,128)S(1)} %get-tuple-element.33), channel_id=1, source_target_pairs={{1,0},{2,1},{3,2},{4,3},{5,4},{6,5},{7,6},{9,8},{10,9},{11,10},{12... | collective-permute-start | bytes 245768 | tf_op jit(solution)/shard_map/ppermute | solution.py:29
  10.9 7.6 %collective-permute-start.3 = (f32[32,640]{1,0:T(8,128)S(1)}, f32[32,640]{1,0:T(8,128)S(1)}, u32[]{:S(2)}, u32[]{:S(2)}) collective-permute-start(f32[32,640]{1,0:T(8,128)S(1)} %get-tuple-element.34), channel_id=1, source_target_pairs={{0,1},{1,2},{2,3},{3,4},{4,5},{5,6},{6,7},{8,9},{9,10},{10,11},{11... | collective-permute-start | bytes 245768 | tf_op jit(solution)/shard_map/ppermute | solution.py:29
  19.0 11.2 %collective-permute-start.4 = (f32[3,4,40,128]{3,2,1,0:T(8,128)S(1)}, f32[3,4,40,128]{3,2,1,0:T(8,128)S(1)}, u32[]{:S(2)}, u32[]{:S(2)}) collective-permute-start(f32[3,4,40,128]{3,2,1,0:T(8,128)S(1)} %get-tuple-element.29), channel_id=1, source_target_pairs={{64,128},{128,64},{192,256},{256,192},{320,384},{384,320},{448,512... | collective-permute-start | bytes 737288 | tf_op jit(solution)/shard_map/ppermute | solution.py:24
  26.4 3.9 %collective-permute-start.5 = (f32[3,4,40,128]{3,2,1,0:T(8,128)S(1)}, f32[3,4,40,128]{3,2,1,0:T(8,128)S(1)}, u32[]{:S(2)}, u32[]{:S(2)}) collective-permute-start(f32[3,4,40,128]{3,2,1,0:T(8,128)S(1)} %get-tuple-element.30), channel_id=1, source_target_pairs={{0,64},{64,0},{128,192},{192,128},{256,320},{320,256},{384,448},{4... | collective-permute-start | bytes 737288 | tf_op jit(solution)/shard_map/ppermute | solution.py:24
  31.8 5.9 %collective-permute-start.6 = (f32[2,4,12,128]{3,2,1,0:T(8,128)S(1)}, f32[2,4,12,128]{3,2,1,0:T(8,128)S(1)}, u32[]{:S(2)}, u32[]{:S(2)}) collective-permute-start(f32[2,4,12,128]{3,2,1,0:T(8,128)S(1)} %get-tuple-element.22), channel_id=1, source_target_pairs={{8,0},{16,8},{24,16},{32,24},{40,32},{48,40},{56,48},{9,1},{17,9},... | collective-permute-start | bytes 147464 | tf_op jit(solution)/shard_map/ppermute | solution.py:29
  35.2 5.6 %collective-permute-start.7 = (f32[2,4,12,128]{3,2,1,0:T(8,128)S(1)}, f32[2,4,12,128]{3,2,1,0:T(8,128)S(1)}, u32[]{:S(2)}, u32[]{:S(2)}) collective-permute-start(f32[2,4,12,128]{3,2,1,0:T(8,128)S(1)} %get-tuple-element.23), channel_id=1, source_target_pairs={{0,8},{8,16},{16,24},{24,32},{32,40},{40,48},{48,56},{1,9},{9,17},... | collective-permute-start | bytes 147464 | tf_op jit(solution)/shard_map/ppermute | solution.py:29
  40.8 8.7 %collective-permute-start.8 = (f32[2,4,40,128]{3,2,1,0:T(8,128)S(1)}, f32[2,4,40,128]{3,2,1,0:T(8,128)S(1)}, u32[]{:S(2)}, u32[]{:S(2)}) collective-permute-start(f32[2,4,40,128]{3,2,1,0:T(8,128)S(1)} %pad_maximum_fusion.4), channel_id=1, source_target_pairs={{64,128},{128,64},{192,256},{256,192},{320,384},{384,320},{448,512... | collective-permute-start | bytes 491528 | tf_op jit(solution)/shard_map/ppermute | solution.py:24
  49.5 3.5 %collective-permute-start.9 = (f32[2,8,40,128]{3,2,1,0:T(8,128)S(1)}, f32[2,8,40,128]{3,2,1,0:T(8,128)S(1)}, u32[]{:S(2)}, u32[]{:S(2)}) collective-permute-start(f32[2,8,40,128]{3,2,1,0:T(8,128)S(1)} %maximum_select_fusion.1), channel_id=1, source_target_pairs={{0,64},{64,0},{128,192},{192,128},{256,320},{320,256},{384,448},{4... | collective-permute-start | bytes 983048 | tf_op jit(solution)/shard_map/ppermute | solution.py:24
  54.7 6.6 %collective-permute-start.10 = (f32[4,24,128]{2,1,0:T(8,128)S(1)}, f32[4,24,128]{2,1,0:T(8,128)S(1)}, u32[]{:S(2)}, u32[]{:S(2)}) collective-permute-start(f32[4,24,128]{2,1,0:T(8,128)S(1)} %slice_select_fusion.3), channel_id=1, source_target_pairs={{64,128},{128,64},{192,256},{256,192},{320,384},{384,320},{448,512... | collective-permute-start | bytes 147464 | tf_op jit(solution)/shard_map/ppermute | solution.py:24
